TPU v7x, 128 devices: a whole 4x4x4 slice. The times are simulated.
128 devices in a mesh: batch: 8 (over x, core), ctx: 16 (over y, z).
Axes of the slice: x: 4, y: 4, z: 4, core: 2. Of those that a mesh axis runs over, the one named last changes fastest.
Arguments:
- event_rows: bfloat16 [8, 4096, 256], P('batch', 'ctx'), may hold values from -6 to 6
- event_index: int32 [8, 4096], P('batch', 'ctx'), may hold values from 0 to 65535, as said below
- decay: float32 [8, 16, 4096], P('batch', None, 'ctx'), may hold values from 0.15 to 1
- saved_state: float32 [8, 16, 16, 128, 64], P('batch', 'ctx'), may hold values from -6 to 6
- dout: bfloat16 [8, 4096, 512], P('batch', 'ctx'), may hold values from -0.29882812 to 0.29882812
- w_up: bfloat16 [256, 512], replicated, may hold values from -0.375 to 0.375
- w_in: bfloat16 [512, 1280], replicated, may hold values from -0.25 to 0.25
- w_out: bfloat16 [1024, 512], replicated, may hold values from -0.1875 to 0.1875
- skip: float32 [16], replicated, may hold values from 0.5 to 2
Outputs:
- grad_up: float32 [256, 512], replicated
- grad_in: float32 [512, 1280], replicated
- grad_out: float32 [1024, 512], replicated
- grad_skip: float32 [16], replicated
- grad_table: float32 [65536, 256], P(('batch', 'ctx'))
Inputs may be any that keep to these rules, and one draw needn't show every extreme that they name: `event_index`: rows are in blocks of 512; block k is held by device k of batch+ctx. The 256 events of one device name rows of at most 4 events in any one block, and in every draw some block is named by exactly 4 events of every device.
All inputs are finite; a program needn't handle non-finite values.
Results may differ from a plain program's by a relative error of at most 0.011.
Values may be sent and summed in bfloat16 or wider, within the bound.
No kernel may reach another device: no remote copies, remote signals or barrier semaphores. Data moves between devices by JAX's collectives and lax.ppermute only.
A program may use at most 128 MiB of HBM per device.

v0:
```python
from functools import partial

import jax
import jax.numpy as jnp
from jax import lax
from jax.sharding import PartitionSpec as P

CH = 256
ROWS_DEV = 512


STEP_SIZE = 0.0625
exact_sum = partial(jnp.einsum, precision=lax.Precision.HIGHEST)
plain_sum = partial(jnp.einsum, preferred_element_type=jnp.float32)


def entering(part, axis, combine, identity):
    count = lax.axis_size(axis)
    place = lax.axis_index(axis)
    ahead = count - 1 - place
    gathered = jax.tree.map(lambda a: lax.all_gather(a, axis), part)
    state = jax.tree.map(lambda a, e: jnp.zeros_like(a) + jnp.asarray(e, a.dtype), part, identity)

    def one(lap, state):
        source = count - 1 - lap
        return combine(
            state, jax.tree.map(lambda a: lax.dynamic_index_in_dim(a, source, 0, False), gathered)
        )

    return lax.fori_loop(0, ahead, one, state)


def block_parts(log_decay):
    cum_log = jnp.cumsum(log_decay, axis=1)
    length = log_decay.shape[1]
    causal = jnp.arange(length)[:, None] >= jnp.arange(length)[None, :]
    log_gap = cum_log[:, :, None] - cum_log[:, None, :]
    decay_mask = jnp.where(causal[None], jnp.exp(jnp.where(causal[None], log_gap, 0.0)), 0.0)
    return (cum_log, decay_mask)


def forward_block(h_start, x_half, b_half, c_half, log_decay, skip):
    state_scale = c_half.shape[1] ** (-0.5)
    x_part = x_half.astype(jnp.float32)
    b_part = b_half.astype(jnp.float32)
    c_part = c_half.astype(jnp.float32)
    cum_log, decay_mask = block_parts(log_decay)
    start_decay = jnp.exp(cum_log)
    c_dot_b = plain_sum("tn,sn->ts", c_half, b_half)
    within = STEP_SIZE * exact_sum("hts,ts,shp->thp", decay_mask, c_dot_b, x_part)
    from_start = exact_sum("tn,hnp->thp", c_part, h_start) * start_decay.T[:, :, None]
    y_out = state_scale * (from_start + within) + skip[None, :, None] * x_part
    tail_decay = jnp.exp(cum_log[:, -1:] - cum_log)
    h_end = jnp.exp(cum_log[:, -1])[:, None, None] * h_start + STEP_SIZE * exact_sum(
        "hs,sn,shp->hnp", tail_decay, b_part, x_part
    )
    return (y_out, h_end)


def block_summary(c_half, dy_half, log_decay):
    state_scale = c_half.shape[1] ** (-0.5)
    cum_log = jnp.cumsum(log_decay, axis=1)
    amount = jnp.exp(cum_log[:, -1])
    block_sums = state_scale * exact_sum(
        "ht,tn,thp->hnp", jnp.exp(cum_log), c_half.astype(jnp.float32), dy_half.astype(jnp.float32)
    )
    return (amount, block_sums)


def backward_block(carry_in, h_start, x_half, b_half, c_half, dy_half, log_decay, skip):
    state_scale = c_half.shape[1] ** (-0.5)
    x_part = x_half.astype(jnp.float32)
    b_part = b_half.astype(jnp.float32)
    c_part = c_half.astype(jnp.float32)
    dy_part = dy_half.astype(jnp.float32)
    cum_log, decay_mask = block_parts(log_decay)
    start_decay = jnp.exp(cum_log)
    tail_decay = jnp.exp(cum_log[:, -1:] - cum_log)
    mask_back = jnp.swapaxes(decay_mask, 1, 2)
    b_dot_c = plain_sum("tn,sn->ts", b_half, c_half)
    x_dot_dy = plain_sum("thp,shp->hts", x_half, dy_half)
    dy_dot_x = jnp.swapaxes(x_dot_dy, 1, 2)
    dx_part = (
        STEP_SIZE
        * (
            state_scale * exact_sum("hts,ts,shp->thp", mask_back, b_dot_c, dy_part)
            + tail_decay.T[:, :, None] * exact_sum("tn,hnp->thp", b_part, carry_in)
        )
        + skip[None, :, None] * dy_part
    )
    db_part = STEP_SIZE * (
        state_scale * exact_sum("hts,sn->tn", mask_back * x_dot_dy, c_part)
        + exact_sum("ht,hnp,thp->tn", tail_decay, carry_in, x_part)
    )
    dc_part = state_scale * (
        exact_sum("ht,hnp,thp->tn", start_decay, h_start, dy_part)
        + STEP_SIZE * exact_sum("hts,sn->tn", decay_mask * dy_dot_x, b_part)
    )
    dskip_part = plain_sum("thp,thp->h", x_half, dy_half)
    return (dx_part, db_part, dc_part, dskip_part)


def combine_pieces(earlier_item, later_item):
    return (
        later_item[0] * earlier_item[0],
        later_item[1] + later_item[0][:, None, None] * earlier_item[1],
    )


def local(event_rows, event_index, decay, saved_state, dout, w_up, w_in, w_out, skip):
    history_rows = event_rows[0]
    history_dout = dout[0]
    tokens = history_rows.shape[0]
    width = history_rows.shape[1]
    inner_width = w_out.shape[0]
    head_count = skip.shape[0]
    head_size = inner_width // head_count
    state_width = (w_in.shape[1] - inner_width) // 2
    block_count = tokens // CH
    batch_count = lax.axis_size("batch")
    piece_count = lax.axis_size("ctx")
    owner_count = batch_count * piece_count
    capacity = max(2, 2 * tokens // owner_count)
    owners = event_index[0] // ROWS_DEV
    local_row = event_index[0] - owners * ROWS_DEV
    owner_hits = (owners[:, None] == jnp.arange(owner_count, dtype=jnp.int32)[None, :]).astype(
        jnp.int32
    )
    bucket_rank = jnp.sum((jnp.cumsum(owner_hits, axis=0) - owner_hits) * owner_hits, axis=1)
    send_slot = owners * capacity + bucket_rank
    slot_rows = (
        jnp.full((owner_count * capacity,), ROWS_DEV, jnp.int32).at[send_slot].set(local_row)
    )
    received_rows = lax.all_to_all(
        slot_rows.reshape(owner_count, capacity),
        ("batch", "ctx"),
        split_axis=0,
        concat_axis=0,
        tiled=True,
    )
    u_rows = jnp.dot(history_rows, w_up, preferred_element_type=jnp.float32).astype(jnp.bfloat16)
    projected = jnp.dot(u_rows, w_in, preferred_element_type=jnp.float32).astype(jnp.bfloat16)
    dy_rows = jnp.dot(history_dout, w_out.T, preferred_element_type=jnp.float32).astype(
        jnp.bfloat16
    )
    x_all = projected[:, :inner_width].reshape(block_count, CH, head_count, head_size)
    b_all = projected[:, inner_width : inner_width + state_width].reshape(
        block_count, CH, state_width
    )
    c_all = projected[:, inner_width + state_width :].reshape(block_count, CH, state_width)
    dy_all = dy_rows.reshape(block_count, CH, head_count, head_size)
    log_all = jnp.log(decay[0]).reshape(head_count, block_count, CH).transpose(1, 0, 2)

    def forward_step(h_state, block):
        x_part, b_part, c_part, log_decay = block
        y_out, h_end = forward_block(h_state, x_part, b_part, c_part, log_decay, skip)
        return (h_end, (y_out, h_state))

    _, (y_blocks, starts) = lax.scan(
        forward_step, saved_state[0, 0], (x_all, b_all, c_all, log_all)
    )
    y_rows = y_blocks.reshape(tokens, inner_width).astype(jnp.bfloat16)
    grad_out = jnp.dot(y_rows.T, history_dout, preferred_element_type=jnp.float32)
    amounts, block_sums = jax.vmap(block_summary)(c_all, dy_all, log_all)

    def local_step(carried, block):
        local_carry, later_decay = carried
        amount, sums_here = block
        return (
            (sums_here + amount[:, None, None] * local_carry, amount * later_decay),
            (local_carry, later_decay),
        )

    zero_state = jnp.zeros((head_count, state_width, head_size), jnp.float32)
    (piece_sums, piece_amount), (local_carries, later_decays) = lax.scan(
        local_step,
        (zero_state, jnp.ones((head_count,), jnp.float32)),
        (amounts, block_sums),
        reverse=True,
    )
    _, outside_carry = entering(
        (piece_amount, piece_sums),
        "ctx",
        combine_pieces,
        (jnp.ones_like(piece_amount), jnp.zeros_like(piece_sums)),
    )
    block_carries = local_carries + later_decays[:, :, None, None] * outside_carry[None]

    def backward_step(block):
        carry_in, h_start, x_part, b_part, c_part, dy_part, log_decay = block
        return backward_block(carry_in, h_start, x_part, b_part, c_part, dy_part, log_decay, skip)

    dx_all, db_all, dc_all, dskip_all = lax.map(
        backward_step, (block_carries, starts, x_all, b_all, c_all, dy_all, log_all)
    )
    grad_skip = jnp.sum(dskip_all, axis=0)
    dprojected = jnp.concatenate(
        [
            dx_all.reshape(tokens, inner_width),
            db_all.reshape(tokens, state_width),
            dc_all.reshape(tokens, state_width),
        ],
        axis=1,
    ).astype(jnp.bfloat16)
    grad_in = jnp.dot(u_rows.T, dprojected, preferred_element_type=jnp.float32)
    du_rows = jnp.dot(dprojected, w_in.T, preferred_element_type=jnp.float32).astype(jnp.bfloat16)
    grad_up = jnp.dot(history_rows.T, du_rows, preferred_element_type=jnp.float32)
    de_rows = jnp.dot(du_rows, w_up.T, preferred_element_type=jnp.float32).astype(jnp.bfloat16)
    send_rows = jnp.zeros((owner_count * capacity, width), jnp.bfloat16).at[send_slot].set(de_rows)
    arrived = lax.all_to_all(
        send_rows.reshape(owner_count, capacity, width),
        ("batch", "ctx"),
        split_axis=0,
        concat_axis=0,
        tiled=True,
    )
    arrived = arrived.reshape(owner_count * capacity, width)
    grad_table = jax.ops.segment_sum(
        arrived.astype(jnp.float32), received_rows.reshape(-1), num_segments=ROWS_DEV + 1
    )[:ROWS_DEV]
    grad_up, grad_in, grad_out, grad_skip = lax.psum(
        (grad_up, grad_in, grad_out, grad_skip), ("batch", "ctx")
    )
    return (grad_up, grad_in, grad_out, grad_skip, grad_table)


def solution(mesh):
    in_specs = (
        P("batch", "ctx", None),
        P("batch", "ctx"),
        P("batch", None, "ctx"),
        P("batch", "ctx", None, None, None),
        P("batch", "ctx", None),
        P(),
        P(),
        P(),
        P(),
    )
    out_specs = (P(), P(), P(), P(), P(("batch", "ctx"), None))
    return jax.shard_map(local, mesh=mesh, in_specs=in_specs, out_specs=out_specs, check_vma=False)
```

profile of v0, /device:TPU:1, one launch (start us, length us, event | category | flops | bytes accessed | tf_op | source)
XLA Modules:
  0.0 335.1 jit_solution(3388913136029684892)
XLA Ops:
  17.1 2.7 fusion.106
  19.9 5.4 %copy.86 = f32[16,256,256]{1,2,0:T(8,128)} copy(f32[16,256,256]{2,1,0:T(8,128)} %fusion.106) | data formatting | bytes 8388608 | tf_op jit(solution)/shard_map/while/body/eval_jaxpr/thp,shp->hts/dot_general | solution.py:81
  25.3 21.9 %all-gather = f32[16,16,1]{1,2,0:T(1,128)} all-gather(f32[1,16,1]{1,2,0:T(1,128)} %copy.82), channel_id=2, replica_groups=mesh['batch'=8,'ctx'=16] {'ctx'}, dimensions={0}, use_global_device_ids=true | all-gather | bytes 1088 | tf_op jit(solution)/shard_map/all_gather | solution.py:21
  51.7 5.7 %multiply_reduce_fusion = (f32[256,256]{0,1:T(8,128)}, f32[256,256]{0,1:T(8,128)S(1)}) fusion(f32[16,256,256]{1,2,0:T(8,128)} %copy.86, f32[16,256]{1,0:T(8,128)S(1)} %copy_bitcast_fusion, pred[256,256]{0,1:T(8,128)(4,1)S(1)} %get-tuple-element.241, f32[16,256,256]{2,1,0:T(8,128)} %fusion.106, pred[256,256]{0,1:T(8,128)(4,1)S(1)} %get-tuple-element.240), kind=kLoop, calls=%fused_computation.14 | loop fusion | flops 10354688 | bytes 9060352 | tf_op jit(solution)/shard_map/while/body/eval_jaxpr/hts,sn->tn/reduce_sum | solution.py:92
  58.9 3.1 fusion.47
  63.8 25.3 %all-gather.3.cloned.1.call-done = f32[16,16,128,64]{2,3,1,0:T(8,128)} async-done(((f32[1,16,128,64]{2,3,1,0:T(8,128)}), f32[16,16,128,64]{2,3,1,0:T(8,128)}) %all-gather.3.cloned.1.call-update) | async-done | bytes 8388624 | tf_op jit(solution)/shard_map/all_gather | solution.py:21
  89.2 63.3 %while.9 = (s32[]{:T(128)}, f32[16,128,64]{2,1,0:T(8,128)S(1)}, s32[]{:T(128)}, f32[16,16,128,64]{2,3,1,0:T(8,128)}, f32[16,16]{1,0:T(8,128)}, /*index=5*/s32[]{:T(128)}, s32[]{:T(128)}, s32[]{:T(128)}, s32[]{:T(128)}) while((s32[]{:T(128)}, f32[16,128,64]{2,1,0:T(8,128)S(1)}, s32[]{:T(128)}, f32[16,16,128,64]{2,3,1,0:T(8,128)}, ...), condition=%wide.region_5.6_spmd, body=%wide.region_4.5_spmd.sunk | while | flops 262150 | bytes 3670355 | solution.py:30
  97.7 1.9 constant_dynamic-slice_fusion.2
  101.9 1.9 constant_dynamic-slice_fusion.2
  114.5 1.9 constant_dynamic-slice_fusion.2
  135.5 1.9 constant_dynamic-slice_fusion.2
  139.7 1.9 constant_dynamic-slice_fusion.2
  144.0 1.9 constant_dynamic-slice_fusion.2
  152.9 2.2 convolution_bitcast_fusion.2
  157.8 4.1 %fusion.50 = bf16[256,16,64]{0,2,1:T(8,128)(2,1)S(1)} fusion(bf16[256,16,64]{0,2,1:T(8,128)(2,1)S(1)} %bitcast.200, f32[256,256]{0,1:T(8,128)} %fusion.88, f32[16,256]{1,0:T(8,128)S(1)} %copy-done.17, pred[256,256]{0,1:T(8,128)(4,1)S(1)} %copy-done.14, f32[256,16,64]{0,2,1:T(8,128)S(1)} %bitcast.208, f32[16]{0:T(128)S(1)} %copy-done.20, ...), kind=kOutput, calls=%fused_computation.45 | convolution fusion | flops 811597824 | bytes 2457664 | tf_op jit(solution)/shard_map/while/body/eval_jaxpr/hts,ts,shp->thp/dot_general | solution.py:86
  161.9 2.0 fusion.67
  168.4 4.5 %all-to-all-start = ((s32[128,1,4]{2,1,0:T(1,128)}), s32[128,1,4]{2,1,0:T(1,128)S(1)}, u32[]{:S(2)}, u32[]{:S(2)}) async-start(s32[128,1,4]{2,1,0:T(1,128)} %bitcast.47), calls=%async_computation | async-start | bytes 131072 | tf_op jit(solution)/shard_map/all_to_all | solution.py:134
  175.5 7.0 %all-to-all-done = s32[128,1,4]{2,1,0:T(1,128)S(1)} async-done(((s32[128,1,4]{2,1,0:T(1,128)}), s32[128,1,4]{2,1,0:T(1,128)S(1)}, u32[]{:S(2)}, u32[]{:S(2)}) %all-to-all-start) | async-done | bytes 2080 | tf_op jit(solution)/shard_map/all_to_all | solution.py:134
  182.5 4.5 %all-to-all-start.1 = ((bf16[128,4,256]{2,1,0:T(4,128)(2,1)}), bf16[128,4,256]{2,1,0:T(4,128)(2,1)S(1)}, u32[]{:S(2)}, u32[]{:S(2)}) async-start(bf16[128,4,256]{2,1,0:T(4,128)(2,1)} %reshape.323), calls=%async_computation.1 | async-start | bytes 524288 | tf_op jit(solution)/shard_map/all_to_all | solution.py:210
  187.3 67.8 %psum.31 = f32[16]{0:T(128)} all-reduce(f32[16]{0:T(128)S(1)} %fusion.62), channel_id=1, replica_groups=mesh['batch'=8,'ctx'=16] {'batch','ctx'}, use_global_device_ids=true, to_apply=%region_11.12 | all-reduce | flops 16 | bytes 128 | tf_op jit(solution)/shard_map/psum | solution.py:221
  256.5 3.4 %scatter_custom_fusion.2 = f32[513,256]{1,0:T(8,128)S(1)} fusion(s32[512]{0:T(512)S(1)} %reshape.343, f32[512,256]{1,0:T(8,128)S(1)} %reshape.345, f32[]{:T(128)} %constant.131.clone.1), kind=kCustom, calls=%fused_computation.72 | custom fusion | flops 131072 | bytes 525316 | tf_op jit(solution)/shard_map/scatter-add | solution.py:218
  260.8 60.5 %all-reduce.3.cloned.1.call-done = (f32[256,512]{0,1:T(8,128)}, f32[512,1280]{1,0:T(8,128)}, f32[1024,512]{1,0:T(8,128)}) async-done(((f32[256,512]{0,1:T(8,128)}, f32[512,1280]{1,0:T(8,128)}, f32[1024,512]{1,0:T(8,128)}), (f32[256,512]{0,1:T(8,128)}, f32[512,1280]{1,0:T(8,128)}, f32[1024,512]{1,0:T(8,128)})) %all-reduce.3.cloned.1.call-update) | async-done | bytes 5242896 | tf_op jit(solution)/shard_map/psum | solution.py:221
  321.3 2.2 copy.93
  323.5 3.4 %copy.134 = f32[512,1280]{1,0:T(8,128)} copy(f32[512,1280]{1,0:T(8,128)} %get-tuple-element.302) | data formatting | bytes 5242880
  (167 shorter events, 82.7 us)
Async XLA Ops:
  7.2 5.2 %copy-start = (bf16[512,1280]{1,0:T(8,128)(2,1)S(1)}, bf16[512,1280]{1,0:T(8,128)(2,1)}, u32[]{:S(2)}) copy-start(bf16[512,1280]{1,0:T(8,128)(2,1)} %param.17) | copy-start | bytes 3932164
  7.2 81.9 %all-gather.3.cloned.1.call-start = ((), (), s32[]{:S(2)}) async-start(), calls=%async_computation.2 | async-start | bytes 8912896 | tf_op jit(solution)/shard_map/all_gather | solution.py:21
  11.0 38.6 %copy-start.1 = (bf16[256,1024]{0,1:T(8,128)(2,1)}, bf16[256,1024]{0,1:T(8,128)(2,1)S(1)}, u32[]{:S(2)}) copy-start(bf16[256,1024]{0,1:T(8,128)(2,1)S(1)} %copy.76) | copy-start | bytes 1572868
  12.4 3.9 %copy-start.6 = (bf16[256,512]{1,0:T(8,128)(2,1)}, bf16[256,512]{1,0:T(8,128)(2,1)S(1)}, u32[]{:S(2)}) copy-start(bf16[256,512]{1,0:T(8,128)(2,1)S(1)} %convolution_convert_fusion.3) | copy-start | bytes 786436
  12.9 45.4 %copy-start.5 = (bf16[256,1280]{1,0:T(8,128)(2,1)}, bf16[256,1280]{1,0:T(8,128)(2,1)S(1)}, u32[]{:S(2)}) copy-start(bf16[256,1280]{1,0:T(8,128)(2,1)S(1)} %convolution_convert_fusion) | copy-start | bytes 1966084
  14.8 306.5 %all-reduce.3.cloned.1.call-start = ((), (), s32[]{:S(2)}) async-start(), calls=%async_computation.3 | async-start | bytes 10485760 | tf_op jit(solution)/shard_map/psum | solution.py:221
  17.1 41.8 %copy-start.3 = (bf16[256,1024]{0,1:T(8,128)(2,1)}, bf16[256,1024]{0,1:T(8,128)(2,1)S(1)}, u32[]{:S(2)}) copy-start(bf16[256,1024]{0,1:T(8,128)(2,1)S(1)} %copy.85) | copy-start | bytes 1572868
  19.9 29.7 %copy-start.8 = (f32[1,1,16,128,64]{3,4,2,1,0:T(8,128)S(1)}, f32[1,1,16,128,64]{3,4,2,1,0:T(8,128)}, u32[]{:S(2)}) copy-start(f32[1,1,16,128,64]{3,4,2,1,0:T(8,128)} %param.14) | copy-start | bytes 1572868
  47.9 11.0 %copy-start.16 = (f32[16,256]{1,0:T(8,128)}, f32[16,256]{1,0:T(8,128)S(1)}, u32[]{:S(2)}) copy-start(f32[16,256]{1,0:T(8,128)S(1)} %copy_bitcast_fusion) | copy-start | bytes 49156
  48.1 9.3 %copy-start.13 = (pred[256,256]{0,1:T(8,128)(4,1)}, pred[256,256]{0,1:T(8,128)(4,1)S(1)}, u32[]{:S(2)}) copy-start(pred[256,256]{0,1:T(8,128)(4,1)S(1)} %get-tuple-element.241) | copy-start | bytes 196612
  51.7 7.2 %copy-start.20 = (f32[16]{0:T(128)S(1)}, f32[16]{0:T(128)}, u32[]{:S(2)}) copy-start(f32[16]{0:T(128)} %param.19) | copy-start | bytes 196
  58.9 3.1 copy-start.11
  89.2 63.7 %copy-start.18 = (f32[256,16]{0,1:T(8,128)S(1)}, f32[256,16]{0,1:T(8,128)}, u32[]{:S(2)}) copy-start(f32[256,16]{0,1:T(8,128)} %get-tuple-element.236) | copy-start | bytes 49156
  152.5 5.2 %copy-start.2 = (bf16[256,1024]{0,1:T(8,128)(2,1)S(1)}, bf16[256,1024]{0,1:T(8,128)(2,1)}, u32[]{:S(2)}) copy-start(bf16[256,1024]{0,1:T(8,128)(2,1)} %copy-done.1) | copy-start | bytes 1572868
  152.5 5.2 %copy-start.14 = (pred[256,256]{0,1:T(8,128)(4,1)S(1)}, pred[256,256]{0,1:T(8,128)(4,1)}, u32[]{:S(2)}) copy-start(pred[256,256]{0,1:T(8,128)(4,1)} %copy-done.13) | copy-start | bytes 196612
  152.6 5.2 %copy-start.17 = (f32[16,256]{1,0:T(8,128)S(1)}, f32[16,256]{1,0:T(8,128)}, u32[]{:S(2)}) copy-start(f32[16,256]{1,0:T(8,128)} %copy-done.16) | copy-start | bytes 49156
  157.8 4.1 %copy-start.7 = (bf16[256,512]{1,0:T(8,128)(2,1)S(1)}, bf16[256,512]{1,0:T(8,128)(2,1)}, u32[]{:S(2)}) copy-start(bf16[256,512]{1,0:T(8,128)(2,1)} %copy-done.6) | copy-start | bytes 786436
  157.8 4.1 %copy-start.15 = (bf16[256,128]{0,1:T(8,128)(2,1)S(1)}, bf16[256,128]{0,1:T(8,128)(2,1)}, u32[]{:S(2)}) copy-start(bf16[256,128]{0,1:T(8,128)(2,1)} %fusion.61) | copy-start | bytes 196612
  161.9 2.7 copy-start.12
  164.5 8.4 %copy-start.10 = (bf16[256,512]{1,0:T(8,128)(2,1)S(1)}, bf16[256,512]{1,0:T(8,128)(2,1)}, u32[]{:S(2)}) copy-start(bf16[256,512]{1,0:T(8,128)(2,1)} %param.16) | copy-start | bytes 786436
  165.6 21.4 %copy-start.4 = (bf16[256,1024]{0,1:T(8,128)(2,1)S(1)}, bf16[256,1024]{0,1:T(8,128)(2,1)}, u32[]{:S(2)}) copy-start(bf16[256,1024]{0,1:T(8,128)(2,1)} %copy-done.3) | copy-start | bytes 1572868
  168.4 14.1 %all-to-all-start = ((s32[128,1,4]{2,1,0:T(1,128)}), s32[128,1,4]{2,1,0:T(1,128)S(1)}, u32[]{:S(2)}, u32[]{:S(2)}) async-start(s32[128,1,4]{2,1,0:T(1,128)} %bitcast.47), calls=%async_computation | async-start | bytes 131072 | tf_op jit(solution)/shard_map/all_to_all | solution.py:134
  182.5 73.9 %all-to-all-start.1 = ((bf16[128,4,256]{2,1,0:T(4,128)(2,1)}), bf16[128,4,256]{2,1,0:T(4,128)(2,1)S(1)}, u32[]{:S(2)}, u32[]{:S(2)}) async-start(bf16[128,4,256]{2,1,0:T(4,128)(2,1)} %reshape.323), calls=%async_computation.1 | async-start | bytes 524288 | tf_op jit(solution)/shard_map/all_to_all | solution.py:210
  321.3 5.6 %copy-start.9 = (f32[1024,512]{1,0:T(8,128)S(1)}, f32[1024,512]{1,0:T(8,128)}, u32[]{:S(2)}) copy-start(f32[1024,512]{1,0:T(8,128)} %get-tuple-element.303) | copy-start | bytes 6291460
  (1 other events, 1.7 us)
Sparse Core Ops, SparseCore 0:
  15.0 74.1 all-gather.2
  165.8 155.4 all-reduce.2
where the time goes:
time: 338 us; the launch traced here: 335 us
  waiting for transfers between devices  92.9 us (27%)
  blocking collectives  89.6 us (27%)
  local copies, waits for them, and re-layouts  81.2 us (24%)
  matrix products  29.2 us (9%)
  other arithmetic  17.7 us (5%)
  between operations  14.6 us (4%)
  starting transfers between devices  9.04 us (3%)
    psum x1, blocking collectives, local(): lax.psum((grad_up, grad_in, grad_out, grad_skip), ('batch', 'ctx'))  67.8 us
    psum x1, waiting for transfers between devices, local(): lax.psum((grad_up, grad_in, grad_out, grad_skip), ('batch', 'ctx'))  60.5 us
    dynamic_slice x30, local copies, waits for them, and re-layouts, one(): lax.dynamic_index_in_dim(a, source, 0, False)  49 us
    all_gather x1, waiting for transfers between devices, entering(): gathered = jax.tree.map(lambda a: lax.all_gather(a, axis), part)  25.3 us
    all_gather x1, blocking collectives, entering(): gathered = jax.tree.map(lambda a: lax.all_gather(a, axis), part)  21.9 us
    mul x15, local copies, waits for them, and re-layouts, combine_pieces(): later_item[0][:, None, None] * earlier_item[1]  10.2 us
    unnamed x47, local copies, waits for them, and re-layouts  7.83 us
    all_to_all x1, waiting for transfers between devices, local(): lax.all_to_all(slot_rows.reshape(owner_count, capacity), ('batch', 'ctx')...  7 us
  transfers between devices with their start and end apart: 4, of which 3 were waited for; matrix products, arithmetic and copies ran while one was open for 11% of the time, Pallas kernels for 0%

commit v1 on v0

v1 whole, which is shorter than its diff:
```python
from functools import partial

import jax
import jax.numpy as jnp
from jax import lax
from jax.experimental import pallas as pl
from jax.experimental.pallas import tpu as pltpu
from jax.sharding import PartitionSpec as P

T = 256
E = 256
D = 512
H = 16
HP = 64
N = 128
INNER = H * HP
PROJ = INNER + 2 * N
ROWS_DEV = 512
CAP = 4
DEV = 128
CTX = 16
SROWS = 80

DT = 0.0625
SC = 128.0**-0.5
F32 = jnp.float32
BF = jnp.bfloat16
NN = (((1,), (0,)), ((), ()))
NT = (((1,), (1,)), ((), ()))
TN = (((0,), (0,)), ((), ()))
MB = 1 << 20


def dot(a, b, dims=NN):
    return lax.dot_general(a, b, dims, preferred_element_type=F32)


def split3(v):
    hi = v.astype(BF)
    rest = v - hi.astype(F32)
    mid = rest.astype(BF)
    return hi, mid, (rest - mid.astype(F32)).astype(BF)


def call(kernel, outs, vmem, flops, nbytes, **kw):
    return pl.pallas_call(
        kernel,
        out_shape=tuple(jax.ShapeDtypeStruct(s, d) for s, d in outs),
        compiler_params=pltpu.CompilerParams(vmem_limit_bytes=vmem * MB),
        cost_estimate=pl.CostEstimate(flops=flops, bytes_accessed=nbytes, transcendentals=0),
        **kw,
    )


VM = pl.BlockSpec(memory_space=pltpu.VMEM)
SM = pl.BlockSpec(memory_space=pltpu.SMEM)


def project_kernel(rows_ref, dout_ref, decay_ref, w_up_ref, w_in_ref, w_out_ref,
                   proj_ref, dy_ref, cum_ref, cumt_ref, send_ref):
    u = dot(rows_ref[...], w_up_ref[...]).astype(BF)
    proj_ref[...] = dot(u, w_in_ref[...]).astype(BF)
    dy_ref[...] = dot(w_out_ref[...], dout_ref[...], NT).astype(BF)
    logs = split3(jnp.log(decay_ref[...]))
    r = lax.broadcasted_iota(jnp.int32, (T, T), 0)
    c = lax.broadcasted_iota(jnp.int32, (T, T), 1)
    upper = (r <= c).astype(F32).astype(BF)
    lower = (c <= r).astype(F32).astype(BF)
    cum = sum(dot(p, upper) for p in logs)
    cum_ref[...] = cum
    cumt_ref[...] = sum(dot(lower, p, NT) for p in logs)
    start = jnp.exp(cum)
    c_nat = proj_ref[:, INNER + N :]
    scaled = jnp.concatenate(
        [
            (dy_ref[h * HP : (h + 1) * HP, :].astype(F32) * (SC * start[h : h + 1, :])).astype(BF)
            for h in range(H)
        ],
        axis=0,
    )
    sums = dot(scaled, c_nat).astype(BF)
    amount = jnp.exp(cum[:, T - 1 : T])
    parts = [jnp.broadcast_to(p.astype(F32), (H, N)) for p in split3(amount)]
    row = lax.broadcasted_iota(jnp.int32, (SROWS - HP, N), 0)
    for h in range(H):
        send_ref[h, 0:HP, :] = sums[h * HP : (h + 1) * HP, :]
        tail = jnp.where(
            row == 0,
            parts[0][h : h + 1, :],
            jnp.where(row == 1, parts[1][h : h + 1, :], jnp.where(row == 2, parts[2][h : h + 1, :], 0.0)),
        )
        send_ref[h, HP:SROWS, :] = tail.astype(BF)


def scan_kernel(got_ref, out_ref):
    carry = jnp.zeros((HP, N), F32)
    for j in range(CTX - 1, -1, -1):
        out_ref[j, :, :] = carry.astype(BF)
        if j:
            tail = got_ref[j, HP:SROWS, :].astype(F32)
            amount = tail[0:1, :] + tail[1:2, :] + tail[2:3, :]
            carry = got_ref[j, 0:HP, :].astype(F32) + amount * carry


def local_kernel(proj_ref, dy_ref, cum_ref, cumt_ref, h0_ref, dout_ref, index_ref, skip_ref,
                 gout_ref, dx_ref, dbt_ref, dct_ref, misc_ref, hits_ref, y_ref, sdy_ref, h0t_ref, sum_ref):
    proj_t = jnp.transpose(proj_ref[...])
    bt = proj_t[INNER : INNER + N, :]
    ct = proj_t[INNER + N :, :]
    b_nat = proj_ref[:, INNER : INNER + N]
    c_nat = proj_ref[:, INNER + N :]
    pair = (SC * DT) * dot(b_nat, c_nat, NT)
    r = lax.broadcasted_iota(jnp.int32, (N, N), 0)
    c = lax.broadcasted_iota(jnp.int32, (N, N), 1)
    causal = r <= c
    cum = cum_ref[...]
    cumt = cumt_ref[...]
    start = jnp.exp(cum)
    for h in range(H):
        h0t_ref[h * HP : (h + 1) * HP, :] = jnp.transpose(h0_ref[h]).astype(BF)
    y_ref[...] = dot(h0t_ref[...], ct)
    skip_sums = []
    a00 = jnp.zeros((N, N), F32)
    a01 = jnp.zeros((N, N), F32)
    a11 = jnp.zeros((N, N), F32)
    zero = jnp.zeros((N, N), BF)
    zrow = jnp.zeros((HP, T), BF)
    for h in range(H):
        lo, hi = h * HP, (h + 1) * HP
        row0, row1 = cum[h : h + 1, :N], cum[h : h + 1, N:]
        col0, col1 = cumt[:N, h : h + 1], cumt[N:, h : h + 1]
        m00 = jnp.exp(jnp.where(causal, row0 - col0, -1e30))
        m01 = jnp.exp(row1 - col0)
        m11 = jnp.exp(jnp.where(causal, row1 - col1, -1e30))
        weights = jnp.concatenate(
            [
                jnp.concatenate([(m00 * pair[:N, :N]).astype(BF), (m01 * pair[:N, N:]).astype(BF)], axis=1),
                jnp.concatenate([zero, (m11 * pair[N:, N:]).astype(BF)], axis=1),
            ],
            axis=0,
        )
        x_h = proj_t[lo:hi, :]
        dy_h = dy_ref[lo:hi, :]
        x_f, dy_f = x_h.astype(F32), dy_h.astype(F32)
        st = start[h : h + 1, :]
        skip = skip_ref[h]
        y_ref[lo:hi, :] = dot(x_h, weights) + SC * st * y_ref[lo:hi, :] + skip * x_f
        dx_ref[lo:hi, :] = dot(dy_h, weights, NT) + skip * dy_f
        sdy_ref[lo:hi, :] = (st * dy_f).astype(BF)
        x_pair = proj_ref[:, (h // 2) * N : (h // 2 + 1) * N]
        dy_z = jnp.concatenate([dy_h, zrow] if h % 2 == 0 else [zrow, dy_h], axis=0)
        q0 = dot(x_pair[:N, :], dy_z)
        q11 = dot(x_pair[N:, :], dy_z[:, N:])
        a00 += m00 * q0[:, :N]
        a01 += m01 * q0[:, N:]
        a11 += m11 * q11
        skip_sums.append(jnp.sum(x_f * dy_f, keepdims=True))
    gout_ref[...] = dot(y_ref[...].astype(BF), dout_ref[...]).astype(BF)
    sum_ref[:N, :N] = a00.astype(BF)
    sum_ref[:N, N:] = a01.astype(BF)
    sum_ref[N:, :N] = zero
    sum_ref[N:, N:] = a11.astype(BF)
    a = sum_ref[...]
    dct_ref[...] = (SC * (DT * dot(bt, a) + dot(h0t_ref[...], sdy_ref[...], TN))).astype(BF)
    dbt_ref[...] = (DT * SC) * dot(ct, a, NT)
    index = index_ref[...]
    owner_row = lax.shift_right_logical(index, 9)
    rr = lax.broadcasted_iota(jnp.int32, (T, T), 0)
    cc = lax.broadcasted_iota(jnp.int32, (T, T), 1)
    index_col = jnp.sum(jnp.where(rr == cc, index.astype(F32), 0.0), axis=1, keepdims=True)
    index_col = index_col.astype(jnp.int32)
    owner_col = lax.shift_right_logical(index_col, 9)
    same = owner_col == owner_row
    rank_row = jnp.sum(jnp.where(same & (rr < cc), 1.0, 0.0), axis=0, keepdims=True).astype(jnp.int32)
    rank_col = jnp.sum(jnp.where(same & (cc < rr), 1.0, 0.0), axis=1, keepdims=True).astype(jnp.int32)
    local_col = index_col - owner_col * ROWS_DEV
    id_hi = lax.shift_right_logical(local_col, 1)
    id_lo = local_col - 2 * id_hi
    v = jnp.where(cc == rank_col, id_hi, jnp.where(cc == rank_col + 64, id_lo, 0))
    row_id = lax.broadcasted_iota(jnp.int32, (8 * DEV, T), 0)
    hits_ref[...] = jnp.where(row_id == owner_row * 8 + 2 + rank_row, 1.0, 0.0).astype(BF)
    heads = jnp.where(row_id == owner_row * 8 + 6, 1.0, 0.0).astype(BF)
    lane = lax.broadcasted_iota(jnp.int32, (1, T), 1)
    extra = jnp.zeros((1, T), F32)
    for h in range(H):
        whole = skip_sums[h]
        top = whole.astype(BF).astype(F32)
        extra = extra + jnp.where(lane == 128 + h, top, 0.0) + jnp.where(lane == 160 + h, whole - top, 0.0)
    misc = dot(heads, v.astype(F32).astype(BF))
    misc_ref[...] = misc + jnp.where((row_id & 7) == 6, extra, 0.0)


def finish_kernel(carry_ref, proj_ref, cum_ref, dx_ref, dbt_ref, dct_ref, misc_ref, hits_ref, rows_ref,
                  w_in_ref, w_up_ref, out_ref, d_ref, tx_ref):
    proj_t = jnp.transpose(proj_ref[...])
    bt = proj_t[INNER : INNER + N, :]
    cum = cum_ref[...]
    tail = DT * jnp.exp(cum[:, T - 1 : T] - cum)
    carry = carry_ref[...]
    entering = dot(carry, bt)
    for h in range(H):
        lo, hi = h * HP, (h + 1) * HP
        tl = tail[h : h + 1, :]
        d_ref[lo:hi, :] = (dx_ref[lo:hi, :] + tl * entering[lo:hi, :]).astype(BF)
        tx_ref[lo:hi, :] = (tl * proj_t[lo:hi, :].astype(F32)).astype(BF)
    d_ref[INNER : INNER + N, :] = (dbt_ref[...] + dot(carry, tx_ref[...], TN)).astype(BF)
    d_ref[INNER + N :, :] = dct_ref[...]
    d = d_ref[...]
    g = dot(d, rows_ref[...]).astype(BF)
    out_ref[:, :E] = g[:INNER, :]
    du = dot(w_in_ref[...], d).astype(BF)
    de = dot(w_up_ref[...], du).astype(BF)
    r = lax.broadcasted_iota(jnp.int32, (8 * DEV, 2 * N), 0)
    j = lax.broadcasted_iota(jnp.int32, (1, 2 * N), 1)
    place = jnp.where(r == 8 * lax.shift_right_logical(j, 1) + (j & 1), 1.0, 0.0).astype(BF)
    misc = misc_ref[...] + dot(hits_ref[...], de, NT) + dot(place, g[INNER:, :])
    out_ref[:, E:] = misc.astype(BF)


def sum_kernel(got_ref, go_ref, chunk_ref, skip_ref):
    a = jnp.sum(got_ref[...].astype(F32), axis=0)
    b = jnp.sum(go_ref[...].astype(F32), axis=0)
    chunk = jnp.concatenate([a, b], axis=1)
    chunk_ref[...] = jnp.broadcast_to(chunk[None], chunk_ref.shape).astype(BF)
    skip_ref[...] = a[6:7, E + 128 : E + 256]


def table_kernel(got_ref, table_ref):
    misc = got_ref[:, :, E:]
    ids = misc[:, 6:7, 0:128].astype(F32)
    sub = lax.broadcasted_iota(jnp.int32, (DEV, 8, 128), 1) - 2
    lane = lax.broadcasted_iota(jnp.int32, (DEV, 8, 128), 2)
    want = jnp.where(lane == sub, 2.0, jnp.where(lane == sub + 64, 1.0, 0.0))
    row = jnp.sum(ids * want, axis=2, keepdims=True)
    row = jnp.where((sub[:, :, :1] >= 0) & (sub[:, :, :1] < CAP), row, -1.0)
    rid = lax.broadcasted_iota(jnp.int32, (DEV, 8, ROWS_DEV), 2).astype(F32)
    hits = jnp.where(rid == row, 1.0, 0.0).reshape(DEV * 8, ROWS_DEV).astype(BF)
    table_ref[...] = dot(hits, got_ref[...].reshape(DEV * 8, 2 * E)[:, E:], TN)


def last_kernel(got_ref, w_up_ref, w_in_ref, up_ref, in_ref, out_ref):
    got = got_ref[...].reshape(DEV * 8, 4 * E)
    out_ref[...] = got[:, 2 * E :].astype(F32)
    j = lax.broadcasted_iota(jnp.int32, (2 * N, 8 * DEV), 0)
    r = lax.broadcasted_iota(jnp.int32, (2 * N, 8 * DEV), 1)
    pick = jnp.where(r == 8 * lax.shift_right_logical(j, 1) + (j & 1), 1.0, 0.0).astype(BF)
    g = jnp.concatenate([got[:, :E], dot(pick, got[:, E : 2 * E]).astype(BF)], axis=0)
    in_ref[...] = lax.dot_general(w_up_ref[...], g, (((0,), (1,)), ((), ())), preferred_element_type=F32)
    up_ref[...] = jnp.transpose(dot(w_in_ref[...], g))


def local(event_rows, event_index, decay, saved_state, dout, w_up, w_in, w_out, skip):
    every = ("batch", "ctx")
    rows, d_out = event_rows[0], dout[0]
    proj, dy, cum, cumt, send = call(
        project_kernel,
        [((T, PROJ), BF), ((INNER, T), BF), ((H, T), F32), ((T, H), F32), ((H, SROWS, N), BF)],
        32, 750_000_000, 4_500_000,
        in_specs=[VM] * 6, out_specs=(VM,) * 5,
    )(rows, d_out, decay[0], w_up, w_in, w_out)
    got = lax.all_to_all(send, "ctx", 0, 0, tiled=True)
    gout, dx, dbt, dct, misc, hits = call(
        local_kernel,
        [((INNER, D), BF), ((INNER, T), F32), ((N, T), F32), ((N, T), BF), ((8 * DEV, E), F32), ((8 * DEV, T), BF)],
        40, 2_500_000_000, 6_000_000,
        in_specs=[VM] * 7 + [SM], out_specs=(VM,) * 6,
        scratch_shapes=[
            pltpu.VMEM((INNER, T), F32), pltpu.VMEM((INNER, T), BF),
            pltpu.VMEM((INNER, N), BF), pltpu.VMEM((T, T), BF),
        ],
    )(proj, dy, cum, cumt, saved_state[0, 0], d_out, event_index, skip)
    (carries,) = call(
        scan_kernel, [((CTX, HP, N), BF)], 8, 4_000_000, 600_000, in_specs=[VM], out_specs=(VM,)
    )(got)
    carry = lax.all_to_all(carries, "ctx", 0, 0, tiled=True)
    go_got = lax.all_to_all(gout.reshape(DEV, 8, D), every, 0, 0, tiled=True)
    (pay,) = call(
        finish_kernel, [((8 * DEV, 2 * E), BF)], 32, 1_400_000_000, 6_000_000,
        in_specs=[VM] * 11, out_specs=(VM,),
        scratch_shapes=[pltpu.VMEM((PROJ, T), BF), pltpu.VMEM((INNER, T), BF)],
    )(carry.reshape(INNER, N), proj, cum, dx, dbt, dct, misc, hits, rows, w_in, w_up)
    pay_got = lax.all_to_all(pay.reshape(DEV, 8, 2 * E), every, 0, 0, tiled=True)
    chunk, skip_sum = call(
        sum_kernel, [((DEV, 8, 4 * E), BF), ((1, 128), F32)], 24, 2_000_000, 4_000_000,
        in_specs=[VM] * 2, out_specs=(VM,) * 2,
    )(pay_got, go_got)
    whole = lax.all_to_all(chunk, every, 0, 0, tiled=True)
    (table,) = call(
        table_kernel, [((ROWS_DEV, E), F32)], 24, 400_000_000, 2_000_000, in_specs=[VM], out_specs=(VM,)
    )(pay_got)
    grad_up, grad_in, grad_out = call(
        last_kernel, [((E, D), F32), ((D, PROJ), F32), ((INNER, D), F32)], 40, 700_000_000, 9_000_000,
        in_specs=[VM] * 3, out_specs=(VM,) * 3,
    )(whole, w_up, w_in)
    grad_skip = skip_sum[0, :H] + skip_sum[0, 32 : 32 + H]
    return (grad_up, grad_in, grad_out, grad_skip, table)


def solution(mesh):
    in_specs = (
        P("batch", "ctx", None),
        P("batch", "ctx"),
        P("batch", None, "ctx"),
        P("batch", "ctx", None, None, None),
        P("batch", "ctx", None),
        P(),
        P(),
        P(),
        P(),
    )
    out_specs = (P(), P(), P(), P(), P(("batch", "ctx"), None))
    return jax.shard_map(local, mesh=mesh, in_specs=in_specs, out_specs=out_specs, check_vma=False)
```

time: 338 us -> 136 us (0.40)
  local copies, waits for them, and re-layouts: 81.2 us -> 23 us
  waiting for transfers between devices: 92.9 us -> 35.8 us
  blocking collectives: 89.6 us -> 39.5 us
  matrix products: 29.2 us -> 0 us
  other arithmetic: 17.7 us -> 0.58 us
  Pallas kernels: 0 us -> 14.6 us
  between operations: 14.6 us -> 0.84 us
  starting transfers between devices: 9.04 us -> 21 us
    psum x1 -> x0, blocking collectives: 67.8 us -> none  [local(): lax.psum((grad_up, grad_in, grad_out, grad_skip), ('batch', 'ctx'))]
    psum x1 -> x0, waiting for transfers between devices: 60.5 us -> none  [local(): lax.psum((grad_up, grad_in, grad_out, grad_skip), ('batch', 'ctx'))]
    dynamic_slice x30 -> x0, local copies, waits for them, and re-layouts: 49 us -> none  [one(): lax.dynamic_index_in_dim(a, source, 0, False)]
    all_to_all x0 -> x2, blocking collectives: none -> 39.5 us  [the longest x1 23.1 us: local(): lax.all_to_all(pay.reshape(DEV, 8, 2 * E), every, 0, 0, tiled=True)]
    all_to_all x2 -> x3, waiting for transfers between devices: 7 us -> 35.8 us  [the longest x1 27.2 us: local(): whole = lax.all_to_all(chunk, every, 0, 0, tiled=True)]
    dot_general x18 -> x0, matrix products: 27.2 us -> none  [the longest x1 4.06 us: backward_block(): exact_sum('hts,ts,shp->thp', mask_back, b_dot_c, dy_part)]
    all_gather x1 -> x0, waiting for transfers between devices: 25.3 us -> none  [entering(): gathered = jax.tree.map(lambda a: lax.all_gather(a, axis), part)]
    all_gather x1 -> x0, blocking collectives: 21.9 us -> none  [entering(): gathered = jax.tree.map(lambda a: lax.all_gather(a, axis), part)]
  transfers between devices with their start and end apart: 4 -> 3, of which waited for: 3 -> 2; matrix products, arithmetic and copies ran while one was open for 11% -> 1% of each run, Pallas kernels for 0% -> 5%
where the time goes in v1:
time: 136 us; the launch traced here: 135 us
  blocking collectives  39.5 us (29%)
  waiting for transfers between devices  35.8 us (26%)
  local copies, waits for them, and re-layouts  23 us (17%)
  starting transfers between devices  21 us (15%)
  Pallas kernels  14.6 us (11%)
    all_to_all x1, waiting for transfers between devices, local(): whole = lax.all_to_all(chunk, every, 0, 0, tiled=True)  27.2 us
    all_to_all x1, blocking collectives, local(): lax.all_to_all(pay.reshape(DEV, 8, 2 * E), every, 0, 0, tiled=True)  23.1 us
    unnamed x63, local copies, waits for them, and re-layouts  23 us
    all_to_all x1, blocking collectives, local(): got = lax.all_to_all(send, 'ctx', 0, 0, tiled=True)  16.4 us
    all_to_all x1, starting transfers between devices, local(): go_got = lax.all_to_all(gout.reshape(DEV, 8, D), every, 0, 0, tiled=True)  11.3 us
    all_to_all x1, waiting for transfers between devices, local(): go_got = lax.all_to_all(gout.reshape(DEV, 8, D), every, 0, 0, tiled=True)  8.55 us
    all_to_all x1, starting transfers between devices, local(): whole = lax.all_to_all(chunk, every, 0, 0, tiled=True)  5.84 us
    pallas_call x1, Pallas kernels, local(): call(last_kernel, [((E, D), F32), ((D, PROJ), F32), ((INNER, D), F32)], 4...  4.93 us
  transfers between devices with their start and end apart: 3, of which 2 were waited for; matrix products, arithmetic and copies ran while one was open for 1% of the time, Pallas kernels for 5%

profile of v1, /device:TPU:1, one launch (start us, length us, event | category | flops | bytes accessed | tf_op | source)
XLA Modules:
  0.0 135.2 jit_solution(8542370506407246955)
XLA Ops:
  0.6 1.3 copy-done
  2.9 1.2 copy-done.8
  6.7 1.3 shard_map.128
  8.0 16.4 %all_to_all.25.got_ref = bf16[16,80,128]{2,1,0:T(8,128)(2,1)S(1)} all-to-all(bf16[16,80,128]{2,1,0:T(8,128)(2,1)S(1)} %get-tuple-element.21), channel_id=1, replica_groups=mesh['batch'=8,'ctx'=16] {'ctx'}, dimensions={0} | all-to-all | bytes 655360 | tf_op jit(solution)/shard_map/all_to_all | solution.py:261
  25.1 3.8 %all-to-all-start.1 = ((bf16[16,64,128]{2,1,0:T(8,128)(2,1)}), bf16[16,64,128]{2,1,0:T(8,128)(2,1)S(1)}, u32[]{:S(2)}, u32[]{:S(2)}) async-start(bf16[16,64,128]{2,1,0:T(8,128)(2,1)} %shard_map.129), calls=%async_computation.1 | async-start | bytes 524288 | tf_op jit(solution)/shard_map/all_to_all | solution.py:275
  29.0 1.4 %copy.14 = f32[1,1,16,128,64]{4,3,2,1,0:T(8,128)S(1)} copy(f32[1,1,16,128,64]{3,4,2,1,0:T(8,128)} %param.12) | data formatting | bytes 1048576 | tf_op args[3]
  30.4 3.5 %shard_map.130 = (bf16[1024,512]{1,0:T(8,128)(2,1)S(1)}, f32[1024,256]{1,0:T(8,128)S(1)}, f32[128,256]{1,0:T(8,128)S(1)}, bf16[128,256]{1,0:T(8,128)(2,1)S(1)}, ...) custom-call(bf16[256,1280]{1,0:T(8,128)(2,1)S(1)} %get-tuple-element.22.proj_ref, ...), custom_call_target="tpu_custom_call" | custom-call | flops 2500000000 | bytes 6000000 | tf_op jit(solution)/shard_map/pallas_call | solution.py:262
  33.9 1.0 copy-done.9
  34.9 1.0 copy-done.11
  35.8 1.0 copy-done.15
  38.9 11.3 %all-to-all-start.3 = ((bf16[128,8,512]{2,1,0:T(8,128)(2,1)}), bf16[128,8,512]{2,1,0:T(8,128)(2,1)S(1)}, u32[]{:S(2)}, u32[]{:S(2)}) async-start(bf16[128,8,512]{2,1,0:T(8,128)(2,1)} %bitcast.12), calls=%async_computation.3 | async-start | bytes 2097152 | tf_op jit(solution)/shard_map/all_to_all | solution.py:276
  51.2 1.2 copy-done.10
  52.4 1.2 copy-done.12
  54.6 1.1 copy-done.17
  55.7 1.0 copy-done.19
  58.5 2.1 %shard_map.131 = bf16[1024,512]{1,0:T(8,128)(2,1)S(1)} custom-call(bf16[1024,128]{1,0:T(8,128)(2,1)S(1)} %bitcast.10, bf16[256,1280]{1,0:T(8,128)(2,1)S(1)} %copy-done.17, f32[16,256]{1,0:T(8,128)S(1)} %get-tuple-element.23.cum_ref, f32[1024,256]{1,0:T(8,128)S(1)} %copy-done.10, f32[128,256]{1,0:T(8,128)S(1)} %copy-done.25, bf16[128,256]{1,0:T(8,128)(2,1)S(1)} %copy-done.27, ...), custom_call_target="tpu_custom_call" | custom-call | flops 1400000000 | bytes 6000000 | tf_op jit(solution)/shard_map/pallas_call | solution.py:277
  60.6 8.5 %all-to-all-done.3.go_ref = bf16[128,8,512]{2,1,0:T(8,128)(2,1)S(1)} async-done(((bf16[128,8,512]{2,1,0:T(8,128)(2,1)}), bf16[128,8,512]{2,1,0:T(8,128)(2,1)S(1)}, u32[]{:S(2)}, u32[]{:S(2)}) %all-to-all-start.3) | async-done | bytes 1048608 | tf_op jit(solution)/shard_map/all_to_all | solution.py:276
  69.1 1.0 copy-done.2
  70.1 23.1 %all_to_all.26.got_ref = bf16[128,8,512]{2,1,0:T(8,128)(2,1)S(1)} all-to-all(bf16[128,8,512]{2,1,0:T(8,128)(2,1)S(1)} %bitcast.9), channel_id=1, replica_groups=mesh['batch'=8,'ctx'=16] {'batch','ctx'}, dimensions={0} | all-to-all | bytes 2097152 | tf_op jit(solution)/shard_map/all_to_all | solution.py:282
  93.8 1.3 copy-done.7
  95.1 5.8 %all-to-all-start.4 = ((bf16[128,8,1024]{2,1,0:T(8,128)(2,1)}), bf16[128,8,1024]{2,1,0:T(8,128)(2,1)}, u32[]{:S(2)}, u32[]{:S(2)}) async-start(bf16[128,8,1024]{2,1,0:T(8,128)(2,1)} %copy-done.7), calls=%async_computation.4 | async-start | bytes 4194304 | tf_op jit(solution)/shard_map/all_to_all | solution.py:287
  101.0 1.5 %shard_map.134 = f32[512,256]{1,0:T(8,128)} custom-call(bf16[128,8,512]{2,1,0:T(8,128)(2,1)S(1)} %all_to_all.26.got_ref), custom_call_target="tpu_custom_call" | custom-call | flops 400000000 | bytes 2000000 | tf_op jit(solution)/shard_map/pallas_call | solution.py:288
  103.0 27.2 %all-to-all-done.4.got_ref = bf16[128,8,1024]{2,1,0:T(8,128)(2,1)} async-done(((bf16[128,8,1024]{2,1,0:T(8,128)(2,1)}), bf16[128,8,1024]{2,1,0:T(8,128)(2,1)}, u32[]{:S(2)}, u32[]{:S(2)}) %all-to-all-start.4) | async-done | bytes 2097184 | tf_op jit(solution)/shard_map/all_to_all | solution.py:287
  130.3 4.9 %shard_map.133 = (f32[256,512]{1,0:T(8,128)}, f32[512,1280]{1,0:T(8,128)}, f32[1024,512]{1,0:T(8,128)}) custom-call(bf16[128,8,1024]{2,1,0:T(8,128)(2,1)} %all-to-all-done.4.got_ref, bf16[256,512]{1,0:T(8,128)(2,1)S(1)} %copy-done.6, bf16[512,1280]{1,0:T(8,128)(2,1)S(1)} %copy-done.1), custom_call_target="tpu_custom_call" | custom-call | flops 700000000 | bytes 9000000 | tf_op jit(solution)/shard_map/pallas_call | solution.py:291
  (55 shorter events, 11.2 us)
Async XLA Ops:
  0.6 1.3 copy-start
  2.9 1.2 copy-start.8
  8.0 22.4 %copy-start.16 = (bf16[256,1280]{1,0:T(8,128)(2,1)}, bf16[256,1280]{1,0:T(8,128)(2,1)S(1)}, u32[]{:S(2)}) copy-start(bf16[256,1280]{1,0:T(8,128)(2,1)S(1)} %get-tuple-element.22.proj_ref) | copy-start | bytes 1966084
  8.0 22.4 %copy-start.23 = (bf16[1,256,512]{2,1,0:T(8,128)(2,1)S(1)}, bf16[1,256,512]{2,1,0:T(8,128)(2,1)}, u32[]{:S(2)}) copy-start(bf16[1,256,512]{2,1,0:T(8,128)(2,1)} %param.13) | copy-start | bytes 786436
  8.0 22.4 %copy-start.29 = (s32[1,256]{1,0:T(1,128)S(1)}, s32[1,256]{1,0:T(1,128)}, u32[]{:S(2)}) copy-start(s32[1,256]{1,0:T(1,128)} %index_ref.1) | copy-start | bytes 3076
  8.0 22.4 %copy-start.30 = (f32[16]{0:T(128)S(1)}, f32[16]{0:T(128)}, u32[]{:S(2)}) copy-start(f32[16]{0:T(128)} %skip_ref.1) | copy-start | bytes 196
  25.1 13.8 %all-to-all-start.1 = ((bf16[16,64,128]{2,1,0:T(8,128)(2,1)}), bf16[16,64,128]{2,1,0:T(8,128)(2,1)S(1)}, u32[]{:S(2)}, u32[]{:S(2)}) async-start(bf16[16,64,128]{2,1,0:T(8,128)(2,1)} %shard_map.129), calls=%async_computation.1 | async-start | bytes 524288 | tf_op jit(solution)/shard_map/all_to_all | solution.py:275
  33.9 1.0 copy-start.9
  34.9 1.0 copy-start.11
  35.8 1.0 copy-start.15
  38.9 11.3 %copy-start.1 = (bf16[512,1280]{1,0:T(8,128)(2,1)S(1)}, bf16[512,1280]{1,0:T(8,128)(2,1)}, u32[]{:S(2)}) copy-start(bf16[512,1280]{1,0:T(8,128)(2,1)} %w_in_ref.5) | copy-start | bytes 3932164
  38.9 11.4 %copy-start.21 = (bf16[1,256,256]{2,1,0:T(8,128)(2,1)S(1)}, bf16[1,256,256]{2,1,0:T(8,128)(2,1)}, u32[]{:S(2)}) copy-start(bf16[1,256,256]{2,1,0:T(8,128)(2,1)} %param.9) | copy-start | bytes 393220
  38.9 11.3 %copy-start.13 = (bf16[16,64,128]{2,1,0:T(8,128)(2,1)}, bf16[16,64,128]{2,1,0:T(8,128)(2,1)S(1)}, u32[]{:S(2)}) copy-start(bf16[16,64,128]{2,1,0:T(8,128)(2,1)S(1)} %all-to-all-done.1) | copy-start | bytes 786436
  38.9 30.2 %all-to-all-start.3 = ((bf16[128,8,512]{2,1,0:T(8,128)(2,1)}), bf16[128,8,512]{2,1,0:T(8,128)(2,1)S(1)}, u32[]{:S(2)}, u32[]{:S(2)}) async-start(bf16[128,8,512]{2,1,0:T(8,128)(2,1)} %bitcast.12), calls=%async_computation.3 | async-start | bytes 2097152 | tf_op jit(solution)/shard_map/all_to_all | solution.py:276
  50.3 1.0 copy-start.5
  51.2 1.2 copy-start.10
  52.4 1.2 copy-start.12
  54.6 1.1 copy-start.17
  55.7 1.0 copy-start.19
  69.1 1.0 copy-start.2
  70.1 23.2 %copy-start.3 = (bf16[128,8,512]{2,1,0:T(8,128)(2,1)S(1)}, bf16[128,8,512]{2,1,0:T(8,128)(2,1)}, u32[]{:S(2)}) copy-start(bf16[128,8,512]{2,1,0:T(8,128)(2,1)} %copy-done.2) | copy-start | bytes 3145732
  93.8 1.3 copy-start.7
  95.1 35.1 %copy-start.6 = (bf16[256,512]{1,0:T(8,128)(2,1)S(1)}, bf16[256,512]{1,0:T(8,128)(2,1)}, u32[]{:S(2)}) copy-start(bf16[256,512]{1,0:T(8,128)(2,1)} %w_up_ref.5) | copy-start | bytes 786436
  95.1 35.1 %all-to-all-start.4 = ((bf16[128,8,1024]{2,1,0:T(8,128)(2,1)}), bf16[128,8,1024]{2,1,0:T(8,128)(2,1)}, u32[]{:S(2)}, u32[]{:S(2)}) async-start(bf16[128,8,1024]{2,1,0:T(8,128)(2,1)} %copy-done.7), calls=%async_computation.4 | async-start | bytes 4194304 | tf_op jit(solution)/shard_map/all_to_all | solution.py:287
  (10 other events, 8.3 us)

commit v2 on v1

--- a/solution.py
+++ b/solution.py
@@ -29,6 +29,7 @@
 NT = (((1,), (1,)), ((), ()))
 TN = (((0,), (0,)), ((), ()))
 MB = 1 << 20
+BIG = 60
 
 
 def dot(a, b, dims=NN):
@@ -53,14 +54,29 @@
 
 
 VM = pl.BlockSpec(memory_space=pltpu.VMEM)
+HBM = pl.BlockSpec(memory_space=pltpu.HBM)
 SM = pl.BlockSpec(memory_space=pltpu.SMEM)
 
 
-def project_kernel(rows_ref, dout_ref, decay_ref, w_up_ref, w_in_ref, w_out_ref,
-                   proj_ref, dy_ref, cum_ref, cumt_ref, send_ref):
+def project_kernel(rows_hbm, dout_hbm, decay_hbm, w_up_hbm, w_in_hbm, w_out_hbm,
+                   proj_ref, dy_ref, cum_ref, cumt_ref, send_ref,
+                   rows_ref, dout_ref, decay_ref, w_up_ref, w_in_ref, w_out_ref, sems):
+    pairs = (
+        (rows_hbm, rows_ref), (w_up_hbm, w_up_ref), (w_in_hbm, w_in_ref),
+        (dout_hbm, dout_ref), (w_out_hbm, w_out_ref), (decay_hbm, decay_ref),
+    )
+    copies = [pltpu.make_async_copy(a, b, sems.at[i]) for i, (a, b) in enumerate(pairs)]
+    for copy in copies:
+        copy.start()
+    copies[0].wait()
+    copies[1].wait()
     u = dot(rows_ref[...], w_up_ref[...]).astype(BF)
+    copies[2].wait()
     proj_ref[...] = dot(u, w_in_ref[...]).astype(BF)
+    copies[3].wait()
+    copies[4].wait()
     dy_ref[...] = dot(w_out_ref[...], dout_ref[...], NT).astype(BF)
+    copies[5].wait()
     logs = split3(jnp.log(decay_ref[...]))
     r = lax.broadcasted_iota(jnp.int32, (T, T), 0)
     c = lax.broadcasted_iota(jnp.int32, (T, T), 1)
@@ -116,8 +132,7 @@
     cum = cum_ref[...]
     cumt = cumt_ref[...]
     start = jnp.exp(cum)
-    for h in range(H):
-        h0t_ref[h * HP : (h + 1) * HP, :] = jnp.transpose(h0_ref[h]).astype(BF)
+    h0t_ref[...] = h0_ref[...].astype(BF)
     y_ref[...] = dot(h0t_ref[...], ct)
     skip_sums = []
     a00 = jnp.zeros((N, N), F32)
@@ -190,7 +205,7 @@
     misc_ref[...] = misc + jnp.where((row_id & 7) == 6, extra, 0.0)
 
 
-def finish_kernel(carry_ref, proj_ref, cum_ref, dx_ref, dbt_ref, dct_ref, misc_ref, hits_ref, rows_ref,
+def finish_kernel(carry_ref, proj_ref, cum_ref, dx_ref, dbt_ref, dct_ref, misc_ref, hits_ref, gout_ref, rows_ref,
                   w_in_ref, w_up_ref, out_ref, d_ref, tx_ref):
     proj_t = jnp.transpose(proj_ref[...])
     bt = proj_t[INNER : INNER + N, :]
@@ -214,19 +229,18 @@
     j = lax.broadcasted_iota(jnp.int32, (1, 2 * N), 1)
     place = jnp.where(r == 8 * lax.shift_right_logical(j, 1) + (j & 1), 1.0, 0.0).astype(BF)
     misc = misc_ref[...] + dot(hits_ref[...], de, NT) + dot(place, g[INNER:, :])
-    out_ref[:, E:] = misc.astype(BF)
-
-
-def sum_kernel(got_ref, go_ref, chunk_ref, skip_ref):
-    a = jnp.sum(got_ref[...].astype(F32), axis=0)
-    b = jnp.sum(go_ref[...].astype(F32), axis=0)
-    chunk = jnp.concatenate([a, b], axis=1)
-    chunk_ref[...] = jnp.broadcast_to(chunk[None], chunk_ref.shape).astype(BF)
-    skip_ref[...] = a[6:7, E + 128 : E + 256]
+    out_ref[:, E : 2 * E] = misc.astype(BF)
+    out_ref[:, 2 * E :] = gout_ref[...]
+
+
+def sum_kernel(got_ref, chunk_ref, skip_ref):
+    total = jnp.sum(got_ref[...].astype(F32), axis=0)
+    chunk_ref[...] = jnp.broadcast_to(total[None], chunk_ref.shape).astype(BF)
+    skip_ref[...] = total[6:7, E + 128 : E + 256]
 
 
 def table_kernel(got_ref, table_ref):
-    misc = got_ref[:, :, E:]
+    misc = got_ref[:, :, E : 2 * E]
     ids = misc[:, 6:7, 0:128].astype(F32)
     sub = lax.broadcasted_iota(jnp.int32, (DEV, 8, 128), 1) - 2
     lane = lax.broadcasted_iota(jnp.int32, (DEV, 8, 128), 2)
@@ -235,7 +249,7 @@
     row = jnp.where((sub[:, :, :1] >= 0) & (sub[:, :, :1] < CAP), row, -1.0)
     rid = lax.broadcasted_iota(jnp.int32, (DEV, 8, ROWS_DEV), 2).astype(F32)
     hits = jnp.where(rid == row, 1.0, 0.0).reshape(DEV * 8, ROWS_DEV).astype(BF)
-    table_ref[...] = dot(hits, got_ref[...].reshape(DEV * 8, 2 * E)[:, E:], TN)
+    table_ref[...] = dot(hits, misc.reshape(DEV * 8, E), TN)
 
 
 def last_kernel(got_ref, w_up_ref, w_in_ref, up_ref, in_ref, out_ref):
@@ -255,41 +269,46 @@
     proj, dy, cum, cumt, send = call(
         project_kernel,
         [((T, PROJ), BF), ((INNER, T), BF), ((H, T), F32), ((T, H), F32), ((H, SROWS, N), BF)],
-        32, 750_000_000, 4_500_000,
-        in_specs=[VM] * 6, out_specs=(VM,) * 5,
+        BIG, 750_000_000, 4_500_000,
+        in_specs=[HBM] * 6, out_specs=(VM,) * 5,
+        scratch_shapes=[
+            pltpu.VMEM((T, E), BF), pltpu.VMEM((T, D), BF), pltpu.VMEM((H, T), F32),
+            pltpu.VMEM((E, D), BF), pltpu.VMEM((D, PROJ), BF), pltpu.VMEM((INNER, D), BF),
+            pltpu.SemaphoreType.DMA((6,)),
+        ],
     )(rows, d_out, decay[0], w_up, w_in, w_out)
     got = lax.all_to_all(send, "ctx", 0, 0, tiled=True)
     gout, dx, dbt, dct, misc, hits = call(
         local_kernel,
         [((INNER, D), BF), ((INNER, T), F32), ((N, T), F32), ((N, T), BF), ((8 * DEV, E), F32), ((8 * DEV, T), BF)],
-        40, 2_500_000_000, 6_000_000,
+        BIG, 2_500_000_000, 6_000_000,
         in_specs=[VM] * 7 + [SM], out_specs=(VM,) * 6,
         scratch_shapes=[
             pltpu.VMEM((INNER, T), F32), pltpu.VMEM((INNER, T), BF),
             pltpu.VMEM((INNER, N), BF), pltpu.VMEM((T, T), BF),
         ],
-    )(proj, dy, cum, cumt, saved_state[0, 0], d_out, event_index, skip)
+    )(proj, dy, cum, cumt, jnp.swapaxes(saved_state[0, 0], 1, 2).reshape(INNER, N), d_out, event_index, skip)
+    got, dct = lax.optimization_barrier((got, dct))
     (carries,) = call(
         scan_kernel, [((CTX, HP, N), BF)], 8, 4_000_000, 600_000, in_specs=[VM], out_specs=(VM,)
     )(got)
     carry = lax.all_to_all(carries, "ctx", 0, 0, tiled=True)
-    go_got = lax.all_to_all(gout.reshape(DEV, 8, D), every, 0, 0, tiled=True)
     (pay,) = call(
-        finish_kernel, [((8 * DEV, 2 * E), BF)], 32, 1_400_000_000, 6_000_000,
-        in_specs=[VM] * 11, out_specs=(VM,),
+        finish_kernel, [((8 * DEV, 4 * E), BF)], BIG, 1_400_000_000, 6_000_000,
+        in_specs=[VM] * 12, out_specs=(VM,),
         scratch_shapes=[pltpu.VMEM((PROJ, T), BF), pltpu.VMEM((INNER, T), BF)],
-    )(carry.reshape(INNER, N), proj, cum, dx, dbt, dct, misc, hits, rows, w_in, w_up)
-    pay_got = lax.all_to_all(pay.reshape(DEV, 8, 2 * E), every, 0, 0, tiled=True)
+    )(carry.reshape(INNER, N), proj, cum, dx, dbt, dct, misc, hits, gout, rows, w_in, w_up)
+    pay_got = lax.all_to_all(pay.reshape(DEV, 8, 4 * E), every, 0, 0, tiled=True)
     chunk, skip_sum = call(
-        sum_kernel, [((DEV, 8, 4 * E), BF), ((1, 128), F32)], 24, 2_000_000, 4_000_000,
-        in_specs=[VM] * 2, out_specs=(VM,) * 2,
-    )(pay_got, go_got)
+        sum_kernel, [((DEV, 8, 4 * E), BF), ((1, 128), F32)], 12, 2_000_000, 4_000_000,
+        in_specs=[VM], out_specs=(VM,) * 2,
+    )(pay_got)
     whole = lax.all_to_all(chunk, every, 0, 0, tiled=True)
     (table,) = call(
-        table_kernel, [((ROWS_DEV, E), F32)], 24, 400_000_000, 2_000_000, in_specs=[VM], out_specs=(VM,)
+        table_kernel, [((ROWS_DEV, E), F32)], 12, 400_000_000, 2_000_000, in_specs=[VM], out_specs=(VM,)
     )(pay_got)
     grad_up, grad_in, grad_out = call(
-        last_kernel, [((E, D), F32), ((D, PROJ), F32), ((INNER, D), F32)], 40, 700_000_000, 9_000_000,
+        last_kernel, [((E, D), F32), ((D, PROJ), F32), ((INNER, D), F32)], 20, 700_000_000, 9_000_000,
         in_specs=[VM] * 3, out_specs=(VM,) * 3,
     )(whole, w_up, w_in)
     grad_skip = skip_sum[0, :H] + skip_sum[0, 32 : 32 + H]

time: 136 us -> 121 us (0.89)
  local copies, waits for them, and re-layouts: 23 us -> 2.27 us
  blocking collectives: 39.5 us -> 49.5 us
  Pallas kernels: 14.6 us -> 23.3 us
  starting transfers between devices: 21 us -> 14.4 us
  waiting for transfers between devices: 35.8 us -> 29.4 us
    unnamed x63 -> x6, local copies, waits for them, and re-layouts: 23 us -> 2.27 us
    all_to_all x2, blocking collectives: 39.5 us -> 49.5 us  [the longest x1 37.8 us: local(): lax.all_to_all(pay.reshape(DEV, 8, 4 * E), every, 0, 0, tiled=True)]
    all_to_all x2 -> x1, starting transfers between devices: 15.1 us -> 8.61 us  [local(): got = lax.all_to_all(send, 'ctx', 0, 0, tiled=True)]
    all_to_all x2 -> x1, waiting for transfers between devices: 8.55 us -> 2.18 us  [local(): got = lax.all_to_all(send, 'ctx', 0, 0, tiled=True)]
    pallas_call x4, Pallas kernels: 9.05 us -> 13.2 us  [the longest x1 6.26 us: local(): call(finish_kernel, [((8 * DEV, 4 * E), BF)], BIG, 1400000000, 6000000, i...]
    pallas_call x1, Pallas kernels: 1.25 us -> 4.36 us  [local(): call(project_kernel, [((T, PROJ), BF), ((INNER, T), BF), ((H, T), F32), (...]
    pallas_call x1, Pallas kernels: 3.51 us -> 5.65 us  [local(): call(local_kernel, [((INNER, D), BF), ((INNER, T), F32), ((N, T), F32), (...]
  transfers between devices with their start and end apart: 3 -> 2, of which waited for: 2 -> 2; matrix products, arithmetic and copies ran while one was open for 1% -> 0% of each run, Pallas kernels for 5% -> 6%
where the time goes in v2:
time: 121 us; the launch traced here: 120 us
  blocking collectives  49.5 us (41%)
  waiting for transfers between devices  29.4 us (24%)
  Pallas kernels  23.3 us (19%)
  starting transfers between devices  14.4 us (12%)
  local copies, waits for them, and re-layouts  2.27 us (2%)
    all_to_all x1, blocking collectives, local(): lax.all_to_all(pay.reshape(DEV, 8, 4 * E), every, 0, 0, tiled=True)  37.8 us
    all_to_all x1, waiting for transfers between devices, local(): whole = lax.all_to_all(chunk, every, 0, 0, tiled=True)  27.2 us
    all_to_all x1, blocking collectives, local(): carry = lax.all_to_all(carries, 'ctx', 0, 0, tiled=True)  11.7 us
    all_to_all x1, starting transfers between devices, local(): got = lax.all_to_all(send, 'ctx', 0, 0, tiled=True)  8.61 us
    pallas_call x1, Pallas kernels, local(): call(finish_kernel, [((8 * DEV, 4 * E), BF)], BIG, 1400000000, 6000000, i...  6.26 us
    all_to_all x1, starting transfers between devices, local(): whole = lax.all_to_all(chunk, every, 0, 0, tiled=True)  5.79 us
    pallas_call x1, Pallas kernels, local(): call(local_kernel, [((INNER, D), BF), ((INNER, T), F32), ((N, T), F32), (...  5.65 us
    pallas_call x1, Pallas kernels, local(): call(last_kernel, [((E, D), F32), ((D, PROJ), F32), ((INNER, D), F32)], 2...  4.93 us
  transfers between devices with their start and end apart: 2, of which 2 were waited for; matrix products, arithmetic and copies ran while one was open for 0% of the time, Pallas kernels for 6%

profile of v2, /device:TPU:1, one launch (start us, length us, event | category | flops | bytes accessed | tf_op | source)
XLA Modules:
  0.0 120.1 jit_solution(10629210187393666220)
XLA Ops:
  0.6 4.4 %shard_map.128 = (bf16[256,1280]{1,0:T(8,128)(2,1)}, bf16[1024,256]{1,0:T(8,128)(2,1)}, f32[16,256]{1,0:T(8,128)}, f32[256,16]{1,0:T(8,128)}, bf16[16,80,128]{2,1,0:T(8,128)(2,1)}) custom-call(bf16[256,256]{1,0:T(8,128)(2,1)} %bitcast.14, bf16[256,512]{1,0:T(8,128)(2,1)} %bitcast.16, f32[16,256]{1,0:T(8,128)} %bitcast.18, bf16[256,512]{1,0:T(8,128)(2,1)} %w_up_ref.3, ...), custom_call_target="tpu_custom_call" | custom-call | flops 750000000 | bytes 4500000 | tf_op jit(solution)/shard_map/pallas_call | solution.py:269
  5.0 8.6 %all-to-all-start = ((bf16[16,80,128]{2,1,0:T(8,128)(2,1)}), bf16[16,80,128]{2,1,0:T(8,128)(2,1)S(1)}, u32[]{:S(2)}, u32[]{:S(2)}) async-start(bf16[16,80,128]{2,1,0:T(8,128)(2,1)} %get-tuple-element.23), calls=%async_computation | async-start | bytes 655360 | tf_op jit(solution)/shard_map/all_to_all | solution.py:280
  13.6 5.6 %shard_map.129 = (bf16[1024,512]{1,0:T(8,128)(2,1)}, f32[1024,256]{1,0:T(8,128)}, f32[128,256]{1,0:T(8,128)}, bf16[128,256]{1,0:T(8,128)(2,1)}, f32[1024,256]{1,0:T(8,128)}, /*index=5*/bf16[1024,256]{1,0:T(8,128)(2,1)}) custom-call(bf16[256,1280]{1,0:T(8,128)(2,1)} %get-tuple-element.24.proj_ref, bf16[1024,256]{1,0:T(8,128)(2,1)} %get-tuple-element.25.dy_ref, ...), custom_call_target="tpu_custom_call" | custom-call | flops 2500000000 | bytes 6000000 | tf_op jit(solution)/shard_map/pallas_call | solution.py:281
  19.3 2.2 %all-to-all-done.got_ref = bf16[16,80,128]{2,1,0:T(8,128)(2,1)S(1)} async-done(((bf16[16,80,128]{2,1,0:T(8,128)(2,1)}), bf16[16,80,128]{2,1,0:T(8,128)(2,1)S(1)}, u32[]{:S(2)}, u32[]{:S(2)}) %all-to-all-start) | async-done | bytes 327712 | tf_op jit(solution)/shard_map/all_to_all | solution.py:280
  21.4 0.1 shard_map.130
  21.5 11.7 %all_to_all.20 = bf16[16,64,128]{2,1,0:T(8,128)(2,1)} all-to-all(bf16[16,64,128]{2,1,0:T(8,128)(2,1)S(1)} %shard_map.130), channel_id=1, replica_groups=mesh['batch'=8,'ctx'=16] {'ctx'}, dimensions={0} | all-to-all | bytes 524288 | tf_op jit(solution)/shard_map/all_to_all | solution.py:295
  33.2 6.3 %shard_map.131 = bf16[1024,1024]{1,0:T(8,128)(2,1)} custom-call(bf16[1024,128]{1,0:T(8,128)(2,1)} %bitcast.13, bf16[256,1280]{1,0:T(8,128)(2,1)} %get-tuple-element.24.proj_ref, f32[16,256]{1,0:T(8,128)} %get-tuple-element.26.cum_ref, f32[1024,256]{1,0:T(8,128)} %get-tuple-element.30.dx_ref, f32[128,256]{1,0:T(8,128)} %get-tuple-element.31.dbt_ref, ...), custom_call_target="tpu_custom_call" | custom-call | flops 1400000000 | bytes 6000000 | tf_op jit(solution)/shard_map/pallas_call | solution.py:296
  39.5 37.8 %all_to_all.21.got_ref = bf16[128,8,1024]{2,1,0:T(8,128)(2,1)S(1)} all-to-all(bf16[128,8,1024]{2,1,0:T(8,128)(2,1)} %bitcast.12), channel_id=1, replica_groups=mesh['batch'=8,'ctx'=16] {'batch','ctx'}, dimensions={0} | all-to-all | bytes 4194304 | tf_op jit(solution)/shard_map/all_to_all | solution.py:301
  77.3 0.5 shard_map.132
  77.8 0.0 copy-start.2
  77.8 1.3 %copy-done.2 = bf16[128,8,1024]{2,1,0:T(8,128)(2,1)} copy-done((bf16[128,8,1024]{2,1,0:T(8,128)(2,1)}, bf16[128,8,1024]{2,1,0:T(8,128)(2,1)S(1)}, u32[]{:S(2)}) %copy-start.2) | copy-done | bytes 2097176
  79.1 5.8 %all-to-all-start.3 = ((bf16[128,8,1024]{2,1,0:T(8,128)(2,1)}), bf16[128,8,1024]{2,1,0:T(8,128)(2,1)}, u32[]{:S(2)}, u32[]{:S(2)}) async-start(bf16[128,8,1024]{2,1,0:T(8,128)(2,1)} %copy-done.2), calls=%async_computation.3 | async-start | bytes 4194304 | tf_op jit(solution)/shard_map/all_to_all | solution.py:306
  84.9 0.0 copy-start
  84.9 1.5 %shard_map.134 = f32[512,256]{1,0:T(8,128)} custom-call(bf16[128,8,1024]{2,1,0:T(8,128)(2,1)S(1)} %all_to_all.21.got_ref), custom_call_target="tpu_custom_call" | custom-call | flops 400000000 | bytes 2000000 | tf_op jit(solution)/shard_map/pallas_call | solution.py:307
  86.4 0.6 add_bitcast_fusion
  87.0 27.2 %all-to-all-done.3.got_ref = bf16[128,8,1024]{2,1,0:T(8,128)(2,1)} async-done(((bf16[128,8,1024]{2,1,0:T(8,128)(2,1)}), bf16[128,8,1024]{2,1,0:T(8,128)(2,1)}, u32[]{:S(2)}, u32[]{:S(2)}) %all-to-all-start.3) | async-done | bytes 2097184 | tf_op jit(solution)/shard_map/all_to_all | solution.py:306
  114.2 0.0 copy-done
  114.2 0.0 copy-start.1
  114.2 0.9 copy-done.1
  115.2 4.9 %shard_map.133 = (f32[256,512]{1,0:T(8,128)}, f32[512,1280]{1,0:T(8,128)}, f32[1024,512]{1,0:T(8,128)}) custom-call(bf16[128,8,1024]{2,1,0:T(8,128)(2,1)} %all-to-all-done.3.got_ref, bf16[256,512]{1,0:T(8,128)(2,1)S(1)} %copy-done.1, bf16[512,1280]{1,0:T(8,128)(2,1)S(1)} %copy-done), custom_call_target="tpu_custom_call" | custom-call | flops 700000000 | bytes 9000000 | tf_op jit(solution)/shard_map/pallas_call | solution.py:310
Async XLA Ops:
  5.0 16.4 %all-to-all-start = ((bf16[16,80,128]{2,1,0:T(8,128)(2,1)}), bf16[16,80,128]{2,1,0:T(8,128)(2,1)S(1)}, u32[]{:S(2)}, u32[]{:S(2)}) async-start(bf16[16,80,128]{2,1,0:T(8,128)(2,1)} %get-tuple-element.23), calls=%async_computation | async-start | bytes 655360 | tf_op jit(solution)/shard_map/all_to_all | solution.py:280
  77.8 1.3 %copy-start.2 = (bf16[128,8,1024]{2,1,0:T(8,128)(2,1)}, bf16[128,8,1024]{2,1,0:T(8,128)(2,1)S(1)}, u32[]{:S(2)}) copy-start(bf16[128,8,1024]{2,1,0:T(8,128)(2,1)S(1)} %get-tuple-element.36) | copy-start | bytes 6291460
  79.1 35.1 %all-to-all-start.3 = ((bf16[128,8,1024]{2,1,0:T(8,128)(2,1)}), bf16[128,8,1024]{2,1,0:T(8,128)(2,1)}, u32[]{:S(2)}, u32[]{:S(2)}) async-start(bf16[128,8,1024]{2,1,0:T(8,128)(2,1)} %copy-done.2), calls=%async_computation.3 | async-start | bytes 4194304 | tf_op jit(solution)/shard_map/all_to_all | solution.py:306
  84.9 29.3 %copy-start = (bf16[512,1280]{1,0:T(8,128)(2,1)S(1)}, bf16[512,1280]{1,0:T(8,128)(2,1)}, u32[]{:S(2)}) copy-start(bf16[512,1280]{1,0:T(8,128)(2,1)} %w_in_ref.3) | copy-start | bytes 3932164
  114.2 1.0 copy-start.1

commit v3 on v2

--- a/solution.py
+++ b/solution.py
@@ -118,8 +118,8 @@
             carry = got_ref[j, 0:HP, :].astype(F32) + amount * carry
 
 
-def local_kernel(proj_ref, dy_ref, cum_ref, cumt_ref, h0_ref, dout_ref, index_ref, skip_ref,
-                 gout_ref, dx_ref, dbt_ref, dct_ref, misc_ref, hits_ref, y_ref, sdy_ref, h0t_ref, sum_ref):
+def local_kernel(proj_ref, dy_ref, cum_ref, cumt_ref, h0_ref, dout_ref, index_ref, skip_ref, pos_ref,
+                 keep_ref, give_ref, dx_ref, dbt_ref, dct_ref, misc_ref, hits_ref, y_ref, sdy_ref, h0t_ref, sum_ref):
     proj_t = jnp.transpose(proj_ref[...])
     bt = proj_t[INNER : INNER + N, :]
     ct = proj_t[INNER + N :, :]
@@ -170,7 +170,12 @@
         a01 += m01 * q0[:, N:]
         a11 += m11 * q11
         skip_sums.append(jnp.sum(x_f * dy_f, keepdims=True))
-    gout_ref[...] = dot(y_ref[...].astype(BF), dout_ref[...]).astype(BF)
+    core = pos_ref[1]
+    half = INNER // 2
+    mine = pl.ds(pl.multiple_of(core * half, half), half)
+    other = pl.ds(pl.multiple_of((1 - core) * half, half), half)
+    give_ref[...] = dot(y_ref[other, :].astype(BF), dout_ref[...]).astype(BF)
+    keep_ref[...] = dot(y_ref[mine, :].astype(BF), dout_ref[...])
     sum_ref[:N, :N] = a00.astype(BF)
     sum_ref[:N, N:] = a01.astype(BF)
     sum_ref[N:, :N] = zero
@@ -202,40 +207,99 @@
         top = whole.astype(BF).astype(F32)
         extra = extra + jnp.where(lane == 128 + h, top, 0.0) + jnp.where(lane == 160 + h, whole - top, 0.0)
     misc = dot(heads, v.astype(F32).astype(BF))
-    misc_ref[...] = misc + jnp.where((row_id & 7) == 6, extra, 0.0)
-
-
-def finish_kernel(carry_ref, proj_ref, cum_ref, dx_ref, dbt_ref, dct_ref, misc_ref, hits_ref, gout_ref, rows_ref,
-                  w_in_ref, w_up_ref, out_ref, d_ref, tx_ref):
+    misc_ref[...] = (misc + jnp.where((row_id & 7) == 6, extra, 0.0)).astype(BF)
+
+
+def finish_kernel(carry_hbm, proj_hbm, cum_hbm, dx_hbm, dbt_hbm, dct_hbm, misc_hbm, hits_hbm, rows_hbm,
+                  w_in_hbm, w_up_hbm, out_hbm,
+                  carry_ref, proj_ref, cum_ref, dx_ref, dbt_ref, d_ref, misc_ref, hits_ref, rows_ref,
+                  w_in_ref, w_up_ref, tx_ref, left_ref, right_ref, sems):
+    copies = [
+        pltpu.make_async_copy(a, b, sems.at[n])
+        for n, (a, b) in enumerate((
+            (carry_hbm, carry_ref), (proj_hbm, proj_ref), (cum_hbm, cum_ref), (dx_hbm, dx_ref),
+            (dbt_hbm, dbt_ref), (dct_hbm, d_ref.at[INNER + N :, :]), (rows_hbm, rows_ref),
+            (w_in_hbm, w_in_ref), (w_up_hbm, w_up_ref), (hits_hbm, hits_ref), (misc_hbm, misc_ref),
+        ))
+    ]
+    for copy in copies:
+        copy.start()
+    for copy in copies[:3]:
+        copy.wait()
     proj_t = jnp.transpose(proj_ref[...])
     bt = proj_t[INNER : INNER + N, :]
     cum = cum_ref[...]
     tail = DT * jnp.exp(cum[:, T - 1 : T] - cum)
     carry = carry_ref[...]
     entering = dot(carry, bt)
+    copies[3].wait()
     for h in range(H):
         lo, hi = h * HP, (h + 1) * HP
         tl = tail[h : h + 1, :]
         d_ref[lo:hi, :] = (dx_ref[lo:hi, :] + tl * entering[lo:hi, :]).astype(BF)
         tx_ref[lo:hi, :] = (tl * proj_t[lo:hi, :].astype(F32)).astype(BF)
+    for copy in copies[4:7]:
+        copy.wait()
     d_ref[INNER : INNER + N, :] = (dbt_ref[...] + dot(carry, tx_ref[...], TN)).astype(BF)
-    d_ref[INNER + N :, :] = dct_ref[...]
     d = d_ref[...]
     g = dot(d, rows_ref[...]).astype(BF)
-    out_ref[:, :E] = g[:INNER, :]
+    left_ref[...] = g[:INNER, :]
+    out_left = pltpu.make_async_copy(left_ref, out_hbm.at[:, :E], sems.at[11])
+    out_left.start()
+    copies[7].wait()
     du = dot(w_in_ref[...], d).astype(BF)
+    copies[8].wait()
     de = dot(w_up_ref[...], du).astype(BF)
     r = lax.broadcasted_iota(jnp.int32, (8 * DEV, 2 * N), 0)
     j = lax.broadcasted_iota(jnp.int32, (1, 2 * N), 1)
     place = jnp.where(r == 8 * lax.shift_right_logical(j, 1) + (j & 1), 1.0, 0.0).astype(BF)
-    misc = misc_ref[...] + dot(hits_ref[...], de, NT) + dot(place, g[INNER:, :])
-    out_ref[:, E : 2 * E] = misc.astype(BF)
-    out_ref[:, 2 * E :] = gout_ref[...]
+    copies[9].wait()
+    copies[10].wait()
+    misc = misc_ref[...].astype(F32) + dot(hits_ref[...], de, NT) + dot(place, g[INNER:, :])
+    right_ref[...] = misc.astype(BF)
+    out_right = pltpu.make_async_copy(right_ref, out_hbm.at[:, E:], sems.at[12])
+    out_right.start()
+    out_left.wait()
+    out_right.wait()
+
+
+def split_kernel(which, pos_ref, own_ref, *refs):
+    got, (keep_ref, *give_refs, acc_ref) = refs[:-5], refs[-5:]
+    total = own_ref[...]
+    for ref in got:
+        total = total + ref[...].astype(F32)
+    acc_ref[...] = total
+    at = pos_ref[which]
+    part = keep_ref.shape[0]
+    keep_ref[...] = acc_ref[pl.ds(pl.multiple_of(at * part, part), part), :]
+    for k in range(1, 4):
+        start = pl.multiple_of(((at + k) & 3) * part, part)
+        give_refs[k - 1][...] = acc_ref[pl.ds(start, part), :].astype(BF)
+
+
+def total_kernel(own_ref, a_ref, b_ref, c_ref, out_ref):
+    total = own_ref[...] + a_ref[...].astype(F32) + b_ref[...].astype(F32) + c_ref[...].astype(F32)
+    out_ref[...] = total.astype(BF)
+
+
+def join_kernel(which, pos_ref, own_ref, a_ref, b_ref, c_ref, out_ref):
+    at = pos_ref[which]
+    out_ref[at] = own_ref[...]
+    for k, ref in enumerate((a_ref, b_ref, c_ref)):
+        out_ref[(at + 3 - k) & 3] = ref[...]
+
+
+def write_kernel(pos_ref, own_ref, other_ref, out_ref):
+    core = pos_ref[1]
+    out_ref[core] = own_ref[...].astype(F32)
+    out_ref[1 - core] = other_ref[...].astype(F32)
 
 
 def sum_kernel(got_ref, chunk_ref, skip_ref):
     total = jnp.sum(got_ref[...].astype(F32), axis=0)
-    chunk_ref[...] = jnp.broadcast_to(total[None], chunk_ref.shape).astype(BF)
+    side = jnp.concatenate([total[0:2, E : E + N], total[0:2, E + N :], jnp.zeros((4, N), F32)], axis=0)
+    chunk = jnp.concatenate([total[:, :E], side], axis=1)
+    chunk_ref[...] = jnp.broadcast_to(chunk[None], chunk_ref.shape).astype(BF)
     skip_ref[...] = total[6:7, E + 128 : E + 256]
 
 
@@ -252,21 +316,60 @@
     table_ref[...] = dot(hits, misc.reshape(DEV * 8, E), TN)
 
 
-def last_kernel(got_ref, w_up_ref, w_in_ref, up_ref, in_ref, out_ref):
-    got = got_ref[...].reshape(DEV * 8, 4 * E)
-    out_ref[...] = got[:, 2 * E :].astype(F32)
-    j = lax.broadcasted_iota(jnp.int32, (2 * N, 8 * DEV), 0)
-    r = lax.broadcasted_iota(jnp.int32, (2 * N, 8 * DEV), 1)
-    pick = jnp.where(r == 8 * lax.shift_right_logical(j, 1) + (j & 1), 1.0, 0.0).astype(BF)
-    g = jnp.concatenate([got[:, :E], dot(pick, got[:, E : 2 * E]).astype(BF)], axis=0)
+def last_kernel(got_ref, w_up_ref, w_in_ref, up_ref, in_ref, g_ref):
+    @pl.when(pl.program_id(0) == 0)
+    def _():
+        g_ref[:INNER, :] = got_ref[:, :E]
+        j = lax.broadcasted_iota(jnp.int32, (2 * N, 8 * DEV), 0)
+        r = lax.broadcasted_iota(jnp.int32, (2 * N, 8 * DEV), 1)
+        first = r - (8 * lax.shift_right_logical(j, 1) + (j & 1))
+        for m in range(2):
+            pick = jnp.where(first == 2 * m, 1.0, 0.0).astype(BF)
+            g_ref[INNER:, m * N : (m + 1) * N] = dot(pick, got_ref[:, E:]).astype(BF)
+
+    g = g_ref[...]
     in_ref[...] = lax.dot_general(w_up_ref[...], g, (((0,), (1,)), ((), ())), preferred_element_type=F32)
     up_ref[...] = jnp.transpose(dot(w_in_ref[...], g))
+
+
+def hop(step, axis):
+    if axis == "x":
+        return [(i, (i + 2 * step) % 8) for i in range(8)]
+    if axis == "core":
+        return [(i, i ^ 1) for i in range(8)]
+    if axis == "y":
+        return [(i, (i + 4 * step) % 16) for i in range(16)]
+    return [(i, i // 4 * 4 + (i + step) % 4) for i in range(16)]
+
+
+def send(value, axis, step):
+    return lax.ppermute(value, "batch" if axis in ("x", "core") else "ctx", hop(step, axis))
+
+
+def spread(pos, own, got, which, axis, rows):
+    keep, *give = call(
+        partial(split_kernel, which),
+        [((rows // 4, D), F32)] + [((rows // 4, D), BF)] * 3,
+        4, rows * D * 4, rows * D * 8,
+        in_specs=[SM] + [VM] * (1 + len(got)), out_specs=(VM,) * 4,
+        scratch_shapes=[pltpu.VMEM((rows, D), F32)],
+    )(pos, own, *got)
+    return keep, [send(v, axis, k + 1) for k, v in enumerate(give)]
+
+
+def gather(pos, own, which, axis, rows):
+    got = [send(own, axis, k) for k in range(1, 4)]
+    (out,) = call(
+        partial(join_kernel, which), [((4, rows, D), BF)], 4, 0, rows * D * 16,
+        in_specs=[SM] + [VM] * 4, out_specs=(VM,),
+    )(pos, own, *got)
+    return out.reshape(4 * rows, D)
 
 
 def local(event_rows, event_index, decay, saved_state, dout, w_up, w_in, w_out, skip):
     every = ("batch", "ctx")
     rows, d_out = event_rows[0], dout[0]
-    proj, dy, cum, cumt, send = call(
+    proj, dy, cum, cumt, sums = call(
         project_kernel,
         [((T, PROJ), BF), ((INNER, T), BF), ((H, T), F32), ((T, H), F32), ((H, SROWS, N), BF)],
         BIG, 750_000_000, 4_500_000,
@@ -277,42 +380,79 @@
             pltpu.SemaphoreType.DMA((6,)),
         ],
     )(rows, d_out, decay[0], w_up, w_in, w_out)
-    got = lax.all_to_all(send, "ctx", 0, 0, tiled=True)
-    gout, dx, dbt, dct, misc, hits = call(
+    got = lax.all_to_all(sums, "ctx", 0, 0, tiled=True)
+    place, lane = lax.axis_index("batch"), lax.axis_index("ctx")
+    pos = jnp.stack([place >> 1, place & 1, lane >> 2, lane & 3])
+    keep, give, dx, dbt, dct, misc, hits = call(
         local_kernel,
-        [((INNER, D), BF), ((INNER, T), F32), ((N, T), F32), ((N, T), BF), ((8 * DEV, E), F32), ((8 * DEV, T), BF)],
+        [((INNER // 2, D), F32), ((INNER // 2, D), BF), ((INNER, T), F32), ((N, T), F32), ((N, T), BF),
+         ((8 * DEV, E), BF), ((8 * DEV, T), BF)],
         BIG, 2_500_000_000, 6_000_000,
-        in_specs=[VM] * 7 + [SM], out_specs=(VM,) * 6,
+        in_specs=[VM] * 7 + [SM] * 2, out_specs=(VM,) * 7,
         scratch_shapes=[
             pltpu.VMEM((INNER, T), F32), pltpu.VMEM((INNER, T), BF),
             pltpu.VMEM((INNER, N), BF), pltpu.VMEM((T, T), BF),
         ],
-    )(proj, dy, cum, cumt, jnp.swapaxes(saved_state[0, 0], 1, 2).reshape(INNER, N), d_out, event_index, skip)
-    got, dct = lax.optimization_barrier((got, dct))
+    )(proj, dy, cum, cumt, jnp.swapaxes(saved_state[0, 0], 1, 2).reshape(INNER, N), d_out, event_index, skip, pos)
+    got, give = lax.optimization_barrier((got, give))
     (carries,) = call(
         scan_kernel, [((CTX, HP, N), BF)], 8, 4_000_000, 600_000, in_specs=[VM], out_specs=(VM,)
     )(got)
     carry = lax.all_to_all(carries, "ctx", 0, 0, tiled=True)
+    own, got_go = spread(pos, keep, [send(give, "core", 1)], 0, "x", 512)
+    carry, got_go = lax.optimization_barrier((carry, got_go))
+    own, got_go = spread(pos, own, got_go, 2, "y", 128)
+    own, got_go = spread(pos, own, got_go, 3, "z", 32)
+    (part,) = call(
+        total_kernel, [((8, D), BF)], 4, 20_000, 60_000, in_specs=[VM] * 4, out_specs=(VM,)
+    )(own, *got_go)
+    part = gather(pos, part, 3, "z", 8)
+    part = gather(pos, part, 2, "y", 32)
     (pay,) = call(
-        finish_kernel, [((8 * DEV, 4 * E), BF)], BIG, 1_400_000_000, 6_000_000,
-        in_specs=[VM] * 12, out_specs=(VM,),
-        scratch_shapes=[pltpu.VMEM((PROJ, T), BF), pltpu.VMEM((INNER, T), BF)],
-    )(carry.reshape(INNER, N), proj, cum, dx, dbt, dct, misc, hits, gout, rows, w_in, w_up)
-    pay_got = lax.all_to_all(pay.reshape(DEV, 8, 4 * E), every, 0, 0, tiled=True)
+        finish_kernel, [((8 * DEV, 2 * E), BF)], BIG, 1_400_000_000, 6_000_000,
+        in_specs=[HBM] * 11, out_specs=(HBM,),
+        scratch_shapes=[
+            pltpu.VMEM((INNER, N), BF), pltpu.VMEM((T, PROJ), BF), pltpu.VMEM((H, T), F32),
+            pltpu.VMEM((INNER, T), F32), pltpu.VMEM((N, T), F32), pltpu.VMEM((PROJ, T), BF),
+            pltpu.VMEM((8 * DEV, E), BF), pltpu.VMEM((8 * DEV, T), BF), pltpu.VMEM((T, E), BF),
+            pltpu.VMEM((D, PROJ), BF), pltpu.VMEM((E, D), BF), pltpu.VMEM((INNER, T), BF),
+            pltpu.VMEM((INNER, E), BF), pltpu.VMEM((8 * DEV, E), BF), pltpu.SemaphoreType.DMA((13,)),
+        ],
+    )(carry.reshape(INNER, N), proj, cum, dx, dbt, dct, misc, hits, rows, w_in, w_up)
+    pay_got = lax.all_to_all(pay.reshape(DEV, 8, 2 * E), every, 0, 0, tiled=True)
+    pay_got, part = lax.optimization_barrier((pay_got, part))
     chunk, skip_sum = call(
-        sum_kernel, [((DEV, 8, 4 * E), BF), ((1, 128), F32)], 12, 2_000_000, 4_000_000,
+        sum_kernel, [((DEV, 8, 3 * N), BF), ((1, 128), F32)], 12, 2_000_000, 2_000_000,
         in_specs=[VM], out_specs=(VM,) * 2,
     )(pay_got)
     whole = lax.all_to_all(chunk, every, 0, 0, tiled=True)
+    part = gather(pos, part, 0, "x", 128)
+    (grad_out,) = call(
+        write_kernel, [((2, INNER // 2, D), F32)], 8, 500_000, 3_000_000,
+        in_specs=[SM, VM, VM], out_specs=(VM,),
+    )(pos, part, send(part, "core", 1))
     (table,) = call(
         table_kernel, [((ROWS_DEV, E), F32)], 12, 400_000_000, 2_000_000, in_specs=[VM], out_specs=(VM,)
     )(pay_got)
-    grad_up, grad_in, grad_out = call(
-        last_kernel, [((E, D), F32), ((D, PROJ), F32), ((INNER, D), F32)], 20, 700_000_000, 9_000_000,
-        in_specs=[VM] * 3, out_specs=(VM,) * 3,
-    )(whole, w_up, w_in)
+    grad_up, grad_in = pl.pallas_call(
+        last_kernel,
+        grid=(4,),
+        out_shape=(jax.ShapeDtypeStruct((E, D), F32), jax.ShapeDtypeStruct((D, PROJ), F32)),
+        in_specs=[
+            pl.BlockSpec((8 * DEV, 3 * N), lambda i: (0, 0)),
+            pl.BlockSpec((E, D // 4), lambda i: (0, i)),
+            pl.BlockSpec((D // 4, PROJ), lambda i: (i, 0)),
+        ],
+        out_specs=(
+            pl.BlockSpec((E, D // 4), lambda i: (0, i)),
+            pl.BlockSpec((D // 4, PROJ), lambda i: (i, 0)),
+        ),
+        scratch_shapes=[pltpu.VMEM((PROJ, E), BF)],
+        compiler_params=pltpu.CompilerParams(vmem_limit_bytes=24 * MB),
+        cost_estimate=pl.CostEstimate(flops=700_000_000, bytes_accessed=5_000_000, transcendentals=0),
+    )(whole.reshape(DEV * 8, 3 * N), w_up, w_in)
     grad_skip = skip_sum[0, :H] + skip_sum[0, 32 : 32 + H]
-    return (grad_up, grad_in, grad_out, grad_skip, table)
+    return (grad_up, grad_in, grad_out.reshape(INNER, D), grad_skip, table)
 
 
 def solution(mesh):

time: 121 us -> 131 us (1.083)
  blocking collectives: 49.5 us -> 0 us
  starting transfers between devices: 14.4 us -> 62.7 us
  waiting for transfers between devices: 29.4 us -> 36.6 us
  Pallas kernels: 23.3 us -> 28 us
    all_to_all x2 -> x0, blocking collectives: 49.5 us -> none  [the longest x1 37.8 us: local(): lax.all_to_all(pay.reshape(DEV, 8, 4 * E), every, 0, 0, tiled=True)]
    ppermute x0 -> x20, waiting for transfers between devices: none -> 34.3 us  [send(): lax.ppermute(value, 'batch' if axis in ('x', 'core') else 'ctx', hop(step...]
    ppermute x0 -> x20, starting transfers between devices: none -> 27.3 us  [send(): lax.ppermute(value, 'batch' if axis in ('x', 'core') else 'ctx', hop(step...]
    all_to_all x1, waiting for transfers between devices: 27.2 us -> 0.01 us  [local(): whole = lax.all_to_all(chunk, every, 0, 0, tiled=True)]
    all_to_all x1 -> x3, starting transfers between devices: 8.61 us -> 22.6 us  [the longest x1 9.63 us: local(): lax.all_to_all(pay.reshape(DEV, 8, 2 * E), every, 0, 0, tiled=True)]
    all_to_all x1, starting transfers between devices: 5.79 us -> 12.9 us  [local(): whole = lax.all_to_all(chunk, every, 0, 0, tiled=True)]
    pallas_call x4 -> x12, Pallas kernels: 17.4 us -> 21.4 us  [the longest x1 5.9 us: local(): call(local_kernel, [((INNER // 2, D), F32), ((INNER // 2, D), BF), ((INNE...]
  transfers between devices with their start and end apart: 2 -> 24, of which waited for: 2 -> 16; matrix products, arithmetic and copies ran while one was open for 0% -> 1% of each run, Pallas kernels for 6% -> 11%
where the time goes in v3:
time: 131 us
  starting transfers between devices  62.7 us (48%)
  waiting for transfers between devices  36.6 us (28%)
  Pallas kernels  28 us (21%)
    ppermute x20, waiting for transfers between devices, send(): lax.ppermute(value, 'batch' if axis in ('x', 'core') else 'ctx', hop(step...  34.3 us
    ppermute x20, starting transfers between devices, send(): lax.ppermute(value, 'batch' if axis in ('x', 'core') else 'ctx', hop(step...  27.3 us
    all_to_all x1, starting transfers between devices, local(): whole = lax.all_to_all(chunk, every, 0, 0, tiled=True)  12.9 us
    all_to_all x1, starting transfers between devices, local(): lax.all_to_all(pay.reshape(DEV, 8, 2 * E), every, 0, 0, tiled=True)  9.63 us
    all_to_all x1, starting transfers between devices, local(): got = lax.all_to_all(sums, 'ctx', 0, 0, tiled=True)  8.61 us
    pallas_call x1, Pallas kernels, local(): call(local_kernel, [((INNER // 2, D), F32), ((INNER // 2, D), BF), ((INNE...  5.9 us
    pallas_call x1, Pallas kernels, local(): call(finish_kernel, [((8 * DEV, 2 * E), BF)], BIG, 1400000000, 6000000, i...  5.11 us
    all_to_all x1, starting transfers between devices, local(): carry = lax.all_to_all(carries, 'ctx', 0, 0, tiled=True)  4.36 us
  transfers between devices with their start and end apart: 24, of which 16 were waited for; matrix products, arithmetic and copies ran while one was open for 1% of the time, Pallas kernels for 11%

profile of v3, /device:TPU:1, one launch (start us, length us, event | category | flops | bytes accessed | tf_op | source)
XLA Modules:
  0.0 130.6 jit_solution(6748068908054376607)
XLA Ops:
  0.6 4.4 %shard_map.128 = (bf16[256,1280]{1,0:T(8,128)(2,1)}, bf16[1024,256]{1,0:T(8,128)(2,1)}, f32[16,256]{1,0:T(8,128)}, f32[256,16]{1,0:T(8,128)}, bf16[16,80,128]{2,1,0:T(8,128)(2,1)}) custom-call(bf16[256,256]{1,0:T(8,128)(2,1)} %bitcast.35, bf16[256,512]{1,0:T(8,128)(2,1)} %bitcast.37, f32[16,256]{1,0:T(8,128)} %bitcast.39, bf16[256,512]{1,0:T(8,128)(2,1)} %w_up_ref.1, ...), custom_call_target="tpu_custom_call" | custom-call | flops 750000000 | bytes 4500000 | tf_op jit(solution)/shard_map/pallas_call | solution.py:372
  5.0 8.6 %all-to-all-start = ((bf16[16,80,128]{2,1,0:T(8,128)(2,1)}), bf16[16,80,128]{2,1,0:T(8,128)(2,1)S(1)}, u32[]{:S(2)}, u32[]{:S(2)}) async-start(bf16[16,80,128]{2,1,0:T(8,128)(2,1)} %get-tuple-element.41), calls=%async_computation | async-start | bytes 655360 | tf_op jit(solution)/shard_map/all_to_all | solution.py:383
  14.2 5.9 %shard_map.129 = (f32[512,512]{1,0:T(8,128)}, bf16[512,512]{1,0:T(8,128)(2,1)}, f32[1024,256]{1,0:T(8,128)}, f32[128,256]{1,0:T(8,128)}, bf16[128,256]{1,0:T(8,1...) custom-call(bf16[256,1280]{1,0:T(8,128)(2,1)} %get-tuple-element.42.proj_ref.proj_hbm, ...), custom_call_target="tpu_custom_call" | custom-call | flops 2500000000 | bytes 6000000 | tf_op jit(solution)/shard_map/pallas_call | solution.py:386
  21.4 2.3 %collective-permute-start = (bf16[512,512]{1,0:T(8,128)(2,1)}, bf16[512,512]{1,0:T(8,128)(2,1)S(1)}, u32[]{:S(2)}, u32[]{:S(2)}) collective-permute-start(bf16[512,512]{1,0:T(8,128)(2,1)} %get-tuple-element.49), channel_id=1, source_target_pairs={{0,16},{16,0},{32,48},{48,32},{64,80},{80,64},{96,112},{112,96},{1... | collective-permute-start | bytes 1572872 | tf_op jit(solution)/shard_map/ppermute | solution.py:346
  24.5 4.4 %all-to-all-start.1 = ((bf16[16,64,128]{2,1,0:T(8,128)(2,1)}), bf16[16,64,128]{2,1,0:T(8,128)(2,1)S(1)}, u32[]{:S(2)}, u32[]{:S(2)}) async-start(bf16[16,64,128]{2,1,0:T(8,128)(2,1)} %shard_map.130), calls=%async_computation.1 | async-start | bytes 524288 | tf_op jit(solution)/shard_map/all_to_all | solution.py:401
  32.1 2.4 %collective-permute-start.2 = (bf16[128,512]{1,0:T(8,128)(2,1)S(1)}, bf16[128,512]{1,0:T(8,128)(2,1)S(1)}, u32[]{:S(2)}, u32[]{:S(2)}) collective-permute-start(bf16[128,512]{1,0:T(8,128)(2,1)S(1)} %get-tuple-element.51), channel_id=1, source_target_pairs={{0,64},{16,80},{32,96},{48,112},{64,0},{80,16},{96,32},{112,48},{1... | collective-permute-start | bytes 393224 | tf_op jit(solution)/shard_map/ppermute | solution.py:346
  36.9 3.8 %collective-permute-done.2.refs_1_ = bf16[128,512]{1,0:T(8,128)(2,1)S(1)} collective-permute-done((bf16[128,512]{1,0:T(8,128)(2,1)S(1)}, bf16[128,512]{1,0:T(8,128)(2,1)S(1)}, u32[]{:S(2)}, u32[]{:S(2)}) %collective-permute-start.2) | collective-permute-done | bytes 131104 | tf_op jit(solution)/shard_map/ppermute | solution.py:346
  40.7 5.1 %shard_map.132 = bf16[1024,512]{1,0:T(8,128)(2,1)} custom-call(bf16[1024,128]{1,0:T(8,128)(2,1)} %bitcast.34, bf16[256,1280]{1,0:T(8,128)(2,1)} %get-tuple-element.42.proj_ref.proj_hbm, f32[16,256]{1,0:T(8,128)} %get-tuple-element.44.cum_ref.cum_hbm, f32[1024,256]{1,0:T(8,128)} %get-tuple-element.54.dx_hbm, f32[128,256]{1,0:T(8,128)} %get-tuple-element.55.dbt_hbm, ...), custom_call_target="tpu_custom_call" | custom-call | flops 1400000000 | bytes 6000000 | tf_op jit(solution)/shard_map/pallas_call | solution.py:411
  45.9 9.6 %all-to-all-start.2 = ((bf16[128,8,512]{2,1,0:T(8,128)(2,1)}), bf16[128,8,512]{2,1,0:T(8,128)(2,1)S(1)}, u32[]{:S(2)}, u32[]{:S(2)}) async-start(bf16[128,8,512]{2,1,0:T(8,128)(2,1)} %bitcast.32), calls=%async_computation.2 | async-start | bytes 2097152 | tf_op jit(solution)/shard_map/all_to_all | solution.py:422
  57.6 2.4 %collective-permute-start.5 = (bf16[32,512]{1,0:T(8,128)(2,1)S(1)}, bf16[32,512]{1,0:T(8,128)(2,1)S(1)}, u32[]{:S(2)}, u32[]{:S(2)}) collective-permute-start(bf16[32,512]{1,0:T(8,128)(2,1)S(1)} %get-tuple-element.65), channel_id=1, source_target_pairs={{0,8},{1,9},{2,10},{3,11},{4,12},{5,13},{6,14},{7,15},{8,0},{9,1},... | collective-permute-start | bytes 98312 | tf_op jit(solution)/shard_map/ppermute | solution.py:346
  61.2 7.6 %collective-permute-done.4.refs_0_ = bf16[32,512]{1,0:T(8,128)(2,1)S(1)} collective-permute-done((bf16[32,512]{1,0:T(8,128)(2,1)S(1)}, bf16[32,512]{1,0:T(8,128)(2,1)S(1)}, u32[]{:S(2)}, u32[]{:S(2)}) %collective-permute-start.4) | collective-permute-done | bytes 32800 | tf_op jit(solution)/shard_map/ppermute | solution.py:346
  69.4 1.6 %collective-permute-start.7 = (bf16[8,512]{1,0:T(8,128)(2,1)S(1)}, bf16[8,512]{1,0:T(8,128)(2,1)S(1)}, u32[]{:S(2)}, u32[]{:S(2)}) collective-permute-start(bf16[8,512]{1,0:T(8,128)(2,1)S(1)} %get-tuple-element.68), channel_id=1, source_target_pairs={{0,1},{1,2},{2,3},{3,0},{4,5},{5,6},{6,7},{7,4},{8,9},{9,10},{10,1... | collective-permute-start | bytes 24584 | tf_op jit(solution)/shard_map/ppermute | solution.py:346
  71.0 5.1 %collective-permute-start.8 = (bf16[8,512]{1,0:T(8,128)(2,1)S(1)}, bf16[8,512]{1,0:T(8,128)(2,1)S(1)}, u32[]{:S(2)}, u32[]{:S(2)}) collective-permute-start(bf16[8,512]{1,0:T(8,128)(2,1)S(1)} %get-tuple-element.69), channel_id=1, source_target_pairs={{0,2},{1,3},{2,0},{3,1},{4,6},{5,7},{6,4},{7,5},{8,10},{9,11},{10,... | collective-permute-start | bytes 24584 | tf_op jit(solution)/shard_map/ppermute | solution.py:346
  77.2 1.7 %collective-permute-done.9.c_ref = bf16[8,512]{1,0:T(8,128)(2,1)S(1)} collective-permute-done((bf16[8,512]{1,0:T(8,128)(2,1)S(1)}, bf16[8,512]{1,0:T(8,128)(2,1)S(1)}, u32[]{:S(2)}, u32[]{:S(2)}) %collective-permute-start.9) | collective-permute-done | bytes 8224 | tf_op jit(solution)/shard_map/ppermute | solution.py:346
  81.5 2.4 %collective-permute-done.11.b_ref = bf16[8,512]{1,0:T(8,128)(2,1)S(1)} collective-permute-done((bf16[8,512]{1,0:T(8,128)(2,1)S(1)}, bf16[8,512]{1,0:T(8,128)(2,1)S(1)}, u32[]{:S(2)}, u32[]{:S(2)}) %collective-permute-start.11) | collective-permute-done | bytes 8224 | tf_op jit(solution)/shard_map/ppermute | solution.py:346
  86.3 1.6 %collective-permute-done.15.c_ref = bf16[32,512]{1,0:T(8,128)(2,1)S(1)} collective-permute-done((bf16[32,512]{1,0:T(8,128)(2,1)S(1)}, bf16[32,512]{1,0:T(8,128)(2,1)S(1)}, u32[]{:S(2)}, u32[]{:S(2)}) %collective-permute-start.15) | collective-permute-done | bytes 32800 | tf_op jit(solution)/shard_map/ppermute | solution.py:346
  91.6 12.9 %all-to-all-start.3 = ((bf16[128,8,384]{2,1,0:T(8,128)(2,1)}), bf16[128,8,384]{2,1,0:T(8,128)(2,1)S(1)}, u32[]{:S(2)}, u32[]{:S(2)}) async-start(bf16[128,8,384]{2,1,0:T(8,128)(2,1)} %get-tuple-element.72), calls=%async_computation.3 | async-start | bytes 1572864 | tf_op jit(solution)/shard_map/all_to_all | solution.py:428
  104.5 2.7 %collective-permute-start.18 = (bf16[128,512]{1,0:T(8,128)(2,1)S(1)}, bf16[128,512]{1,0:T(8,128)(2,1)S(1)}, u32[]{:S(2)}, u32[]{:S(2)}) collective-permute-start(bf16[128,512]{1,0:T(8,128)(2,1)S(1)} %bitcast.24), channel_id=1, source_target_pairs={{0,96},{16,112},{32,0},{48,16},{64,32},{80,48},{96,64},{112,80},{1... | collective-permute-start | bytes 393224 | tf_op jit(solution)/shard_map/ppermute | solution.py:346
  108.3 8.9 %collective-permute-done.18.c_ref = bf16[128,512]{1,0:T(8,128)(2,1)S(1)} collective-permute-done((bf16[128,512]{1,0:T(8,128)(2,1)S(1)}, bf16[128,512]{1,0:T(8,128)(2,1)S(1)}, u32[]{:S(2)}, u32[]{:S(2)}) %collective-permute-start.18) | collective-permute-done | bytes 131104 | tf_op jit(solution)/shard_map/ppermute | solution.py:346
  117.2 1.5 %collective-permute-done.17.b_ref = bf16[128,512]{1,0:T(8,128)(2,1)S(1)} collective-permute-done((bf16[128,512]{1,0:T(8,128)(2,1)S(1)}, bf16[128,512]{1,0:T(8,128)(2,1)S(1)}, u32[]{:S(2)}, u32[]{:S(2)}) %collective-permute-start.17) | collective-permute-done | bytes 131104 | tf_op jit(solution)/shard_map/ppermute | solution.py:346
  118.7 2.6 %collective-permute-done.16.a_ref = bf16[128,512]{1,0:T(8,128)(2,1)S(1)} collective-permute-done((bf16[128,512]{1,0:T(8,128)(2,1)S(1)}, bf16[128,512]{1,0:T(8,128)(2,1)S(1)}, u32[]{:S(2)}, u32[]{:S(2)}) %collective-permute-start.16) | collective-permute-done | bytes 131104 | tf_op jit(solution)/shard_map/ppermute | solution.py:346
  122.8 1.5 %shard_map.142 = f32[512,256]{1,0:T(8,128)} custom-call(bf16[128,8,512]{2,1,0:T(8,128)(2,1)S(1)} %all-to-all-done.2.got_ref), custom_call_target="tpu_custom_call" | custom-call | flops 400000000 | bytes 2000000 | tf_op jit(solution)/shard_map/pallas_call | solution.py:434
  124.9 2.0 %shard_map.141 = f32[2,512,512]{2,1,0:T(8,128)} custom-call(s32[4]{0:T(128)S(1)} %copy-done.3, bf16[512,512]{1,0:T(8,128)(2,1)S(1)} %bitcast.22, bf16[512,512]{1,0:T(8,128)(2,1)S(1)} %collective-permute-done.19.other_ref), custom_call_target="tpu_custom_call" | custom-call | flops 500000 | bytes 3000000 | tf_op jit(solution)/shard_map/pallas_call | solution.py:430
  126.9 3.7 %shard_map.139 = (f32[256,512]{1,0:T(8,128)}, f32[512,1280]{1,0:T(8,128)}) custom-call(bf16[1024,384]{1,0:T(8,128)(2,1)S(1)} %bitcast.23, bf16[256,512]{1,0:T(8,128)(2,1)S(1)} %copy-done.1, bf16[512,1280]{1,0:T(8,128)(2,1)S(1)} %copy-done), custom_call_target="tpu_custom_call" | custom-call | flops 700000000 | bytes 5000000 | tf_op jit(solution)/shard_map/pallas_call | solution.py:437
  (51 shorter events, 25.0 us)
Async XLA Ops:
  5.0 16.4 %all-to-all-start = ((bf16[16,80,128]{2,1,0:T(8,128)(2,1)}), bf16[16,80,128]{2,1,0:T(8,128)(2,1)S(1)}, u32[]{:S(2)}, u32[]{:S(2)}) async-start(bf16[16,80,128]{2,1,0:T(8,128)(2,1)} %get-tuple-element.41), calls=%async_computation | async-start | bytes 655360 | tf_op jit(solution)/shard_map/all_to_all | solution.py:383
  21.4 7.4 %collective-permute-start = (bf16[512,512]{1,0:T(8,128)(2,1)}, bf16[512,512]{1,0:T(8,128)(2,1)S(1)}, u32[]{:S(2)}, u32[]{:S(2)}) collective-permute-start(bf16[512,512]{1,0:T(8,128)(2,1)} %get-tuple-element.49), channel_id=1, source_target_pairs={{0,16},{16,0},{32,48},{48,32},{64,80},{80,64},{96,112},{112,96},{1... | collective-permute-start | bytes 1572872 | tf_op jit(solution)/shard_map/ppermute | solution.py:346
  24.5 12.2 %all-to-all-start.1 = ((bf16[16,64,128]{2,1,0:T(8,128)(2,1)}), bf16[16,64,128]{2,1,0:T(8,128)(2,1)S(1)}, u32[]{:S(2)}, u32[]{:S(2)}) async-start(bf16[16,64,128]{2,1,0:T(8,128)(2,1)} %shard_map.130), calls=%async_computation.1 | async-start | bytes 524288 | tf_op jit(solution)/shard_map/all_to_all | solution.py:401
  30.9 6.1 %collective-permute-start.1 = (bf16[128,512]{1,0:T(8,128)(2,1)S(1)}, bf16[128,512]{1,0:T(8,128)(2,1)S(1)}, u32[]{:S(2)}, u32[]{:S(2)}) collective-permute-start(bf16[128,512]{1,0:T(8,128)(2,1)S(1)} %get-tuple-element.50), channel_id=1, source_target_pairs={{0,32},{16,48},{32,64},{48,80},{64,96},{80,112},{96,0},{112,16},{1... | collective-permute-start | bytes 393224 | tf_op jit(solution)/shard_map/ppermute | solution.py:346
  32.1 8.6 %collective-permute-start.2 = (bf16[128,512]{1,0:T(8,128)(2,1)S(1)}, bf16[128,512]{1,0:T(8,128)(2,1)S(1)}, u32[]{:S(2)}, u32[]{:S(2)}) collective-permute-start(bf16[128,512]{1,0:T(8,128)(2,1)S(1)} %get-tuple-element.51), channel_id=1, source_target_pairs={{0,64},{16,80},{32,96},{48,112},{64,0},{80,16},{96,32},{112,48},{1... | collective-permute-start | bytes 393224 | tf_op jit(solution)/shard_map/ppermute | solution.py:346
  34.6 6.1 %collective-permute-start.3 = (bf16[128,512]{1,0:T(8,128)(2,1)S(1)}, bf16[128,512]{1,0:T(8,128)(2,1)S(1)}, u32[]{:S(2)}, u32[]{:S(2)}) collective-permute-start(bf16[128,512]{1,0:T(8,128)(2,1)S(1)} %get-tuple-element.52), channel_id=1, source_target_pairs={{0,96},{16,112},{32,0},{48,16},{64,32},{80,48},{96,64},{112,80},{1... | collective-permute-start | bytes 393224 | tf_op jit(solution)/shard_map/ppermute | solution.py:346
  45.9 44.7 %all-to-all-start.2 = ((bf16[128,8,512]{2,1,0:T(8,128)(2,1)}), bf16[128,8,512]{2,1,0:T(8,128)(2,1)S(1)}, u32[]{:S(2)}, u32[]{:S(2)}) async-start(bf16[128,8,512]{2,1,0:T(8,128)(2,1)} %bitcast.32), calls=%async_computation.2 | async-start | bytes 2097152 | tf_op jit(solution)/shard_map/all_to_all | solution.py:422
  56.1 12.6 %collective-permute-start.4 = (bf16[32,512]{1,0:T(8,128)(2,1)S(1)}, bf16[32,512]{1,0:T(8,128)(2,1)S(1)}, u32[]{:S(2)}, u32[]{:S(2)}) collective-permute-start(bf16[32,512]{1,0:T(8,128)(2,1)S(1)} %get-tuple-element.64), channel_id=1, source_target_pairs={{0,4},{1,5},{2,6},{3,7},{4,8},{5,9},{6,10},{7,11},{8,12},{9,13},{1... | collective-permute-start | bytes 98312 | tf_op jit(solution)/shard_map/ppermute | solution.py:346
  57.6 11.2 %collective-permute-start.5 = (bf16[32,512]{1,0:T(8,128)(2,1)S(1)}, bf16[32,512]{1,0:T(8,128)(2,1)S(1)}, u32[]{:S(2)}, u32[]{:S(2)}) collective-permute-start(bf16[32,512]{1,0:T(8,128)(2,1)S(1)} %get-tuple-element.65), channel_id=1, source_target_pairs={{0,8},{1,9},{2,10},{3,11},{4,12},{5,13},{6,14},{7,15},{8,0},{9,1},... | collective-permute-start | bytes 98312 | tf_op jit(solution)/shard_map/ppermute | solution.py:346
  60.0 8.8 %collective-permute-start.6 = (bf16[32,512]{1,0:T(8,128)(2,1)S(1)}, bf16[32,512]{1,0:T(8,128)(2,1)S(1)}, u32[]{:S(2)}, u32[]{:S(2)}) collective-permute-start(bf16[32,512]{1,0:T(8,128)(2,1)S(1)} %get-tuple-element.66), channel_id=1, source_target_pairs={{0,12},{1,13},{2,14},{3,15},{4,0},{5,1},{6,2},{7,3},{8,4},{9,5},{1... | collective-permute-start | bytes 98312 | tf_op jit(solution)/shard_map/ppermute | solution.py:346
  69.4 6.7 %collective-permute-start.7 = (bf16[8,512]{1,0:T(8,128)(2,1)S(1)}, bf16[8,512]{1,0:T(8,128)(2,1)S(1)}, u32[]{:S(2)}, u32[]{:S(2)}) collective-permute-start(bf16[8,512]{1,0:T(8,128)(2,1)S(1)} %get-tuple-element.68), channel_id=1, source_target_pairs={{0,1},{1,2},{2,3},{3,0},{4,5},{5,6},{6,7},{7,4},{8,9},{9,10},{10,1... | collective-permute-start | bytes 24584 | tf_op jit(solution)/shard_map/ppermute | solution.py:346
  71.0 6.2 %collective-permute-start.8 = (bf16[8,512]{1,0:T(8,128)(2,1)S(1)}, bf16[8,512]{1,0:T(8,128)(2,1)S(1)}, u32[]{:S(2)}, u32[]{:S(2)}) collective-permute-start(bf16[8,512]{1,0:T(8,128)(2,1)S(1)} %get-tuple-element.69), channel_id=1, source_target_pairs={{0,2},{1,3},{2,0},{3,1},{4,6},{5,7},{6,4},{7,5},{8,10},{9,11},{10,... | collective-permute-start | bytes 24584 | tf_op jit(solution)/shard_map/ppermute | solution.py:346
  76.1 2.8 %collective-permute-start.9 = (bf16[8,512]{1,0:T(8,128)(2,1)S(1)}, bf16[8,512]{1,0:T(8,128)(2,1)S(1)}, u32[]{:S(2)}, u32[]{:S(2)}) collective-permute-start(bf16[8,512]{1,0:T(8,128)(2,1)S(1)} %get-tuple-element.70), channel_id=1, source_target_pairs={{0,3},{1,0},{2,1},{3,2},{4,7},{5,4},{6,5},{7,6},{8,11},{9,8},{10,9... | collective-permute-start | bytes 24584 | tf_op jit(solution)/shard_map/ppermute | solution.py:346
  78.9 2.6 %collective-permute-start.12 = (bf16[8,512]{1,0:T(8,128)(2,1)S(1)}, bf16[8,512]{1,0:T(8,128)(2,1)S(1)}, u32[]{:S(2)}, u32[]{:S(2)}) collective-permute-start(bf16[8,512]{1,0:T(8,128)(2,1)S(1)} %shard_map.135.own_ref), channel_id=1, source_target_pairs={{0,3},{1,0},{2,1},{3,2},{4,7},{5,4},{6,5},{7,6},{8,11},{9,8},{10,9... | collective-permute-start | bytes 24584 | tf_op jit(solution)/shard_map/ppermute | solution.py:346
  79.9 4.0 %collective-permute-start.11 = (bf16[8,512]{1,0:T(8,128)(2,1)S(1)}, bf16[8,512]{1,0:T(8,128)(2,1)S(1)}, u32[]{:S(2)}, u32[]{:S(2)}) collective-permute-start(bf16[8,512]{1,0:T(8,128)(2,1)S(1)} %shard_map.135.own_ref), channel_id=1, source_target_pairs={{0,2},{1,3},{2,0},{3,1},{4,6},{5,7},{6,4},{7,5},{8,10},{9,11},{10,... | collective-permute-start | bytes 24584 | tf_op jit(solution)/shard_map/ppermute | solution.py:346
  80.5 3.7 %collective-permute-start.10 = (bf16[8,512]{1,0:T(8,128)(2,1)S(1)}, bf16[8,512]{1,0:T(8,128)(2,1)S(1)}, u32[]{:S(2)}, u32[]{:S(2)}) collective-permute-start(bf16[8,512]{1,0:T(8,128)(2,1)S(1)} %shard_map.135.own_ref), channel_id=1, source_target_pairs={{0,1},{1,2},{2,3},{3,0},{4,5},{5,6},{6,7},{7,4},{8,9},{9,10},{10,1... | collective-permute-start | bytes 24584 | tf_op jit(solution)/shard_map/ppermute | solution.py:346
  84.7 3.1 %collective-permute-start.15 = (bf16[32,512]{1,0:T(8,128)(2,1)S(1)}, bf16[32,512]{1,0:T(8,128)(2,1)S(1)}, u32[]{:S(2)}, u32[]{:S(2)}) collective-permute-start(bf16[32,512]{1,0:T(8,128)(2,1)S(1)} %bitcast.28), channel_id=1, source_target_pairs={{0,12},{1,13},{2,14},{3,15},{4,0},{5,1},{6,2},{7,3},{8,4},{9,5},{1... | collective-permute-start | bytes 98312 | tf_op jit(solution)/shard_map/ppermute | solution.py:346
  84.8 4.3 %collective-permute-start.14 = (bf16[32,512]{1,0:T(8,128)(2,1)S(1)}, bf16[32,512]{1,0:T(8,128)(2,1)S(1)}, u32[]{:S(2)}, u32[]{:S(2)}) collective-permute-start(bf16[32,512]{1,0:T(8,128)(2,1)S(1)} %bitcast.29), channel_id=1, source_target_pairs={{0,8},{1,9},{2,10},{3,11},{4,12},{5,13},{6,14},{7,15},{8,0},{9,1},... | collective-permute-start | bytes 98312 | tf_op jit(solution)/shard_map/ppermute | solution.py:346
  84.9 5.1 %collective-permute-start.13 = (bf16[32,512]{1,0:T(8,128)(2,1)S(1)}, bf16[32,512]{1,0:T(8,128)(2,1)S(1)}, u32[]{:S(2)}, u32[]{:S(2)}) collective-permute-start(bf16[32,512]{1,0:T(8,128)(2,1)S(1)} %bitcast.30), channel_id=1, source_target_pairs={{0,4},{1,5},{2,6},{3,7},{4,8},{5,9},{6,10},{7,11},{8,12},{9,13},{1... | collective-permute-start | bytes 98312 | tf_op jit(solution)/shard_map/ppermute | solution.py:346
  91.6 35.3 %all-to-all-start.3 = ((bf16[128,8,384]{2,1,0:T(8,128)(2,1)}), bf16[128,8,384]{2,1,0:T(8,128)(2,1)S(1)}, u32[]{:S(2)}, u32[]{:S(2)}) async-start(bf16[128,8,384]{2,1,0:T(8,128)(2,1)} %get-tuple-element.72), calls=%async_computation.3 | async-start | bytes 1572864 | tf_op jit(solution)/shard_map/all_to_all | solution.py:428
  104.5 12.7 %collective-permute-start.18 = (bf16[128,512]{1,0:T(8,128)(2,1)S(1)}, bf16[128,512]{1,0:T(8,128)(2,1)S(1)}, u32[]{:S(2)}, u32[]{:S(2)}) collective-permute-start(bf16[128,512]{1,0:T(8,128)(2,1)S(1)} %bitcast.24), channel_id=1, source_target_pairs={{0,96},{16,112},{32,0},{48,16},{64,32},{80,48},{96,64},{112,80},{1... | collective-permute-start | bytes 393224 | tf_op jit(solution)/shard_map/ppermute | solution.py:346
  107.2 11.6 %collective-permute-start.17 = (bf16[128,512]{1,0:T(8,128)(2,1)S(1)}, bf16[128,512]{1,0:T(8,128)(2,1)S(1)}, u32[]{:S(2)}, u32[]{:S(2)}) collective-permute-start(bf16[128,512]{1,0:T(8,128)(2,1)S(1)} %bitcast.25), channel_id=1, source_target_pairs={{0,64},{16,80},{32,96},{48,112},{64,0},{80,16},{96,32},{112,48},{1... | collective-permute-start | bytes 393224 | tf_op jit(solution)/shard_map/ppermute | solution.py:346
  107.8 13.6 %collective-permute-start.16 = (bf16[128,512]{1,0:T(8,128)(2,1)S(1)}, bf16[128,512]{1,0:T(8,128)(2,1)S(1)}, u32[]{:S(2)}, u32[]{:S(2)}) collective-permute-start(bf16[128,512]{1,0:T(8,128)(2,1)S(1)} %bitcast.26), channel_id=1, source_target_pairs={{0,32},{16,48},{32,64},{48,80},{64,96},{80,112},{96,0},{112,16},{1... | collective-permute-start | bytes 393224 | tf_op jit(solution)/shard_map/ppermute | solution.py:346
  122.0 2.9 %collective-permute-start.19 = (bf16[512,512]{1,0:T(8,128)(2,1)S(1)}, bf16[512,512]{1,0:T(8,128)(2,1)S(1)}, u32[]{:S(2)}, u32[]{:S(2)}) collective-permute-start(bf16[512,512]{1,0:T(8,128)(2,1)S(1)} %bitcast.21), channel_id=1, source_target_pairs={{0,16},{16,0},{32,48},{48,32},{64,80},{80,64},{96,112},{112,96},{1... | collective-permute-start | bytes 1572872 | tf_op jit(solution)/shard_map/ppermute | solution.py:346
  (5 other events, 29.8 us)

commit v4 on v2

--- a/solution.py
+++ b/solution.py
@@ -5,7 +5,7 @@
 from jax import lax
 from jax.experimental import pallas as pl
 from jax.experimental.pallas import tpu as pltpu
-from jax.sharding import PartitionSpec as P
+from jax.sharding import Mesh, PartitionSpec as P
 
 T = 256
 E = 256
@@ -118,8 +118,8 @@
             carry = got_ref[j, 0:HP, :].astype(F32) + amount * carry
 
 
-def local_kernel(proj_ref, dy_ref, cum_ref, cumt_ref, h0_ref, dout_ref, index_ref, skip_ref,
-                 gout_ref, dx_ref, dbt_ref, dct_ref, misc_ref, hits_ref, y_ref, sdy_ref, h0t_ref, sum_ref):
+def local_kernel(proj_ref, dy_ref, cum_ref, cumt_ref, h0_ref, dout_ref, index_ref, skip_ref, core_ref,
+                 keep_ref, give_ref, dx_ref, dbt_ref, dct_ref, misc_ref, hits_ref, y_ref, sdy_ref, h0t_ref, sum_ref):
     proj_t = jnp.transpose(proj_ref[...])
     bt = proj_t[INNER : INNER + N, :]
     ct = proj_t[INNER + N :, :]
@@ -170,7 +170,12 @@
         a01 += m01 * q0[:, N:]
         a11 += m11 * q11
         skip_sums.append(jnp.sum(x_f * dy_f, keepdims=True))
-    gout_ref[...] = dot(y_ref[...].astype(BF), dout_ref[...]).astype(BF)
+    core = core_ref[0]
+    half = INNER // 2
+    mine = pl.ds(pl.multiple_of(core * half, half), half)
+    other = pl.ds(pl.multiple_of((1 - core) * half, half), half)
+    give_ref[...] = dot(y_ref[other, :].astype(BF), dout_ref[...]).astype(BF)
+    keep_ref[...] = dot(y_ref[mine, :].astype(BF), dout_ref[...])
     sum_ref[:N, :N] = a00.astype(BF)
     sum_ref[:N, N:] = a01.astype(BF)
     sum_ref[N:, :N] = zero
@@ -202,40 +207,77 @@
         top = whole.astype(BF).astype(F32)
         extra = extra + jnp.where(lane == 128 + h, top, 0.0) + jnp.where(lane == 160 + h, whole - top, 0.0)
     misc = dot(heads, v.astype(F32).astype(BF))
-    misc_ref[...] = misc + jnp.where((row_id & 7) == 6, extra, 0.0)
-
-
-def finish_kernel(carry_ref, proj_ref, cum_ref, dx_ref, dbt_ref, dct_ref, misc_ref, hits_ref, gout_ref, rows_ref,
-                  w_in_ref, w_up_ref, out_ref, d_ref, tx_ref):
+    misc_ref[...] = (misc + jnp.where((row_id & 7) == 6, extra, 0.0)).astype(BF)
+
+
+def finish_kernel(carry_hbm, proj_hbm, cum_hbm, dx_hbm, dbt_hbm, dct_hbm, misc_hbm, hits_hbm, rows_hbm,
+                  w_in_hbm, w_up_hbm, outer_hbm, out_hbm,
+                  carry_ref, proj_ref, cum_ref, dx_ref, dbt_ref, d_ref, misc_ref, hits_ref, rows_ref,
+                  w_in_ref, w_up_ref, tx_ref, left_ref, right_ref, sems):
+    copies = [
+        pltpu.make_async_copy(a, b, sems.at[n])
+        for n, (a, b) in enumerate((
+            (carry_hbm, carry_ref), (proj_hbm, proj_ref), (cum_hbm, cum_ref), (dx_hbm, dx_ref),
+            (dbt_hbm, dbt_ref), (dct_hbm, d_ref.at[INNER + N :, :]), (rows_hbm, rows_ref),
+            (w_in_hbm, w_in_ref), (w_up_hbm, w_up_ref), (hits_hbm, hits_ref), (misc_hbm, misc_ref),
+            (outer_hbm, out_hbm.at[:, 2 * E :]),
+        ))
+    ]
+    for copy in copies:
+        copy.start()
+    for copy in copies[:3]:
+        copy.wait()
     proj_t = jnp.transpose(proj_ref[...])
     bt = proj_t[INNER : INNER + N, :]
     cum = cum_ref[...]
     tail = DT * jnp.exp(cum[:, T - 1 : T] - cum)
     carry = carry_ref[...]
     entering = dot(carry, bt)
+    copies[3].wait()
     for h in range(H):
         lo, hi = h * HP, (h + 1) * HP
         tl = tail[h : h + 1, :]
         d_ref[lo:hi, :] = (dx_ref[lo:hi, :] + tl * entering[lo:hi, :]).astype(BF)
         tx_ref[lo:hi, :] = (tl * proj_t[lo:hi, :].astype(F32)).astype(BF)
+    for copy in copies[4:7]:
+        copy.wait()
     d_ref[INNER : INNER + N, :] = (dbt_ref[...] + dot(carry, tx_ref[...], TN)).astype(BF)
-    d_ref[INNER + N :, :] = dct_ref[...]
     d = d_ref[...]
     g = dot(d, rows_ref[...]).astype(BF)
-    out_ref[:, :E] = g[:INNER, :]
+    left_ref[...] = g[:INNER, :]
+    out_left = pltpu.make_async_copy(left_ref, out_hbm.at[:, :E], sems.at[12])
+    out_left.start()
+    copies[7].wait()
     du = dot(w_in_ref[...], d).astype(BF)
+    copies[8].wait()
     de = dot(w_up_ref[...], du).astype(BF)
     r = lax.broadcasted_iota(jnp.int32, (8 * DEV, 2 * N), 0)
     j = lax.broadcasted_iota(jnp.int32, (1, 2 * N), 1)
     place = jnp.where(r == 8 * lax.shift_right_logical(j, 1) + (j & 1), 1.0, 0.0).astype(BF)
-    misc = misc_ref[...] + dot(hits_ref[...], de, NT) + dot(place, g[INNER:, :])
-    out_ref[:, E : 2 * E] = misc.astype(BF)
-    out_ref[:, 2 * E :] = gout_ref[...]
+    copies[9].wait()
+    copies[10].wait()
+    misc = misc_ref[...].astype(F32) + dot(hits_ref[...], de, NT) + dot(place, g[INNER:, :])
+    right_ref[...] = misc.astype(BF)
+    out_right = pltpu.make_async_copy(right_ref, out_hbm.at[:, E : 2 * E], sems.at[13])
+    out_right.start()
+    copies[11].wait()
+    out_left.wait()
+    out_right.wait()
+
+
+def pair_kernel(keep_ref, got_ref, out_ref):
+    total = (keep_ref[...] + got_ref[...].astype(F32)).astype(BF)
+    out_ref[: INNER // 2, :] = total[:, :E]
+    out_ref[INNER // 2 :, :] = total[:, E:]
 
 
 def sum_kernel(got_ref, chunk_ref, skip_ref):
-    total = jnp.sum(got_ref[...].astype(F32), axis=0)
-    chunk_ref[...] = jnp.broadcast_to(total[None], chunk_ref.shape).astype(BF)
+    total = jnp.sum(got_ref[:, :, : 2 * E].astype(F32), axis=0)
+    side = jnp.concatenate([total[0:2, E : E + N], total[0:2, E + N :], jnp.zeros((4, N), F32)], axis=0)
+    outer = got_ref[:, :, 2 * E :].reshape(4, 2, CTX, 8, E)
+    halves = [jnp.sum(outer[:, c].reshape(DEV // 2, 8, E).astype(F32), axis=0) for c in range(2)]
+    chunk = jnp.concatenate([total[:, :E], side] + halves, axis=1)
+    chunk_ref[...] = jnp.broadcast_to(chunk[None], chunk_ref.shape).astype(BF)
     skip_ref[...] = total[6:7, E + 128 : E + 256]
 
 
@@ -252,21 +294,39 @@
     table_ref[...] = dot(hits, misc.reshape(DEV * 8, E), TN)
 
 
-def last_kernel(got_ref, w_up_ref, w_in_ref, up_ref, in_ref, out_ref):
-    got = got_ref[...].reshape(DEV * 8, 4 * E)
-    out_ref[...] = got[:, 2 * E :].astype(F32)
-    j = lax.broadcasted_iota(jnp.int32, (2 * N, 8 * DEV), 0)
-    r = lax.broadcasted_iota(jnp.int32, (2 * N, 8 * DEV), 1)
-    pick = jnp.where(r == 8 * lax.shift_right_logical(j, 1) + (j & 1), 1.0, 0.0).astype(BF)
-    g = jnp.concatenate([got[:, :E], dot(pick, got[:, E : 2 * E]).astype(BF)], axis=0)
+def last_kernel(core_ref, own_ref, other_ref, w_up_ref, w_in_ref, up_ref, in_ref, go_ref, g_ref, side_ref):
+    step = pl.program_id(0)
+    core = core_ref[0]
+    sources = ((core, own_ref), (1 - core, other_ref))
+
+    @pl.when(step == 0)
+    def _():
+        for x in range(4):
+            for at, ref in sources:
+                rows = pl.ds(pl.multiple_of((2 * x + at) * N, N), N)
+                g_ref[rows, :] = ref[x * N : (x + 1) * N, :E]
+                side_ref[rows, :] = ref[x * N : (x + 1) * N, E : E + N]
+        j = lax.broadcasted_iota(jnp.int32, (2 * N, 8 * DEV), 0)
+        r = lax.broadcasted_iota(jnp.int32, (2 * N, 8 * DEV), 1)
+        first = r - (8 * lax.shift_right_logical(j, 1) + (j & 1))
+        for m in range(2):
+            pick = jnp.where(first == 2 * m, 1.0, 0.0).astype(BF)
+            g_ref[INNER:, m * N : (m + 1) * N] = dot(pick, side_ref[...]).astype(BF)
+
+    g = g_ref[...]
     in_ref[...] = lax.dot_general(w_up_ref[...], g, (((0,), (1,)), ((), ())), preferred_element_type=F32)
     up_ref[...] = jnp.transpose(dot(w_in_ref[...], g))
+    lanes = pl.ds(pl.multiple_of(E + N + E * lax.shift_right_logical(step, 1), N), E)
+    for m in range(2):
+        rows = pl.ds(pl.multiple_of((2 * m + (step & 1)) * N, N), N)
+        for at, ref in sources:
+            go_ref[pl.ds(pl.multiple_of(at * N, N), N), m * E : (m + 1) * E] = ref[rows, lanes].astype(F32)
 
 
 def local(event_rows, event_index, decay, saved_state, dout, w_up, w_in, w_out, skip):
-    every = ("batch", "ctx")
+    every = ("x", "core", "y", "z")
     rows, d_out = event_rows[0], dout[0]
-    proj, dy, cum, cumt, send = call(
+    proj, dy, cum, cumt, sums = call(
         project_kernel,
         [((T, PROJ), BF), ((INNER, T), BF), ((H, T), F32), ((T, H), F32), ((H, SROWS, N), BF)],
         BIG, 750_000_000, 4_500_000,
@@ -277,55 +337,79 @@
             pltpu.SemaphoreType.DMA((6,)),
         ],
     )(rows, d_out, decay[0], w_up, w_in, w_out)
-    got = lax.all_to_all(send, "ctx", 0, 0, tiled=True)
-    gout, dx, dbt, dct, misc, hits = call(
+    got = lax.all_to_all(sums, ("y", "z"), 0, 0, tiled=True)
+    core = lax.axis_index("core").reshape(1)
+    keep, give, dx, dbt, dct, misc, hits = call(
         local_kernel,
-        [((INNER, D), BF), ((INNER, T), F32), ((N, T), F32), ((N, T), BF), ((8 * DEV, E), F32), ((8 * DEV, T), BF)],
+        [((INNER // 2, D), F32), ((INNER // 2, D), BF), ((INNER, T), F32), ((N, T), F32), ((N, T), BF),
+         ((8 * DEV, E), BF), ((8 * DEV, T), BF)],
         BIG, 2_500_000_000, 6_000_000,
-        in_specs=[VM] * 7 + [SM], out_specs=(VM,) * 6,
+        in_specs=[VM] * 7 + [SM] * 2, out_specs=(VM,) * 7,
         scratch_shapes=[
             pltpu.VMEM((INNER, T), F32), pltpu.VMEM((INNER, T), BF),
             pltpu.VMEM((INNER, N), BF), pltpu.VMEM((T, T), BF),
         ],
-    )(proj, dy, cum, cumt, jnp.swapaxes(saved_state[0, 0], 1, 2).reshape(INNER, N), d_out, event_index, skip)
-    got, dct = lax.optimization_barrier((got, dct))
+    )(proj, dy, cum, cumt, jnp.swapaxes(saved_state[0, 0], 1, 2).reshape(INNER, N), d_out, event_index, skip, core)
+    got, give = lax.optimization_barrier((got, give))
     (carries,) = call(
         scan_kernel, [((CTX, HP, N), BF)], 8, 4_000_000, 600_000, in_specs=[VM], out_specs=(VM,)
     )(got)
-    carry = lax.all_to_all(carries, "ctx", 0, 0, tiled=True)
+    carry = lax.all_to_all(carries, ("y", "z"), 0, 0, tiled=True)
+    (outer,) = call(
+        pair_kernel, [((8 * DEV, E), BF)], 8, 300_000, 2_000_000, in_specs=[VM] * 2, out_specs=(VM,)
+    )(keep, lax.ppermute(give, "core", [(0, 1), (1, 0)]))
+    carry, outer = lax.optimization_barrier((carry, outer))
     (pay,) = call(
-        finish_kernel, [((8 * DEV, 4 * E), BF)], BIG, 1_400_000_000, 6_000_000,
-        in_specs=[VM] * 12, out_specs=(VM,),
-        scratch_shapes=[pltpu.VMEM((PROJ, T), BF), pltpu.VMEM((INNER, T), BF)],
-    )(carry.reshape(INNER, N), proj, cum, dx, dbt, dct, misc, hits, gout, rows, w_in, w_up)
-    pay_got = lax.all_to_all(pay.reshape(DEV, 8, 4 * E), every, 0, 0, tiled=True)
+        finish_kernel, [((8 * DEV, 3 * E), BF)], BIG, 1_400_000_000, 6_000_000,
+        in_specs=[HBM] * 12, out_specs=(HBM,),
+        scratch_shapes=[
+            pltpu.VMEM((INNER, N), BF), pltpu.VMEM((T, PROJ), BF), pltpu.VMEM((H, T), F32),
+            pltpu.VMEM((INNER, T), F32), pltpu.VMEM((N, T), F32), pltpu.VMEM((PROJ, T), BF),
+            pltpu.VMEM((8 * DEV, E), BF), pltpu.VMEM((8 * DEV, T), BF), pltpu.VMEM((T, E), BF),
+            pltpu.VMEM((D, PROJ), BF), pltpu.VMEM((E, D), BF), pltpu.VMEM((INNER, T), BF),
+            pltpu.VMEM((INNER, E), BF), pltpu.VMEM((8 * DEV, E), BF), pltpu.SemaphoreType.DMA((14,)),
+        ],
+    )(carry.reshape(INNER, N), proj, cum, dx, dbt, dct, misc, hits, rows, w_in, w_up, outer)
+    pay_got = lax.all_to_all(pay.reshape(DEV, 8, 3 * E), every, 0, 0, tiled=True)
     chunk, skip_sum = call(
-        sum_kernel, [((DEV, 8, 4 * E), BF), ((1, 128), F32)], 12, 2_000_000, 4_000_000,
+        sum_kernel, [((DEV // 2, 8, 7 * N), BF), ((1, 128), F32)], 12, 2_000_000, 3_000_000,
         in_specs=[VM], out_specs=(VM,) * 2,
     )(pay_got)
-    whole = lax.all_to_all(chunk, every, 0, 0, tiled=True)
+    whole = lax.all_to_all(chunk, ("x", "y", "z"), 0, 0, tiled=True).reshape(DEV * 4, 7 * N)
+    other = lax.ppermute(whole, "core", [(0, 1), (1, 0)])
     (table,) = call(
         table_kernel, [((ROWS_DEV, E), F32)], 12, 400_000_000, 2_000_000, in_specs=[VM], out_specs=(VM,)
     )(pay_got)
-    grad_up, grad_in, grad_out = call(
-        last_kernel, [((E, D), F32), ((D, PROJ), F32), ((INNER, D), F32)], 20, 700_000_000, 9_000_000,
-        in_specs=[VM] * 3, out_specs=(VM,) * 3,
-    )(whole, w_up, w_in)
+    full = pl.BlockSpec((DEV * 4, 7 * N), lambda i: (0, 0))
+    column = pl.BlockSpec((E, D // 4), lambda i: (0, i))
+    row = pl.BlockSpec((D // 4, PROJ), lambda i: (i, 0))
+    grad_up, grad_in, grad_out = pl.pallas_call(
+        last_kernel,
+        grid=(4,),
+        out_shape=tuple(jax.ShapeDtypeStruct(s, F32) for s in ((E, D), (D, PROJ), (INNER, D))),
+        in_specs=[SM, full, full, column, row],
+        out_specs=(column, row, pl.BlockSpec((INNER // 4, D), lambda i: (i, 0))),
+        scratch_shapes=[pltpu.VMEM((PROJ, E), BF), pltpu.VMEM((8 * DEV, N), BF)],
+        compiler_params=pltpu.CompilerParams(vmem_limit_bytes=24 * MB),
+        cost_estimate=pl.CostEstimate(flops=700_000_000, bytes_accessed=8_000_000, transcendentals=0),
+    )(core, whole, other, w_up, w_in)
     grad_skip = skip_sum[0, :H] + skip_sum[0, 32 : 32 + H]
     return (grad_up, grad_in, grad_out, grad_skip, table)
 
 
 def solution(mesh):
+    mesh = Mesh(mesh.devices.reshape(4, 2, 4, 4), ("x", "core", "y", "z"))
+    batch, ctx = ("x", "core"), ("y", "z")
     in_specs = (
-        P("batch", "ctx", None),
-        P("batch", "ctx"),
-        P("batch", None, "ctx"),
-        P("batch", "ctx", None, None, None),
-        P("batch", "ctx", None),
+        P(batch, ctx, None),
+        P(batch, ctx),
+        P(batch, None, ctx),
+        P(batch, ctx, None, None, None),
+        P(batch, ctx, None),
         P(),
         P(),
         P(),
         P(),
     )
-    out_specs = (P(), P(), P(), P(), P(("batch", "ctx"), None))
+    out_specs = (P(), P(), P(), P(), P(batch + ctx, None))
     return jax.shard_map(local, mesh=mesh, in_specs=in_specs, out_specs=out_specs, check_vma=False)

time: 121 us -> 115 us (0.950)
  waiting for transfers between devices: 29.4 us -> 8.88 us
  Pallas kernels: 23.3 us -> 34.1 us
  starting transfers between devices: 14.4 us -> 17.5 us
  blocking collectives: 49.5 us -> 51.8 us
    all_to_all x2, waiting for transfers between devices: 29.4 us -> 8.84 us  [the longest x1 6.9 us: local(): carry = lax.all_to_all(carries, ('y', 'z'), 0, 0, tiled=True)]
    pallas_call x4 -> x5, Pallas kernels: 17.4 us -> 27.5 us  [the longest x1 17.1 us: local(): call(finish_kernel, [((8 * DEV, 3 * E), BF)], BIG, 1400000000, 6000000, i...]
    ppermute x0 -> x2, starting transfers between devices: none -> 5.12 us  [the longest x1 2.83 us: local(): other = lax.ppermute(whole, 'core', [(0, 1), (1, 0)])]
    all_to_all x2, blocking collectives: 49.5 us -> 51.8 us  [the longest x1 31.2 us: local(): lax.all_to_all(pay.reshape(DEV, 8, 3 * E), every, 0, 0, tiled=True)]
    all_to_all x2, starting transfers between devices: 14.4 us -> 12.3 us  [the longest x1 8.61 us: local(): got = lax.all_to_all(sums, ('y', 'z'), 0, 0, tiled=True)]
  transfers between devices with their start and end apart: 2 -> 4, of which waited for: 2 -> 2; matrix products, arithmetic and copies ran while one was open for 0% -> 1% of each run, Pallas kernels for 6% -> 7%
where the time goes in v4:
time: 115 us
  blocking collectives  51.8 us (45%)
  Pallas kernels  34.1 us (30%)
  starting transfers between devices  17.5 us (15%)
  waiting for transfers between devices  8.88 us (8%)
  local copies, waits for them, and re-layouts  1.51 us (1%)
    all_to_all x1, blocking collectives, local(): lax.all_to_all(pay.reshape(DEV, 8, 3 * E), every, 0, 0, tiled=True)  31.2 us
    all_to_all x1, blocking collectives, local(): lax.all_to_all(chunk, ('x', 'y', 'z'), 0, 0, tiled=True)  20.6 us
    pallas_call x1, Pallas kernels, local(): call(finish_kernel, [((8 * DEV, 3 * E), BF)], BIG, 1400000000, 6000000, i...  17.1 us
    all_to_all x1, starting transfers between devices, local(): got = lax.all_to_all(sums, ('y', 'z'), 0, 0, tiled=True)  8.61 us
    all_to_all x1, waiting for transfers between devices, local(): carry = lax.all_to_all(carries, ('y', 'z'), 0, 0, tiled=True)  6.9 us
    pallas_call x1, Pallas kernels, local(): call(local_kernel, [((INNER // 2, D), F32), ((INNER // 2, D), BF), ((INNE...  5.87 us
    pallas_call x1, Pallas kernels, local(): call(project_kernel, [((T, PROJ), BF), ((INNER, T), BF), ((H, T), F32), (...  4.38 us
    pallas_call x1, Pallas kernels, local(): pl.pallas_call(last_kernel, grid=(4,), out_shape=tuple((jax.ShapeDtypeStr...  4.06 us
  transfers between devices with their start and end apart: 4, of which 2 were waited for; matrix products, arithmetic and copies ran while one was open for 1% of the time, Pallas kernels for 7%

profile of v4, /device:TPU:1, one launch (start us, length us, event | category | flops | bytes accessed | tf_op | source)
XLA Modules:
  0.0 115.0 jit_solution(9117748470219407055)
XLA Ops:
  0.6 4.4 %shard_map.128 = (bf16[256,1280]{1,0:T(8,128)(2,1)}, bf16[1024,256]{1,0:T(8,128)(2,1)}, f32[16,256]{1,0:T(8,128)}, f32[256,16]{1,0:T(8,128)}, bf16[16,80,128]{2,1,0:T(8,128)(2,1)}) custom-call(bf16[256,256]{1,0:T(8,128)(2,1)} %bitcast.18, bf16[256,512]{1,0:T(8,128)(2,1)} %bitcast.20, f32[16,256]{1,0:T(8,128)} %bitcast.22, bf16[256,512]{1,0:T(8,128)(2,1)} %w_up_ref.1, ...), custom_call_target="tpu_custom_call" | custom-call | flops 750000000 | bytes 4500000 | tf_op jit(solution)/shard_map/pallas_call | solution.py:329
  5.0 8.6 %all-to-all-start = ((bf16[16,80,128]{2,1,0:T(8,128)(2,1)}), bf16[16,80,128]{2,1,0:T(8,128)(2,1)S(1)}, u32[]{:S(2)}, u32[]{:S(2)}) async-start(bf16[16,80,128]{2,1,0:T(8,128)(2,1)} %get-tuple-element.26), calls=%async_computation | async-start | bytes 655360 | tf_op jit(solution)/shard_map/all_to_all | solution.py:340
  13.6 5.9 %shard_map.129 = (f32[512,512]{1,0:T(8,128)}, bf16[512,512]{1,0:T(8,128)(2,1)}, f32[1024,256]{1,0:T(8,128)}, f32[128,256]{1,0:T(8,128)}, bf16[128,256]{1,0:T(8,1...) custom-call(bf16[256,1280]{1,0:T(8,128)(2,1)} %get-tuple-element.27.proj_ref.proj_hbm, ...), custom_call_target="tpu_custom_call" | custom-call | flops 2500000000 | bytes 6000000 | tf_op jit(solution)/shard_map/pallas_call | solution.py:342
  19.5 1.9 %all-to-all-done.got_ref = bf16[16,80,128]{2,1,0:T(8,128)(2,1)S(1)} async-done(((bf16[16,80,128]{2,1,0:T(8,128)(2,1)}), bf16[16,80,128]{2,1,0:T(8,128)(2,1)S(1)}, u32[]{:S(2)}, u32[]{:S(2)}) %all-to-all-start) | async-done | bytes 327712 | tf_op jit(solution)/shard_map/all_to_all | solution.py:340
  21.5 2.3 %collective-permute-start = (bf16[512,512]{1,0:T(8,128)(2,1)}, bf16[512,512]{1,0:T(8,128)(2,1)S(1)}, u32[]{:S(2)}, u32[]{:S(2)}) collective-permute-start(bf16[512,512]{1,0:T(8,128)(2,1)} %get-tuple-element.34), channel_id=1, source_target_pairs={{0,16},{16,0},{1,17},{17,1},{2,18},{18,2},{3,19},{19,3},{4,20},{20... | collective-permute-start | bytes 1572872 | tf_op jit(solution)/shard_map/ppermute | solution.py:360
  23.8 0.8 shard_map.130
  24.5 3.7 %all-to-all-start.1 = ((bf16[16,64,128]{2,1,0:T(8,128)(2,1)}), bf16[16,64,128]{2,1,0:T(8,128)(2,1)S(1)}, u32[]{:S(2)}, u32[]{:S(2)}) async-start(bf16[16,64,128]{2,1,0:T(8,128)(2,1)} %shard_map.130), calls=%async_computation.1 | async-start | bytes 524288 | tf_op jit(solution)/shard_map/all_to_all | solution.py:357
  28.3 0.0 collective-permute-done.got_ref
  28.3 0.1 shard_map.131.outer_hbm
  28.4 0.0 copy-start.2
  28.4 0.8 copy-done.2
  29.2 6.9 %all-to-all-done.1 = bf16[16,64,128]{2,1,0:T(8,128)(2,1)S(1)} async-done(((bf16[16,64,128]{2,1,0:T(8,128)(2,1)}), bf16[16,64,128]{2,1,0:T(8,128)(2,1)S(1)}, u32[]{:S(2)}, u32[]{:S(2)}) %all-to-all-start.1) | async-done | bytes 262176 | tf_op jit(solution)/shard_map/all_to_all | solution.py:357
  36.1 0.7 copy-done.4
  36.8 17.1 %shard_map.132 = bf16[1024,768]{1,0:T(8,128)(2,1)} custom-call(bf16[1024,128]{1,0:T(8,128)(2,1)} %bitcast.17, bf16[256,1280]{1,0:T(8,128)(2,1)} %get-tuple-element.27.proj_ref.proj_hbm, f32[16,256]{1,0:T(8,128)} %get-tuple-element.29.cum_ref.cum_hbm, f32[1024,256]{1,0:T(8,128)} %get-tuple-element.36.dx_hbm, f32[128,256]{1,0:T(8,128)} %get-tuple-element.37.dbt_hbm, ...), custom_call_target="tpu_custom_call" | custom-call | flops 1400000000 | bytes 6000000 | tf_op jit(solution)/shard_map/pallas_call | solution.py:362
  53.9 31.2 %all_to_all.20.got_ref = bf16[128,8,768]{2,1,0:T(8,128)(2,1)S(1)} all-to-all(bf16[128,8,768]{2,1,0:T(8,128)(2,1)} %bitcast.16), channel_id=1, replica_groups=mesh['x'=4,'core'=2,'y'=4,'z'=4] {'x','core','y','z'}, dimensions={0} | all-to-all | bytes 3145728 | tf_op jit(solution)/shard_map/all_to_all | solution.py:373
  85.1 0.3 shard_map.133
  85.4 0.0 copy-start
  85.4 0.0 copy-start.1
  85.4 20.6 %all_to_all.21 = bf16[64,8,896]{2,1,0:T(8,128)(2,1)S(1)} all-to-all(bf16[64,8,896]{2,1,0:T(8,128)(2,1)S(1)} %get-tuple-element.42), channel_id=1, replica_groups=mesh['x'=4,'core'=2,'y'=4,'z'=4] {'x','y','z'}, dimensions={0} | all-to-all | bytes 1835008 | tf_op jit(solution)/shard_map/all_to_all | solution.py:378
  106.0 2.8 %collective-permute-start.1 = (bf16[512,896]{1,0:T(8,128)(2,1)S(1)}, bf16[512,896]{1,0:T(8,128)(2,1)S(1)}, u32[]{:S(2)}, u32[]{:S(2)}) collective-permute-start(bf16[512,896]{1,0:T(8,128)(2,1)S(1)} %bitcast.14), channel_id=1, source_target_pairs={{0,16},{16,0},{1,17},{17,1},{2,18},{18,2},{3,19},{19,3},{4,20},{20... | collective-permute-start | bytes 2752520 | tf_op jit(solution)/shard_map/ppermute | solution.py:379
  108.8 1.5 %shard_map.135 = f32[512,256]{1,0:T(8,128)} custom-call(bf16[128,8,768]{2,1,0:T(8,128)(2,1)S(1)} %all_to_all.20.got_ref), custom_call_target="tpu_custom_call" | custom-call | flops 400000000 | bytes 2000000 | tf_op jit(solution)/shard_map/pallas_call | solution.py:380
  110.3 0.6 add_bitcast_fusion
  110.9 0.0 collective-permute-done.1.other_ref
  110.9 4.1 %shard_map.134 = (f32[256,512]{1,0:T(8,128)}, f32[512,1280]{1,0:T(8,128)}, f32[1024,512]{1,0:T(8,128)}) custom-call(s32[1]{0:T(128)} %bitcast.core_ref, bf16[512,896]{1,0:T(8,128)(2,1)S(1)} %bitcast.15, bf16[512,896]{1,0:T(8,128)(2,1)S(1)} %collective-permute-done.1.other_ref, bf16[256,512]{1,0:T(8,128)(2,1)S(1)} %copy-done.1, bf16[512,1280]{1,0:T(8,128)(2,1)S(1)} %copy-done), custom_call_target="tpu_custom_call" | custom-call | flops 700000000 | bytes 8000000 | tf_op jit(solution)/shard_map/pallas_call | solution.py:386
  (5 shorter events, 0.0 us)
Async XLA Ops:
  5.0 16.4 %all-to-all-start = ((bf16[16,80,128]{2,1,0:T(8,128)(2,1)}), bf16[16,80,128]{2,1,0:T(8,128)(2,1)S(1)}, u32[]{:S(2)}, u32[]{:S(2)}) async-start(bf16[16,80,128]{2,1,0:T(8,128)(2,1)} %get-tuple-element.26), calls=%async_computation | async-start | bytes 655360 | tf_op jit(solution)/shard_map/all_to_all | solution.py:340
  19.5 8.8 %copy-start.3 = (f32[512,512]{1,0:T(8,128)S(1)}, f32[512,512]{1,0:T(8,128)}, u32[]{:S(2)}) copy-start(f32[512,512]{1,0:T(8,128)} %get-tuple-element.33.keep_ref) | copy-start | bytes 3145732
  21.5 6.8 %collective-permute-start = (bf16[512,512]{1,0:T(8,128)(2,1)}, bf16[512,512]{1,0:T(8,128)(2,1)S(1)}, u32[]{:S(2)}, u32[]{:S(2)}) collective-permute-start(bf16[512,512]{1,0:T(8,128)(2,1)} %get-tuple-element.34), channel_id=1, source_target_pairs={{0,16},{16,0},{1,17},{17,1},{2,18},{18,2},{3,19},{19,3},{4,20},{20... | collective-permute-start | bytes 1572872 | tf_op jit(solution)/shard_map/ppermute | solution.py:360
  24.5 11.6 %all-to-all-start.1 = ((bf16[16,64,128]{2,1,0:T(8,128)(2,1)}), bf16[16,64,128]{2,1,0:T(8,128)(2,1)S(1)}, u32[]{:S(2)}, u32[]{:S(2)}) async-start(bf16[16,64,128]{2,1,0:T(8,128)(2,1)} %shard_map.130), calls=%async_computation.1 | async-start | bytes 524288 | tf_op jit(solution)/shard_map/all_to_all | solution.py:357
  28.4 0.8 copy-start.2
  36.1 0.7 copy-start.4
  85.4 25.5 %copy-start = (bf16[512,1280]{1,0:T(8,128)(2,1)S(1)}, bf16[512,1280]{1,0:T(8,128)(2,1)}, u32[]{:S(2)}) copy-start(bf16[512,1280]{1,0:T(8,128)(2,1)} %w_in_ref.1) | copy-start | bytes 3932164
  85.4 25.5 %copy-start.1 = (bf16[256,512]{1,0:T(8,128)(2,1)S(1)}, bf16[256,512]{1,0:T(8,128)(2,1)}, u32[]{:S(2)}) copy-start(bf16[256,512]{1,0:T(8,128)(2,1)} %w_up_ref.1) | copy-start | bytes 786436
  106.0 4.9 %collective-permute-start.1 = (bf16[512,896]{1,0:T(8,128)(2,1)S(1)}, bf16[512,896]{1,0:T(8,128)(2,1)S(1)}, u32[]{:S(2)}, u32[]{:S(2)}) collective-permute-start(bf16[512,896]{1,0:T(8,128)(2,1)S(1)} %bitcast.14), channel_id=1, source_target_pairs={{0,16},{16,0},{1,17},{17,1},{2,18},{18,2},{3,19},{19,3},{4,20},{20... | collective-permute-start | bytes 2752520 | tf_op jit(solution)/shard_map/ppermute | solution.py:379

commit v5 on v4

--- a/solution.py
+++ b/solution.py
@@ -119,7 +119,7 @@
 
 
 def local_kernel(proj_ref, dy_ref, cum_ref, cumt_ref, h0_ref, dout_ref, index_ref, skip_ref, core_ref,
-                 keep_ref, give_ref, dx_ref, dbt_ref, dct_ref, misc_ref, hits_ref, y_ref, sdy_ref, h0t_ref, sum_ref):
+                 keep_ref, give_ref, dx_ref, tx_ref, bt_ref, dbt_ref, dct_ref, misc_ref, hits_ref, y_ref, sdy_ref, h0t_ref, sum_ref):
     proj_t = jnp.transpose(proj_ref[...])
     bt = proj_t[INNER : INNER + N, :]
     ct = proj_t[INNER + N :, :]
@@ -132,6 +132,8 @@
     cum = cum_ref[...]
     cumt = cumt_ref[...]
     start = jnp.exp(cum)
+    tail = DT * jnp.exp(cum[:, T - 1 : T] - cum)
+    bt_ref[...] = bt
     h0t_ref[...] = h0_ref[...].astype(BF)
     y_ref[...] = dot(h0t_ref[...], ct)
     skip_sums = []
@@ -162,6 +164,7 @@
         y_ref[lo:hi, :] = dot(x_h, weights) + SC * st * y_ref[lo:hi, :] + skip * x_f
         dx_ref[lo:hi, :] = dot(dy_h, weights, NT) + skip * dy_f
         sdy_ref[lo:hi, :] = (st * dy_f).astype(BF)
+        tx_ref[lo:hi, :] = (tail[h : h + 1, :] * x_f).astype(BF)
         x_pair = proj_ref[:, (h // 2) * N : (h // 2 + 1) * N]
         dy_z = jnp.concatenate([dy_h, zrow] if h % 2 == 0 else [zrow, dy_h], axis=0)
         q0 = dot(x_pair[:N, :], dy_z)
@@ -210,59 +213,56 @@
     misc_ref[...] = (misc + jnp.where((row_id & 7) == 6, extra, 0.0)).astype(BF)
 
 
-def finish_kernel(carry_hbm, proj_hbm, cum_hbm, dx_hbm, dbt_hbm, dct_hbm, misc_hbm, hits_hbm, rows_hbm,
-                  w_in_hbm, w_up_hbm, outer_hbm, out_hbm,
-                  carry_ref, proj_ref, cum_ref, dx_ref, dbt_ref, d_ref, misc_ref, hits_ref, rows_ref,
-                  w_in_ref, w_up_ref, tx_ref, left_ref, right_ref, sems):
+def finish_kernel(carry_hbm, bt_hbm, cum_hbm, dx_hbm, tx_hbm, dbt_hbm, dct_hbm, rows_hbm,
+                  w_in_hbm, w_up_hbm, hits_hbm, misc_hbm, outer_hbm, out_hbm,
+                  carry_ref, bt_ref, cum_ref, dx_ref, tx_ref, dbt_ref, d_ref, rows_ref,
+                  w_in_ref, w_up_ref, hits_ref, misc_ref, outer_ref, left_ref, right_ref, sems):
     copies = [
         pltpu.make_async_copy(a, b, sems.at[n])
         for n, (a, b) in enumerate((
-            (carry_hbm, carry_ref), (proj_hbm, proj_ref), (cum_hbm, cum_ref), (dx_hbm, dx_ref),
+            (carry_hbm, carry_ref), (bt_hbm, bt_ref), (cum_hbm, cum_ref), (dx_hbm, dx_ref), (tx_hbm, tx_ref),
             (dbt_hbm, dbt_ref), (dct_hbm, d_ref.at[INNER + N :, :]), (rows_hbm, rows_ref),
             (w_in_hbm, w_in_ref), (w_up_hbm, w_up_ref), (hits_hbm, hits_ref), (misc_hbm, misc_ref),
-            (outer_hbm, out_hbm.at[:, 2 * E :]),
+            (outer_hbm, outer_ref),
         ))
     ]
     for copy in copies:
         copy.start()
     for copy in copies[:3]:
         copy.wait()
-    proj_t = jnp.transpose(proj_ref[...])
-    bt = proj_t[INNER : INNER + N, :]
     cum = cum_ref[...]
     tail = DT * jnp.exp(cum[:, T - 1 : T] - cum)
     carry = carry_ref[...]
-    entering = dot(carry, bt)
+    entering = dot(carry, bt_ref[...])
     copies[3].wait()
     for h in range(H):
         lo, hi = h * HP, (h + 1) * HP
-        tl = tail[h : h + 1, :]
-        d_ref[lo:hi, :] = (dx_ref[lo:hi, :] + tl * entering[lo:hi, :]).astype(BF)
-        tx_ref[lo:hi, :] = (tl * proj_t[lo:hi, :].astype(F32)).astype(BF)
-    for copy in copies[4:7]:
+        d_ref[lo:hi, :] = (dx_ref[lo:hi, :] + tail[h : h + 1, :] * entering[lo:hi, :]).astype(BF)
+    for copy in copies[4:8]:
         copy.wait()
     d_ref[INNER : INNER + N, :] = (dbt_ref[...] + dot(carry, tx_ref[...], TN)).astype(BF)
     d = d_ref[...]
     g = dot(d, rows_ref[...]).astype(BF)
     left_ref[...] = g[:INNER, :]
-    out_left = pltpu.make_async_copy(left_ref, out_hbm.at[:, :E], sems.at[12])
-    out_left.start()
-    copies[7].wait()
+    outs = [pltpu.make_async_copy(left_ref, out_hbm.at[:, :E], sems.at[13])]
+    outs[0].start()
+    copies[8].wait()
     du = dot(w_in_ref[...], d).astype(BF)
-    copies[8].wait()
+    copies[9].wait()
     de = dot(w_up_ref[...], du).astype(BF)
     r = lax.broadcasted_iota(jnp.int32, (8 * DEV, 2 * N), 0)
     j = lax.broadcasted_iota(jnp.int32, (1, 2 * N), 1)
     place = jnp.where(r == 8 * lax.shift_right_logical(j, 1) + (j & 1), 1.0, 0.0).astype(BF)
-    copies[9].wait()
-    copies[10].wait()
+    for copy in copies[10:]:
+        copy.wait()
+    outs.append(pltpu.make_async_copy(outer_ref, out_hbm.at[:, 2 * E :], sems.at[14]))
+    outs[1].start()
     misc = misc_ref[...].astype(F32) + dot(hits_ref[...], de, NT) + dot(place, g[INNER:, :])
     right_ref[...] = misc.astype(BF)
-    out_right = pltpu.make_async_copy(right_ref, out_hbm.at[:, E : 2 * E], sems.at[13])
-    out_right.start()
-    copies[11].wait()
-    out_left.wait()
-    out_right.wait()
+    outs.append(pltpu.make_async_copy(right_ref, out_hbm.at[:, E : 2 * E], sems.at[15]))
+    outs[2].start()
+    for copy in outs:
+        copy.wait()
 
 
 def pair_kernel(keep_ref, got_ref, out_ref):
@@ -339,12 +339,12 @@
     )(rows, d_out, decay[0], w_up, w_in, w_out)
     got = lax.all_to_all(sums, ("y", "z"), 0, 0, tiled=True)
     core = lax.axis_index("core").reshape(1)
-    keep, give, dx, dbt, dct, misc, hits = call(
+    keep, give, dx, tx, bt, dbt, dct, misc, hits = call(
         local_kernel,
-        [((INNER // 2, D), F32), ((INNER // 2, D), BF), ((INNER, T), F32), ((N, T), F32), ((N, T), BF),
-         ((8 * DEV, E), BF), ((8 * DEV, T), BF)],
+        [((INNER // 2, D), F32), ((INNER // 2, D), BF), ((INNER, T), F32), ((INNER, T), BF), ((N, T), BF),
+         ((N, T), F32), ((N, T), BF), ((8 * DEV, E), BF), ((8 * DEV, T), BF)],
         BIG, 2_500_000_000, 6_000_000,
-        in_specs=[VM] * 7 + [SM] * 2, out_specs=(VM,) * 7,
+        in_specs=[VM] * 7 + [SM] * 2, out_specs=(VM,) * 9,
         scratch_shapes=[
             pltpu.VMEM((INNER, T), F32), pltpu.VMEM((INNER, T), BF),
             pltpu.VMEM((INNER, N), BF), pltpu.VMEM((T, T), BF),
@@ -361,15 +361,15 @@
     carry, outer = lax.optimization_barrier((carry, outer))
     (pay,) = call(
         finish_kernel, [((8 * DEV, 3 * E), BF)], BIG, 1_400_000_000, 6_000_000,
-        in_specs=[HBM] * 12, out_specs=(HBM,),
+        in_specs=[HBM] * 13, out_specs=(HBM,),
         scratch_shapes=[
-            pltpu.VMEM((INNER, N), BF), pltpu.VMEM((T, PROJ), BF), pltpu.VMEM((H, T), F32),
-            pltpu.VMEM((INNER, T), F32), pltpu.VMEM((N, T), F32), pltpu.VMEM((PROJ, T), BF),
-            pltpu.VMEM((8 * DEV, E), BF), pltpu.VMEM((8 * DEV, T), BF), pltpu.VMEM((T, E), BF),
-            pltpu.VMEM((D, PROJ), BF), pltpu.VMEM((E, D), BF), pltpu.VMEM((INNER, T), BF),
-            pltpu.VMEM((INNER, E), BF), pltpu.VMEM((8 * DEV, E), BF), pltpu.SemaphoreType.DMA((14,)),
+            pltpu.VMEM((INNER, N), BF), pltpu.VMEM((N, T), BF), pltpu.VMEM((H, T), F32),
+            pltpu.VMEM((INNER, T), F32), pltpu.VMEM((INNER, T), BF), pltpu.VMEM((N, T), F32),
+            pltpu.VMEM((PROJ, T), BF), pltpu.VMEM((T, E), BF), pltpu.VMEM((D, PROJ), BF), pltpu.VMEM((E, D), BF),
+            pltpu.VMEM((8 * DEV, T), BF), pltpu.VMEM((8 * DEV, E), BF), pltpu.VMEM((8 * DEV, E), BF),
+            pltpu.VMEM((INNER, E), BF), pltpu.VMEM((8 * DEV, E), BF), pltpu.SemaphoreType.DMA((16,)),
         ],
-    )(carry.reshape(INNER, N), proj, cum, dx, dbt, dct, misc, hits, rows, w_in, w_up, outer)
+    )(carry.reshape(INNER, N), bt, cum, dx, tx, dbt, dct, rows, w_in, w_up, hits, misc, outer)
     pay_got = lax.all_to_all(pay.reshape(DEV, 8, 3 * E), every, 0, 0, tiled=True)
     chunk, skip_sum = call(
         sum_kernel, [((DEV // 2, 8, 7 * N), BF), ((1, 128), F32)], 12, 2_000_000, 3_000_000,

time: 115 us -> 104 us (0.904)
  Pallas kernels: 34.1 us -> 22.2 us
    pallas_call x1, Pallas kernels: 17.1 us -> 4.88 us  [local(): call(finish_kernel, [((8 * DEV, 3 * E), BF)], BIG, 1400000000, 6000000, i...]
  transfers between devices with their start and end apart: 4 -> 4, of which waited for: 2 -> 2; matrix products, arithmetic and copies ran while one was open for 1% -> 1% of each run, Pallas kernels for 7% -> 8%
where the time goes in v5:
time: 104 us; the launch traced here: 103 us
  blocking collectives  51.8 us (50%)
  Pallas kernels  22.2 us (21%)
  starting transfers between devices  17.8 us (17%)
  waiting for transfers between devices  8.49 us (8%)
  local copies, waits for them, and re-layouts  1.51 us (1%)
    all_to_all x1, blocking collectives, local(): lax.all_to_all(pay.reshape(DEV, 8, 3 * E), every, 0, 0, tiled=True)  31.2 us
    all_to_all x1, blocking collectives, local(): lax.all_to_all(chunk, ('x', 'y', 'z'), 0, 0, tiled=True)  20.6 us
    all_to_all x1, starting transfers between devices, local(): got = lax.all_to_all(sums, ('y', 'z'), 0, 0, tiled=True)  8.61 us
    all_to_all x1, waiting for transfers between devices, local(): carry = lax.all_to_all(carries, ('y', 'z'), 0, 0, tiled=True)  6.9 us
    pallas_call x1, Pallas kernels, local(): call(local_kernel, [((INNER // 2, D), F32), ((INNER // 2, D), BF), ((INNE...  6.26 us
    pallas_call x1, Pallas kernels, local(): call(finish_kernel, [((8 * DEV, 3 * E), BF)], BIG, 1400000000, 6000000, i...  4.88 us
    pallas_call x1, Pallas kernels, local(): call(project_kernel, [((T, PROJ), BF), ((INNER, T), BF), ((H, T), F32), (...  4.37 us
    all_to_all x1, starting transfers between devices, local(): carry = lax.all_to_all(carries, ('y', 'z'), 0, 0, tiled=True)  4.11 us
  transfers between devices with their start and end apart: 4, of which 2 were waited for; matrix products, arithmetic and copies ran while one was open for 1% of the time, Pallas kernels for 8%

profile of v5, /device:TPU:1, one launch (start us, length us, event | category | flops | bytes accessed | tf_op | source)
XLA Modules:
  0.0 103.1 jit_solution(16689181975207987350)
XLA Ops:
  0.6 4.4 %shard_map.128 = (bf16[256,1280]{1,0:T(8,128)(2,1)}, bf16[1024,256]{1,0:T(8,128)(2,1)}, f32[16,256]{1,0:T(8,128)}, f32[256,16]{1,0:T(8,128)}, bf16[16,80,128]{2,1,0:T(8,128)(2,1)}) custom-call(bf16[256,256]{1,0:T(8,128)(2,1)} %bitcast.18, bf16[256,512]{1,0:T(8,128)(2,1)} %bitcast.20, f32[16,256]{1,0:T(8,128)} %bitcast.22, bf16[256,512]{1,0:T(8,128)(2,1)} %w_up_ref.1, ...), custom_call_target="tpu_custom_call" | custom-call | flops 750000000 | bytes 4500000 | tf_op jit(solution)/shard_map/pallas_call | solution.py:329
  5.0 8.6 %all-to-all-start = ((bf16[16,80,128]{2,1,0:T(8,128)(2,1)}), bf16[16,80,128]{2,1,0:T(8,128)(2,1)S(1)}, u32[]{:S(2)}, u32[]{:S(2)}) async-start(bf16[16,80,128]{2,1,0:T(8,128)(2,1)} %get-tuple-element.28), calls=%async_computation | async-start | bytes 655360 | tf_op jit(solution)/shard_map/all_to_all | solution.py:340
  13.6 6.3 %shard_map.129 = (f32[512,512]{1,0:T(8,128)}, bf16[512,512]{1,0:T(8,128)(2,1)}, f32[1024,256]{1,0:T(8,128)}, bf16[1024,256]{1,0:T(8,128)(2,1)}, bf16[128,256]{1,...) custom-call(bf16[256,1280]{1,0:T(8,128)(2,1)} %get-tuple-element.29., ...), custom_call_target="tpu_custom_call" | custom-call | flops 2500000000 | bytes 6000000 | tf_op jit(solution)/shard_map/pallas_call | solution.py:342
  19.9 1.6 %all-to-all-done.got_ref = bf16[16,80,128]{2,1,0:T(8,128)(2,1)S(1)} async-done(((bf16[16,80,128]{2,1,0:T(8,128)(2,1)}), bf16[16,80,128]{2,1,0:T(8,128)(2,1)S(1)}, u32[]{:S(2)}, u32[]{:S(2)}) %all-to-all-start) | async-done | bytes 327712 | tf_op jit(solution)/shard_map/all_to_all | solution.py:340
  21.4 2.3 %collective-permute-start = (bf16[512,512]{1,0:T(8,128)(2,1)}, bf16[512,512]{1,0:T(8,128)(2,1)S(1)}, u32[]{:S(2)}, u32[]{:S(2)}) collective-permute-start(bf16[512,512]{1,0:T(8,128)(2,1)} %get-tuple-element.36), channel_id=1, source_target_pairs={{0,16},{16,0},{1,17},{17,1},{2,18},{18,2},{3,19},{19,3},{4,20},{20... | collective-permute-start | bytes 1572872 | tf_op jit(solution)/shard_map/ppermute | solution.py:360
  23.7 0.8 shard_map.130
  24.5 4.1 %all-to-all-start.1 = ((bf16[16,64,128]{2,1,0:T(8,128)(2,1)}), bf16[16,64,128]{2,1,0:T(8,128)(2,1)S(1)}, u32[]{:S(2)}, u32[]{:S(2)}) async-start(bf16[16,64,128]{2,1,0:T(8,128)(2,1)} %shard_map.130), calls=%async_computation.1 | async-start | bytes 524288 | tf_op jit(solution)/shard_map/all_to_all | solution.py:357
  28.6 0.0 collective-permute-done.got_ref
  28.7 0.1 shard_map.131.outer_hbm
  28.8 0.0 copy-start.2
  28.8 0.8 copy-done.2
  29.6 6.9 %all-to-all-done.1 = bf16[16,64,128]{2,1,0:T(8,128)(2,1)S(1)} async-done(((bf16[16,64,128]{2,1,0:T(8,128)(2,1)}), bf16[16,64,128]{2,1,0:T(8,128)(2,1)S(1)}, u32[]{:S(2)}, u32[]{:S(2)}) %all-to-all-start.1) | async-done | bytes 262176 | tf_op jit(solution)/shard_map/all_to_all | solution.py:357
  36.5 0.7 copy-done.4
  37.2 4.9 %shard_map.132 = bf16[1024,768]{1,0:T(8,128)(2,1)} custom-call(bf16[1024,128]{1,0:T(8,128)(2,1)} %bitcast.17, bf16[128,256]{1,0:T(8,128)(2,1)} %get-tuple-element.38.bt_hbm, f32[16,256]{1,0:T(8,128)} %get-tuple-element.31.cum_ref.cum_hbm, f32[1024,256]{1,0:T(8,128)} %get-tuple-element.39.dx_hbm, bf16[1024,256]{1,0:T(8,128)(2,1)} %get-tuple-element.40.tx_hbm, ...), custom_call_target="tpu_custom_call" | custom-call | flops 1400000000 | bytes 6000000 | tf_op jit(solution)/shard_map/pallas_call | solution.py:362
  42.0 31.2 %all_to_all.20.got_ref = bf16[128,8,768]{2,1,0:T(8,128)(2,1)S(1)} all-to-all(bf16[128,8,768]{2,1,0:T(8,128)(2,1)} %bitcast.16), channel_id=1, replica_groups=mesh['x'=4,'core'=2,'y'=4,'z'=4] {'x','core','y','z'}, dimensions={0} | all-to-all | bytes 3145728 | tf_op jit(solution)/shard_map/all_to_all | solution.py:373
  73.2 0.3 shard_map.133
  73.5 0.0 copy-start
  73.6 0.0 copy-start.1
  73.6 20.6 %all_to_all.21 = bf16[64,8,896]{2,1,0:T(8,128)(2,1)S(1)} all-to-all(bf16[64,8,896]{2,1,0:T(8,128)(2,1)S(1)} %get-tuple-element.46), channel_id=1, replica_groups=mesh['x'=4,'core'=2,'y'=4,'z'=4] {'x','y','z'}, dimensions={0} | all-to-all | bytes 1835008 | tf_op jit(solution)/shard_map/all_to_all | solution.py:378
  94.1 2.8 %collective-permute-start.1 = (bf16[512,896]{1,0:T(8,128)(2,1)S(1)}, bf16[512,896]{1,0:T(8,128)(2,1)S(1)}, u32[]{:S(2)}, u32[]{:S(2)}) collective-permute-start(bf16[512,896]{1,0:T(8,128)(2,1)S(1)} %bitcast.14), channel_id=1, source_target_pairs={{0,16},{16,0},{1,17},{17,1},{2,18},{18,2},{3,19},{19,3},{4,20},{20... | collective-permute-start | bytes 2752520 | tf_op jit(solution)/shard_map/ppermute | solution.py:379
  97.0 1.5 %shard_map.135 = f32[512,256]{1,0:T(8,128)} custom-call(bf16[128,8,768]{2,1,0:T(8,128)(2,1)S(1)} %all_to_all.20.got_ref), custom_call_target="tpu_custom_call" | custom-call | flops 400000000 | bytes 2000000 | tf_op jit(solution)/shard_map/pallas_call | solution.py:380
  98.5 0.6 add_bitcast_fusion
  99.0 0.0 collective-permute-done.1.other_ref
  99.1 4.1 %shard_map.134 = (f32[256,512]{1,0:T(8,128)}, f32[512,1280]{1,0:T(8,128)}, f32[1024,512]{1,0:T(8,128)}) custom-call(s32[1]{0:T(128)} %bitcast.core_ref, bf16[512,896]{1,0:T(8,128)(2,1)S(1)} %bitcast.15, bf16[512,896]{1,0:T(8,128)(2,1)S(1)} %collective-permute-done.1.other_ref, bf16[256,512]{1,0:T(8,128)(2,1)S(1)} %copy-done.1, bf16[512,1280]{1,0:T(8,128)(2,1)S(1)} %copy-done), custom_call_target="tpu_custom_call" | custom-call | flops 700000000 | bytes 8000000 | tf_op jit(solution)/shard_map/pallas_call | solution.py:386
  (5 shorter events, 0.0 us)
Async XLA Ops:
  5.0 16.4 %all-to-all-start = ((bf16[16,80,128]{2,1,0:T(8,128)(2,1)}), bf16[16,80,128]{2,1,0:T(8,128)(2,1)S(1)}, u32[]{:S(2)}, u32[]{:S(2)}) async-start(bf16[16,80,128]{2,1,0:T(8,128)(2,1)} %get-tuple-element.28), calls=%async_computation | async-start | bytes 655360 | tf_op jit(solution)/shard_map/all_to_all | solution.py:340
  19.9 8.8 %copy-start.3 = (f32[512,512]{1,0:T(8,128)S(1)}, f32[512,512]{1,0:T(8,128)}, u32[]{:S(2)}) copy-start(f32[512,512]{1,0:T(8,128)} %get-tuple-element.35.keep_ref) | copy-start | bytes 3145732
  21.4 7.2 %collective-permute-start = (bf16[512,512]{1,0:T(8,128)(2,1)}, bf16[512,512]{1,0:T(8,128)(2,1)S(1)}, u32[]{:S(2)}, u32[]{:S(2)}) collective-permute-start(bf16[512,512]{1,0:T(8,128)(2,1)} %get-tuple-element.36), channel_id=1, source_target_pairs={{0,16},{16,0},{1,17},{17,1},{2,18},{18,2},{3,19},{19,3},{4,20},{20... | collective-permute-start | bytes 1572872 | tf_op jit(solution)/shard_map/ppermute | solution.py:360
  24.5 11.9 %all-to-all-start.1 = ((bf16[16,64,128]{2,1,0:T(8,128)(2,1)}), bf16[16,64,128]{2,1,0:T(8,128)(2,1)S(1)}, u32[]{:S(2)}, u32[]{:S(2)}) async-start(bf16[16,64,128]{2,1,0:T(8,128)(2,1)} %shard_map.130), calls=%async_computation.1 | async-start | bytes 524288 | tf_op jit(solution)/shard_map/all_to_all | solution.py:357
  28.8 0.8 copy-start.2
  36.5 0.7 copy-start.4
  73.5 25.5 %copy-start = (bf16[512,1280]{1,0:T(8,128)(2,1)S(1)}, bf16[512,1280]{1,0:T(8,128)(2,1)}, u32[]{:S(2)}) copy-start(bf16[512,1280]{1,0:T(8,128)(2,1)} %w_in_ref.1) | copy-start | bytes 3932164
  73.6 25.5 %copy-start.1 = (bf16[256,512]{1,0:T(8,128)(2,1)S(1)}, bf16[256,512]{1,0:T(8,128)(2,1)}, u32[]{:S(2)}) copy-start(bf16[256,512]{1,0:T(8,128)(2,1)} %w_up_ref.1) | copy-start | bytes 786436
  94.1 4.9 %collective-permute-start.1 = (bf16[512,896]{1,0:T(8,128)(2,1)S(1)}, bf16[512,896]{1,0:T(8,128)(2,1)S(1)}, u32[]{:S(2)}, u32[]{:S(2)}) collective-permute-start(bf16[512,896]{1,0:T(8,128)(2,1)S(1)} %bitcast.14), channel_id=1, source_target_pairs={{0,16},{16,0},{1,17},{17,1},{2,18},{18,2},{3,19},{19,3},{4,20},{20... | collective-permute-start | bytes 2752520 | tf_op jit(solution)/shard_map/ppermute | solution.py:379

commit v6 on v5

--- a/solution.py
+++ b/solution.py
@@ -19,7 +19,9 @@
 CAP = 4
 DEV = 128
 CTX = 16
-SROWS = 80
+GH = 4
+GR = GH * HP
+MR = GR + 16
 
 DT = 0.0625
 SC = 128.0**-0.5
@@ -58,9 +60,27 @@
 SM = pl.BlockSpec(memory_space=pltpu.SMEM)
 
 
-def project_kernel(rows_hbm, dout_hbm, decay_hbm, w_up_hbm, w_in_hbm, w_out_hbm,
-                   proj_ref, dy_ref, cum_ref, cumt_ref, send_ref,
-                   rows_ref, dout_ref, decay_ref, w_up_ref, w_in_ref, w_out_ref, sems):
+def decay_rows(amounts):
+    row = lax.broadcasted_iota(jnp.int32, (MR - GR, N), 0)
+    out = jnp.zeros((MR - GR, N), F32)
+    for i, amount in enumerate(amounts):
+        for k, part in enumerate(split3(amount)):
+            out = jnp.where(row == 3 * i + k, part.astype(F32), out)
+    return out.astype(BF)
+
+
+def decays(ref, at):
+    rows = ref[at, GR:, :].astype(F32)
+    return [rows[3 * i : 3 * i + 1] + rows[3 * i + 1 : 3 * i + 2] + rows[3 * i + 2 : 3 * i + 3] for i in range(GH)]
+
+
+def sums_of(ref, at, i):
+    return ref[at, i * HP : (i + 1) * HP, :].astype(F32)
+
+
+def project_kernel(z_ref, rows_hbm, dout_hbm, decay_hbm, w_up_hbm, w_in_hbm, w_out_hbm,
+                   proj_ref, dy_ref, cum_ref, cumt_ref, g0_ref, g1_ref, g2_ref, g3_ref,
+                   rows_ref, dout_ref, decay_ref, w_up_ref, w_in_ref, w_out_ref, all_ref, sems):
     pairs = (
         (rows_hbm, rows_ref), (w_up_hbm, w_up_ref), (w_in_hbm, w_in_ref),
         (dout_hbm, dout_ref), (w_out_hbm, w_out_ref), (decay_hbm, decay_ref),
@@ -96,30 +116,50 @@
     )
     sums = dot(scaled, c_nat).astype(BF)
     amount = jnp.exp(cum[:, T - 1 : T])
-    parts = [jnp.broadcast_to(p.astype(F32), (H, N)) for p in split3(amount)]
-    row = lax.broadcasted_iota(jnp.int32, (SROWS - HP, N), 0)
-    for h in range(H):
-        send_ref[h, 0:HP, :] = sums[h * HP : (h + 1) * HP, :]
-        tail = jnp.where(
-            row == 0,
-            parts[0][h : h + 1, :],
-            jnp.where(row == 1, parts[1][h : h + 1, :], jnp.where(row == 2, parts[2][h : h + 1, :], 0.0)),
-        )
-        send_ref[h, HP:SROWS, :] = tail.astype(BF)
-
-
-def scan_kernel(got_ref, out_ref):
-    carry = jnp.zeros((HP, N), F32)
-    for j in range(CTX - 1, -1, -1):
-        out_ref[j, :, :] = carry.astype(BF)
-        if j:
-            tail = got_ref[j, HP:SROWS, :].astype(F32)
-            amount = tail[0:1, :] + tail[1:2, :] + tail[2:3, :]
-            carry = got_ref[j, 0:HP, :].astype(F32) + amount * carry
-
-
-def local_kernel(proj_ref, dy_ref, cum_ref, cumt_ref, h0_ref, dout_ref, index_ref, skip_ref, core_ref,
-                 keep_ref, give_ref, dx_ref, tx_ref, bt_ref, dbt_ref, dct_ref, misc_ref, hits_ref, y_ref, sdy_ref, h0t_ref, sum_ref):
+    for q in range(H // GH):
+        all_ref[q, :GR, :] = sums[q * GR : (q + 1) * GR, :]
+        all_ref[q, GR:, :] = decay_rows([jnp.broadcast_to(amount[h : h + 1, :], (1, N)) for h in range(q * GH, (q + 1) * GH)])
+    for k, ref in enumerate((g0_ref, g1_ref, g2_ref, g3_ref)):
+        ref[...] = all_ref[(z_ref[0] + k) & 3]
+
+
+def place(at, refs, out_ref):
+    for k, ref in enumerate(refs):
+        out_ref[(at + 4 - k) & 3] = ref[...]
+
+
+def inner_kernel(z_ref, a_ref, b_ref, c_ref, d_ref, out_ref, st_ref):
+    place(z_ref[0], (a_ref, b_ref, c_ref, d_ref), st_ref)
+    amounts = [decays(st_ref, zz) for zz in range(4)]
+    for i in range(GH):
+        carry = sums_of(st_ref, 3, i)
+        for zz in (2, 1, 0):
+            carry = sums_of(st_ref, zz, i) + amounts[zz][i] * carry
+        out_ref[i * HP : (i + 1) * HP, :] = carry.astype(BF)
+    out_ref[GR:, :] = decay_rows([amounts[0][i] * amounts[1][i] * amounts[2][i] * amounts[3][i] for i in range(GH)])
+
+
+def outer_kernel(y_ref, z_ref, a_ref, b_ref, c_ref, d_ref, ta_ref, tb_ref, tc_ref, td_ref,
+                 g0_ref, g1_ref, g2_ref, g3_ref, st_ref, tt_ref, ct_ref):
+    y, z = y_ref[0], z_ref[0]
+    place(z, (a_ref, b_ref, c_ref, d_ref), st_ref)
+    place(y, (ta_ref, tb_ref, tc_ref, td_ref), tt_ref)
+    inner = [decays(st_ref, zz) for zz in range(4)]
+    outer = [decays(tt_ref, yy) for yy in range(4)]
+    for i in range(GH):
+        carry = jnp.zeros((HP, N), F32)
+        for yy in (3, 2, 1):
+            carry = jnp.where(yy > y, sums_of(tt_ref, yy, i) + outer[yy][i] * carry, carry)
+        for zz in (3, 2, 1, 0):
+            ct_ref[zz, i * HP : (i + 1) * HP, :] = carry.astype(BF)
+            if zz:
+                carry = sums_of(st_ref, zz, i) + inner[zz][i] * carry
+    for k, ref in enumerate((g0_ref, g1_ref, g2_ref, g3_ref)):
+        ref[...] = ct_ref[(z + k) & 3]
+
+
+def local_kernel(proj_ref, dy_ref, cum_ref, cumt_ref, h0_ref, dout_ref, skip_ref, core_ref,
+                 keep_ref, give_ref, dx_ref, tx_ref, bt_ref, dbt_ref, dct_ref, extra_ref, y_ref, sdy_ref, h0t_ref, sum_ref):
     proj_t = jnp.transpose(proj_ref[...])
     bt = proj_t[INNER : INNER + N, :]
     ct = proj_t[INNER + N :, :]
@@ -186,6 +226,16 @@
     a = sum_ref[...]
     dct_ref[...] = (SC * (DT * dot(bt, a) + dot(h0t_ref[...], sdy_ref[...], TN))).astype(BF)
     dbt_ref[...] = (DT * SC) * dot(ct, a, NT)
+    lane = lax.broadcasted_iota(jnp.int32, (1, T), 1)
+    extra = jnp.zeros((1, T), F32)
+    for h in range(H):
+        whole = skip_sums[h]
+        top = whole.astype(BF).astype(F32)
+        extra = extra + jnp.where(lane == 128 + h, top, 0.0) + jnp.where(lane == 160 + h, whole - top, 0.0)
+    extra_ref[...] = extra
+
+
+def slot_kernel(index_ref, extra_ref, misc_ref, hits_ref):
     index = index_ref[...]
     owner_row = lax.shift_right_logical(index, 9)
     rr = lax.broadcasted_iota(jnp.int32, (T, T), 0)
@@ -203,63 +253,58 @@
     row_id = lax.broadcasted_iota(jnp.int32, (8 * DEV, T), 0)
     hits_ref[...] = jnp.where(row_id == owner_row * 8 + 2 + rank_row, 1.0, 0.0).astype(BF)
     heads = jnp.where(row_id == owner_row * 8 + 6, 1.0, 0.0).astype(BF)
-    lane = lax.broadcasted_iota(jnp.int32, (1, T), 1)
-    extra = jnp.zeros((1, T), F32)
-    for h in range(H):
-        whole = skip_sums[h]
-        top = whole.astype(BF).astype(F32)
-        extra = extra + jnp.where(lane == 128 + h, top, 0.0) + jnp.where(lane == 160 + h, whole - top, 0.0)
     misc = dot(heads, v.astype(F32).astype(BF))
-    misc_ref[...] = (misc + jnp.where((row_id & 7) == 6, extra, 0.0)).astype(BF)
-
-
-def finish_kernel(carry_hbm, bt_hbm, cum_hbm, dx_hbm, tx_hbm, dbt_hbm, dct_hbm, rows_hbm,
-                  w_in_hbm, w_up_hbm, hits_hbm, misc_hbm, outer_hbm, out_hbm,
+    misc_ref[...] = (misc + jnp.where((row_id & 7) == 6, extra_ref[...], 0.0)).astype(BF)
+
+
+def finish_kernel(z_ref, c0_ref, c1_ref, c2_ref, c3_ref, outer_ref, bt_hbm, cum_hbm, dx_hbm, tx_hbm, dbt_hbm, dct_hbm, rows_hbm,
+                  w_in_hbm, w_up_hbm, hits_hbm, misc_hbm, out_hbm,
                   carry_ref, bt_ref, cum_ref, dx_ref, tx_ref, dbt_ref, d_ref, rows_ref,
-                  w_in_ref, w_up_ref, hits_ref, misc_ref, outer_ref, left_ref, right_ref, sems):
+                  w_in_ref, w_up_ref, hits_ref, misc_ref, left_ref, right_ref, sems):
     copies = [
         pltpu.make_async_copy(a, b, sems.at[n])
         for n, (a, b) in enumerate((
-            (carry_hbm, carry_ref), (bt_hbm, bt_ref), (cum_hbm, cum_ref), (dx_hbm, dx_ref), (tx_hbm, tx_ref),
+            (bt_hbm, bt_ref), (cum_hbm, cum_ref), (dx_hbm, dx_ref), (tx_hbm, tx_ref),
             (dbt_hbm, dbt_ref), (dct_hbm, d_ref.at[INNER + N :, :]), (rows_hbm, rows_ref),
             (w_in_hbm, w_in_ref), (w_up_hbm, w_up_ref), (hits_hbm, hits_ref), (misc_hbm, misc_ref),
-            (outer_hbm, outer_ref),
         ))
     ]
     for copy in copies:
         copy.start()
-    for copy in copies[:3]:
+    outs = [pltpu.make_async_copy(outer_ref, out_hbm.at[:, 2 * E :], sems.at[11])]
+    outs[0].start()
+    for k, ref in enumerate((c0_ref, c1_ref, c2_ref, c3_ref)):
+        carry_ref[pl.ds(pl.multiple_of(((z_ref[0] + 4 - k) & 3) * GR, GR), GR), :] = ref[...]
+    for copy in copies[:2]:
         copy.wait()
     cum = cum_ref[...]
     tail = DT * jnp.exp(cum[:, T - 1 : T] - cum)
     carry = carry_ref[...]
     entering = dot(carry, bt_ref[...])
-    copies[3].wait()
+    copies[2].wait()
     for h in range(H):
         lo, hi = h * HP, (h + 1) * HP
         d_ref[lo:hi, :] = (dx_ref[lo:hi, :] + tail[h : h + 1, :] * entering[lo:hi, :]).astype(BF)
-    for copy in copies[4:8]:
+    for copy in copies[3:7]:
         copy.wait()
     d_ref[INNER : INNER + N, :] = (dbt_ref[...] + dot(carry, tx_ref[...], TN)).astype(BF)
     d = d_ref[...]
     g = dot(d, rows_ref[...]).astype(BF)
     left_ref[...] = g[:INNER, :]
-    outs = [pltpu.make_async_copy(left_ref, out_hbm.at[:, :E], sems.at[13])]
-    outs[0].start()
+    outs.append(pltpu.make_async_copy(left_ref, out_hbm.at[:, :E], sems.at[12]))
+    outs[1].start()
+    copies[7].wait()
+    du = dot(w_in_ref[...], d).astype(BF)
     copies[8].wait()
-    du = dot(w_in_ref[...], d).astype(BF)
-    copies[9].wait()
     de = dot(w_up_ref[...], du).astype(BF)
     r = lax.broadcasted_iota(jnp.int32, (8 * DEV, 2 * N), 0)
     j = lax.broadcasted_iota(jnp.int32, (1, 2 * N), 1)
     place = jnp.where(r == 8 * lax.shift_right_logical(j, 1) + (j & 1), 1.0, 0.0).astype(BF)
-    for copy in copies[10:]:
+    for copy in copies[9:]:
         copy.wait()
-    outs.append(pltpu.make_async_copy(outer_ref, out_hbm.at[:, 2 * E :], sems.at[14]))
-    outs[1].start()
     misc = misc_ref[...].astype(F32) + dot(hits_ref[...], de, NT) + dot(place, g[INNER:, :])
     right_ref[...] = misc.astype(BF)
-    outs.append(pltpu.make_async_copy(right_ref, out_hbm.at[:, E : 2 * E], sems.at[15]))
+    outs.append(pltpu.make_async_copy(right_ref, out_hbm.at[:, E : 2 * E], sems.at[13]))
     outs[2].start()
     for copy in outs:
         copy.wait()
@@ -323,53 +368,69 @@
             go_ref[pl.ds(pl.multiple_of(at * N, N), N), m * E : (m + 1) * E] = ref[rows, lanes].astype(F32)
 
 
+def hop(value, axis, step):
+    return lax.ppermute(value, axis, [(i, (i + step) % 4) for i in range(4)])
+
+
 def local(event_rows, event_index, decay, saved_state, dout, w_up, w_in, w_out, skip):
     every = ("x", "core", "y", "z")
     rows, d_out = event_rows[0], dout[0]
-    proj, dy, cum, cumt, sums = call(
+    core, y, z = (lax.axis_index(a).reshape(1) for a in ("core", "y", "z"))
+    proj, dy, cum, cumt, *sums = call(
         project_kernel,
-        [((T, PROJ), BF), ((INNER, T), BF), ((H, T), F32), ((T, H), F32), ((H, SROWS, N), BF)],
+        [((T, PROJ), BF), ((INNER, T), BF), ((H, T), F32), ((T, H), F32)] + [((MR, N), BF)] * 4,
         BIG, 750_000_000, 4_500_000,
-        in_specs=[HBM] * 6, out_specs=(VM,) * 5,
+        in_specs=[SM] + [HBM] * 6, out_specs=(VM,) * 8,
         scratch_shapes=[
             pltpu.VMEM((T, E), BF), pltpu.VMEM((T, D), BF), pltpu.VMEM((H, T), F32),
             pltpu.VMEM((E, D), BF), pltpu.VMEM((D, PROJ), BF), pltpu.VMEM((INNER, D), BF),
-            pltpu.SemaphoreType.DMA((6,)),
+            pltpu.VMEM((4, MR, N), BF), pltpu.SemaphoreType.DMA((6,)),
         ],
-    )(rows, d_out, decay[0], w_up, w_in, w_out)
-    got = lax.all_to_all(sums, ("y", "z"), 0, 0, tiled=True)
-    core = lax.axis_index("core").reshape(1)
-    keep, give, dx, tx, bt, dbt, dct, misc, hits = call(
+    )(z, rows, d_out, decay[0], w_up, w_in, w_out)
+    sums = sums[:1] + [hop(v, "z", k + 1) for k, v in enumerate(sums[1:])]
+    keep, give, dx, tx, bt, dbt, dct, extra = call(
         local_kernel,
         [((INNER // 2, D), F32), ((INNER // 2, D), BF), ((INNER, T), F32), ((INNER, T), BF), ((N, T), BF),
-         ((N, T), F32), ((N, T), BF), ((8 * DEV, E), BF), ((8 * DEV, T), BF)],
+         ((N, T), F32), ((N, T), BF), ((1, T), F32)],
         BIG, 2_500_000_000, 6_000_000,
-        in_specs=[VM] * 7 + [SM] * 2, out_specs=(VM,) * 9,
+        in_specs=[VM] * 6 + [SM] * 2, out_specs=(VM,) * 8,
         scratch_shapes=[
             pltpu.VMEM((INNER, T), F32), pltpu.VMEM((INNER, T), BF),
             pltpu.VMEM((INNER, N), BF), pltpu.VMEM((T, T), BF),
         ],
-    )(proj, dy, cum, cumt, jnp.swapaxes(saved_state[0, 0], 1, 2).reshape(INNER, N), d_out, event_index, skip, core)
-    got, give = lax.optimization_barrier((got, give))
-    (carries,) = call(
-        scan_kernel, [((CTX, HP, N), BF)], 8, 4_000_000, 600_000, in_specs=[VM], out_specs=(VM,)
-    )(got)
-    carry = lax.all_to_all(carries, ("y", "z"), 0, 0, tiled=True)
+    )(proj, dy, cum, cumt, jnp.swapaxes(saved_state[0, 0], 1, 2).reshape(INNER, N), d_out, skip, core)
+    sums, give = lax.optimization_barrier((sums, give))
+    (total,) = call(
+        inner_kernel, [((MR, N), BF)], 8, 2_000_000, 400_000,
+        in_specs=[SM] + [VM] * 4, out_specs=(VM,), scratch_shapes=[pltpu.VMEM((4, MR, N), BF)],
+    )(z, *sums)
+    totals = [total] + [hop(total, "y", k) for k in range(1, 4)]
+    misc, hits = call(
+        slot_kernel, [((8 * DEV, E), BF), ((8 * DEV, T), BF)], BIG, 300_000_000, 1_500_000,
+        in_specs=[VM] * 2, out_specs=(VM,) * 2,
+    )(event_index, extra)
+    totals, hits = lax.optimization_barrier((totals, hits))
+    carries = call(
+        outer_kernel, [((GR, N), BF)] * 4, 8, 4_000_000, 800_000,
+        in_specs=[SM] * 2 + [VM] * 8, out_specs=(VM,) * 4,
+        scratch_shapes=[pltpu.VMEM((4, MR, N), BF)] * 2 + [pltpu.VMEM((4, GR, N), BF)],
+    )(y, z, *sums, *totals)
+    carries = [carries[0]] + [hop(v, "z", k + 1) for k, v in enumerate(carries[1:])]
     (outer,) = call(
         pair_kernel, [((8 * DEV, E), BF)], 8, 300_000, 2_000_000, in_specs=[VM] * 2, out_specs=(VM,)
     )(keep, lax.ppermute(give, "core", [(0, 1), (1, 0)]))
-    carry, outer = lax.optimization_barrier((carry, outer))
+    carries, outer = lax.optimization_barrier((carries, outer))
     (pay,) = call(
-        finish_kernel, [((8 * DEV, 3 * E), BF)], BIG, 1_400_000_000, 6_000_000,
-        in_specs=[HBM] * 13, out_specs=(HBM,),
+        finish_kernel, [((8 * DEV, 3 * E), BF)], 52, 1_400_000_000, 6_000_000,
+        in_specs=[SM] + [VM] * 5 + [HBM] * 11, out_specs=(HBM,),
         scratch_shapes=[
             pltpu.VMEM((INNER, N), BF), pltpu.VMEM((N, T), BF), pltpu.VMEM((H, T), F32),
             pltpu.VMEM((INNER, T), F32), pltpu.VMEM((INNER, T), BF), pltpu.VMEM((N, T), F32),
             pltpu.VMEM((PROJ, T), BF), pltpu.VMEM((T, E), BF), pltpu.VMEM((D, PROJ), BF), pltpu.VMEM((E, D), BF),
-            pltpu.VMEM((8 * DEV, T), BF), pltpu.VMEM((8 * DEV, E), BF), pltpu.VMEM((8 * DEV, E), BF),
-            pltpu.VMEM((INNER, E), BF), pltpu.VMEM((8 * DEV, E), BF), pltpu.SemaphoreType.DMA((16,)),
+            pltpu.VMEM((8 * DEV, T), BF), pltpu.VMEM((8 * DEV, E), BF),
+            pltpu.VMEM((INNER, E), BF), pltpu.VMEM((8 * DEV, E), BF), pltpu.SemaphoreType.DMA((14,)),
         ],
-    )(carry.reshape(INNER, N), bt, cum, dx, tx, dbt, dct, rows, w_in, w_up, hits, misc, outer)
+    )(z, *carries, outer, bt, cum, dx, tx, dbt, dct, rows, w_in, w_up, hits, misc)
     pay_got = lax.all_to_all(pay.reshape(DEV, 8, 3 * E), every, 0, 0, tiled=True)
     chunk, skip_sum = call(
         sum_kernel, [((DEV // 2, 8, 7 * N), BF), ((1, 128), F32)], 12, 2_000_000, 3_000_000,

time: 104 us -> 102 us (0.981)
  waiting for transfers between devices: 8.49 us -> 6.41 us
  local copies, waits for them, and re-layouts: 1.51 us -> 0.04 us
    ppermute x0 -> x9, starting transfers between devices: none -> 13.7 us  [hop(): return lax.ppermute(value, axis, [(i, (i + step) % 4) for i in range(4)])]
    all_to_all x2 -> x0, starting transfers between devices: 12.7 us -> none  [the longest x1 8.61 us: local(): got = lax.all_to_all(sums, ('y', 'z'), 0, 0, tiled=True)]
    all_to_all x2 -> x0, waiting for transfers between devices: 8.45 us -> none  [the longest x1 6.9 us: local(): carry = lax.all_to_all(carries, ('y', 'z'), 0, 0, tiled=True)]
    ppermute x0 -> x9, waiting for transfers between devices: none -> 6.37 us  [hop(): return lax.ppermute(value, axis, [(i, (i + step) % 4) for i in range(4)])]
    pallas_call x2 -> x4, Pallas kernels: 5.66 us -> 7.38 us  [the longest x1 4.92 us: local(): call(finish_kernel, [((8 * DEV, 3 * E), BF)], 52, 1400000000, 6000000, in...]
    unnamed x10 -> x20, local copies, waits for them, and re-layouts: 1.51 us -> 0.04 us
  transfers between devices with their start and end apart: 4 -> 11, of which waited for: 2 -> 5; matrix products, arithmetic and copies ran while one was open for 1% -> 1% of each run, Pallas kernels for 8% -> 9%
where the time goes in v6:
time: 102 us; the launch traced here: 101 us
  blocking collectives  52.4 us (51%)
  Pallas kernels  23 us (23%)
  starting transfers between devices  18.1 us (18%)
  waiting for transfers between devices  6.41 us (6%)
    all_to_all x1, blocking collectives, local(): lax.all_to_all(pay.reshape(DEV, 8, 3 * E), every, 0, 0, tiled=True)  31.8 us
    all_to_all x1, blocking collectives, local(): lax.all_to_all(chunk, ('x', 'y', 'z'), 0, 0, tiled=True)  20.6 us
    ppermute x9, starting transfers between devices, hop(): return lax.ppermute(value, axis, [(i, (i + step) % 4) for i in range(4)])  13.7 us
    ppermute x9, waiting for transfers between devices, hop(): return lax.ppermute(value, axis, [(i, (i + step) % 4) for i in range(4)])  6.37 us
    pallas_call x1, Pallas kernels, local(): call(local_kernel, [((INNER // 2, D), F32), ((INNER // 2, D), BF), ((INNE...  5.4 us
    pallas_call x1, Pallas kernels, local(): call(finish_kernel, [((8 * DEV, 3 * E), BF)], 52, 1400000000, 6000000, in...  4.92 us
    pallas_call x1, Pallas kernels, local(): call(project_kernel, [((T, PROJ), BF), ((INNER, T), BF), ((H, T), F32), (...  4.25 us
    pallas_call x1, Pallas kernels, local(): pl.pallas_call(last_kernel, grid=(4,), out_shape=tuple((jax.ShapeDtypeStr...  4.06 us
  transfers between devices with their start and end apart: 11, of which 5 were waited for; matrix products, arithmetic and copies ran while one was open for 1% of the time, Pallas kernels for 9%

profile of v6, /device:TPU:1, one launch (start us, length us, event | category | flops | bytes accessed | tf_op | source)
XLA Modules:
  0.0 101.4 jit_solution(1939711157825153356)
XLA Ops:
  0.6 4.3 %shard_map.128 = (bf16[256,1280]{1,0:T(8,128)(2,1)}, bf16[1024,256]{1,0:T(8,128)(2,1)}, f32[16,256]{1,0:T(8,128)}, f32[256,16]{1,0:T(8,128)}, bf16[272,128]{1,0:...) custom-call(s32[1]{0:T(128)} %bitcast.1.z_ref, ...), custom_call_target="tpu_custom_call" | custom-call | flops 750000000 | bytes 4500000 | tf_op jit(solution)/shard_map/pallas_call | solution.py:379
  4.9 2.5 %collective-permute-start = (bf16[272,128]{1,0:T(8,128)(2,1)}, bf16[272,128]{1,0:T(8,128)(2,1)S(1)}, u32[]{:S(2)}, u32[]{:S(2)}) collective-permute-start(bf16[272,128]{1,0:T(8,128)(2,1)} %get-tuple-element.48), channel_id=1, source_target_pairs={{0,1},{1,2},{2,3},{3,0},{4,5},{5,6},{6,7},{7,4},{8,9},{9,10},{10,1... | collective-permute-start | bytes 208904 | tf_op jit(solution)/shard_map/ppermute | solution.py:372
  7.4 3.3 %collective-permute-start.1 = (bf16[272,128]{1,0:T(8,128)(2,1)}, bf16[272,128]{1,0:T(8,128)(2,1)S(1)}, u32[]{:S(2)}, u32[]{:S(2)}) collective-permute-start(bf16[272,128]{1,0:T(8,128)(2,1)} %get-tuple-element.49), channel_id=1, source_target_pairs={{0,2},{1,3},{2,0},{3,1},{4,6},{5,7},{6,4},{7,5},{8,10},{9,11},{10,... | collective-permute-start | bytes 208904 | tf_op jit(solution)/shard_map/ppermute | solution.py:372
  10.8 0.7 collective-permute-start.2
  11.5 5.4 %shard_map.129 = (f32[512,512]{1,0:T(8,128)}, bf16[512,512]{1,0:T(8,128)(2,1)}, f32[1024,256]{1,0:T(8,128)}, bf16[1024,256]{1,0:T(8,128)(2,1)}, bf16[128,256]{1,...) custom-call(bf16[256,1280]{1,0:T(8,128)(2,1)} %get-tuple-element.51.proj_ref, ...), custom_call_target="tpu_custom_call" | custom-call | flops 2500000000 | bytes 6000000 | tf_op jit(solution)/shard_map/pallas_call | solution.py:391
  16.9 1.6 %collective-permute-start.9 = (bf16[512,512]{1,0:T(8,128)(2,1)}, bf16[512,512]{1,0:T(8,128)(2,1)S(1)}, u32[]{:S(2)}, u32[]{:S(2)}) collective-permute-start(bf16[512,512]{1,0:T(8,128)(2,1)} %get-tuple-element.71), channel_id=1, source_target_pairs={{0,16},{16,0},{1,17},{17,1},{2,18},{18,2},{3,19},{19,3},{4,20},{20... | collective-permute-start | bytes 1572872 | tf_op jit(solution)/shard_map/ppermute | solution.py:421
  18.6 2.8 %collective-permute-start.5 = (bf16[272,128]{1,0:T(8,128)(2,1)S(1)}, bf16[272,128]{1,0:T(8,128)(2,1)S(1)}, u32[]{:S(2)}, u32[]{:S(2)}) collective-permute-start(bf16[272,128]{1,0:T(8,128)(2,1)S(1)} %shard_map.130.ta_ref), channel_id=1, source_target_pairs={{0,12},{4,0},{8,4},{12,8},{1,13},{5,1},{9,5},{13,9},{2,14},{6,2},{... | collective-permute-start | bytes 208904 | tf_op jit(solution)/shard_map/ppermute | solution.py:372
  21.8 0.7 collective-permute-start.3
  22.5 2.2 %shard_map.131 = (bf16[1024,256]{1,0:T(8,128)(2,1)}, bf16[1024,256]{1,0:T(8,128)(2,1)}) custom-call(s32[1,256]{1,0:T(1,128)} %index_ref.1, f32[1,256]{1,0:T(1,128)} %get-tuple-element.60.extra_ref), custom_call_target="tpu_custom_call" | custom-call | flops 300000000 | bytes 1500000 | tf_op jit(solution)/shard_map/pallas_call | solution.py:408
  24.7 1.4 %collective-permute-done.4.tc_ref = bf16[272,128]{1,0:T(8,128)(2,1)S(1)} collective-permute-done((bf16[272,128]{1,0:T(8,128)(2,1)S(1)}, bf16[272,128]{1,0:T(8,128)(2,1)S(1)}, u32[]{:S(2)}, u32[]{:S(2)}) %collective-permute-start.4) | collective-permute-done | bytes 69664 | tf_op jit(solution)/shard_map/ppermute | solution.py:372
  26.1 2.3 %collective-permute-done.3.tb_ref = bf16[272,128]{1,0:T(8,128)(2,1)S(1)} collective-permute-done((bf16[272,128]{1,0:T(8,128)(2,1)S(1)}, bf16[272,128]{1,0:T(8,128)(2,1)S(1)}, u32[]{:S(2)}, u32[]{:S(2)}) %collective-permute-start.3) | collective-permute-done | bytes 69664 | tf_op jit(solution)/shard_map/ppermute | solution.py:372
  28.6 0.8 collective-permute-start.6
  29.4 0.4 collective-permute-start.7
  29.8 2.1 %collective-permute-start.8 = (bf16[256,128]{1,0:T(8,128)(2,1)S(1)}, bf16[256,128]{1,0:T(8,128)(2,1)S(1)}, u32[]{:S(2)}, u32[]{:S(2)}) collective-permute-start(bf16[256,128]{1,0:T(8,128)(2,1)S(1)} %get-tuple-element.69), channel_id=1, source_target_pairs={{0,3},{1,0},{2,1},{3,2},{4,7},{5,4},{6,5},{7,6},{8,11},{9,8},{10,9... | collective-permute-start | bytes 196616 | tf_op jit(solution)/shard_map/ppermute | solution.py:372
  32.0 1.0 collective-permute-done.6.c1_ref
  33.0 1.1 %collective-permute-done.7.c2_ref = bf16[256,128]{1,0:T(8,128)(2,1)S(1)} collective-permute-done((bf16[256,128]{1,0:T(8,128)(2,1)S(1)}, bf16[256,128]{1,0:T(8,128)(2,1)S(1)}, u32[]{:S(2)}, u32[]{:S(2)}) %collective-permute-start.7) | collective-permute-done | bytes 65568 | tf_op jit(solution)/shard_map/ppermute | solution.py:372
  34.1 0.5 collective-permute-done.8.c3_ref
  34.7 4.9 %shard_map.134 = bf16[1024,768]{1,0:T(8,128)(2,1)} custom-call(s32[1]{0:T(128)} %bitcast.1.z_ref, bf16[256,128]{1,0:T(8,128)(2,1)S(1)} %get-tuple-element.72.c0_ref, bf16[256,128]{1,0:T(8,128)(2,1)S(1)} %collective-permute-done.6.c1_ref, bf16[256,128]{1,0:T(8,128)(2,1)S(1)} %collective-permute-done.7.c2_ref, ...), custom_call_target="tpu_custom_call" | custom-call | flops 1400000000 | bytes 6000000 | tf_op jit(solution)/shard_map/pallas_call | solution.py:423
  39.6 31.8 %all_to_all.10.got_ref = bf16[128,8,768]{2,1,0:T(8,128)(2,1)S(1)} all-to-all(bf16[128,8,768]{2,1,0:T(8,128)(2,1)} %bitcast.19), channel_id=1, replica_groups=mesh['x'=4,'core'=2,'y'=4,'z'=4] {'x','core','y','z'}, dimensions={0} | all-to-all | bytes 3145728 | tf_op jit(solution)/shard_map/all_to_all | solution.py:434
  71.8 20.6 %all_to_all.11 = bf16[64,8,896]{2,1,0:T(8,128)(2,1)S(1)} all-to-all(bf16[64,8,896]{2,1,0:T(8,128)(2,1)S(1)} %get-tuple-element.84), channel_id=1, replica_groups=mesh['x'=4,'core'=2,'y'=4,'z'=4] {'x','y','z'}, dimensions={0} | all-to-all | bytes 1835008 | tf_op jit(solution)/shard_map/all_to_all | solution.py:439
  92.4 2.8 %collective-permute-start.10 = (bf16[512,896]{1,0:T(8,128)(2,1)S(1)}, bf16[512,896]{1,0:T(8,128)(2,1)S(1)}, u32[]{:S(2)}, u32[]{:S(2)}) collective-permute-start(bf16[512,896]{1,0:T(8,128)(2,1)S(1)} %bitcast.15), channel_id=1, source_target_pairs={{0,16},{16,0},{1,17},{17,1},{2,18},{18,2},{3,19},{19,3},{4,20},{20... | collective-permute-start | bytes 2752520 | tf_op jit(solution)/shard_map/ppermute | solution.py:440
  95.2 1.5 %shard_map.137 = f32[512,256]{1,0:T(8,128)} custom-call(bf16[128,8,768]{2,1,0:T(8,128)(2,1)S(1)} %all_to_all.10.got_ref), custom_call_target="tpu_custom_call" | custom-call | flops 400000000 | bytes 2000000 | tf_op jit(solution)/shard_map/pallas_call | solution.py:441
  96.7 0.6 add_bitcast_fusion
  97.3 4.1 %shard_map.136 = (f32[256,512]{1,0:T(8,128)}, f32[512,1280]{1,0:T(8,128)}, f32[1024,512]{1,0:T(8,128)}) custom-call(s32[1]{0:T(128)} %bitcast.core_ref, bf16[512,896]{1,0:T(8,128)(2,1)S(1)} %bitcast.16, bf16[512,896]{1,0:T(8,128)(2,1)S(1)} %collective-permute-done.10.other_ref, bf16[256,512]{1,0:T(8,128)(2,1)S(1)} %copy-done.1, bf16[512,1280]{1,0:T(8,128)(2,1)S(1)} %copy-done), custom_call_target="tpu_custom_call" | custom-call | flops 700000000 | bytes 8000000 | tf_op jit(solution)/shard_map/pallas_call | solution.py:447
  (31 shorter events, 1.1 us)
Async XLA Ops:
  4.9 12.0 %collective-permute-start = (bf16[272,128]{1,0:T(8,128)(2,1)}, bf16[272,128]{1,0:T(8,128)(2,1)S(1)}, u32[]{:S(2)}, u32[]{:S(2)}) collective-permute-start(bf16[272,128]{1,0:T(8,128)(2,1)} %get-tuple-element.48), channel_id=1, source_target_pairs={{0,1},{1,2},{2,3},{3,0},{4,5},{5,6},{6,7},{7,4},{8,9},{9,10},{10,1... | collective-permute-start | bytes 208904 | tf_op jit(solution)/shard_map/ppermute | solution.py:372
  7.4 9.5 %collective-permute-start.1 = (bf16[272,128]{1,0:T(8,128)(2,1)}, bf16[272,128]{1,0:T(8,128)(2,1)S(1)}, u32[]{:S(2)}, u32[]{:S(2)}) collective-permute-start(bf16[272,128]{1,0:T(8,128)(2,1)} %get-tuple-element.49), channel_id=1, source_target_pairs={{0,2},{1,3},{2,0},{3,1},{4,6},{5,7},{6,4},{7,5},{8,10},{9,11},{10,... | collective-permute-start | bytes 208904 | tf_op jit(solution)/shard_map/ppermute | solution.py:372
  10.8 6.1 %collective-permute-start.2 = (bf16[272,128]{1,0:T(8,128)(2,1)}, bf16[272,128]{1,0:T(8,128)(2,1)S(1)}, u32[]{:S(2)}, u32[]{:S(2)}) collective-permute-start(bf16[272,128]{1,0:T(8,128)(2,1)} %get-tuple-element.50), channel_id=1, source_target_pairs={{0,3},{1,0},{2,1},{3,2},{4,7},{5,4},{6,5},{7,6},{8,11},{9,8},{10,9... | collective-permute-start | bytes 208904 | tf_op jit(solution)/shard_map/ppermute | solution.py:372
  11.5 7.0 %copy-start.5 = (bf16[272,128]{1,0:T(8,128)(2,1)S(1)}, bf16[272,128]{1,0:T(8,128)(2,1)}, u32[]{:S(2)}) copy-start(bf16[272,128]{1,0:T(8,128)(2,1)} %get-tuple-element.56.a_ref) | copy-start | bytes 208900
  16.9 15.0 %copy-start.2 = (f32[512,512]{1,0:T(8,128)S(1)}, f32[512,512]{1,0:T(8,128)}, u32[]{:S(2)}) copy-start(f32[512,512]{1,0:T(8,128)} %get-tuple-element.70.keep_ref) | copy-start | bytes 3145732
  16.9 15.0 %collective-permute-start.9 = (bf16[512,512]{1,0:T(8,128)(2,1)}, bf16[512,512]{1,0:T(8,128)(2,1)S(1)}, u32[]{:S(2)}, u32[]{:S(2)}) collective-permute-start(bf16[512,512]{1,0:T(8,128)(2,1)} %get-tuple-element.71), channel_id=1, source_target_pairs={{0,16},{16,0},{1,17},{17,1},{2,18},{18,2},{3,19},{19,3},{4,20},{20... | collective-permute-start | bytes 1572872 | tf_op jit(solution)/shard_map/ppermute | solution.py:421
  18.6 6.1 %collective-permute-start.5 = (bf16[272,128]{1,0:T(8,128)(2,1)S(1)}, bf16[272,128]{1,0:T(8,128)(2,1)S(1)}, u32[]{:S(2)}, u32[]{:S(2)}) collective-permute-start(bf16[272,128]{1,0:T(8,128)(2,1)S(1)} %shard_map.130.ta_ref), channel_id=1, source_target_pairs={{0,12},{4,0},{8,4},{12,8},{1,13},{5,1},{9,5},{13,9},{2,14},{6,2},{... | collective-permute-start | bytes 208904 | tf_op jit(solution)/shard_map/ppermute | solution.py:372
  21.4 4.7 %collective-permute-start.4 = (bf16[272,128]{1,0:T(8,128)(2,1)S(1)}, bf16[272,128]{1,0:T(8,128)(2,1)S(1)}, u32[]{:S(2)}, u32[]{:S(2)}) collective-permute-start(bf16[272,128]{1,0:T(8,128)(2,1)S(1)} %shard_map.130.ta_ref), channel_id=1, source_target_pairs={{0,8},{4,12},{8,0},{12,4},{1,9},{5,13},{9,1},{13,5},{2,10},{6,14},... | collective-permute-start | bytes 208904 | tf_op jit(solution)/shard_map/ppermute | solution.py:372
  21.8 6.7 %collective-permute-start.3 = (bf16[272,128]{1,0:T(8,128)(2,1)S(1)}, bf16[272,128]{1,0:T(8,128)(2,1)S(1)}, u32[]{:S(2)}, u32[]{:S(2)}) collective-permute-start(bf16[272,128]{1,0:T(8,128)(2,1)S(1)} %shard_map.130.ta_ref), channel_id=1, source_target_pairs={{0,4},{4,8},{8,12},{12,0},{1,5},{5,9},{9,13},{13,1},{2,6},{6,10},{... | collective-permute-start | bytes 208904 | tf_op jit(solution)/shard_map/ppermute | solution.py:372
  24.7 10.0 %copy-start.1 = (bf16[256,512]{1,0:T(8,128)(2,1)S(1)}, bf16[256,512]{1,0:T(8,128)(2,1)}, u32[]{:S(2)}) copy-start(bf16[256,512]{1,0:T(8,128)(2,1)} %w_up_ref.1) | copy-start | bytes 786436
  24.7 10.0 %copy-start.3 = (bf16[1,256,256]{2,1,0:T(8,128)(2,1)S(1)}, bf16[1,256,256]{2,1,0:T(8,128)(2,1)}, u32[]{:S(2)}) copy-start(bf16[1,256,256]{2,1,0:T(8,128)(2,1)} %param.9) | copy-start | bytes 393220
  24.7 10.0 %copy-start.4 = (bf16[1024,256]{1,0:T(8,128)(2,1)S(1)}, bf16[1024,256]{1,0:T(8,128)(2,1)}, u32[]{:S(2)}) copy-start(bf16[1024,256]{1,0:T(8,128)(2,1)} %get-tuple-element.79.tx_hbm) | copy-start | bytes 1572868
  24.7 10.0 %copy-start.6 = (f32[128,256]{1,0:T(8,128)S(1)}, f32[128,256]{1,0:T(8,128)}, u32[]{:S(2)}) copy-start(f32[128,256]{1,0:T(8,128)} %get-tuple-element.80.dbt_hbm) | copy-start | bytes 393220
  24.7 10.0 %copy-start.7 = (bf16[128,256]{1,0:T(8,128)(2,1)S(1)}, bf16[128,256]{1,0:T(8,128)(2,1)}, u32[]{:S(2)}) copy-start(bf16[128,256]{1,0:T(8,128)(2,1)} %get-tuple-element.77.bt_hbm) | copy-start | bytes 196612
  24.7 10.0 %copy-start.8 = (bf16[128,256]{1,0:T(8,128)(2,1)S(1)}, bf16[128,256]{1,0:T(8,128)(2,1)}, u32[]{:S(2)}) copy-start(bf16[128,256]{1,0:T(8,128)(2,1)} %get-tuple-element.81.dct_hbm) | copy-start | bytes 196612
  24.7 10.0 %copy-start.9 = (f32[16,256]{1,0:T(8,128)S(1)}, f32[16,256]{1,0:T(8,128)}, u32[]{:S(2)}) copy-start(f32[16,256]{1,0:T(8,128)} %get-tuple-element.53.cum_ref.cum_hbm) | copy-start | bytes 49156
  28.6 4.4 %collective-permute-start.6 = (bf16[256,128]{1,0:T(8,128)(2,1)S(1)}, bf16[256,128]{1,0:T(8,128)(2,1)S(1)}, u32[]{:S(2)}, u32[]{:S(2)}) collective-permute-start(bf16[256,128]{1,0:T(8,128)(2,1)S(1)} %get-tuple-element.67), channel_id=1, source_target_pairs={{0,1},{1,2},{2,3},{3,0},{4,5},{5,6},{6,7},{7,4},{8,9},{9,10},{10,1... | collective-permute-start | bytes 196616 | tf_op jit(solution)/shard_map/ppermute | solution.py:372
  29.4 4.7 %collective-permute-start.7 = (bf16[256,128]{1,0:T(8,128)(2,1)S(1)}, bf16[256,128]{1,0:T(8,128)(2,1)S(1)}, u32[]{:S(2)}, u32[]{:S(2)}) collective-permute-start(bf16[256,128]{1,0:T(8,128)(2,1)S(1)} %get-tuple-element.68), channel_id=1, source_target_pairs={{0,2},{1,3},{2,0},{3,1},{4,6},{5,7},{6,4},{7,5},{8,10},{9,11},{10,... | collective-permute-start | bytes 196616 | tf_op jit(solution)/shard_map/ppermute | solution.py:372
  29.8 4.8 %collective-permute-start.8 = (bf16[256,128]{1,0:T(8,128)(2,1)S(1)}, bf16[256,128]{1,0:T(8,128)(2,1)S(1)}, u32[]{:S(2)}, u32[]{:S(2)}) collective-permute-start(bf16[256,128]{1,0:T(8,128)(2,1)S(1)} %get-tuple-element.69), channel_id=1, source_target_pairs={{0,3},{1,0},{2,1},{3,2},{4,7},{5,4},{6,5},{7,6},{8,11},{9,8},{10,9... | collective-permute-start | bytes 196616 | tf_op jit(solution)/shard_map/ppermute | solution.py:372
  71.8 25.5 %copy-start = (bf16[512,1280]{1,0:T(8,128)(2,1)S(1)}, bf16[512,1280]{1,0:T(8,128)(2,1)}, u32[]{:S(2)}) copy-start(bf16[512,1280]{1,0:T(8,128)(2,1)} %w_in_ref.1) | copy-start | bytes 3932164
  92.4 4.9 %collective-permute-start.10 = (bf16[512,896]{1,0:T(8,128)(2,1)S(1)}, bf16[512,896]{1,0:T(8,128)(2,1)S(1)}, u32[]{:S(2)}, u32[]{:S(2)}) collective-permute-start(bf16[512,896]{1,0:T(8,128)(2,1)S(1)} %bitcast.15), channel_id=1, source_target_pairs={{0,16},{16,0},{1,17},{17,1},{2,18},{18,2},{3,19},{19,3},{4,20},{20... | collective-permute-start | bytes 2752520 | tf_op jit(solution)/shard_map/ppermute | solution.py:440

commit v7 on v6

--- a/solution.py
+++ b/solution.py
@@ -79,8 +79,8 @@
 
 
 def project_kernel(z_ref, rows_hbm, dout_hbm, decay_hbm, w_up_hbm, w_in_hbm, w_out_hbm,
-                   proj_ref, dy_ref, cum_ref, cumt_ref, g0_ref, g1_ref, g2_ref, g3_ref,
-                   rows_ref, dout_ref, decay_ref, w_up_ref, w_in_ref, w_out_ref, all_ref, sems):
+                   proj_hbm, dy_hbm, cum_ref, cumt_ref, g0_ref, g1_ref, g2_ref, g3_ref,
+                   rows_ref, dout_ref, decay_ref, w_up_ref, w_in_ref, w_out_ref, proj_ref, dy_ref, all_ref, sems):
     pairs = (
         (rows_hbm, rows_ref), (w_up_hbm, w_up_ref), (w_in_hbm, w_in_ref),
         (dout_hbm, dout_ref), (w_out_hbm, w_out_ref), (decay_hbm, decay_ref),
@@ -93,9 +93,13 @@
     u = dot(rows_ref[...], w_up_ref[...]).astype(BF)
     copies[2].wait()
     proj_ref[...] = dot(u, w_in_ref[...]).astype(BF)
+    outs = [pltpu.make_async_copy(proj_ref, proj_hbm, sems.at[6])]
+    outs[0].start()
     copies[3].wait()
     copies[4].wait()
     dy_ref[...] = dot(w_out_ref[...], dout_ref[...], NT).astype(BF)
+    outs.append(pltpu.make_async_copy(dy_ref, dy_hbm, sems.at[7]))
+    outs[1].start()
     copies[5].wait()
     logs = split3(jnp.log(decay_ref[...]))
     r = lax.broadcasted_iota(jnp.int32, (T, T), 0)
@@ -121,6 +125,8 @@
         all_ref[q, GR:, :] = decay_rows([jnp.broadcast_to(amount[h : h + 1, :], (1, N)) for h in range(q * GH, (q + 1) * GH)])
     for k, ref in enumerate((g0_ref, g1_ref, g2_ref, g3_ref)):
         ref[...] = all_ref[(z_ref[0] + k) & 3]
+    for copy in outs:
+        copy.wait()
 
 
 def place(at, refs, out_ref):
@@ -158,8 +164,15 @@
         ref[...] = ct_ref[(z + k) & 3]
 
 
-def local_kernel(proj_ref, dy_ref, cum_ref, cumt_ref, h0_ref, dout_ref, skip_ref, core_ref,
-                 keep_ref, give_ref, dx_ref, tx_ref, bt_ref, dbt_ref, dct_ref, extra_ref, y_ref, sdy_ref, h0t_ref, sum_ref):
+def local_kernel(proj_hbm, dy_hbm, cum_ref, cumt_ref, h0_hbm, dout_hbm, skip_ref, core_ref,
+                 keep_hbm, give_hbm, dx_hbm, tx_hbm, bt_ref, dbt_ref, dct_ref, extra_ref,
+                 proj_ref, dy_ref, h0_ref, dout_ref, keep_ref, give_ref, dx_ref, tx_ref,
+                 y_ref, sdy_ref, h0t_ref, sum_ref, sems):
+    pairs = ((proj_hbm, proj_ref), (dy_hbm, dy_ref), (h0_hbm, h0_ref), (dout_hbm, dout_ref))
+    copies = [pltpu.make_async_copy(a, b, sems.at[i]) for i, (a, b) in enumerate(pairs)]
+    for copy in copies:
+        copy.start()
+    copies[0].wait()
     proj_t = jnp.transpose(proj_ref[...])
     bt = proj_t[INNER : INNER + N, :]
     ct = proj_t[INNER + N :, :]
@@ -174,6 +187,8 @@
     start = jnp.exp(cum)
     tail = DT * jnp.exp(cum[:, T - 1 : T] - cum)
     bt_ref[...] = bt
+    copies[1].wait()
+    copies[2].wait()
     h0t_ref[...] = h0_ref[...].astype(BF)
     y_ref[...] = dot(h0t_ref[...], ct)
     skip_sums = []
@@ -213,12 +228,19 @@
         a01 += m01 * q0[:, N:]
         a11 += m11 * q11
         skip_sums.append(jnp.sum(x_f * dy_f, keepdims=True))
+    pairs = ((dx_ref, dx_hbm), (tx_ref, tx_hbm), (give_ref, give_hbm), (keep_ref, keep_hbm))
+    outs = [pltpu.make_async_copy(a, b, sems.at[4 + i]) for i, (a, b) in enumerate(pairs)]
+    outs[0].start()
+    outs[1].start()
+    copies[3].wait()
     core = core_ref[0]
     half = INNER // 2
     mine = pl.ds(pl.multiple_of(core * half, half), half)
     other = pl.ds(pl.multiple_of((1 - core) * half, half), half)
     give_ref[...] = dot(y_ref[other, :].astype(BF), dout_ref[...]).astype(BF)
+    outs[2].start()
     keep_ref[...] = dot(y_ref[mine, :].astype(BF), dout_ref[...])
+    outs[3].start()
     sum_ref[:N, :N] = a00.astype(BF)
     sum_ref[:N, N:] = a01.astype(BF)
     sum_ref[N:, :N] = zero
@@ -233,6 +255,8 @@
         top = whole.astype(BF).astype(F32)
         extra = extra + jnp.where(lane == 128 + h, top, 0.0) + jnp.where(lane == 160 + h, whole - top, 0.0)
     extra_ref[...] = extra
+    for copy in outs:
+        copy.wait()
 
 
 def slot_kernel(index_ref, extra_ref, misc_ref, hits_ref):
@@ -359,8 +383,9 @@
             g_ref[INNER:, m * N : (m + 1) * N] = dot(pick, side_ref[...]).astype(BF)
 
     g = g_ref[...]
-    in_ref[...] = lax.dot_general(w_up_ref[...], g, (((0,), (1,)), ((), ())), preferred_element_type=F32)
-    up_ref[...] = jnp.transpose(dot(w_in_ref[...], g))
+    part = pl.ds(pl.multiple_of(step * N, N), N)
+    in_ref[...] = lax.dot_general(w_up_ref[:, part], g, (((0,), (1,)), ((), ())), preferred_element_type=F32)
+    up_ref[...] = jnp.transpose(dot(w_in_ref[part, :], g))
     lanes = pl.ds(pl.multiple_of(E + N + E * lax.shift_right_logical(step, 1), N), E)
     for m in range(2):
         rows = pl.ds(pl.multiple_of((2 * m + (step & 1)) * N, N), N)
@@ -380,11 +405,12 @@
         project_kernel,
         [((T, PROJ), BF), ((INNER, T), BF), ((H, T), F32), ((T, H), F32)] + [((MR, N), BF)] * 4,
         BIG, 750_000_000, 4_500_000,
-        in_specs=[SM] + [HBM] * 6, out_specs=(VM,) * 8,
+        in_specs=[SM] + [HBM] * 6, out_specs=(HBM,) * 2 + (VM,) * 6,
         scratch_shapes=[
             pltpu.VMEM((T, E), BF), pltpu.VMEM((T, D), BF), pltpu.VMEM((H, T), F32),
             pltpu.VMEM((E, D), BF), pltpu.VMEM((D, PROJ), BF), pltpu.VMEM((INNER, D), BF),
-            pltpu.VMEM((4, MR, N), BF), pltpu.SemaphoreType.DMA((6,)),
+            pltpu.VMEM((T, PROJ), BF), pltpu.VMEM((INNER, T), BF),
+            pltpu.VMEM((4, MR, N), BF), pltpu.SemaphoreType.DMA((8,)),
         ],
     )(z, rows, d_out, decay[0], w_up, w_in, w_out)
     sums = sums[:1] + [hop(v, "z", k + 1) for k, v in enumerate(sums[1:])]
@@ -393,10 +419,13 @@
         [((INNER // 2, D), F32), ((INNER // 2, D), BF), ((INNER, T), F32), ((INNER, T), BF), ((N, T), BF),
          ((N, T), F32), ((N, T), BF), ((1, T), F32)],
         BIG, 2_500_000_000, 6_000_000,
-        in_specs=[VM] * 6 + [SM] * 2, out_specs=(VM,) * 8,
+        in_specs=[HBM] * 2 + [VM] * 2 + [HBM] * 2 + [SM] * 2, out_specs=(HBM,) * 4 + (VM,) * 4,
         scratch_shapes=[
+            pltpu.VMEM((T, PROJ), BF), pltpu.VMEM((INNER, T), BF), pltpu.VMEM((INNER, N), F32), pltpu.VMEM((T, D), BF),
+            pltpu.VMEM((INNER // 2, D), F32), pltpu.VMEM((INNER // 2, D), BF),
             pltpu.VMEM((INNER, T), F32), pltpu.VMEM((INNER, T), BF),
-            pltpu.VMEM((INNER, N), BF), pltpu.VMEM((T, T), BF),
+            pltpu.VMEM((INNER, T), F32), pltpu.VMEM((INNER, T), BF),
+            pltpu.VMEM((INNER, N), BF), pltpu.VMEM((T, T), BF), pltpu.SemaphoreType.DMA((8,)),
         ],
     )(proj, dy, cum, cumt, jnp.swapaxes(saved_state[0, 0], 1, 2).reshape(INNER, N), d_out, skip, core)
     sums, give = lax.optimization_barrier((sums, give))
@@ -421,7 +450,7 @@
     )(keep, lax.ppermute(give, "core", [(0, 1), (1, 0)]))
     carries, outer = lax.optimization_barrier((carries, outer))
     (pay,) = call(
-        finish_kernel, [((8 * DEV, 3 * E), BF)], 52, 1_400_000_000, 6_000_000,
+        finish_kernel, [((8 * DEV, 3 * E), BF)], 51, 1_400_000_000, 6_000_000,
         in_specs=[SM] + [VM] * 5 + [HBM] * 11, out_specs=(HBM,),
         scratch_shapes=[
             pltpu.VMEM((INNER, N), BF), pltpu.VMEM((N, T), BF), pltpu.VMEM((H, T), F32),
@@ -441,14 +470,13 @@
     (table,) = call(
         table_kernel, [((ROWS_DEV, E), F32)], 12, 400_000_000, 2_000_000, in_specs=[VM], out_specs=(VM,)
     )(pay_got)
-    full = pl.BlockSpec((DEV * 4, 7 * N), lambda i: (0, 0))
     column = pl.BlockSpec((E, D // 4), lambda i: (0, i))
     row = pl.BlockSpec((D // 4, PROJ), lambda i: (i, 0))
     grad_up, grad_in, grad_out = pl.pallas_call(
         last_kernel,
         grid=(4,),
         out_shape=tuple(jax.ShapeDtypeStruct(s, F32) for s in ((E, D), (D, PROJ), (INNER, D))),
-        in_specs=[SM, full, full, column, row],
+        in_specs=[SM] + [VM] * 4,
         out_specs=(column, row, pl.BlockSpec((INNER // 4, D), lambda i: (i, 0))),
         scratch_shapes=[pltpu.VMEM((PROJ, E), BF), pltpu.VMEM((8 * DEV, N), BF)],
         compiler_params=pltpu.CompilerParams(vmem_limit_bytes=24 * MB),

time: 102 us -> 103 us (level)
  Pallas kernels: 23 us -> 24.3 us
    pallas_call x1, Pallas kernels: 5.4 us -> 6.65 us  [local(): call(local_kernel, [((INNER // 2, D), F32), ((INNER // 2, D), BF), ((INNE...]
  transfers between devices with their start and end apart: 11 -> 11, of which waited for: 5 -> 5; matrix products, arithmetic and copies ran while one was open for 1% -> 1% of each run, Pallas kernels for 9% -> 10%
where the time goes in v7:
time: 103 us
  blocking collectives  52.6 us (51%)
  Pallas kernels  24.3 us (24%)
  starting transfers between devices  18.1 us (18%)
  waiting for transfers between devices  6.38 us (6%)
    all_to_all x1, blocking collectives, local(): lax.all_to_all(pay.reshape(DEV, 8, 3 * E), every, 0, 0, tiled=True)  31.8 us
    all_to_all x1, blocking collectives, local(): lax.all_to_all(chunk, ('x', 'y', 'z'), 0, 0, tiled=True)  20.8 us
    ppermute x9, starting transfers between devices, hop(): return lax.ppermute(value, axis, [(i, (i + step) % 4) for i in range(4)])  13.7 us
    pallas_call x1, Pallas kernels, local(): call(local_kernel, [((INNER // 2, D), F32), ((INNER // 2, D), BF), ((INNE...  6.65 us
    ppermute x9, waiting for transfers between devices, hop(): return lax.ppermute(value, axis, [(i, (i + step) % 4) for i in range(4)])  6.34 us
    pallas_call x1, Pallas kernels, local(): call(finish_kernel, [((8 * DEV, 3 * E), BF)], 51, 1400000000, 6000000, in...  4.92 us
    pallas_call x1, Pallas kernels, local(): call(project_kernel, [((T, PROJ), BF), ((INNER, T), BF), ((H, T), F32), (...  4.39 us
    pallas_call x1, Pallas kernels, local(): pl.pallas_call(last_kernel, grid=(4,), out_shape=tuple((jax.ShapeDtypeStr...  3.99 us
  transfers between devices with their start and end apart: 11, of which 5 were waited for; matrix products, arithmetic and copies ran while one was open for 1% of the time, Pallas kernels for 10%

profile of v7, /device:TPU:1, one launch (start us, length us, event | category | flops | bytes accessed | tf_op | source)
XLA Modules:
  0.0 102.9 jit_solution(371970142012976130)
XLA Ops:
  0.6 4.4 %shard_map.128 = (bf16[256,1280]{1,0:T(8,128)(2,1)}, bf16[1024,256]{1,0:T(8,128)(2,1)}, f32[16,256]{1,0:T(8,128)}, f32[256,16]{1,0:T(8,128)}, bf16[272,128]{1,0:...) custom-call(s32[1]{0:T(128)} %bitcast.1.z_ref, ...), custom_call_target="tpu_custom_call" | custom-call | flops 750000000 | bytes 4500000 | tf_op jit(solution)/shard_map/pallas_call | solution.py:404
  5.0 2.5 %collective-permute-start = (bf16[272,128]{1,0:T(8,128)(2,1)}, bf16[272,128]{1,0:T(8,128)(2,1)S(1)}, u32[]{:S(2)}, u32[]{:S(2)}) collective-permute-start(bf16[272,128]{1,0:T(8,128)(2,1)} %get-tuple-element.48), channel_id=1, source_target_pairs={{0,1},{1,2},{2,3},{3,0},{4,5},{5,6},{6,7},{7,4},{8,9},{9,10},{10,1... | collective-permute-start | bytes 208904 | tf_op jit(solution)/shard_map/ppermute | solution.py:397
  7.6 3.3 %collective-permute-start.1 = (bf16[272,128]{1,0:T(8,128)(2,1)}, bf16[272,128]{1,0:T(8,128)(2,1)S(1)}, u32[]{:S(2)}, u32[]{:S(2)}) collective-permute-start(bf16[272,128]{1,0:T(8,128)(2,1)} %get-tuple-element.49), channel_id=1, source_target_pairs={{0,2},{1,3},{2,0},{3,1},{4,6},{5,7},{6,4},{7,5},{8,10},{9,11},{10,... | collective-permute-start | bytes 208904 | tf_op jit(solution)/shard_map/ppermute | solution.py:397
  10.9 0.7 collective-permute-start.2
  11.6 6.6 %shard_map.129 = (f32[512,512]{1,0:T(8,128)}, bf16[512,512]{1,0:T(8,128)(2,1)}, f32[1024,256]{1,0:T(8,128)}, bf16[1024,256]{1,0:T(8,128)(2,1)}, bf16[128,256]{1,...) custom-call(bf16[256,1280]{1,0:T(8,128)(2,1)} %get-tuple-element.51.proj_hbm, ...), custom_call_target="tpu_custom_call" | custom-call | flops 2500000000 | bytes 6000000 | tf_op jit(solution)/shard_map/pallas_call | solution.py:417
  18.3 1.6 %collective-permute-start.9 = (bf16[512,512]{1,0:T(8,128)(2,1)}, bf16[512,512]{1,0:T(8,128)(2,1)S(1)}, u32[]{:S(2)}, u32[]{:S(2)}) collective-permute-start(bf16[512,512]{1,0:T(8,128)(2,1)} %get-tuple-element.71), channel_id=1, source_target_pairs={{0,16},{16,0},{1,17},{17,1},{2,18},{18,2},{3,19},{19,3},{4,20},{20... | collective-permute-start | bytes 1572872 | tf_op jit(solution)/shard_map/ppermute | solution.py:450
  20.0 2.8 %collective-permute-start.5 = (bf16[272,128]{1,0:T(8,128)(2,1)S(1)}, bf16[272,128]{1,0:T(8,128)(2,1)S(1)}, u32[]{:S(2)}, u32[]{:S(2)}) collective-permute-start(bf16[272,128]{1,0:T(8,128)(2,1)S(1)} %shard_map.130.ta_ref), channel_id=1, source_target_pairs={{0,12},{4,0},{8,4},{12,8},{1,13},{5,1},{9,5},{13,9},{2,14},{6,2},{... | collective-permute-start | bytes 208904 | tf_op jit(solution)/shard_map/ppermute | solution.py:397
  22.8 0.3 collective-permute-start.4
  23.2 0.7 collective-permute-start.3
  23.8 2.2 %shard_map.131 = (bf16[1024,256]{1,0:T(8,128)(2,1)}, bf16[1024,256]{1,0:T(8,128)(2,1)}) custom-call(s32[1,256]{1,0:T(1,128)} %index_ref.1, f32[1,256]{1,0:T(1,128)} %get-tuple-element.60.extra_ref), custom_call_target="tpu_custom_call" | custom-call | flops 300000000 | bytes 1500000 | tf_op jit(solution)/shard_map/pallas_call | solution.py:437
  26.1 1.4 %collective-permute-done.4.tc_ref = bf16[272,128]{1,0:T(8,128)(2,1)S(1)} collective-permute-done((bf16[272,128]{1,0:T(8,128)(2,1)S(1)}, bf16[272,128]{1,0:T(8,128)(2,1)S(1)}, u32[]{:S(2)}, u32[]{:S(2)}) %collective-permute-start.4) | collective-permute-done | bytes 69664 | tf_op jit(solution)/shard_map/ppermute | solution.py:397
  27.5 2.3 %collective-permute-done.3.tb_ref = bf16[272,128]{1,0:T(8,128)(2,1)S(1)} collective-permute-done((bf16[272,128]{1,0:T(8,128)(2,1)S(1)}, bf16[272,128]{1,0:T(8,128)(2,1)S(1)}, u32[]{:S(2)}, u32[]{:S(2)}) %collective-permute-start.3) | collective-permute-done | bytes 69664 | tf_op jit(solution)/shard_map/ppermute | solution.py:397
  30.0 0.8 collective-permute-start.6
  31.0 2.3 %collective-permute-start.8 = (bf16[256,128]{1,0:T(8,128)(2,1)S(1)}, bf16[256,128]{1,0:T(8,128)(2,1)S(1)}, u32[]{:S(2)}, u32[]{:S(2)}) collective-permute-start(bf16[256,128]{1,0:T(8,128)(2,1)S(1)} %get-tuple-element.69), channel_id=1, source_target_pairs={{0,3},{1,0},{2,1},{3,2},{4,7},{5,4},{6,5},{7,6},{8,11},{9,8},{10,9... | collective-permute-start | bytes 196616 | tf_op jit(solution)/shard_map/ppermute | solution.py:397
  33.4 1.0 collective-permute-done.6.c1_ref
  34.4 1.1 %collective-permute-done.7.c2_ref = bf16[256,128]{1,0:T(8,128)(2,1)S(1)} collective-permute-done((bf16[256,128]{1,0:T(8,128)(2,1)S(1)}, bf16[256,128]{1,0:T(8,128)(2,1)S(1)}, u32[]{:S(2)}, u32[]{:S(2)}) %collective-permute-start.7) | collective-permute-done | bytes 65568 | tf_op jit(solution)/shard_map/ppermute | solution.py:397
  35.5 0.5 collective-permute-done.8.c3_ref
  36.1 4.9 %shard_map.134 = bf16[1024,768]{1,0:T(8,128)(2,1)} custom-call(s32[1]{0:T(128)} %bitcast.1.z_ref, bf16[256,128]{1,0:T(8,128)(2,1)S(1)} %get-tuple-element.72.c0_ref, bf16[256,128]{1,0:T(8,128)(2,1)S(1)} %collective-permute-done.6.c1_ref, bf16[256,128]{1,0:T(8,128)(2,1)S(1)} %collective-permute-done.7.c2_ref, ...), custom_call_target="tpu_custom_call" | custom-call | flops 1400000000 | bytes 6000000 | tf_op jit(solution)/shard_map/pallas_call | solution.py:452
  41.0 31.8 %all_to_all.10.got_ref = bf16[128,8,768]{2,1,0:T(8,128)(2,1)S(1)} all-to-all(bf16[128,8,768]{2,1,0:T(8,128)(2,1)} %bitcast.19), channel_id=1, replica_groups=mesh['x'=4,'core'=2,'y'=4,'z'=4] {'x','core','y','z'}, dimensions={0} | all-to-all | bytes 3145728 | tf_op jit(solution)/shard_map/all_to_all | solution.py:463
  73.2 20.8 %all_to_all.11 = bf16[64,8,896]{2,1,0:T(8,128)(2,1)S(1)} all-to-all(bf16[64,8,896]{2,1,0:T(8,128)(2,1)S(1)} %get-tuple-element.84), channel_id=1, replica_groups=mesh['x'=4,'core'=2,'y'=4,'z'=4] {'x','y','z'}, dimensions={0} | all-to-all | bytes 1835008 | tf_op jit(solution)/shard_map/all_to_all | solution.py:468
  94.0 2.8 %collective-permute-start.10 = (bf16[512,896]{1,0:T(8,128)(2,1)S(1)}, bf16[512,896]{1,0:T(8,128)(2,1)S(1)}, u32[]{:S(2)}, u32[]{:S(2)}) collective-permute-start(bf16[512,896]{1,0:T(8,128)(2,1)S(1)} %bitcast.15), channel_id=1, source_target_pairs={{0,16},{16,0},{1,17},{17,1},{2,18},{18,2},{3,19},{19,3},{4,20},{20... | collective-permute-start | bytes 2752520 | tf_op jit(solution)/shard_map/ppermute | solution.py:469
  96.8 1.5 %shard_map.137 = f32[512,256]{1,0:T(8,128)} custom-call(bf16[128,8,768]{2,1,0:T(8,128)(2,1)S(1)} %all_to_all.10.got_ref), custom_call_target="tpu_custom_call" | custom-call | flops 400000000 | bytes 2000000 | tf_op jit(solution)/shard_map/pallas_call | solution.py:470
  98.3 0.6 add_bitcast_fusion
  98.9 4.0 %shard_map.136 = (f32[256,512]{1,0:T(8,128)}, f32[512,1280]{1,0:T(8,128)}, f32[1024,512]{1,0:T(8,128)}) custom-call(s32[1]{0:T(128)} %bitcast.core_ref, bf16[512,896]{1,0:T(8,128)(2,1)S(1)} %bitcast.16, bf16[512,896]{1,0:T(8,128)(2,1)S(1)} %collective-permute-done.10.other_ref, bf16[256,512]{1,0:T(8,128)(2,1)S(1)} %copy-done.1, bf16[512,1280]{1,0:T(8,128)(2,1)S(1)} %copy-done), custom_call_target="tpu_custom_call" | custom-call | flops 700000000 | bytes 8000000 | tf_op jit(solution)/shard_map/pallas_call | solution.py:475
  (35 shorter events, 1.0 us)
Async XLA Ops:
  5.0 13.2 %collective-permute-start = (bf16[272,128]{1,0:T(8,128)(2,1)}, bf16[272,128]{1,0:T(8,128)(2,1)S(1)}, u32[]{:S(2)}, u32[]{:S(2)}) collective-permute-start(bf16[272,128]{1,0:T(8,128)(2,1)} %get-tuple-element.48), channel_id=1, source_target_pairs={{0,1},{1,2},{2,3},{3,0},{4,5},{5,6},{6,7},{7,4},{8,9},{9,10},{10,1... | collective-permute-start | bytes 208904 | tf_op jit(solution)/shard_map/ppermute | solution.py:397
  7.6 10.7 %collective-permute-start.1 = (bf16[272,128]{1,0:T(8,128)(2,1)}, bf16[272,128]{1,0:T(8,128)(2,1)S(1)}, u32[]{:S(2)}, u32[]{:S(2)}) collective-permute-start(bf16[272,128]{1,0:T(8,128)(2,1)} %get-tuple-element.49), channel_id=1, source_target_pairs={{0,2},{1,3},{2,0},{3,1},{4,6},{5,7},{6,4},{7,5},{8,10},{9,11},{10,... | collective-permute-start | bytes 208904 | tf_op jit(solution)/shard_map/ppermute | solution.py:397
  10.9 7.4 %collective-permute-start.2 = (bf16[272,128]{1,0:T(8,128)(2,1)}, bf16[272,128]{1,0:T(8,128)(2,1)S(1)}, u32[]{:S(2)}, u32[]{:S(2)}) collective-permute-start(bf16[272,128]{1,0:T(8,128)(2,1)} %get-tuple-element.50), channel_id=1, source_target_pairs={{0,3},{1,0},{2,1},{3,2},{4,7},{5,4},{6,5},{7,6},{8,11},{9,8},{10,9... | collective-permute-start | bytes 208904 | tf_op jit(solution)/shard_map/ppermute | solution.py:397
  11.6 8.3 %copy-start.7 = (bf16[272,128]{1,0:T(8,128)(2,1)S(1)}, bf16[272,128]{1,0:T(8,128)(2,1)}, u32[]{:S(2)}) copy-start(bf16[272,128]{1,0:T(8,128)(2,1)} %get-tuple-element.56.a_ref) | copy-start | bytes 208900
  18.3 15.0 %copy-start.2 = (f32[512,512]{1,0:T(8,128)S(1)}, f32[512,512]{1,0:T(8,128)}, u32[]{:S(2)}) copy-start(f32[512,512]{1,0:T(8,128)} %get-tuple-element.70.keep_ref) | copy-start | bytes 3145732
  18.3 15.0 %collective-permute-start.9 = (bf16[512,512]{1,0:T(8,128)(2,1)}, bf16[512,512]{1,0:T(8,128)(2,1)S(1)}, u32[]{:S(2)}, u32[]{:S(2)}) collective-permute-start(bf16[512,512]{1,0:T(8,128)(2,1)} %get-tuple-element.71), channel_id=1, source_target_pairs={{0,16},{16,0},{1,17},{17,1},{2,18},{18,2},{3,19},{19,3},{4,20},{20... | collective-permute-start | bytes 1572872 | tf_op jit(solution)/shard_map/ppermute | solution.py:450
  20.0 6.1 %collective-permute-start.5 = (bf16[272,128]{1,0:T(8,128)(2,1)S(1)}, bf16[272,128]{1,0:T(8,128)(2,1)S(1)}, u32[]{:S(2)}, u32[]{:S(2)}) collective-permute-start(bf16[272,128]{1,0:T(8,128)(2,1)S(1)} %shard_map.130.ta_ref), channel_id=1, source_target_pairs={{0,12},{4,0},{8,4},{12,8},{1,13},{5,1},{9,5},{13,9},{2,14},{6,2},{... | collective-permute-start | bytes 208904 | tf_op jit(solution)/shard_map/ppermute | solution.py:397
  22.8 4.7 %collective-permute-start.4 = (bf16[272,128]{1,0:T(8,128)(2,1)S(1)}, bf16[272,128]{1,0:T(8,128)(2,1)S(1)}, u32[]{:S(2)}, u32[]{:S(2)}) collective-permute-start(bf16[272,128]{1,0:T(8,128)(2,1)S(1)} %shard_map.130.ta_ref), channel_id=1, source_target_pairs={{0,8},{4,12},{8,0},{12,4},{1,9},{5,13},{9,1},{13,5},{2,10},{6,14},... | collective-permute-start | bytes 208904 | tf_op jit(solution)/shard_map/ppermute | solution.py:397
  23.2 6.7 %collective-permute-start.3 = (bf16[272,128]{1,0:T(8,128)(2,1)S(1)}, bf16[272,128]{1,0:T(8,128)(2,1)S(1)}, u32[]{:S(2)}, u32[]{:S(2)}) collective-permute-start(bf16[272,128]{1,0:T(8,128)(2,1)S(1)} %shard_map.130.ta_ref), channel_id=1, source_target_pairs={{0,4},{4,8},{8,12},{12,0},{1,5},{5,9},{9,13},{13,1},{2,6},{6,10},{... | collective-permute-start | bytes 208904 | tf_op jit(solution)/shard_map/ppermute | solution.py:397
  26.1 10.0 %copy-start.1 = (bf16[256,512]{1,0:T(8,128)(2,1)S(1)}, bf16[256,512]{1,0:T(8,128)(2,1)}, u32[]{:S(2)}) copy-start(bf16[256,512]{1,0:T(8,128)(2,1)} %w_up_ref.1) | copy-start | bytes 786436
  26.1 10.0 %copy-start.3 = (bf16[1,256,256]{2,1,0:T(8,128)(2,1)S(1)}, bf16[1,256,256]{2,1,0:T(8,128)(2,1)}, u32[]{:S(2)}) copy-start(bf16[1,256,256]{2,1,0:T(8,128)(2,1)} %param.9) | copy-start | bytes 393220
  26.1 10.0 %copy-start.4 = (bf16[1024,256]{1,0:T(8,128)(2,1)S(1)}, bf16[1024,256]{1,0:T(8,128)(2,1)}, u32[]{:S(2)}) copy-start(bf16[1024,256]{1,0:T(8,128)(2,1)} %get-tuple-element.79.tx_hbm) | copy-start | bytes 1572868
  26.1 10.0 %copy-start.5 = (bf16[1024,256]{1,0:T(8,128)(2,1)S(1)}, bf16[1024,256]{1,0:T(8,128)(2,1)}, u32[]{:S(2)}) copy-start(bf16[1024,256]{1,0:T(8,128)(2,1)} %get-tuple-element.83.misc_hbm) | copy-start | bytes 1572868
  26.1 10.0 %copy-start.6 = (bf16[1024,256]{1,0:T(8,128)(2,1)S(1)}, bf16[1024,256]{1,0:T(8,128)(2,1)}, u32[]{:S(2)}) copy-start(bf16[1024,256]{1,0:T(8,128)(2,1)} %get-tuple-element.82.hits_hbm) | copy-start | bytes 1572868
  26.1 10.0 %copy-start.8 = (f32[128,256]{1,0:T(8,128)S(1)}, f32[128,256]{1,0:T(8,128)}, u32[]{:S(2)}) copy-start(f32[128,256]{1,0:T(8,128)} %get-tuple-element.80.dbt_hbm) | copy-start | bytes 393220
  26.1 10.0 %copy-start.9 = (bf16[128,256]{1,0:T(8,128)(2,1)S(1)}, bf16[128,256]{1,0:T(8,128)(2,1)}, u32[]{:S(2)}) copy-start(bf16[128,256]{1,0:T(8,128)(2,1)} %get-tuple-element.77.bt_hbm) | copy-start | bytes 196612
  26.1 10.0 %copy-start.10 = (bf16[128,256]{1,0:T(8,128)(2,1)S(1)}, bf16[128,256]{1,0:T(8,128)(2,1)}, u32[]{:S(2)}) copy-start(bf16[128,256]{1,0:T(8,128)(2,1)} %get-tuple-element.81.dct_hbm) | copy-start | bytes 196612
  26.1 10.0 %copy-start.11 = (f32[16,256]{1,0:T(8,128)S(1)}, f32[16,256]{1,0:T(8,128)}, u32[]{:S(2)}) copy-start(f32[16,256]{1,0:T(8,128)} %get-tuple-element.53.cum_ref.cum_hbm) | copy-start | bytes 49156
  30.0 4.4 %collective-permute-start.6 = (bf16[256,128]{1,0:T(8,128)(2,1)S(1)}, bf16[256,128]{1,0:T(8,128)(2,1)S(1)}, u32[]{:S(2)}, u32[]{:S(2)}) collective-permute-start(bf16[256,128]{1,0:T(8,128)(2,1)S(1)} %get-tuple-element.67), channel_id=1, source_target_pairs={{0,1},{1,2},{2,3},{3,0},{4,5},{5,6},{6,7},{7,4},{8,9},{9,10},{10,1... | collective-permute-start | bytes 196616 | tf_op jit(solution)/shard_map/ppermute | solution.py:397
  30.8 4.7 %collective-permute-start.7 = (bf16[256,128]{1,0:T(8,128)(2,1)S(1)}, bf16[256,128]{1,0:T(8,128)(2,1)S(1)}, u32[]{:S(2)}, u32[]{:S(2)}) collective-permute-start(bf16[256,128]{1,0:T(8,128)(2,1)S(1)} %get-tuple-element.68), channel_id=1, source_target_pairs={{0,2},{1,3},{2,0},{3,1},{4,6},{5,7},{6,4},{7,5},{8,10},{9,11},{10,... | collective-permute-start | bytes 196616 | tf_op jit(solution)/shard_map/ppermute | solution.py:397
  31.0 5.1 %collective-permute-start.8 = (bf16[256,128]{1,0:T(8,128)(2,1)S(1)}, bf16[256,128]{1,0:T(8,128)(2,1)S(1)}, u32[]{:S(2)}, u32[]{:S(2)}) collective-permute-start(bf16[256,128]{1,0:T(8,128)(2,1)S(1)} %get-tuple-element.69), channel_id=1, source_target_pairs={{0,3},{1,0},{2,1},{3,2},{4,7},{5,4},{6,5},{7,6},{8,11},{9,8},{10,9... | collective-permute-start | bytes 196616 | tf_op jit(solution)/shard_map/ppermute | solution.py:397
  73.2 25.7 %copy-start = (bf16[512,1280]{1,0:T(8,128)(2,1)S(1)}, bf16[512,1280]{1,0:T(8,128)(2,1)}, u32[]{:S(2)}) copy-start(bf16[512,1280]{1,0:T(8,128)(2,1)} %w_in_ref.1) | copy-start | bytes 3932164
  94.0 4.9 %collective-permute-start.10 = (bf16[512,896]{1,0:T(8,128)(2,1)S(1)}, bf16[512,896]{1,0:T(8,128)(2,1)S(1)}, u32[]{:S(2)}, u32[]{:S(2)}) collective-permute-start(bf16[512,896]{1,0:T(8,128)(2,1)S(1)} %bitcast.15), channel_id=1, source_target_pairs={{0,16},{16,0},{1,17},{17,1},{2,18},{18,2},{3,19},{19,3},{4,20},{20... | collective-permute-start | bytes 2752520 | tf_op jit(solution)/shard_map/ppermute | solution.py:469

commit v8 on v6

--- a/solution.py
+++ b/solution.py
@@ -257,57 +257,30 @@
     misc_ref[...] = (misc + jnp.where((row_id & 7) == 6, extra_ref[...], 0.0)).astype(BF)
 
 
-def finish_kernel(z_ref, c0_ref, c1_ref, c2_ref, c3_ref, outer_ref, bt_hbm, cum_hbm, dx_hbm, tx_hbm, dbt_hbm, dct_hbm, rows_hbm,
-                  w_in_hbm, w_up_hbm, hits_hbm, misc_hbm, out_hbm,
-                  carry_ref, bt_ref, cum_ref, dx_ref, tx_ref, dbt_ref, d_ref, rows_ref,
-                  w_in_ref, w_up_ref, hits_ref, misc_ref, left_ref, right_ref, sems):
-    copies = [
-        pltpu.make_async_copy(a, b, sems.at[n])
-        for n, (a, b) in enumerate((
-            (bt_hbm, bt_ref), (cum_hbm, cum_ref), (dx_hbm, dx_ref), (tx_hbm, tx_ref),
-            (dbt_hbm, dbt_ref), (dct_hbm, d_ref.at[INNER + N :, :]), (rows_hbm, rows_ref),
-            (w_in_hbm, w_in_ref), (w_up_hbm, w_up_ref), (hits_hbm, hits_ref), (misc_hbm, misc_ref),
-        ))
-    ]
-    for copy in copies:
-        copy.start()
-    outs = [pltpu.make_async_copy(outer_ref, out_hbm.at[:, 2 * E :], sems.at[11])]
-    outs[0].start()
+def finish_kernel(z_ref, c0_ref, c1_ref, c2_ref, c3_ref, outer_ref, bt_ref, cum_ref, tx_ref, dbt_ref, dct_ref,
+                  rows_ref, w_up_ref, hits_ref, misc_ref, dx_ref, w_in_ref, out_ref, carry_ref, d_ref):
+    out_ref[:, 2 * E :] = outer_ref[...]
     for k, ref in enumerate((c0_ref, c1_ref, c2_ref, c3_ref)):
         carry_ref[pl.ds(pl.multiple_of(((z_ref[0] + 4 - k) & 3) * GR, GR), GR), :] = ref[...]
-    for copy in copies[:2]:
-        copy.wait()
     cum = cum_ref[...]
     tail = DT * jnp.exp(cum[:, T - 1 : T] - cum)
     carry = carry_ref[...]
     entering = dot(carry, bt_ref[...])
-    copies[2].wait()
     for h in range(H):
         lo, hi = h * HP, (h + 1) * HP
         d_ref[lo:hi, :] = (dx_ref[lo:hi, :] + tail[h : h + 1, :] * entering[lo:hi, :]).astype(BF)
-    for copy in copies[3:7]:
-        copy.wait()
+    d_ref[INNER + N :, :] = dct_ref[...]
     d_ref[INNER : INNER + N, :] = (dbt_ref[...] + dot(carry, tx_ref[...], TN)).astype(BF)
     d = d_ref[...]
     g = dot(d, rows_ref[...]).astype(BF)
-    left_ref[...] = g[:INNER, :]
-    outs.append(pltpu.make_async_copy(left_ref, out_hbm.at[:, :E], sems.at[12]))
-    outs[1].start()
-    copies[7].wait()
+    out_ref[:, :E] = g[:INNER, :]
     du = dot(w_in_ref[...], d).astype(BF)
-    copies[8].wait()
     de = dot(w_up_ref[...], du).astype(BF)
     r = lax.broadcasted_iota(jnp.int32, (8 * DEV, 2 * N), 0)
     j = lax.broadcasted_iota(jnp.int32, (1, 2 * N), 1)
     place = jnp.where(r == 8 * lax.shift_right_logical(j, 1) + (j & 1), 1.0, 0.0).astype(BF)
-    for copy in copies[9:]:
-        copy.wait()
     misc = misc_ref[...].astype(F32) + dot(hits_ref[...], de, NT) + dot(place, g[INNER:, :])
-    right_ref[...] = misc.astype(BF)
-    outs.append(pltpu.make_async_copy(right_ref, out_hbm.at[:, E : 2 * E], sems.at[13]))
-    outs[2].start()
-    for copy in outs:
-        copy.wait()
+    out_ref[:, E : 2 * E] = misc.astype(BF)
 
 
 def pair_kernel(keep_ref, got_ref, out_ref):
@@ -359,8 +332,9 @@
             g_ref[INNER:, m * N : (m + 1) * N] = dot(pick, side_ref[...]).astype(BF)
 
     g = g_ref[...]
-    in_ref[...] = lax.dot_general(w_up_ref[...], g, (((0,), (1,)), ((), ())), preferred_element_type=F32)
-    up_ref[...] = jnp.transpose(dot(w_in_ref[...], g))
+    part = pl.ds(pl.multiple_of(step * N, N), N)
+    in_ref[...] = lax.dot_general(w_up_ref[:, part], g, (((0,), (1,)), ((), ())), preferred_element_type=F32)
+    up_ref[...] = jnp.transpose(dot(w_in_ref[part, :], g))
     lanes = pl.ds(pl.multiple_of(E + N + E * lax.shift_right_logical(step, 1), N), E)
     for m in range(2):
         rows = pl.ds(pl.multiple_of((2 * m + (step & 1)) * N, N), N)
@@ -406,7 +380,7 @@
     )(z, *sums)
     totals = [total] + [hop(total, "y", k) for k in range(1, 4)]
     misc, hits = call(
-        slot_kernel, [((8 * DEV, E), BF), ((8 * DEV, T), BF)], BIG, 300_000_000, 1_500_000,
+        slot_kernel, [((8 * DEV, E), BF), ((8 * DEV, T), BF)], 16, 300_000_000, 1_500_000,
         in_specs=[VM] * 2, out_specs=(VM,) * 2,
     )(event_index, extra)
     totals, hits = lax.optimization_barrier((totals, hits))
@@ -421,16 +395,10 @@
     )(keep, lax.ppermute(give, "core", [(0, 1), (1, 0)]))
     carries, outer = lax.optimization_barrier((carries, outer))
     (pay,) = call(
-        finish_kernel, [((8 * DEV, 3 * E), BF)], 52, 1_400_000_000, 6_000_000,
-        in_specs=[SM] + [VM] * 5 + [HBM] * 11, out_specs=(HBM,),
-        scratch_shapes=[
-            pltpu.VMEM((INNER, N), BF), pltpu.VMEM((N, T), BF), pltpu.VMEM((H, T), F32),
-            pltpu.VMEM((INNER, T), F32), pltpu.VMEM((INNER, T), BF), pltpu.VMEM((N, T), F32),
-            pltpu.VMEM((PROJ, T), BF), pltpu.VMEM((T, E), BF), pltpu.VMEM((D, PROJ), BF), pltpu.VMEM((E, D), BF),
-            pltpu.VMEM((8 * DEV, T), BF), pltpu.VMEM((8 * DEV, E), BF),
-            pltpu.VMEM((INNER, E), BF), pltpu.VMEM((8 * DEV, E), BF), pltpu.SemaphoreType.DMA((14,)),
-        ],
-    )(z, *carries, outer, bt, cum, dx, tx, dbt, dct, rows, w_in, w_up, hits, misc)
+        finish_kernel, [((8 * DEV, 3 * E), BF)], 36, 1_400_000_000, 6_000_000,
+        in_specs=[SM] + [VM] * 16, out_specs=(VM,),
+        scratch_shapes=[pltpu.VMEM((INNER, N), BF), pltpu.VMEM((PROJ, T), BF)],
+    )(z, *carries, outer, bt, cum, tx, dbt, dct, rows, w_up, hits, misc, dx, w_in)
     pay_got = lax.all_to_all(pay.reshape(DEV, 8, 3 * E), every, 0, 0, tiled=True)
     chunk, skip_sum = call(
         sum_kernel, [((DEV // 2, 8, 7 * N), BF), ((1, 128), F32)], 12, 2_000_000, 3_000_000,
@@ -441,14 +409,13 @@
     (table,) = call(
         table_kernel, [((ROWS_DEV, E), F32)], 12, 400_000_000, 2_000_000, in_specs=[VM], out_specs=(VM,)
     )(pay_got)
-    full = pl.BlockSpec((DEV * 4, 7 * N), lambda i: (0, 0))
     column = pl.BlockSpec((E, D // 4), lambda i: (0, i))
     row = pl.BlockSpec((D // 4, PROJ), lambda i: (i, 0))
     grad_up, grad_in, grad_out = pl.pallas_call(
         last_kernel,
         grid=(4,),
         out_shape=tuple(jax.ShapeDtypeStruct(s, F32) for s in ((E, D), (D, PROJ), (INNER, D))),
-        in_specs=[SM, full, full, column, row],
+        in_specs=[SM] + [VM] * 4,
         out_specs=(column, row, pl.BlockSpec((INNER // 4, D), lambda i: (i, 0))),
         scratch_shapes=[pltpu.VMEM((PROJ, E), BF), pltpu.VMEM((8 * DEV, N), BF)],
         compiler_params=pltpu.CompilerParams(vmem_limit_bytes=24 * MB),

time: 102 us -> 99.4 us (0.975)
  Pallas kernels: 23 us -> 18.5 us
  local copies, waits for them, and re-layouts: 0.04 us -> 1.74 us
    pallas_call x2, Pallas kernels: 7.12 us -> 2.69 us  [the longest x1 2.1 us: local(): call(finish_kernel, [((8 * DEV, 3 * E), BF)], 36, 1400000000, 6000000, in...]
    unnamed x20 -> x26, local copies, waits for them, and re-layouts: 0.04 us -> 1.74 us
  transfers between devices with their start and end apart: 11 -> 11, of which waited for: 5 -> 5; matrix products, arithmetic and copies ran while one was open for 1% -> 1% of each run, Pallas kernels for 9% -> 8%
where the time goes in v8:
time: 99.4 us; the launch traced here: 99.2 us
  blocking collectives  52.1 us (52%)
  Pallas kernels  18.5 us (19%)
  starting transfers between devices  18.1 us (18%)
  waiting for transfers between devices  7.34 us (7%)
  local copies, waits for them, and re-layouts  1.74 us (2%)
    all_to_all x1, blocking collectives, local(): lax.all_to_all(pay.reshape(DEV, 8, 3 * E), every, 0, 0, tiled=True)  31.6 us
    all_to_all x1, blocking collectives, local(): lax.all_to_all(chunk, ('x', 'y', 'z'), 0, 0, tiled=True)  20.4 us
    ppermute x9, starting transfers between devices, hop(): return lax.ppermute(value, axis, [(i, (i + step) % 4) for i in range(4)])  13.7 us
    ppermute x9, waiting for transfers between devices, hop(): return lax.ppermute(value, axis, [(i, (i + step) % 4) for i in range(4)])  7.3 us
    pallas_call x1, Pallas kernels, local(): call(local_kernel, [((INNER // 2, D), F32), ((INNER // 2, D), BF), ((INNE...  5.4 us
    pallas_call x1, Pallas kernels, local(): call(project_kernel, [((T, PROJ), BF), ((INNER, T), BF), ((H, T), F32), (...  4.25 us
    pallas_call x1, Pallas kernels, local(): pl.pallas_call(last_kernel, grid=(4,), out_shape=tuple((jax.ShapeDtypeStr...  3.99 us
    ppermute x1, starting transfers between devices, local(): other = lax.ppermute(whole, 'core', [(0, 1), (1, 0)])  2.83 us
  transfers between devices with their start and end apart: 11, of which 5 were waited for; matrix products, arithmetic and copies ran while one was open for 1% of the time, Pallas kernels for 8%

profile of v8, /device:TPU:1, one launch (start us, length us, event | category | flops | bytes accessed | tf_op | source)
XLA Modules:
  0.0 99.2 jit_solution(3252201041564288852)
XLA Ops:
  0.6 4.2 %shard_map.128 = (bf16[256,1280]{1,0:T(8,128)(2,1)}, bf16[1024,256]{1,0:T(8,128)(2,1)}, f32[16,256]{1,0:T(8,128)}, f32[256,16]{1,0:T(8,128)}, bf16[272,128]{1,0:...) custom-call(s32[1]{0:T(128)} %bitcast.1.z_ref, ...), custom_call_target="tpu_custom_call" | custom-call | flops 750000000 | bytes 4500000 | tf_op jit(solution)/shard_map/pallas_call | solution.py:353
  4.9 2.5 %collective-permute-start = (bf16[272,128]{1,0:T(8,128)(2,1)}, bf16[272,128]{1,0:T(8,128)(2,1)S(1)}, u32[]{:S(2)}, u32[]{:S(2)}) collective-permute-start(bf16[272,128]{1,0:T(8,128)(2,1)} %get-tuple-element.48), channel_id=1, source_target_pairs={{0,1},{1,2},{2,3},{3,0},{4,5},{5,6},{6,7},{7,4},{8,9},{9,10},{10,1... | collective-permute-start | bytes 208904 | tf_op jit(solution)/shard_map/ppermute | solution.py:346
  7.4 3.3 %collective-permute-start.1 = (bf16[272,128]{1,0:T(8,128)(2,1)}, bf16[272,128]{1,0:T(8,128)(2,1)S(1)}, u32[]{:S(2)}, u32[]{:S(2)}) collective-permute-start(bf16[272,128]{1,0:T(8,128)(2,1)} %get-tuple-element.49), channel_id=1, source_target_pairs={{0,2},{1,3},{2,0},{3,1},{4,6},{5,7},{6,4},{7,5},{8,10},{9,11},{10,... | collective-permute-start | bytes 208904 | tf_op jit(solution)/shard_map/ppermute | solution.py:346
  10.8 0.7 collective-permute-start.2
  11.5 5.4 %shard_map.129 = (f32[512,512]{1,0:T(8,128)}, bf16[512,512]{1,0:T(8,128)(2,1)}, f32[1024,256]{1,0:T(8,128)}, bf16[1024,256]{1,0:T(8,128)(2,1)}, bf16[128,256]{1,...) custom-call(bf16[256,1280]{1,0:T(8,128)(2,1)} %get-tuple-element.51.proj_ref, ...), custom_call_target="tpu_custom_call" | custom-call | flops 2500000000 | bytes 6000000 | tf_op jit(solution)/shard_map/pallas_call | solution.py:365
  16.9 1.6 %collective-permute-start.9 = (bf16[512,512]{1,0:T(8,128)(2,1)}, bf16[512,512]{1,0:T(8,128)(2,1)S(1)}, u32[]{:S(2)}, u32[]{:S(2)}) collective-permute-start(bf16[512,512]{1,0:T(8,128)(2,1)} %get-tuple-element.71), channel_id=1, source_target_pairs={{0,16},{16,0},{1,17},{17,1},{2,18},{18,2},{3,19},{19,3},{4,20},{20... | collective-permute-start | bytes 1572872 | tf_op jit(solution)/shard_map/ppermute | solution.py:395
  18.6 2.8 %collective-permute-start.5 = (bf16[272,128]{1,0:T(8,128)(2,1)S(1)}, bf16[272,128]{1,0:T(8,128)(2,1)S(1)}, u32[]{:S(2)}, u32[]{:S(2)}) collective-permute-start(bf16[272,128]{1,0:T(8,128)(2,1)S(1)} %shard_map.130.ta_ref), channel_id=1, source_target_pairs={{0,12},{4,0},{8,4},{12,8},{1,13},{5,1},{9,5},{13,9},{2,14},{6,2},{... | collective-permute-start | bytes 208904 | tf_op jit(solution)/shard_map/ppermute | solution.py:346
  21.8 0.7 collective-permute-start.3
  22.5 0.7 copy-done.12
  23.1 0.6 shard_map.131
  23.8 2.4 %collective-permute-done.4.tc_ref = bf16[272,128]{1,0:T(8,128)(2,1)S(1)} collective-permute-done((bf16[272,128]{1,0:T(8,128)(2,1)S(1)}, bf16[272,128]{1,0:T(8,128)(2,1)S(1)}, u32[]{:S(2)}, u32[]{:S(2)}) %collective-permute-start.4) | collective-permute-done | bytes 69664 | tf_op jit(solution)/shard_map/ppermute | solution.py:346
  26.1 2.3 %collective-permute-done.3.tb_ref = bf16[272,128]{1,0:T(8,128)(2,1)S(1)} collective-permute-done((bf16[272,128]{1,0:T(8,128)(2,1)S(1)}, bf16[272,128]{1,0:T(8,128)(2,1)S(1)}, u32[]{:S(2)}, u32[]{:S(2)}) %collective-permute-start.3) | collective-permute-done | bytes 69664 | tf_op jit(solution)/shard_map/ppermute | solution.py:346
  28.6 0.8 collective-permute-start.6
  29.8 2.1 %collective-permute-start.8 = (bf16[256,128]{1,0:T(8,128)(2,1)S(1)}, bf16[256,128]{1,0:T(8,128)(2,1)S(1)}, u32[]{:S(2)}, u32[]{:S(2)}) collective-permute-start(bf16[256,128]{1,0:T(8,128)(2,1)S(1)} %get-tuple-element.69), channel_id=1, source_target_pairs={{0,3},{1,0},{2,1},{3,2},{4,7},{5,4},{6,5},{7,6},{8,11},{9,8},{10,9... | collective-permute-start | bytes 196616 | tf_op jit(solution)/shard_map/ppermute | solution.py:346
  32.0 1.0 %collective-permute-done.6.c1_ref = bf16[256,128]{1,0:T(8,128)(2,1)S(1)} collective-permute-done((bf16[256,128]{1,0:T(8,128)(2,1)S(1)}, bf16[256,128]{1,0:T(8,128)(2,1)S(1)}, u32[]{:S(2)}, u32[]{:S(2)}) %collective-permute-start.6) | collective-permute-done | bytes 65568 | tf_op jit(solution)/shard_map/ppermute | solution.py:346
  33.0 1.1 %collective-permute-done.7.c2_ref = bf16[256,128]{1,0:T(8,128)(2,1)S(1)} collective-permute-done((bf16[256,128]{1,0:T(8,128)(2,1)S(1)}, bf16[256,128]{1,0:T(8,128)(2,1)S(1)}, u32[]{:S(2)}, u32[]{:S(2)}) %collective-permute-start.7) | collective-permute-done | bytes 65568 | tf_op jit(solution)/shard_map/ppermute | solution.py:346
  34.7 1.0 %copy-done.5 = bf16[1024,256]{1,0:T(8,128)(2,1)S(1)} copy-done((bf16[1024,256]{1,0:T(8,128)(2,1)S(1)}, bf16[1024,256]{1,0:T(8,128)(2,1)}, u32[]{:S(2)}) %copy-start.5) | copy-done | bytes 524312
  35.7 2.1 %shard_map.134 = bf16[1024,768]{1,0:T(8,128)(2,1)S(1)} custom-call(s32[1]{0:T(128)} %bitcast.1.z_ref, bf16[256,128]{1,0:T(8,128)(2,1)S(1)} %get-tuple-element.72.c0_ref, bf16[256,128]{1,0:T(8,128)(2,1)S(1)} %collective-permute-done.6.c1_ref, bf16[256,128]{1,0:T(8,128)(2,1)S(1)} %collective-permute-done.7.c2_ref, ...), custom_call_target="tpu_custom_call" | custom-call | flops 1400000000 | bytes 6000000 | tf_op jit(solution)/shard_map/pallas_call | solution.py:397
  37.8 31.6 %all_to_all.10.got_ref = bf16[128,8,768]{2,1,0:T(8,128)(2,1)S(1)} all-to-all(bf16[128,8,768]{2,1,0:T(8,128)(2,1)S(1)} %bitcast.15), channel_id=1, replica_groups=mesh['x'=4,'core'=2,'y'=4,'z'=4] {'x','core','y','z'}, dimensions={0} | all-to-all | bytes 3145728 | tf_op jit(solution)/shard_map/all_to_all | solution.py:402
  69.8 20.4 %all_to_all.11 = bf16[64,8,896]{2,1,0:T(8,128)(2,1)S(1)} all-to-all(bf16[64,8,896]{2,1,0:T(8,128)(2,1)S(1)} %get-tuple-element.84), channel_id=1, replica_groups=mesh['x'=4,'core'=2,'y'=4,'z'=4] {'x','y','z'}, dimensions={0} | all-to-all | bytes 1835008 | tf_op jit(solution)/shard_map/all_to_all | solution.py:407
  90.2 2.8 %collective-permute-start.10 = (bf16[512,896]{1,0:T(8,128)(2,1)S(1)}, bf16[512,896]{1,0:T(8,128)(2,1)S(1)}, u32[]{:S(2)}, u32[]{:S(2)}) collective-permute-start(bf16[512,896]{1,0:T(8,128)(2,1)S(1)} %bitcast.16), channel_id=1, source_target_pairs={{0,16},{16,0},{1,17},{17,1},{2,18},{18,2},{3,19},{19,3},{4,20},{20... | collective-permute-start | bytes 2752520 | tf_op jit(solution)/shard_map/ppermute | solution.py:408
  93.1 1.5 %shard_map.137 = f32[512,256]{1,0:T(8,128)} custom-call(bf16[128,8,768]{2,1,0:T(8,128)(2,1)S(1)} %all_to_all.10.got_ref), custom_call_target="tpu_custom_call" | custom-call | flops 400000000 | bytes 2000000 | tf_op jit(solution)/shard_map/pallas_call | solution.py:409
  94.6 0.6 add_bitcast_fusion
  95.2 4.0 %shard_map.136 = (f32[256,512]{1,0:T(8,128)}, f32[512,1280]{1,0:T(8,128)}, f32[1024,512]{1,0:T(8,128)}) custom-call(s32[1]{0:T(128)} %bitcast.core_ref, bf16[512,896]{1,0:T(8,128)(2,1)S(1)} %bitcast.17, bf16[512,896]{1,0:T(8,128)(2,1)S(1)} %collective-permute-done.10.other_ref, bf16[256,512]{1,0:T(8,128)(2,1)S(1)} %copy-done.1, bf16[512,1280]{1,0:T(8,128)(2,1)S(1)} %copy-done), custom_call_target="tpu_custom_call" | custom-call | flops 700000000 | bytes 8000000 | tf_op jit(solution)/shard_map/pallas_call | solution.py:414
  (37 shorter events, 2.0 us)
Async XLA Ops:
  4.9 12.0 %collective-permute-start = (bf16[272,128]{1,0:T(8,128)(2,1)}, bf16[272,128]{1,0:T(8,128)(2,1)S(1)}, u32[]{:S(2)}, u32[]{:S(2)}) collective-permute-start(bf16[272,128]{1,0:T(8,128)(2,1)} %get-tuple-element.48), channel_id=1, source_target_pairs={{0,1},{1,2},{2,3},{3,0},{4,5},{5,6},{6,7},{7,4},{8,9},{9,10},{10,1... | collective-permute-start | bytes 208904 | tf_op jit(solution)/shard_map/ppermute | solution.py:346
  7.4 9.5 %collective-permute-start.1 = (bf16[272,128]{1,0:T(8,128)(2,1)}, bf16[272,128]{1,0:T(8,128)(2,1)S(1)}, u32[]{:S(2)}, u32[]{:S(2)}) collective-permute-start(bf16[272,128]{1,0:T(8,128)(2,1)} %get-tuple-element.49), channel_id=1, source_target_pairs={{0,2},{1,3},{2,0},{3,1},{4,6},{5,7},{6,4},{7,5},{8,10},{9,11},{10,... | collective-permute-start | bytes 208904 | tf_op jit(solution)/shard_map/ppermute | solution.py:346
  10.8 6.1 %collective-permute-start.2 = (bf16[272,128]{1,0:T(8,128)(2,1)}, bf16[272,128]{1,0:T(8,128)(2,1)S(1)}, u32[]{:S(2)}, u32[]{:S(2)}) collective-permute-start(bf16[272,128]{1,0:T(8,128)(2,1)} %get-tuple-element.50), channel_id=1, source_target_pairs={{0,3},{1,0},{2,1},{3,2},{4,7},{5,4},{6,5},{7,6},{8,11},{9,8},{10,9... | collective-permute-start | bytes 208904 | tf_op jit(solution)/shard_map/ppermute | solution.py:346
  11.5 7.0 %copy-start.6 = (bf16[272,128]{1,0:T(8,128)(2,1)S(1)}, bf16[272,128]{1,0:T(8,128)(2,1)}, u32[]{:S(2)}) copy-start(bf16[272,128]{1,0:T(8,128)(2,1)} %get-tuple-element.56.a_ref) | copy-start | bytes 208900
  11.5 11.0 %copy-start.11 = (s32[1,256]{1,0:T(1,128)S(1)}, s32[1,256]{1,0:T(1,128)}, u32[]{:S(2)}) copy-start(s32[1,256]{1,0:T(1,128)} %index_ref.1) | copy-start | bytes 3076
  16.9 15.0 %copy-start.2 = (f32[512,512]{1,0:T(8,128)S(1)}, f32[512,512]{1,0:T(8,128)}, u32[]{:S(2)}) copy-start(f32[512,512]{1,0:T(8,128)} %get-tuple-element.70.keep_ref) | copy-start | bytes 3145732
  16.9 15.0 %collective-permute-start.9 = (bf16[512,512]{1,0:T(8,128)(2,1)}, bf16[512,512]{1,0:T(8,128)(2,1)S(1)}, u32[]{:S(2)}, u32[]{:S(2)}) collective-permute-start(bf16[512,512]{1,0:T(8,128)(2,1)} %get-tuple-element.71), channel_id=1, source_target_pairs={{0,16},{16,0},{1,17},{17,1},{2,18},{18,2},{3,19},{19,3},{4,20},{20... | collective-permute-start | bytes 1572872 | tf_op jit(solution)/shard_map/ppermute | solution.py:395
  18.6 5.2 %collective-permute-start.5 = (bf16[272,128]{1,0:T(8,128)(2,1)S(1)}, bf16[272,128]{1,0:T(8,128)(2,1)S(1)}, u32[]{:S(2)}, u32[]{:S(2)}) collective-permute-start(bf16[272,128]{1,0:T(8,128)(2,1)S(1)} %shard_map.130.ta_ref), channel_id=1, source_target_pairs={{0,12},{4,0},{8,4},{12,8},{1,13},{5,1},{9,5},{13,9},{2,14},{6,2},{... | collective-permute-start | bytes 208904 | tf_op jit(solution)/shard_map/ppermute | solution.py:346
  21.4 4.7 %collective-permute-start.4 = (bf16[272,128]{1,0:T(8,128)(2,1)S(1)}, bf16[272,128]{1,0:T(8,128)(2,1)S(1)}, u32[]{:S(2)}, u32[]{:S(2)}) collective-permute-start(bf16[272,128]{1,0:T(8,128)(2,1)S(1)} %shard_map.130.ta_ref), channel_id=1, source_target_pairs={{0,8},{4,12},{8,0},{12,4},{1,9},{5,13},{9,1},{13,5},{2,10},{6,14},... | collective-permute-start | bytes 208904 | tf_op jit(solution)/shard_map/ppermute | solution.py:346
  21.8 6.7 %collective-permute-start.3 = (bf16[272,128]{1,0:T(8,128)(2,1)S(1)}, bf16[272,128]{1,0:T(8,128)(2,1)S(1)}, u32[]{:S(2)}, u32[]{:S(2)}) collective-permute-start(bf16[272,128]{1,0:T(8,128)(2,1)S(1)} %shard_map.130.ta_ref), channel_id=1, source_target_pairs={{0,4},{4,8},{8,12},{12,0},{1,5},{5,9},{9,13},{13,1},{2,6},{6,10},{... | collective-permute-start | bytes 208904 | tf_op jit(solution)/shard_map/ppermute | solution.py:346
  22.5 0.7 copy-start.12
  23.1 11.5 %copy-start.4 = (bf16[1,256,256]{2,1,0:T(8,128)(2,1)S(1)}, bf16[1,256,256]{2,1,0:T(8,128)(2,1)}, u32[]{:S(2)}) copy-start(bf16[1,256,256]{2,1,0:T(8,128)(2,1)} %param.9) | copy-start | bytes 393220
  23.1 11.5 %copy-start.7 = (f32[128,256]{1,0:T(8,128)S(1)}, f32[128,256]{1,0:T(8,128)}, u32[]{:S(2)}) copy-start(f32[128,256]{1,0:T(8,128)} %get-tuple-element.79.dbt_ref) | copy-start | bytes 393220
  23.1 11.5 %copy-start.8 = (bf16[128,256]{1,0:T(8,128)(2,1)S(1)}, bf16[128,256]{1,0:T(8,128)(2,1)}, u32[]{:S(2)}) copy-start(bf16[128,256]{1,0:T(8,128)(2,1)} %get-tuple-element.77.bt_ref) | copy-start | bytes 196612
  23.1 11.5 %copy-start.9 = (bf16[128,256]{1,0:T(8,128)(2,1)S(1)}, bf16[128,256]{1,0:T(8,128)(2,1)}, u32[]{:S(2)}) copy-start(bf16[128,256]{1,0:T(8,128)(2,1)} %get-tuple-element.80.dct_ref) | copy-start | bytes 196612
  23.7 10.9 %copy-start = (bf16[512,1280]{1,0:T(8,128)(2,1)S(1)}, bf16[512,1280]{1,0:T(8,128)(2,1)}, u32[]{:S(2)}) copy-start(bf16[512,1280]{1,0:T(8,128)(2,1)} %w_in_ref.3) | copy-start | bytes 3932164
  23.7 10.9 %copy-start.1 = (bf16[256,512]{1,0:T(8,128)(2,1)S(1)}, bf16[256,512]{1,0:T(8,128)(2,1)}, u32[]{:S(2)}) copy-start(bf16[256,512]{1,0:T(8,128)(2,1)} %w_up_ref.3) | copy-start | bytes 786436
  23.7 10.9 %copy-start.3 = (f32[1024,256]{1,0:T(8,128)S(1)}, f32[1024,256]{1,0:T(8,128)}, u32[]{:S(2)}) copy-start(f32[1024,256]{1,0:T(8,128)} %get-tuple-element.83.dx_ref) | copy-start | bytes 3145732
  23.8 10.9 %copy-start.10 = (f32[16,256]{1,0:T(8,128)S(1)}, f32[16,256]{1,0:T(8,128)}, u32[]{:S(2)}) copy-start(f32[16,256]{1,0:T(8,128)} %get-tuple-element.53.cum_ref) | copy-start | bytes 49156
  28.6 4.4 %collective-permute-start.6 = (bf16[256,128]{1,0:T(8,128)(2,1)S(1)}, bf16[256,128]{1,0:T(8,128)(2,1)S(1)}, u32[]{:S(2)}, u32[]{:S(2)}) collective-permute-start(bf16[256,128]{1,0:T(8,128)(2,1)S(1)} %get-tuple-element.67), channel_id=1, source_target_pairs={{0,1},{1,2},{2,3},{3,0},{4,5},{5,6},{6,7},{7,4},{8,9},{9,10},{10,1... | collective-permute-start | bytes 196616 | tf_op jit(solution)/shard_map/ppermute | solution.py:346
  29.4 4.7 %collective-permute-start.7 = (bf16[256,128]{1,0:T(8,128)(2,1)S(1)}, bf16[256,128]{1,0:T(8,128)(2,1)S(1)}, u32[]{:S(2)}, u32[]{:S(2)}) collective-permute-start(bf16[256,128]{1,0:T(8,128)(2,1)S(1)} %get-tuple-element.68), channel_id=1, source_target_pairs={{0,2},{1,3},{2,0},{3,1},{4,6},{5,7},{6,4},{7,5},{8,10},{9,11},{10,... | collective-permute-start | bytes 196616 | tf_op jit(solution)/shard_map/ppermute | solution.py:346
  29.8 4.8 %collective-permute-start.8 = (bf16[256,128]{1,0:T(8,128)(2,1)S(1)}, bf16[256,128]{1,0:T(8,128)(2,1)S(1)}, u32[]{:S(2)}, u32[]{:S(2)}) collective-permute-start(bf16[256,128]{1,0:T(8,128)(2,1)S(1)} %get-tuple-element.69), channel_id=1, source_target_pairs={{0,3},{1,0},{2,1},{3,2},{4,7},{5,4},{6,5},{7,6},{8,11},{9,8},{10,9... | collective-permute-start | bytes 196616 | tf_op jit(solution)/shard_map/ppermute | solution.py:346
  34.7 1.0 %copy-start.5 = (bf16[1024,256]{1,0:T(8,128)(2,1)S(1)}, bf16[1024,256]{1,0:T(8,128)(2,1)}, u32[]{:S(2)}) copy-start(bf16[1024,256]{1,0:T(8,128)(2,1)} %get-tuple-element.78.tx_ref) | copy-start | bytes 1572868
  90.2 4.9 %collective-permute-start.10 = (bf16[512,896]{1,0:T(8,128)(2,1)S(1)}, bf16[512,896]{1,0:T(8,128)(2,1)S(1)}, u32[]{:S(2)}, u32[]{:S(2)}) collective-permute-start(bf16[512,896]{1,0:T(8,128)(2,1)S(1)} %bitcast.16), channel_id=1, source_target_pairs={{0,16},{16,0},{1,17},{17,1},{2,18},{18,2},{3,19},{19,3},{4,20},{20... | collective-permute-start | bytes 2752520 | tf_op jit(solution)/shard_map/ppermute | solution.py:408

commit v9 on v8

--- a/solution.py
+++ b/solution.py
@@ -79,10 +79,10 @@
 
 
 def project_kernel(z_ref, rows_hbm, dout_hbm, decay_hbm, w_up_hbm, w_in_hbm, w_out_hbm,
-                   proj_ref, dy_ref, cum_ref, cumt_ref, g0_ref, g1_ref, g2_ref, g3_ref,
-                   rows_ref, dout_ref, decay_ref, w_up_ref, w_in_ref, w_out_ref, all_ref, sems):
+                   u_ref, c_ref, dy_ref, cum_ref, cumt_ref, g0_ref, g1_ref, g2_ref, g3_ref,
+                   rows_ref, dout_ref, decay_ref, w_up_ref, w_c_ref, w_out_ref, all_ref, sems):
     pairs = (
-        (rows_hbm, rows_ref), (w_up_hbm, w_up_ref), (w_in_hbm, w_in_ref),
+        (rows_hbm, rows_ref), (w_up_hbm, w_up_ref), (w_in_hbm.at[:, INNER + N :], w_c_ref),
         (dout_hbm, dout_ref), (w_out_hbm, w_out_ref), (decay_hbm, decay_ref),
     )
     copies = [pltpu.make_async_copy(a, b, sems.at[i]) for i, (a, b) in enumerate(pairs)]
@@ -90,9 +90,9 @@
         copy.start()
     copies[0].wait()
     copies[1].wait()
-    u = dot(rows_ref[...], w_up_ref[...]).astype(BF)
+    u_ref[...] = dot(rows_ref[...], w_up_ref[...]).astype(BF)
     copies[2].wait()
-    proj_ref[...] = dot(u, w_in_ref[...]).astype(BF)
+    c_ref[...] = dot(u_ref[...], w_c_ref[...]).astype(BF)
     copies[3].wait()
     copies[4].wait()
     dy_ref[...] = dot(w_out_ref[...], dout_ref[...], NT).astype(BF)
@@ -106,7 +106,6 @@
     cum_ref[...] = cum
     cumt_ref[...] = sum(dot(lower, p, NT) for p in logs)
     start = jnp.exp(cum)
-    c_nat = proj_ref[:, INNER + N :]
     scaled = jnp.concatenate(
         [
             (dy_ref[h * HP : (h + 1) * HP, :].astype(F32) * (SC * start[h : h + 1, :])).astype(BF)
@@ -114,7 +113,7 @@
         ],
         axis=0,
     )
-    sums = dot(scaled, c_nat).astype(BF)
+    sums = dot(scaled, c_ref[...]).astype(BF)
     amount = jnp.exp(cum[:, T - 1 : T])
     for q in range(H // GH):
         all_ref[q, :GR, :] = sums[q * GR : (q + 1) * GR, :]
@@ -158,13 +157,14 @@
         ref[...] = ct_ref[(z + k) & 3]
 
 
-def local_kernel(proj_ref, dy_ref, cum_ref, cumt_ref, h0_ref, dout_ref, skip_ref, core_ref,
-                 keep_ref, give_ref, dx_ref, tx_ref, bt_ref, dbt_ref, dct_ref, extra_ref, y_ref, sdy_ref, h0t_ref, sum_ref):
-    proj_t = jnp.transpose(proj_ref[...])
-    bt = proj_t[INNER : INNER + N, :]
-    ct = proj_t[INNER + N :, :]
-    b_nat = proj_ref[:, INNER : INNER + N]
-    c_nat = proj_ref[:, INNER + N :]
+def local_kernel(u_ref, c_ref, w_in_ref, dy_ref, cum_ref, cumt_ref, h0_ref, dout_ref, skip_ref, core_ref,
+                 keep_ref, give_ref, dx_ref, tx_ref, bt_ref, dbt_ref, dct_ref, extra_ref, x_ref, y_ref, sdy_ref, h0t_ref, sum_ref):
+    x_ref[...] = dot(u_ref[...], w_in_ref[:, : INNER + N]).astype(BF)
+    proj_t = jnp.transpose(x_ref[...])
+    bt = proj_t[INNER:, :]
+    c_nat = c_ref[...]
+    ct = jnp.transpose(c_nat)
+    b_nat = x_ref[:, INNER:]
     pair = (SC * DT) * dot(b_nat, c_nat, NT)
     r = lax.broadcasted_iota(jnp.int32, (N, N), 0)
     c = lax.broadcasted_iota(jnp.int32, (N, N), 1)
@@ -205,7 +205,7 @@
         dx_ref[lo:hi, :] = dot(dy_h, weights, NT) + skip * dy_f
         sdy_ref[lo:hi, :] = (st * dy_f).astype(BF)
         tx_ref[lo:hi, :] = (tail[h : h + 1, :] * x_f).astype(BF)
-        x_pair = proj_ref[:, (h // 2) * N : (h // 2 + 1) * N]
+        x_pair = x_ref[:, (h // 2) * N : (h // 2 + 1) * N]
         dy_z = jnp.concatenate([dy_h, zrow] if h % 2 == 0 else [zrow, dy_h], axis=0)
         q0 = dot(x_pair[:N, :], dy_z)
         q11 = dot(x_pair[N:, :], dy_z[:, N:])
@@ -283,7 +283,8 @@
     out_ref[:, E : 2 * E] = misc.astype(BF)
 
 
-def pair_kernel(keep_ref, got_ref, out_ref):
+def pair_kernel(keep_ref, got_ref, tx_ref, out_ref, tx_out_ref):
+    tx_out_ref[...] = tx_ref[...]
     total = (keep_ref[...] + got_ref[...].astype(F32)).astype(BF)
     out_ref[: INNER // 2, :] = total[:, :E]
     out_ref[INNER // 2 :, :] = total[:, E:]
@@ -350,14 +351,14 @@
     every = ("x", "core", "y", "z")
     rows, d_out = event_rows[0], dout[0]
     core, y, z = (lax.axis_index(a).reshape(1) for a in ("core", "y", "z"))
-    proj, dy, cum, cumt, *sums = call(
+    u, c_nat, dy, cum, cumt, *sums = call(
         project_kernel,
-        [((T, PROJ), BF), ((INNER, T), BF), ((H, T), F32), ((T, H), F32)] + [((MR, N), BF)] * 4,
+        [((T, D), BF), ((T, N), BF), ((INNER, T), BF), ((H, T), F32), ((T, H), F32)] + [((MR, N), BF)] * 4,
         BIG, 750_000_000, 4_500_000,
-        in_specs=[SM] + [HBM] * 6, out_specs=(VM,) * 8,
+        in_specs=[SM] + [HBM] * 6, out_specs=(VM,) * 9,
         scratch_shapes=[
             pltpu.VMEM((T, E), BF), pltpu.VMEM((T, D), BF), pltpu.VMEM((H, T), F32),
-            pltpu.VMEM((E, D), BF), pltpu.VMEM((D, PROJ), BF), pltpu.VMEM((INNER, D), BF),
+            pltpu.VMEM((E, D), BF), pltpu.VMEM((D, N), BF), pltpu.VMEM((INNER, D), BF),
             pltpu.VMEM((4, MR, N), BF), pltpu.SemaphoreType.DMA((6,)),
         ],
     )(z, rows, d_out, decay[0], w_up, w_in, w_out)
@@ -367,12 +368,13 @@
         [((INNER // 2, D), F32), ((INNER // 2, D), BF), ((INNER, T), F32), ((INNER, T), BF), ((N, T), BF),
          ((N, T), F32), ((N, T), BF), ((1, T), F32)],
         BIG, 2_500_000_000, 6_000_000,
-        in_specs=[VM] * 6 + [SM] * 2, out_specs=(VM,) * 8,
+        in_specs=[VM] * 8 + [SM] * 2, out_specs=(VM,) * 8,
         scratch_shapes=[
+            pltpu.VMEM((T, INNER + N), BF),
             pltpu.VMEM((INNER, T), F32), pltpu.VMEM((INNER, T), BF),
             pltpu.VMEM((INNER, N), BF), pltpu.VMEM((T, T), BF),
         ],
-    )(proj, dy, cum, cumt, jnp.swapaxes(saved_state[0, 0], 1, 2).reshape(INNER, N), d_out, skip, core)
+    )(u, c_nat, w_in, dy, cum, cumt, jnp.swapaxes(saved_state[0, 0], 1, 2).reshape(INNER, N), d_out, skip, core)
     sums, give = lax.optimization_barrier((sums, give))
     (total,) = call(
         inner_kernel, [((MR, N), BF)], 8, 2_000_000, 400_000,
@@ -390,9 +392,9 @@
         scratch_shapes=[pltpu.VMEM((4, MR, N), BF)] * 2 + [pltpu.VMEM((4, GR, N), BF)],
     )(y, z, *sums, *totals)
     carries = [carries[0]] + [hop(v, "z", k + 1) for k, v in enumerate(carries[1:])]
-    (outer,) = call(
-        pair_kernel, [((8 * DEV, E), BF)], 8, 300_000, 2_000_000, in_specs=[VM] * 2, out_specs=(VM,)
-    )(keep, lax.ppermute(give, "core", [(0, 1), (1, 0)]))
+    outer, tx = call(
+        pair_kernel, [((8 * DEV, E), BF), ((INNER, T), BF)], 8, 300_000, 3_000_000, in_specs=[VM] * 3, out_specs=(VM,) * 2
+    )(keep, lax.ppermute(give, "core", [(0, 1), (1, 0)]), tx)
     carries, outer = lax.optimization_barrier((carries, outer))
     (pay,) = call(
         finish_kernel, [((8 * DEV, 3 * E), BF)], 36, 1_400_000_000, 6_000_000,

time: 99.4 us -> 98.6 us (level)
  waiting for transfers between devices: 7.34 us -> 6.22 us
    ppermute x9, waiting for transfers between devices: 7.3 us -> 6.18 us  [hop(): return lax.ppermute(value, axis, [(i, (i + step) % 4) for i in range(4)])]
  transfers between devices with their start and end apart: 11 -> 11, of which waited for: 5 -> 4; matrix products, arithmetic and copies ran while one was open for 1% -> 1% of each run, Pallas kernels for 8% -> 9%
where the time goes in v9:
time: 98.6 us; the launch traced here: 98.3 us
  blocking collectives  52.1 us (53%)
  Pallas kernels  18.7 us (19%)
  starting transfers between devices  18.1 us (18%)
  waiting for transfers between devices  6.22 us (6%)
  local copies, waits for them, and re-layouts  1.78 us (2%)
    all_to_all x1, blocking collectives, local(): lax.all_to_all(pay.reshape(DEV, 8, 3 * E), every, 0, 0, tiled=True)  31.6 us
    all_to_all x1, blocking collectives, local(): lax.all_to_all(chunk, ('x', 'y', 'z'), 0, 0, tiled=True)  20.4 us
    ppermute x9, starting transfers between devices, hop(): return lax.ppermute(value, axis, [(i, (i + step) % 4) for i in range(4)])  13.7 us
    ppermute x9, waiting for transfers between devices, hop(): return lax.ppermute(value, axis, [(i, (i + step) % 4) for i in range(4)])  6.18 us
    pallas_call x1, Pallas kernels, local(): call(local_kernel, [((INNER // 2, D), F32), ((INNER // 2, D), BF), ((INNE...  6.07 us
    pallas_call x1, Pallas kernels, local(): pl.pallas_call(last_kernel, grid=(4,), out_shape=tuple((jax.ShapeDtypeStr...  3.98 us
    pallas_call x1, Pallas kernels, local(): call(project_kernel, [((T, D), BF), ((T, N), BF), ((INNER, T), BF), ((H,...  3.74 us
    ppermute x1, starting transfers between devices, local(): other = lax.ppermute(whole, 'core', [(0, 1), (1, 0)])  2.83 us
  transfers between devices with their start and end apart: 11, of which 4 were waited for; matrix products, arithmetic and copies ran while one was open for 1% of the time, Pallas kernels for 9%

profile of v9, /device:TPU:1, one launch (start us, length us, event | category | flops | bytes accessed | tf_op | source)
XLA Modules:
  0.0 98.3 jit_solution(8548070399539061361)
XLA Ops:
  0.6 3.7 %shard_map.128 = (bf16[256,512]{1,0:T(8,128)(2,1)}, bf16[256,128]{1,0:T(8,128)(2,1)}, bf16[1024,256]{1,0:T(8,128)(2,1)}, f32[16,256]{1,0:T(8,128)}, f32[256,16]{...) custom-call(s32[1]{0:T(128)} %bitcast.1.z_ref, ...), custom_call_target="tpu_custom_call" | custom-call | flops 750000000 | bytes 4500000 | tf_op jit(solution)/shard_map/pallas_call | solution.py:354
  4.4 2.5 %collective-permute-start = (bf16[272,128]{1,0:T(8,128)(2,1)}, bf16[272,128]{1,0:T(8,128)(2,1)S(1)}, u32[]{:S(2)}, u32[]{:S(2)}) collective-permute-start(bf16[272,128]{1,0:T(8,128)(2,1)} %get-tuple-element.51), channel_id=1, source_target_pairs={{0,1},{1,2},{2,3},{3,0},{4,5},{5,6},{6,7},{7,4},{8,9},{9,10},{10,1... | collective-permute-start | bytes 208904 | tf_op jit(solution)/shard_map/ppermute | solution.py:347
  6.9 3.3 %collective-permute-start.1 = (bf16[272,128]{1,0:T(8,128)(2,1)}, bf16[272,128]{1,0:T(8,128)(2,1)S(1)}, u32[]{:S(2)}, u32[]{:S(2)}) collective-permute-start(bf16[272,128]{1,0:T(8,128)(2,1)} %get-tuple-element.52), channel_id=1, source_target_pairs={{0,2},{1,3},{2,0},{3,1},{4,6},{5,7},{6,4},{7,5},{8,10},{9,11},{10,... | collective-permute-start | bytes 208904 | tf_op jit(solution)/shard_map/ppermute | solution.py:347
  10.2 0.7 collective-permute-start.2
  11.0 6.1 %shard_map.129 = (f32[512,512]{1,0:T(8,128)}, bf16[512,512]{1,0:T(8,128)(2,1)}, f32[1024,256]{1,0:T(8,128)}, bf16[1024,256]{1,0:T(8,128)(2,1)}, bf16[128,256]{1,...) custom-call(bf16[256,512]{1,0:T(8,128)(2,1)} %get-tuple-element.54.u_ref, ...), custom_call_target="tpu_custom_call" | custom-call | flops 2500000000 | bytes 6000000 | tf_op jit(solution)/shard_map/pallas_call | solution.py:366
  17.1 1.6 %collective-permute-start.9 = (bf16[512,512]{1,0:T(8,128)(2,1)}, bf16[512,512]{1,0:T(8,128)(2,1)S(1)}, u32[]{:S(2)}, u32[]{:S(2)}) collective-permute-start(bf16[512,512]{1,0:T(8,128)(2,1)} %get-tuple-element.75), channel_id=1, source_target_pairs={{0,16},{16,0},{1,17},{17,1},{2,18},{18,2},{3,19},{19,3},{4,20},{20... | collective-permute-start | bytes 1572872 | tf_op jit(solution)/shard_map/ppermute | solution.py:397
  18.8 2.8 %collective-permute-start.5 = (bf16[272,128]{1,0:T(8,128)(2,1)S(1)}, bf16[272,128]{1,0:T(8,128)(2,1)S(1)}, u32[]{:S(2)}, u32[]{:S(2)}) collective-permute-start(bf16[272,128]{1,0:T(8,128)(2,1)S(1)} %shard_map.130.ta_ref), channel_id=1, source_target_pairs={{0,12},{4,0},{8,4},{12,8},{1,13},{5,1},{9,5},{13,9},{2,14},{6,2},{... | collective-permute-start | bytes 208904 | tf_op jit(solution)/shard_map/ppermute | solution.py:347
  21.9 0.7 collective-permute-start.3
  22.6 0.7 copy-done.12
  23.3 0.6 shard_map.131
  24.0 2.3 %collective-permute-done.4.tc_ref = bf16[272,128]{1,0:T(8,128)(2,1)S(1)} collective-permute-done((bf16[272,128]{1,0:T(8,128)(2,1)S(1)}, bf16[272,128]{1,0:T(8,128)(2,1)S(1)}, u32[]{:S(2)}, u32[]{:S(2)}) %collective-permute-start.4) | collective-permute-done | bytes 69664 | tf_op jit(solution)/shard_map/ppermute | solution.py:347
  26.3 2.3 %collective-permute-done.3.tb_ref = bf16[272,128]{1,0:T(8,128)(2,1)S(1)} collective-permute-done((bf16[272,128]{1,0:T(8,128)(2,1)S(1)}, bf16[272,128]{1,0:T(8,128)(2,1)S(1)}, u32[]{:S(2)}, u32[]{:S(2)}) %collective-permute-start.3) | collective-permute-done | bytes 69664 | tf_op jit(solution)/shard_map/ppermute | solution.py:347
  28.8 0.8 collective-permute-start.6
  29.7 2.3 %collective-permute-start.8 = (bf16[256,128]{1,0:T(8,128)(2,1)S(1)}, bf16[256,128]{1,0:T(8,128)(2,1)S(1)}, u32[]{:S(2)}, u32[]{:S(2)}) collective-permute-start(bf16[256,128]{1,0:T(8,128)(2,1)S(1)} %get-tuple-element.73), channel_id=1, source_target_pairs={{0,3},{1,0},{2,1},{3,2},{4,7},{5,4},{6,5},{7,6},{8,11},{9,8},{10,9... | collective-permute-start | bytes 196616 | tf_op jit(solution)/shard_map/ppermute | solution.py:347
  32.1 1.0 %copy-done.5 = bf16[1024,256]{1,0:T(8,128)(2,1)S(1)} copy-done((bf16[1024,256]{1,0:T(8,128)(2,1)S(1)}, bf16[1024,256]{1,0:T(8,128)(2,1)}, u32[]{:S(2)}) %copy-start.5) | copy-done | bytes 524312
  33.3 1.0 %collective-permute-done.7.c2_ref = bf16[256,128]{1,0:T(8,128)(2,1)S(1)} collective-permute-done((bf16[256,128]{1,0:T(8,128)(2,1)S(1)}, bf16[256,128]{1,0:T(8,128)(2,1)S(1)}, u32[]{:S(2)}, u32[]{:S(2)}) %collective-permute-start.7) | collective-permute-done | bytes 65568 | tf_op jit(solution)/shard_map/ppermute | solution.py:347
  34.3 0.5 collective-permute-done.8.c3_ref
  34.9 2.1 %shard_map.134 = bf16[1024,768]{1,0:T(8,128)(2,1)S(1)} custom-call(s32[1]{0:T(128)} %bitcast.1.z_ref, bf16[256,128]{1,0:T(8,128)(2,1)S(1)} %get-tuple-element.78.c0_ref, bf16[256,128]{1,0:T(8,128)(2,1)S(1)} %collective-permute-done.6.c1_ref, bf16[256,128]{1,0:T(8,128)(2,1)S(1)} %collective-permute-done.7.c2_ref, ...), custom_call_target="tpu_custom_call" | custom-call | flops 1400000000 | bytes 6000000 | tf_op jit(solution)/shard_map/pallas_call | solution.py:399
  37.0 31.6 %all_to_all.10.got_ref = bf16[128,8,768]{2,1,0:T(8,128)(2,1)S(1)} all-to-all(bf16[128,8,768]{2,1,0:T(8,128)(2,1)S(1)} %bitcast.15), channel_id=1, replica_groups=mesh['x'=4,'core'=2,'y'=4,'z'=4] {'x','core','y','z'}, dimensions={0} | all-to-all | bytes 3145728 | tf_op jit(solution)/shard_map/all_to_all | solution.py:404
  68.9 20.4 %all_to_all.11 = bf16[64,8,896]{2,1,0:T(8,128)(2,1)S(1)} all-to-all(bf16[64,8,896]{2,1,0:T(8,128)(2,1)S(1)} %get-tuple-element.90), channel_id=1, replica_groups=mesh['x'=4,'core'=2,'y'=4,'z'=4] {'x','y','z'}, dimensions={0} | all-to-all | bytes 1835008 | tf_op jit(solution)/shard_map/all_to_all | solution.py:409
  89.4 2.8 %collective-permute-start.10 = (bf16[512,896]{1,0:T(8,128)(2,1)S(1)}, bf16[512,896]{1,0:T(8,128)(2,1)S(1)}, u32[]{:S(2)}, u32[]{:S(2)}) collective-permute-start(bf16[512,896]{1,0:T(8,128)(2,1)S(1)} %bitcast.16), channel_id=1, source_target_pairs={{0,16},{16,0},{1,17},{17,1},{2,18},{18,2},{3,19},{19,3},{4,20},{20... | collective-permute-start | bytes 2752520 | tf_op jit(solution)/shard_map/ppermute | solution.py:410
  92.2 1.5 %shard_map.137 = f32[512,256]{1,0:T(8,128)} custom-call(bf16[128,8,768]{2,1,0:T(8,128)(2,1)S(1)} %all_to_all.10.got_ref), custom_call_target="tpu_custom_call" | custom-call | flops 400000000 | bytes 2000000 | tf_op jit(solution)/shard_map/pallas_call | solution.py:411
  93.7 0.6 add_bitcast_fusion
  94.3 4.0 %shard_map.136 = (f32[256,512]{1,0:T(8,128)}, f32[512,1280]{1,0:T(8,128)}, f32[1024,512]{1,0:T(8,128)}) custom-call(s32[1]{0:T(128)} %bitcast.core_ref, bf16[512,896]{1,0:T(8,128)(2,1)S(1)} %bitcast.17, bf16[512,896]{1,0:T(8,128)(2,1)S(1)} %collective-permute-done.10.other_ref, bf16[256,512]{1,0:T(8,128)(2,1)S(1)} %copy-done.1, bf16[512,1280]{1,0:T(8,128)(2,1)S(1)} %copy-done), custom_call_target="tpu_custom_call" | custom-call | flops 700000000 | bytes 8000000 | tf_op jit(solution)/shard_map/pallas_call | solution.py:416
  (37 shorter events, 1.3 us)
Async XLA Ops:
  4.4 12.7 %collective-permute-start = (bf16[272,128]{1,0:T(8,128)(2,1)}, bf16[272,128]{1,0:T(8,128)(2,1)S(1)}, u32[]{:S(2)}, u32[]{:S(2)}) collective-permute-start(bf16[272,128]{1,0:T(8,128)(2,1)} %get-tuple-element.51), channel_id=1, source_target_pairs={{0,1},{1,2},{2,3},{3,0},{4,5},{5,6},{6,7},{7,4},{8,9},{9,10},{10,1... | collective-permute-start | bytes 208904 | tf_op jit(solution)/shard_map/ppermute | solution.py:347
  6.9 10.1 %collective-permute-start.1 = (bf16[272,128]{1,0:T(8,128)(2,1)}, bf16[272,128]{1,0:T(8,128)(2,1)S(1)}, u32[]{:S(2)}, u32[]{:S(2)}) collective-permute-start(bf16[272,128]{1,0:T(8,128)(2,1)} %get-tuple-element.52), channel_id=1, source_target_pairs={{0,2},{1,3},{2,0},{3,1},{4,6},{5,7},{6,4},{7,5},{8,10},{9,11},{10,... | collective-permute-start | bytes 208904 | tf_op jit(solution)/shard_map/ppermute | solution.py:347
  10.2 6.8 %collective-permute-start.2 = (bf16[272,128]{1,0:T(8,128)(2,1)}, bf16[272,128]{1,0:T(8,128)(2,1)S(1)}, u32[]{:S(2)}, u32[]{:S(2)}) collective-permute-start(bf16[272,128]{1,0:T(8,128)(2,1)} %get-tuple-element.53), channel_id=1, source_target_pairs={{0,3},{1,0},{2,1},{3,2},{4,7},{5,4},{6,5},{7,6},{8,11},{9,8},{10,9... | collective-permute-start | bytes 208904 | tf_op jit(solution)/shard_map/ppermute | solution.py:347
  11.0 7.7 %copy-start.6 = (bf16[272,128]{1,0:T(8,128)(2,1)S(1)}, bf16[272,128]{1,0:T(8,128)(2,1)}, u32[]{:S(2)}) copy-start(bf16[272,128]{1,0:T(8,128)(2,1)} %get-tuple-element.60.a_ref) | copy-start | bytes 208900
  11.0 11.7 %copy-start.11 = (s32[1,256]{1,0:T(1,128)S(1)}, s32[1,256]{1,0:T(1,128)}, u32[]{:S(2)}) copy-start(s32[1,256]{1,0:T(1,128)} %index_ref.1) | copy-start | bytes 3076
  17.0 15.0 %copy-start.2 = (f32[512,512]{1,0:T(8,128)S(1)}, f32[512,512]{1,0:T(8,128)}, u32[]{:S(2)}) copy-start(f32[512,512]{1,0:T(8,128)} %get-tuple-element.74.keep_ref) | copy-start | bytes 3145732
  17.1 15.0 %collective-permute-start.9 = (bf16[512,512]{1,0:T(8,128)(2,1)}, bf16[512,512]{1,0:T(8,128)(2,1)S(1)}, u32[]{:S(2)}, u32[]{:S(2)}) collective-permute-start(bf16[512,512]{1,0:T(8,128)(2,1)} %get-tuple-element.75), channel_id=1, source_target_pairs={{0,16},{16,0},{1,17},{17,1},{2,18},{18,2},{3,19},{19,3},{4,20},{20... | collective-permute-start | bytes 1572872 | tf_op jit(solution)/shard_map/ppermute | solution.py:397
  18.8 5.2 %collective-permute-start.5 = (bf16[272,128]{1,0:T(8,128)(2,1)S(1)}, bf16[272,128]{1,0:T(8,128)(2,1)S(1)}, u32[]{:S(2)}, u32[]{:S(2)}) collective-permute-start(bf16[272,128]{1,0:T(8,128)(2,1)S(1)} %shard_map.130.ta_ref), channel_id=1, source_target_pairs={{0,12},{4,0},{8,4},{12,8},{1,13},{5,1},{9,5},{13,9},{2,14},{6,2},{... | collective-permute-start | bytes 208904 | tf_op jit(solution)/shard_map/ppermute | solution.py:347
  21.6 4.7 %collective-permute-start.4 = (bf16[272,128]{1,0:T(8,128)(2,1)S(1)}, bf16[272,128]{1,0:T(8,128)(2,1)S(1)}, u32[]{:S(2)}, u32[]{:S(2)}) collective-permute-start(bf16[272,128]{1,0:T(8,128)(2,1)S(1)} %shard_map.130.ta_ref), channel_id=1, source_target_pairs={{0,8},{4,12},{8,0},{12,4},{1,9},{5,13},{9,1},{13,5},{2,10},{6,14},... | collective-permute-start | bytes 208904 | tf_op jit(solution)/shard_map/ppermute | solution.py:347
  21.9 6.7 %collective-permute-start.3 = (bf16[272,128]{1,0:T(8,128)(2,1)S(1)}, bf16[272,128]{1,0:T(8,128)(2,1)S(1)}, u32[]{:S(2)}, u32[]{:S(2)}) collective-permute-start(bf16[272,128]{1,0:T(8,128)(2,1)S(1)} %shard_map.130.ta_ref), channel_id=1, source_target_pairs={{0,4},{4,8},{8,12},{12,0},{1,5},{5,9},{9,13},{13,1},{2,6},{6,10},{... | collective-permute-start | bytes 208904 | tf_op jit(solution)/shard_map/ppermute | solution.py:347
  22.6 0.7 copy-start.12
  23.3 11.5 %copy-start.4 = (bf16[1,256,256]{2,1,0:T(8,128)(2,1)S(1)}, bf16[1,256,256]{2,1,0:T(8,128)(2,1)}, u32[]{:S(2)}) copy-start(bf16[1,256,256]{2,1,0:T(8,128)(2,1)} %param.9) | copy-start | bytes 393220
  23.3 11.5 %copy-start.7 = (f32[128,256]{1,0:T(8,128)S(1)}, f32[128,256]{1,0:T(8,128)}, u32[]{:S(2)}) copy-start(f32[128,256]{1,0:T(8,128)} %get-tuple-element.85.dbt_ref) | copy-start | bytes 393220
  23.3 11.5 %copy-start.8 = (bf16[128,256]{1,0:T(8,128)(2,1)S(1)}, bf16[128,256]{1,0:T(8,128)(2,1)}, u32[]{:S(2)}) copy-start(bf16[128,256]{1,0:T(8,128)(2,1)} %get-tuple-element.83.bt_ref) | copy-start | bytes 196612
  23.3 11.5 %copy-start.9 = (bf16[128,256]{1,0:T(8,128)(2,1)S(1)}, bf16[128,256]{1,0:T(8,128)(2,1)}, u32[]{:S(2)}) copy-start(bf16[128,256]{1,0:T(8,128)(2,1)} %get-tuple-element.86.dct_ref) | copy-start | bytes 196612
  23.3 11.5 %copy-start.10 = (f32[16,256]{1,0:T(8,128)S(1)}, f32[16,256]{1,0:T(8,128)}, u32[]{:S(2)}) copy-start(f32[16,256]{1,0:T(8,128)} %get-tuple-element.57.cum_ref) | copy-start | bytes 49156
  23.9 10.9 %copy-start = (bf16[512,1280]{1,0:T(8,128)(2,1)S(1)}, bf16[512,1280]{1,0:T(8,128)(2,1)}, u32[]{:S(2)}) copy-start(bf16[512,1280]{1,0:T(8,128)(2,1)} %w_in_ref.5) | copy-start | bytes 3932164
  23.9 10.9 %copy-start.1 = (bf16[256,512]{1,0:T(8,128)(2,1)S(1)}, bf16[256,512]{1,0:T(8,128)(2,1)}, u32[]{:S(2)}) copy-start(bf16[256,512]{1,0:T(8,128)(2,1)} %w_up_ref.3) | copy-start | bytes 786436
  24.0 10.9 %copy-start.3 = (f32[1024,256]{1,0:T(8,128)S(1)}, f32[1024,256]{1,0:T(8,128)}, u32[]{:S(2)}) copy-start(f32[1024,256]{1,0:T(8,128)} %get-tuple-element.89.dx_ref) | copy-start | bytes 3145732
  28.8 4.5 %collective-permute-start.6 = (bf16[256,128]{1,0:T(8,128)(2,1)S(1)}, bf16[256,128]{1,0:T(8,128)(2,1)S(1)}, u32[]{:S(2)}, u32[]{:S(2)}) collective-permute-start(bf16[256,128]{1,0:T(8,128)(2,1)S(1)} %get-tuple-element.71), channel_id=1, source_target_pairs={{0,1},{1,2},{2,3},{3,0},{4,5},{5,6},{6,7},{7,4},{8,9},{9,10},{10,1... | collective-permute-start | bytes 196616 | tf_op jit(solution)/shard_map/ppermute | solution.py:347
  29.6 4.7 %collective-permute-start.7 = (bf16[256,128]{1,0:T(8,128)(2,1)S(1)}, bf16[256,128]{1,0:T(8,128)(2,1)S(1)}, u32[]{:S(2)}, u32[]{:S(2)}) collective-permute-start(bf16[256,128]{1,0:T(8,128)(2,1)S(1)} %get-tuple-element.72), channel_id=1, source_target_pairs={{0,2},{1,3},{2,0},{3,1},{4,6},{5,7},{6,4},{7,5},{8,10},{9,11},{10,... | collective-permute-start | bytes 196616 | tf_op jit(solution)/shard_map/ppermute | solution.py:347
  29.7 5.1 %collective-permute-start.8 = (bf16[256,128]{1,0:T(8,128)(2,1)S(1)}, bf16[256,128]{1,0:T(8,128)(2,1)S(1)}, u32[]{:S(2)}, u32[]{:S(2)}) collective-permute-start(bf16[256,128]{1,0:T(8,128)(2,1)S(1)} %get-tuple-element.73), channel_id=1, source_target_pairs={{0,3},{1,0},{2,1},{3,2},{4,7},{5,4},{6,5},{7,6},{8,11},{9,8},{10,9... | collective-permute-start | bytes 196616 | tf_op jit(solution)/shard_map/ppermute | solution.py:347
  32.1 1.0 %copy-start.5 = (bf16[1024,256]{1,0:T(8,128)(2,1)S(1)}, bf16[1024,256]{1,0:T(8,128)(2,1)}, u32[]{:S(2)}) copy-start(bf16[1024,256]{1,0:T(8,128)(2,1)} %get-tuple-element.76.tx_ref) | copy-start | bytes 1572868
  89.4 4.9 %collective-permute-start.10 = (bf16[512,896]{1,0:T(8,128)(2,1)S(1)}, bf16[512,896]{1,0:T(8,128)(2,1)S(1)}, u32[]{:S(2)}, u32[]{:S(2)}) collective-permute-start(bf16[512,896]{1,0:T(8,128)(2,1)S(1)} %bitcast.16), channel_id=1, source_target_pairs={{0,16},{16,0},{1,17},{17,1},{2,18},{18,2},{3,19},{19,3},{4,20},{20... | collective-permute-start | bytes 2752520 | tf_op jit(solution)/shard_map/ppermute | solution.py:410

commit v10 on v9

--- a/solution.py
+++ b/solution.py
@@ -313,34 +313,49 @@
     table_ref[...] = dot(hits, misc.reshape(DEV * 8, E), TN)
 
 
-def last_kernel(core_ref, own_ref, other_ref, w_up_ref, w_in_ref, up_ref, in_ref, go_ref, g_ref, side_ref):
+def last_kernel(core_ref, own_ref, other_ref, w_up_ref, w_in_ref, up_ref, in_ref, go_ref, g_ref, side_ref, acc_ref):
     step = pl.program_id(0)
     core = core_ref[0]
     sources = ((core, own_ref), (1 - core, other_ref))
 
-    @pl.when(step == 0)
+    @pl.when(step < 4)
+    def _():
+        for at, ref in sources:
+            g_ref[pl.ds(pl.multiple_of(at * N, N), N), :] = ref[pl.ds(pl.multiple_of(step * N, N), N), :E]
+        lanes = pl.ds(pl.multiple_of(E + N + E * lax.shift_right_logical(step, 1), N), E)
+        for m in range(2):
+            rows = pl.ds(pl.multiple_of((2 * m + (step & 1)) * N, N), N)
+            for at, ref in sources:
+                go_ref[pl.ds(pl.multiple_of(at * N, N), N), m * E : (m + 1) * E] = ref[rows, lanes].astype(F32)
+
+    @pl.when(step == 4)
     def _():
         for x in range(4):
             for at, ref in sources:
                 rows = pl.ds(pl.multiple_of((2 * x + at) * N, N), N)
-                g_ref[rows, :] = ref[x * N : (x + 1) * N, :E]
                 side_ref[rows, :] = ref[x * N : (x + 1) * N, E : E + N]
         j = lax.broadcasted_iota(jnp.int32, (2 * N, 8 * DEV), 0)
         r = lax.broadcasted_iota(jnp.int32, (2 * N, 8 * DEV), 1)
         first = r - (8 * lax.shift_right_logical(j, 1) + (j & 1))
         for m in range(2):
             pick = jnp.where(first == 2 * m, 1.0, 0.0).astype(BF)
-            g_ref[INNER:, m * N : (m + 1) * N] = dot(pick, side_ref[...]).astype(BF)
+            g_ref[:, m * N : (m + 1) * N] = dot(pick, side_ref[...]).astype(BF)
 
     g = g_ref[...]
-    part = pl.ds(pl.multiple_of(step * N, N), N)
-    in_ref[...] = lax.dot_general(w_up_ref[:, part], g, (((0,), (1,)), ((), ())), preferred_element_type=F32)
-    up_ref[...] = jnp.transpose(dot(w_in_ref[part, :], g))
-    lanes = pl.ds(pl.multiple_of(E + N + E * lax.shift_right_logical(step, 1), N), E)
-    for m in range(2):
-        rows = pl.ds(pl.multiple_of((2 * m + (step & 1)) * N, N), N)
-        for at, ref in sources:
-            go_ref[pl.ds(pl.multiple_of(at * N, N), N), m * E : (m + 1) * E] = ref[rows, lanes].astype(F32)
+    in_ref[...] = lax.dot_general(w_up_ref[...], g, (((0,), (1,)), ((), ())), preferred_element_type=F32)
+    part = dot(w_in_ref[:, pl.ds(pl.multiple_of(step * E, E), E)], g)
+
+    @pl.when(step == 0)
+    def _():
+        acc_ref[...] = part
+
+    @pl.when((step > 0) & (step < 4))
+    def _():
+        acc_ref[...] += part
+
+    @pl.when(step == 4)
+    def _():
+        up_ref[...] = jnp.transpose(acc_ref[...] + part)
 
 
 def hop(value, axis, step):
@@ -411,15 +426,17 @@
     (table,) = call(
         table_kernel, [((ROWS_DEV, E), F32)], 12, 400_000_000, 2_000_000, in_specs=[VM], out_specs=(VM,)
     )(pay_got)
-    column = pl.BlockSpec((E, D // 4), lambda i: (0, i))
-    row = pl.BlockSpec((D // 4, PROJ), lambda i: (i, 0))
     grad_up, grad_in, grad_out = pl.pallas_call(
         last_kernel,
-        grid=(4,),
+        grid=(5,),
         out_shape=tuple(jax.ShapeDtypeStruct(s, F32) for s in ((E, D), (D, PROJ), (INNER, D))),
         in_specs=[SM] + [VM] * 4,
-        out_specs=(column, row, pl.BlockSpec((INNER // 4, D), lambda i: (i, 0))),
-        scratch_shapes=[pltpu.VMEM((PROJ, E), BF), pltpu.VMEM((8 * DEV, N), BF)],
+        out_specs=(
+            pl.BlockSpec((E, D), lambda i: (0, 0)),
+            pl.BlockSpec((D, E), lambda i: (0, i)),
+            pl.BlockSpec((INNER // 4, D), lambda i: (jnp.minimum(i, 3), 0)),
+        ),
+        scratch_shapes=[pltpu.VMEM((E, E), BF), pltpu.VMEM((8 * DEV, N), BF), pltpu.VMEM((D, E), F32)],
         compiler_params=pltpu.CompilerParams(vmem_limit_bytes=24 * MB),
         cost_estimate=pl.CostEstimate(flops=700_000_000, bytes_accessed=8_000_000, transcendentals=0),
     )(core, whole, other, w_up, w_in)

time: 98.6 us -> 99.5 us (level)
  no operation moved by 1% of the time
where the time goes in v10:
time: 99.5 us; the launch traced here: 99.2 us
  blocking collectives  52.1 us (52%)
  Pallas kernels  19.6 us (20%)
  starting transfers between devices  18.1 us (18%)
  waiting for transfers between devices  6.22 us (6%)
  local copies, waits for them, and re-layouts  1.78 us (2%)
    all_to_all x1, blocking collectives, local(): lax.all_to_all(pay.reshape(DEV, 8, 3 * E), every, 0, 0, tiled=True)  31.6 us
    all_to_all x1, blocking collectives, local(): lax.all_to_all(chunk, ('x', 'y', 'z'), 0, 0, tiled=True)  20.4 us
    ppermute x9, starting transfers between devices, hop(): return lax.ppermute(value, axis, [(i, (i + step) % 4) for i in range(4)])  13.7 us
    ppermute x9, waiting for transfers between devices, hop(): return lax.ppermute(value, axis, [(i, (i + step) % 4) for i in range(4)])  6.18 us
    pallas_call x1, Pallas kernels, local(): call(local_kernel, [((INNER // 2, D), F32), ((INNER // 2, D), BF), ((INNE...  6.07 us
    pallas_call x1, Pallas kernels, local(): pl.pallas_call(last_kernel, grid=(5,), out_shape=tuple((jax.ShapeDtypeStr...  4.92 us
    pallas_call x1, Pallas kernels, local(): call(project_kernel, [((T, D), BF), ((T, N), BF), ((INNER, T), BF), ((H,...  3.74 us
    ppermute x1, starting transfers between devices, local(): other = lax.ppermute(whole, 'core', [(0, 1), (1, 0)])  2.83 us
  transfers between devices with their start and end apart: 11, of which 4 were waited for; matrix products, arithmetic and copies ran while one was open for 1% of the time, Pallas kernels for 9%

profile of v10, /device:TPU:1, one launch (start us, length us, event | category | flops | bytes accessed | tf_op | source)
XLA Modules:
  0.0 99.2 jit_solution(2933837554109401892)
XLA Ops:
  0.6 3.7 %shard_map.128 = (bf16[256,512]{1,0:T(8,128)(2,1)}, bf16[256,128]{1,0:T(8,128)(2,1)}, bf16[1024,256]{1,0:T(8,128)(2,1)}, f32[16,256]{1,0:T(8,128)}, f32[256,16]{...) custom-call(s32[1]{0:T(128)} %bitcast.1.z_ref, ...), custom_call_target="tpu_custom_call" | custom-call | flops 750000000 | bytes 4500000 | tf_op jit(solution)/shard_map/pallas_call | solution.py:369
  4.4 2.5 %collective-permute-start = (bf16[272,128]{1,0:T(8,128)(2,1)}, bf16[272,128]{1,0:T(8,128)(2,1)S(1)}, u32[]{:S(2)}, u32[]{:S(2)}) collective-permute-start(bf16[272,128]{1,0:T(8,128)(2,1)} %get-tuple-element.51), channel_id=1, source_target_pairs={{0,1},{1,2},{2,3},{3,0},{4,5},{5,6},{6,7},{7,4},{8,9},{9,10},{10,1... | collective-permute-start | bytes 208904 | tf_op jit(solution)/shard_map/ppermute | solution.py:362
  6.9 3.3 %collective-permute-start.1 = (bf16[272,128]{1,0:T(8,128)(2,1)}, bf16[272,128]{1,0:T(8,128)(2,1)S(1)}, u32[]{:S(2)}, u32[]{:S(2)}) collective-permute-start(bf16[272,128]{1,0:T(8,128)(2,1)} %get-tuple-element.52), channel_id=1, source_target_pairs={{0,2},{1,3},{2,0},{3,1},{4,6},{5,7},{6,4},{7,5},{8,10},{9,11},{10,... | collective-permute-start | bytes 208904 | tf_op jit(solution)/shard_map/ppermute | solution.py:362
  10.2 0.7 collective-permute-start.2
  11.0 6.1 %shard_map.129 = (f32[512,512]{1,0:T(8,128)}, bf16[512,512]{1,0:T(8,128)(2,1)}, f32[1024,256]{1,0:T(8,128)}, bf16[1024,256]{1,0:T(8,128)(2,1)}, bf16[128,256]{1,...) custom-call(bf16[256,512]{1,0:T(8,128)(2,1)} %get-tuple-element.54.u_ref, ...), custom_call_target="tpu_custom_call" | custom-call | flops 2500000000 | bytes 6000000 | tf_op jit(solution)/shard_map/pallas_call | solution.py:381
  17.1 1.6 %collective-permute-start.9 = (bf16[512,512]{1,0:T(8,128)(2,1)}, bf16[512,512]{1,0:T(8,128)(2,1)S(1)}, u32[]{:S(2)}, u32[]{:S(2)}) collective-permute-start(bf16[512,512]{1,0:T(8,128)(2,1)} %get-tuple-element.75), channel_id=1, source_target_pairs={{0,16},{16,0},{1,17},{17,1},{2,18},{18,2},{3,19},{19,3},{4,20},{20... | collective-permute-start | bytes 1572872 | tf_op jit(solution)/shard_map/ppermute | solution.py:412
  18.8 2.8 %collective-permute-start.5 = (bf16[272,128]{1,0:T(8,128)(2,1)S(1)}, bf16[272,128]{1,0:T(8,128)(2,1)S(1)}, u32[]{:S(2)}, u32[]{:S(2)}) collective-permute-start(bf16[272,128]{1,0:T(8,128)(2,1)S(1)} %shard_map.130.ta_ref), channel_id=1, source_target_pairs={{0,12},{4,0},{8,4},{12,8},{1,13},{5,1},{9,5},{13,9},{2,14},{6,2},{... | collective-permute-start | bytes 208904 | tf_op jit(solution)/shard_map/ppermute | solution.py:362
  21.9 0.7 collective-permute-start.3
  22.6 0.7 copy-done.12
  23.3 0.6 shard_map.131
  24.0 2.3 %collective-permute-done.4.tc_ref = bf16[272,128]{1,0:T(8,128)(2,1)S(1)} collective-permute-done((bf16[272,128]{1,0:T(8,128)(2,1)S(1)}, bf16[272,128]{1,0:T(8,128)(2,1)S(1)}, u32[]{:S(2)}, u32[]{:S(2)}) %collective-permute-start.4) | collective-permute-done | bytes 69664 | tf_op jit(solution)/shard_map/ppermute | solution.py:362
  26.3 2.3 %collective-permute-done.3.tb_ref = bf16[272,128]{1,0:T(8,128)(2,1)S(1)} collective-permute-done((bf16[272,128]{1,0:T(8,128)(2,1)S(1)}, bf16[272,128]{1,0:T(8,128)(2,1)S(1)}, u32[]{:S(2)}, u32[]{:S(2)}) %collective-permute-start.3) | collective-permute-done | bytes 69664 | tf_op jit(solution)/shard_map/ppermute | solution.py:362
  28.8 0.8 collective-permute-start.6
  29.7 2.3 %collective-permute-start.8 = (bf16[256,128]{1,0:T(8,128)(2,1)S(1)}, bf16[256,128]{1,0:T(8,128)(2,1)S(1)}, u32[]{:S(2)}, u32[]{:S(2)}) collective-permute-start(bf16[256,128]{1,0:T(8,128)(2,1)S(1)} %get-tuple-element.73), channel_id=1, source_target_pairs={{0,3},{1,0},{2,1},{3,2},{4,7},{5,4},{6,5},{7,6},{8,11},{9,8},{10,9... | collective-permute-start | bytes 196616 | tf_op jit(solution)/shard_map/ppermute | solution.py:362
  32.1 1.0 %copy-done.5 = bf16[1024,256]{1,0:T(8,128)(2,1)S(1)} copy-done((bf16[1024,256]{1,0:T(8,128)(2,1)S(1)}, bf16[1024,256]{1,0:T(8,128)(2,1)}, u32[]{:S(2)}) %copy-start.5) | copy-done | bytes 524312
  33.3 1.0 %collective-permute-done.7.c2_ref = bf16[256,128]{1,0:T(8,128)(2,1)S(1)} collective-permute-done((bf16[256,128]{1,0:T(8,128)(2,1)S(1)}, bf16[256,128]{1,0:T(8,128)(2,1)S(1)}, u32[]{:S(2)}, u32[]{:S(2)}) %collective-permute-start.7) | collective-permute-done | bytes 65568 | tf_op jit(solution)/shard_map/ppermute | solution.py:362
  34.3 0.5 collective-permute-done.8.c3_ref
  34.9 2.1 %shard_map.134 = bf16[1024,768]{1,0:T(8,128)(2,1)S(1)} custom-call(s32[1]{0:T(128)} %bitcast.1.z_ref, bf16[256,128]{1,0:T(8,128)(2,1)S(1)} %get-tuple-element.78.c0_ref, bf16[256,128]{1,0:T(8,128)(2,1)S(1)} %collective-permute-done.6.c1_ref, bf16[256,128]{1,0:T(8,128)(2,1)S(1)} %collective-permute-done.7.c2_ref, ...), custom_call_target="tpu_custom_call" | custom-call | flops 1400000000 | bytes 6000000 | tf_op jit(solution)/shard_map/pallas_call | solution.py:414
  37.0 31.6 %all_to_all.10.got_ref = bf16[128,8,768]{2,1,0:T(8,128)(2,1)S(1)} all-to-all(bf16[128,8,768]{2,1,0:T(8,128)(2,1)S(1)} %bitcast.15), channel_id=1, replica_groups=mesh['x'=4,'core'=2,'y'=4,'z'=4] {'x','core','y','z'}, dimensions={0} | all-to-all | bytes 3145728 | tf_op jit(solution)/shard_map/all_to_all | solution.py:419
  68.9 20.4 %all_to_all.11 = bf16[64,8,896]{2,1,0:T(8,128)(2,1)S(1)} all-to-all(bf16[64,8,896]{2,1,0:T(8,128)(2,1)S(1)} %get-tuple-element.90), channel_id=1, replica_groups=mesh['x'=4,'core'=2,'y'=4,'z'=4] {'x','y','z'}, dimensions={0} | all-to-all | bytes 1835008 | tf_op jit(solution)/shard_map/all_to_all | solution.py:424
  89.4 2.8 %collective-permute-start.10 = (bf16[512,896]{1,0:T(8,128)(2,1)S(1)}, bf16[512,896]{1,0:T(8,128)(2,1)S(1)}, u32[]{:S(2)}, u32[]{:S(2)}) collective-permute-start(bf16[512,896]{1,0:T(8,128)(2,1)S(1)} %bitcast.16), channel_id=1, source_target_pairs={{0,16},{16,0},{1,17},{17,1},{2,18},{18,2},{3,19},{19,3},{4,20},{20... | collective-permute-start | bytes 2752520 | tf_op jit(solution)/shard_map/ppermute | solution.py:425
  92.2 1.5 %shard_map.137 = f32[512,256]{1,0:T(8,128)} custom-call(bf16[128,8,768]{2,1,0:T(8,128)(2,1)S(1)} %all_to_all.10.got_ref), custom_call_target="tpu_custom_call" | custom-call | flops 400000000 | bytes 2000000 | tf_op jit(solution)/shard_map/pallas_call | solution.py:426
  93.7 0.6 add_bitcast_fusion
  94.3 4.9 %shard_map.136 = (f32[256,512]{1,0:T(8,128)}, f32[512,1280]{1,0:T(8,128)}, f32[1024,512]{1,0:T(8,128)}) custom-call(s32[1]{0:T(128)} %bitcast.core_ref, bf16[512,896]{1,0:T(8,128)(2,1)S(1)} %bitcast.17, bf16[512,896]{1,0:T(8,128)(2,1)S(1)} %collective-permute-done.10.other_ref, bf16[256,512]{1,0:T(8,128)(2,1)S(1)} %copy-done.1, bf16[512,1280]{1,0:T(8,128)(2,1)S(1)} %copy-done), custom_call_target="tpu_custom_call" | custom-call | flops 700000000 | bytes 8000000 | tf_op jit(solution)/shard_map/pallas_call | solution.py:429
  (37 shorter events, 1.3 us)
Async XLA Ops:
  4.4 12.7 %collective-permute-start = (bf16[272,128]{1,0:T(8,128)(2,1)}, bf16[272,128]{1,0:T(8,128)(2,1)S(1)}, u32[]{:S(2)}, u32[]{:S(2)}) collective-permute-start(bf16[272,128]{1,0:T(8,128)(2,1)} %get-tuple-element.51), channel_id=1, source_target_pairs={{0,1},{1,2},{2,3},{3,0},{4,5},{5,6},{6,7},{7,4},{8,9},{9,10},{10,1... | collective-permute-start | bytes 208904 | tf_op jit(solution)/shard_map/ppermute | solution.py:362
  6.9 10.1 %collective-permute-start.1 = (bf16[272,128]{1,0:T(8,128)(2,1)}, bf16[272,128]{1,0:T(8,128)(2,1)S(1)}, u32[]{:S(2)}, u32[]{:S(2)}) collective-permute-start(bf16[272,128]{1,0:T(8,128)(2,1)} %get-tuple-element.52), channel_id=1, source_target_pairs={{0,2},{1,3},{2,0},{3,1},{4,6},{5,7},{6,4},{7,5},{8,10},{9,11},{10,... | collective-permute-start | bytes 208904 | tf_op jit(solution)/shard_map/ppermute | solution.py:362
  10.2 6.8 %collective-permute-start.2 = (bf16[272,128]{1,0:T(8,128)(2,1)}, bf16[272,128]{1,0:T(8,128)(2,1)S(1)}, u32[]{:S(2)}, u32[]{:S(2)}) collective-permute-start(bf16[272,128]{1,0:T(8,128)(2,1)} %get-tuple-element.53), channel_id=1, source_target_pairs={{0,3},{1,0},{2,1},{3,2},{4,7},{5,4},{6,5},{7,6},{8,11},{9,8},{10,9... | collective-permute-start | bytes 208904 | tf_op jit(solution)/shard_map/ppermute | solution.py:362
  11.0 7.7 %copy-start.6 = (bf16[272,128]{1,0:T(8,128)(2,1)S(1)}, bf16[272,128]{1,0:T(8,128)(2,1)}, u32[]{:S(2)}) copy-start(bf16[272,128]{1,0:T(8,128)(2,1)} %get-tuple-element.60.a_ref) | copy-start | bytes 208900
  11.0 11.7 %copy-start.11 = (s32[1,256]{1,0:T(1,128)S(1)}, s32[1,256]{1,0:T(1,128)}, u32[]{:S(2)}) copy-start(s32[1,256]{1,0:T(1,128)} %index_ref.1) | copy-start | bytes 3076
  17.0 15.0 %copy-start.2 = (f32[512,512]{1,0:T(8,128)S(1)}, f32[512,512]{1,0:T(8,128)}, u32[]{:S(2)}) copy-start(f32[512,512]{1,0:T(8,128)} %get-tuple-element.74.keep_ref) | copy-start | bytes 3145732
  17.1 15.0 %collective-permute-start.9 = (bf16[512,512]{1,0:T(8,128)(2,1)}, bf16[512,512]{1,0:T(8,128)(2,1)S(1)}, u32[]{:S(2)}, u32[]{:S(2)}) collective-permute-start(bf16[512,512]{1,0:T(8,128)(2,1)} %get-tuple-element.75), channel_id=1, source_target_pairs={{0,16},{16,0},{1,17},{17,1},{2,18},{18,2},{3,19},{19,3},{4,20},{20... | collective-permute-start | bytes 1572872 | tf_op jit(solution)/shard_map/ppermute | solution.py:412
  18.8 5.2 %collective-permute-start.5 = (bf16[272,128]{1,0:T(8,128)(2,1)S(1)}, bf16[272,128]{1,0:T(8,128)(2,1)S(1)}, u32[]{:S(2)}, u32[]{:S(2)}) collective-permute-start(bf16[272,128]{1,0:T(8,128)(2,1)S(1)} %shard_map.130.ta_ref), channel_id=1, source_target_pairs={{0,12},{4,0},{8,4},{12,8},{1,13},{5,1},{9,5},{13,9},{2,14},{6,2},{... | collective-permute-start | bytes 208904 | tf_op jit(solution)/shard_map/ppermute | solution.py:362
  21.6 4.7 %collective-permute-start.4 = (bf16[272,128]{1,0:T(8,128)(2,1)S(1)}, bf16[272,128]{1,0:T(8,128)(2,1)S(1)}, u32[]{:S(2)}, u32[]{:S(2)}) collective-permute-start(bf16[272,128]{1,0:T(8,128)(2,1)S(1)} %shard_map.130.ta_ref), channel_id=1, source_target_pairs={{0,8},{4,12},{8,0},{12,4},{1,9},{5,13},{9,1},{13,5},{2,10},{6,14},... | collective-permute-start | bytes 208904 | tf_op jit(solution)/shard_map/ppermute | solution.py:362
  21.9 6.7 %collective-permute-start.3 = (bf16[272,128]{1,0:T(8,128)(2,1)S(1)}, bf16[272,128]{1,0:T(8,128)(2,1)S(1)}, u32[]{:S(2)}, u32[]{:S(2)}) collective-permute-start(bf16[272,128]{1,0:T(8,128)(2,1)S(1)} %shard_map.130.ta_ref), channel_id=1, source_target_pairs={{0,4},{4,8},{8,12},{12,0},{1,5},{5,9},{9,13},{13,1},{2,6},{6,10},{... | collective-permute-start | bytes 208904 | tf_op jit(solution)/shard_map/ppermute | solution.py:362
  22.6 0.7 copy-start.12
  23.3 11.5 %copy-start.4 = (bf16[1,256,256]{2,1,0:T(8,128)(2,1)S(1)}, bf16[1,256,256]{2,1,0:T(8,128)(2,1)}, u32[]{:S(2)}) copy-start(bf16[1,256,256]{2,1,0:T(8,128)(2,1)} %param.9) | copy-start | bytes 393220
  23.3 11.5 %copy-start.7 = (f32[128,256]{1,0:T(8,128)S(1)}, f32[128,256]{1,0:T(8,128)}, u32[]{:S(2)}) copy-start(f32[128,256]{1,0:T(8,128)} %get-tuple-element.85.dbt_ref) | copy-start | bytes 393220
  23.3 11.5 %copy-start.8 = (bf16[128,256]{1,0:T(8,128)(2,1)S(1)}, bf16[128,256]{1,0:T(8,128)(2,1)}, u32[]{:S(2)}) copy-start(bf16[128,256]{1,0:T(8,128)(2,1)} %get-tuple-element.83.bt_ref) | copy-start | bytes 196612
  23.3 11.5 %copy-start.9 = (bf16[128,256]{1,0:T(8,128)(2,1)S(1)}, bf16[128,256]{1,0:T(8,128)(2,1)}, u32[]{:S(2)}) copy-start(bf16[128,256]{1,0:T(8,128)(2,1)} %get-tuple-element.86.dct_ref) | copy-start | bytes 196612
  23.3 11.5 %copy-start.10 = (f32[16,256]{1,0:T(8,128)S(1)}, f32[16,256]{1,0:T(8,128)}, u32[]{:S(2)}) copy-start(f32[16,256]{1,0:T(8,128)} %get-tuple-element.57.cum_ref) | copy-start | bytes 49156
  23.9 10.9 %copy-start = (bf16[512,1280]{1,0:T(8,128)(2,1)S(1)}, bf16[512,1280]{1,0:T(8,128)(2,1)}, u32[]{:S(2)}) copy-start(bf16[512,1280]{1,0:T(8,128)(2,1)} %w_in_ref.5) | copy-start | bytes 3932164
  23.9 10.9 %copy-start.1 = (bf16[256,512]{1,0:T(8,128)(2,1)S(1)}, bf16[256,512]{1,0:T(8,128)(2,1)}, u32[]{:S(2)}) copy-start(bf16[256,512]{1,0:T(8,128)(2,1)} %w_up_ref.3) | copy-start | bytes 786436
  24.0 10.9 %copy-start.3 = (f32[1024,256]{1,0:T(8,128)S(1)}, f32[1024,256]{1,0:T(8,128)}, u32[]{:S(2)}) copy-start(f32[1024,256]{1,0:T(8,128)} %get-tuple-element.89.dx_ref) | copy-start | bytes 3145732
  28.8 4.5 %collective-permute-start.6 = (bf16[256,128]{1,0:T(8,128)(2,1)S(1)}, bf16[256,128]{1,0:T(8,128)(2,1)S(1)}, u32[]{:S(2)}, u32[]{:S(2)}) collective-permute-start(bf16[256,128]{1,0:T(8,128)(2,1)S(1)} %get-tuple-element.71), channel_id=1, source_target_pairs={{0,1},{1,2},{2,3},{3,0},{4,5},{5,6},{6,7},{7,4},{8,9},{9,10},{10,1... | collective-permute-start | bytes 196616 | tf_op jit(solution)/shard_map/ppermute | solution.py:362
  29.6 4.7 %collective-permute-start.7 = (bf16[256,128]{1,0:T(8,128)(2,1)S(1)}, bf16[256,128]{1,0:T(8,128)(2,1)S(1)}, u32[]{:S(2)}, u32[]{:S(2)}) collective-permute-start(bf16[256,128]{1,0:T(8,128)(2,1)S(1)} %get-tuple-element.72), channel_id=1, source_target_pairs={{0,2},{1,3},{2,0},{3,1},{4,6},{5,7},{6,4},{7,5},{8,10},{9,11},{10,... | collective-permute-start | bytes 196616 | tf_op jit(solution)/shard_map/ppermute | solution.py:362
  29.7 5.1 %collective-permute-start.8 = (bf16[256,128]{1,0:T(8,128)(2,1)S(1)}, bf16[256,128]{1,0:T(8,128)(2,1)S(1)}, u32[]{:S(2)}, u32[]{:S(2)}) collective-permute-start(bf16[256,128]{1,0:T(8,128)(2,1)S(1)} %get-tuple-element.73), channel_id=1, source_target_pairs={{0,3},{1,0},{2,1},{3,2},{4,7},{5,4},{6,5},{7,6},{8,11},{9,8},{10,9... | collective-permute-start | bytes 196616 | tf_op jit(solution)/shard_map/ppermute | solution.py:362
  32.1 1.0 %copy-start.5 = (bf16[1024,256]{1,0:T(8,128)(2,1)S(1)}, bf16[1024,256]{1,0:T(8,128)(2,1)}, u32[]{:S(2)}) copy-start(bf16[1024,256]{1,0:T(8,128)(2,1)} %get-tuple-element.76.tx_ref) | copy-start | bytes 1572868
  89.4 4.9 %collective-permute-start.10 = (bf16[512,896]{1,0:T(8,128)(2,1)S(1)}, bf16[512,896]{1,0:T(8,128)(2,1)S(1)}, u32[]{:S(2)}, u32[]{:S(2)}) collective-permute-start(bf16[512,896]{1,0:T(8,128)(2,1)S(1)} %bitcast.16), channel_id=1, source_target_pairs={{0,16},{16,0},{1,17},{17,1},{2,18},{18,2},{3,19},{19,3},{4,20},{20... | collective-permute-start | bytes 2752520 | tf_op jit(solution)/shard_map/ppermute | solution.py:425

commit v11 on v9

--- a/solution.py
+++ b/solution.py
@@ -218,7 +218,7 @@
     mine = pl.ds(pl.multiple_of(core * half, half), half)
     other = pl.ds(pl.multiple_of((1 - core) * half, half), half)
     give_ref[...] = dot(y_ref[other, :].astype(BF), dout_ref[...]).astype(BF)
-    keep_ref[...] = dot(y_ref[mine, :].astype(BF), dout_ref[...])
+    keep_ref[...] = dot(y_ref[mine, :].astype(BF), dout_ref[...]).astype(BF)
     sum_ref[:N, :N] = a00.astype(BF)
     sum_ref[:N, N:] = a01.astype(BF)
     sum_ref[N:, :N] = zero
@@ -285,7 +285,7 @@
 
 def pair_kernel(keep_ref, got_ref, tx_ref, out_ref, tx_out_ref):
     tx_out_ref[...] = tx_ref[...]
-    total = (keep_ref[...] + got_ref[...].astype(F32)).astype(BF)
+    total = (keep_ref[...].astype(F32) + got_ref[...].astype(F32)).astype(BF)
     out_ref[: INNER // 2, :] = total[:, :E]
     out_ref[INNER // 2 :, :] = total[:, E:]
 
@@ -333,14 +333,14 @@
             g_ref[INNER:, m * N : (m + 1) * N] = dot(pick, side_ref[...]).astype(BF)
 
     g = g_ref[...]
-    part = pl.ds(pl.multiple_of(step * N, N), N)
+    part = pl.ds(pl.multiple_of(step * E, E), E)
     in_ref[...] = lax.dot_general(w_up_ref[:, part], g, (((0,), (1,)), ((), ())), preferred_element_type=F32)
     up_ref[...] = jnp.transpose(dot(w_in_ref[part, :], g))
-    lanes = pl.ds(pl.multiple_of(E + N + E * lax.shift_right_logical(step, 1), N), E)
-    for m in range(2):
-        rows = pl.ds(pl.multiple_of((2 * m + (step & 1)) * N, N), N)
+    lanes = pl.ds(pl.multiple_of(E + N + E * step, N), E)
+    for x in range(4):
         for at, ref in sources:
-            go_ref[pl.ds(pl.multiple_of(at * N, N), N), m * E : (m + 1) * E] = ref[rows, lanes].astype(F32)
+            rows = pl.ds(pl.multiple_of((x & 1) * E + at * N, N), N)
+            go_ref[rows, (x >> 1) * E : (x >> 1) * E + E] = ref[x * N : (x + 1) * N, lanes].astype(F32)
 
 
 def hop(value, axis, step):
@@ -365,7 +365,7 @@
     sums = sums[:1] + [hop(v, "z", k + 1) for k, v in enumerate(sums[1:])]
     keep, give, dx, tx, bt, dbt, dct, extra = call(
         local_kernel,
-        [((INNER // 2, D), F32), ((INNER // 2, D), BF), ((INNER, T), F32), ((INNER, T), BF), ((N, T), BF),
+        [((INNER // 2, D), BF), ((INNER // 2, D), BF), ((INNER, T), F32), ((INNER, T), BF), ((N, T), BF),
          ((N, T), F32), ((N, T), BF), ((1, T), F32)],
         BIG, 2_500_000_000, 6_000_000,
         in_specs=[VM] * 8 + [SM] * 2, out_specs=(VM,) * 8,
@@ -411,16 +411,16 @@
     (table,) = call(
         table_kernel, [((ROWS_DEV, E), F32)], 12, 400_000_000, 2_000_000, in_specs=[VM], out_specs=(VM,)
     )(pay_got)
-    column = pl.BlockSpec((E, D // 4), lambda i: (0, i))
-    row = pl.BlockSpec((D // 4, PROJ), lambda i: (i, 0))
+    column = pl.BlockSpec((E, D // 2), lambda i: (0, i))
+    row = pl.BlockSpec((D // 2, PROJ), lambda i: (i, 0))
     grad_up, grad_in, grad_out = pl.pallas_call(
         last_kernel,
-        grid=(4,),
+        grid=(2,),
         out_shape=tuple(jax.ShapeDtypeStruct(s, F32) for s in ((E, D), (D, PROJ), (INNER, D))),
         in_specs=[SM] + [VM] * 4,
-        out_specs=(column, row, pl.BlockSpec((INNER // 4, D), lambda i: (i, 0))),
+        out_specs=(column, row, pl.BlockSpec((INNER // 2, D), lambda i: (i, 0))),
         scratch_shapes=[pltpu.VMEM((PROJ, E), BF), pltpu.VMEM((8 * DEV, N), BF)],
-        compiler_params=pltpu.CompilerParams(vmem_limit_bytes=24 * MB),
+        compiler_params=pltpu.CompilerParams(vmem_limit_bytes=28 * MB),
         cost_estimate=pl.CostEstimate(flops=700_000_000, bytes_accessed=8_000_000, transcendentals=0),
     )(core, whole, other, w_up, w_in)
     grad_skip = skip_sum[0, :H] + skip_sum[0, 32 : 32 + H]

time: 98.6 us -> 97.9 us (level)
  no operation moved by 1% of the time
where the time goes in v11:
time: 97.9 us; the launch traced here: 97.6 us
  blocking collectives  52.1 us (53%)
  starting transfers between devices  18.1 us (18%)
  Pallas kernels  18 us (18%)
  waiting for transfers between devices  6.25 us (6%)
  local copies, waits for them, and re-layouts  1.77 us (2%)
    all_to_all x1, blocking collectives, local(): lax.all_to_all(pay.reshape(DEV, 8, 3 * E), every, 0, 0, tiled=True)  31.6 us
    all_to_all x1, blocking collectives, local(): lax.all_to_all(chunk, ('x', 'y', 'z'), 0, 0, tiled=True)  20.4 us
    ppermute x9, starting transfers between devices, hop(): return lax.ppermute(value, axis, [(i, (i + step) % 4) for i in range(4)])  13.7 us
    ppermute x9, waiting for transfers between devices, hop(): return lax.ppermute(value, axis, [(i, (i + step) % 4) for i in range(4)])  6.21 us
    pallas_call x1, Pallas kernels, local(): call(local_kernel, [((INNER // 2, D), BF), ((INNER // 2, D), BF), ((INNER...  5.92 us
    pallas_call x1, Pallas kernels, local(): call(project_kernel, [((T, D), BF), ((T, N), BF), ((INNER, T), BF), ((H,...  3.74 us
    pallas_call x1, Pallas kernels, local(): pl.pallas_call(last_kernel, grid=(2,), out_shape=tuple((jax.ShapeDtypeStr...  3.44 us
    ppermute x1, starting transfers between devices, local(): other = lax.ppermute(whole, 'core', [(0, 1), (1, 0)])  2.83 us
  transfers between devices with their start and end apart: 11, of which 4 were waited for; matrix products, arithmetic and copies ran while one was open for 1% of the time, Pallas kernels for 9%

profile of v11, /device:TPU:1, one launch (start us, length us, event | category | flops | bytes accessed | tf_op | source)
XLA Modules:
  0.0 97.6 jit_solution(771267973063620370)
XLA Ops:
  0.6 3.7 %shard_map.128 = (bf16[256,512]{1,0:T(8,128)(2,1)}, bf16[256,128]{1,0:T(8,128)(2,1)}, bf16[1024,256]{1,0:T(8,128)(2,1)}, f32[16,256]{1,0:T(8,128)}, f32[256,16]{...) custom-call(s32[1]{0:T(128)} %bitcast.1.z_ref, ...), custom_call_target="tpu_custom_call" | custom-call | flops 750000000 | bytes 4500000 | tf_op jit(solution)/shard_map/pallas_call | solution.py:354
  4.4 2.5 %collective-permute-start = (bf16[272,128]{1,0:T(8,128)(2,1)}, bf16[272,128]{1,0:T(8,128)(2,1)S(1)}, u32[]{:S(2)}, u32[]{:S(2)}) collective-permute-start(bf16[272,128]{1,0:T(8,128)(2,1)} %get-tuple-element.51), channel_id=1, source_target_pairs={{0,1},{1,2},{2,3},{3,0},{4,5},{5,6},{6,7},{7,4},{8,9},{9,10},{10,1... | collective-permute-start | bytes 208904 | tf_op jit(solution)/shard_map/ppermute | solution.py:347
  6.9 3.3 %collective-permute-start.1 = (bf16[272,128]{1,0:T(8,128)(2,1)}, bf16[272,128]{1,0:T(8,128)(2,1)S(1)}, u32[]{:S(2)}, u32[]{:S(2)}) collective-permute-start(bf16[272,128]{1,0:T(8,128)(2,1)} %get-tuple-element.52), channel_id=1, source_target_pairs={{0,2},{1,3},{2,0},{3,1},{4,6},{5,7},{6,4},{7,5},{8,10},{9,11},{10,... | collective-permute-start | bytes 208904 | tf_op jit(solution)/shard_map/ppermute | solution.py:347
  10.2 0.7 collective-permute-start.2
  11.0 5.9 %shard_map.129 = (bf16[512,512]{1,0:T(8,128)(2,1)}, bf16[512,512]{1,0:T(8,128)(2,1)}, f32[1024,256]{1,0:T(8,128)}, bf16[1024,256]{1,0:T(8,128)(2,1)}, bf16[128,2...) custom-call(bf16[256,512]{1,0:T(8,128)(2,1)} %get-tuple-element.54.u_ref, ...), custom_call_target="tpu_custom_call" | custom-call | flops 2500000000 | bytes 6000000 | tf_op jit(solution)/shard_map/pallas_call | solution.py:366
  16.9 1.6 %collective-permute-start.9 = (bf16[512,512]{1,0:T(8,128)(2,1)}, bf16[512,512]{1,0:T(8,128)(2,1)S(1)}, u32[]{:S(2)}, u32[]{:S(2)}) collective-permute-start(bf16[512,512]{1,0:T(8,128)(2,1)} %get-tuple-element.75), channel_id=1, source_target_pairs={{0,16},{16,0},{1,17},{17,1},{2,18},{18,2},{3,19},{19,3},{4,20},{20... | collective-permute-start | bytes 1572872 | tf_op jit(solution)/shard_map/ppermute | solution.py:397
  18.6 2.8 %collective-permute-start.5 = (bf16[272,128]{1,0:T(8,128)(2,1)S(1)}, bf16[272,128]{1,0:T(8,128)(2,1)S(1)}, u32[]{:S(2)}, u32[]{:S(2)}) collective-permute-start(bf16[272,128]{1,0:T(8,128)(2,1)S(1)} %shard_map.130.ta_ref), channel_id=1, source_target_pairs={{0,12},{4,0},{8,4},{12,8},{1,13},{5,1},{9,5},{13,9},{2,14},{6,2},{... | collective-permute-start | bytes 208904 | tf_op jit(solution)/shard_map/ppermute | solution.py:347
  21.8 0.7 collective-permute-start.3
  22.5 0.7 copy-done.12
  23.2 0.6 shard_map.131
  23.8 2.4 %collective-permute-done.4.tc_ref = bf16[272,128]{1,0:T(8,128)(2,1)S(1)} collective-permute-done((bf16[272,128]{1,0:T(8,128)(2,1)S(1)}, bf16[272,128]{1,0:T(8,128)(2,1)S(1)}, u32[]{:S(2)}, u32[]{:S(2)}) %collective-permute-start.4) | collective-permute-done | bytes 69664 | tf_op jit(solution)/shard_map/ppermute | solution.py:347
  26.2 2.3 %collective-permute-done.3.tb_ref = bf16[272,128]{1,0:T(8,128)(2,1)S(1)} collective-permute-done((bf16[272,128]{1,0:T(8,128)(2,1)S(1)}, bf16[272,128]{1,0:T(8,128)(2,1)S(1)}, u32[]{:S(2)}, u32[]{:S(2)}) %collective-permute-start.3) | collective-permute-done | bytes 69664 | tf_op jit(solution)/shard_map/ppermute | solution.py:347
  28.6 0.8 collective-permute-start.6
  29.6 2.3 %collective-permute-start.8 = (bf16[256,128]{1,0:T(8,128)(2,1)S(1)}, bf16[256,128]{1,0:T(8,128)(2,1)S(1)}, u32[]{:S(2)}, u32[]{:S(2)}) collective-permute-start(bf16[256,128]{1,0:T(8,128)(2,1)S(1)} %get-tuple-element.73), channel_id=1, source_target_pairs={{0,3},{1,0},{2,1},{3,2},{4,7},{5,4},{6,5},{7,6},{8,11},{9,8},{10,9... | collective-permute-start | bytes 196616 | tf_op jit(solution)/shard_map/ppermute | solution.py:347
  31.9 1.0 %copy-done.4 = bf16[1024,256]{1,0:T(8,128)(2,1)S(1)} copy-done((bf16[1024,256]{1,0:T(8,128)(2,1)S(1)}, bf16[1024,256]{1,0:T(8,128)(2,1)}, u32[]{:S(2)}) %copy-start.4) | copy-done | bytes 524312
  33.2 1.0 %collective-permute-done.7.c2_ref = bf16[256,128]{1,0:T(8,128)(2,1)S(1)} collective-permute-done((bf16[256,128]{1,0:T(8,128)(2,1)S(1)}, bf16[256,128]{1,0:T(8,128)(2,1)S(1)}, u32[]{:S(2)}, u32[]{:S(2)}) %collective-permute-start.7) | collective-permute-done | bytes 65568 | tf_op jit(solution)/shard_map/ppermute | solution.py:347
  34.2 0.5 collective-permute-done.8.c3_ref
  34.7 2.1 %shard_map.134 = bf16[1024,768]{1,0:T(8,128)(2,1)S(1)} custom-call(s32[1]{0:T(128)} %bitcast.1.z_ref, bf16[256,128]{1,0:T(8,128)(2,1)S(1)} %get-tuple-element.78.c0_ref, bf16[256,128]{1,0:T(8,128)(2,1)S(1)} %collective-permute-done.6.c1_ref, bf16[256,128]{1,0:T(8,128)(2,1)S(1)} %collective-permute-done.7.c2_ref, ...), custom_call_target="tpu_custom_call" | custom-call | flops 1400000000 | bytes 6000000 | tf_op jit(solution)/shard_map/pallas_call | solution.py:399
  36.8 31.6 %all_to_all.10.got_ref = bf16[128,8,768]{2,1,0:T(8,128)(2,1)S(1)} all-to-all(bf16[128,8,768]{2,1,0:T(8,128)(2,1)S(1)} %bitcast.15), channel_id=1, replica_groups=mesh['x'=4,'core'=2,'y'=4,'z'=4] {'x','core','y','z'}, dimensions={0} | all-to-all | bytes 3145728 | tf_op jit(solution)/shard_map/all_to_all | solution.py:404
  68.8 20.4 %all_to_all.11 = bf16[64,8,896]{2,1,0:T(8,128)(2,1)S(1)} all-to-all(bf16[64,8,896]{2,1,0:T(8,128)(2,1)S(1)} %get-tuple-element.90), channel_id=1, replica_groups=mesh['x'=4,'core'=2,'y'=4,'z'=4] {'x','y','z'}, dimensions={0} | all-to-all | bytes 1835008 | tf_op jit(solution)/shard_map/all_to_all | solution.py:409
  89.2 2.8 %collective-permute-start.10 = (bf16[512,896]{1,0:T(8,128)(2,1)S(1)}, bf16[512,896]{1,0:T(8,128)(2,1)S(1)}, u32[]{:S(2)}, u32[]{:S(2)}) collective-permute-start(bf16[512,896]{1,0:T(8,128)(2,1)S(1)} %bitcast.16), channel_id=1, source_target_pairs={{0,16},{16,0},{1,17},{17,1},{2,18},{18,2},{3,19},{19,3},{4,20},{20... | collective-permute-start | bytes 2752520 | tf_op jit(solution)/shard_map/ppermute | solution.py:410
  92.1 1.5 %shard_map.137 = f32[512,256]{1,0:T(8,128)} custom-call(bf16[128,8,768]{2,1,0:T(8,128)(2,1)S(1)} %all_to_all.10.got_ref), custom_call_target="tpu_custom_call" | custom-call | flops 400000000 | bytes 2000000 | tf_op jit(solution)/shard_map/pallas_call | solution.py:411
  93.5 0.6 add_bitcast_fusion
  94.2 3.4 %shard_map.136 = (f32[256,512]{1,0:T(8,128)}, f32[512,1280]{1,0:T(8,128)}, f32[1024,512]{1,0:T(8,128)}) custom-call(s32[1]{0:T(128)} %bitcast.core_ref, bf16[512,896]{1,0:T(8,128)(2,1)S(1)} %bitcast.17, bf16[512,896]{1,0:T(8,128)(2,1)S(1)} %collective-permute-done.10.other_ref, bf16[256,512]{1,0:T(8,128)(2,1)S(1)} %copy-done.1, bf16[512,1280]{1,0:T(8,128)(2,1)S(1)} %copy-done), custom_call_target="tpu_custom_call" | custom-call | flops 700000000 | bytes 8000000 | tf_op jit(solution)/shard_map/pallas_call | solution.py:416
  (37 shorter events, 1.4 us)
Async XLA Ops:
  4.4 12.5 %collective-permute-start = (bf16[272,128]{1,0:T(8,128)(2,1)}, bf16[272,128]{1,0:T(8,128)(2,1)S(1)}, u32[]{:S(2)}, u32[]{:S(2)}) collective-permute-start(bf16[272,128]{1,0:T(8,128)(2,1)} %get-tuple-element.51), channel_id=1, source_target_pairs={{0,1},{1,2},{2,3},{3,0},{4,5},{5,6},{6,7},{7,4},{8,9},{9,10},{10,1... | collective-permute-start | bytes 208904 | tf_op jit(solution)/shard_map/ppermute | solution.py:347
  6.9 10.0 %collective-permute-start.1 = (bf16[272,128]{1,0:T(8,128)(2,1)}, bf16[272,128]{1,0:T(8,128)(2,1)S(1)}, u32[]{:S(2)}, u32[]{:S(2)}) collective-permute-start(bf16[272,128]{1,0:T(8,128)(2,1)} %get-tuple-element.52), channel_id=1, source_target_pairs={{0,2},{1,3},{2,0},{3,1},{4,6},{5,7},{6,4},{7,5},{8,10},{9,11},{10,... | collective-permute-start | bytes 208904 | tf_op jit(solution)/shard_map/ppermute | solution.py:347
  10.2 6.7 %collective-permute-start.2 = (bf16[272,128]{1,0:T(8,128)(2,1)}, bf16[272,128]{1,0:T(8,128)(2,1)S(1)}, u32[]{:S(2)}, u32[]{:S(2)}) collective-permute-start(bf16[272,128]{1,0:T(8,128)(2,1)} %get-tuple-element.53), channel_id=1, source_target_pairs={{0,3},{1,0},{2,1},{3,2},{4,7},{5,4},{6,5},{7,6},{8,11},{9,8},{10,9... | collective-permute-start | bytes 208904 | tf_op jit(solution)/shard_map/ppermute | solution.py:347
  11.0 7.6 %copy-start.6 = (bf16[272,128]{1,0:T(8,128)(2,1)S(1)}, bf16[272,128]{1,0:T(8,128)(2,1)}, u32[]{:S(2)}) copy-start(bf16[272,128]{1,0:T(8,128)(2,1)} %get-tuple-element.60.a_ref) | copy-start | bytes 208900
  11.0 11.5 %copy-start.11 = (s32[1,256]{1,0:T(1,128)S(1)}, s32[1,256]{1,0:T(1,128)}, u32[]{:S(2)}) copy-start(s32[1,256]{1,0:T(1,128)} %index_ref.1) | copy-start | bytes 3076
  11.0 23.7 %copy-start.5 = (bf16[1,256,256]{2,1,0:T(8,128)(2,1)S(1)}, bf16[1,256,256]{2,1,0:T(8,128)(2,1)}, u32[]{:S(2)}) copy-start(bf16[1,256,256]{2,1,0:T(8,128)(2,1)} %param.9) | copy-start | bytes 393220
  11.0 23.7 %copy-start.10 = (f32[16,256]{1,0:T(8,128)S(1)}, f32[16,256]{1,0:T(8,128)}, u32[]{:S(2)}) copy-start(f32[16,256]{1,0:T(8,128)} %get-tuple-element.57.cum_ref) | copy-start | bytes 49156
  16.9 15.0 %copy-start.3 = (bf16[512,512]{1,0:T(8,128)(2,1)S(1)}, bf16[512,512]{1,0:T(8,128)(2,1)}, u32[]{:S(2)}) copy-start(bf16[512,512]{1,0:T(8,128)(2,1)} %get-tuple-element.74.keep_ref) | copy-start | bytes 1572868
  16.9 15.0 %collective-permute-start.9 = (bf16[512,512]{1,0:T(8,128)(2,1)}, bf16[512,512]{1,0:T(8,128)(2,1)S(1)}, u32[]{:S(2)}, u32[]{:S(2)}) collective-permute-start(bf16[512,512]{1,0:T(8,128)(2,1)} %get-tuple-element.75), channel_id=1, source_target_pairs={{0,16},{16,0},{1,17},{17,1},{2,18},{18,2},{3,19},{19,3},{4,20},{20... | collective-permute-start | bytes 1572872 | tf_op jit(solution)/shard_map/ppermute | solution.py:397
  18.6 5.1 %collective-permute-start.5 = (bf16[272,128]{1,0:T(8,128)(2,1)S(1)}, bf16[272,128]{1,0:T(8,128)(2,1)S(1)}, u32[]{:S(2)}, u32[]{:S(2)}) collective-permute-start(bf16[272,128]{1,0:T(8,128)(2,1)S(1)} %shard_map.130.ta_ref), channel_id=1, source_target_pairs={{0,12},{4,0},{8,4},{12,8},{1,13},{5,1},{9,5},{13,9},{2,14},{6,2},{... | collective-permute-start | bytes 208904 | tf_op jit(solution)/shard_map/ppermute | solution.py:347
  21.4 4.7 %collective-permute-start.4 = (bf16[272,128]{1,0:T(8,128)(2,1)S(1)}, bf16[272,128]{1,0:T(8,128)(2,1)S(1)}, u32[]{:S(2)}, u32[]{:S(2)}) collective-permute-start(bf16[272,128]{1,0:T(8,128)(2,1)S(1)} %shard_map.130.ta_ref), channel_id=1, source_target_pairs={{0,8},{4,12},{8,0},{12,4},{1,9},{5,13},{9,1},{13,5},{2,10},{6,14},... | collective-permute-start | bytes 208904 | tf_op jit(solution)/shard_map/ppermute | solution.py:347
  21.8 6.7 %collective-permute-start.3 = (bf16[272,128]{1,0:T(8,128)(2,1)S(1)}, bf16[272,128]{1,0:T(8,128)(2,1)S(1)}, u32[]{:S(2)}, u32[]{:S(2)}) collective-permute-start(bf16[272,128]{1,0:T(8,128)(2,1)S(1)} %shard_map.130.ta_ref), channel_id=1, source_target_pairs={{0,4},{4,8},{8,12},{12,0},{1,5},{5,9},{9,13},{13,1},{2,6},{6,10},{... | collective-permute-start | bytes 208904 | tf_op jit(solution)/shard_map/ppermute | solution.py:347
  22.5 0.7 copy-start.12
  23.2 11.5 %copy-start = (bf16[512,1280]{1,0:T(8,128)(2,1)S(1)}, bf16[512,1280]{1,0:T(8,128)(2,1)}, u32[]{:S(2)}) copy-start(bf16[512,1280]{1,0:T(8,128)(2,1)} %w_in_ref.5) | copy-start | bytes 3932164
  23.2 11.5 %copy-start.1 = (bf16[256,512]{1,0:T(8,128)(2,1)S(1)}, bf16[256,512]{1,0:T(8,128)(2,1)}, u32[]{:S(2)}) copy-start(bf16[256,512]{1,0:T(8,128)(2,1)} %w_up_ref.3) | copy-start | bytes 786436
  23.2 11.5 %copy-start.2 = (f32[1024,256]{1,0:T(8,128)S(1)}, f32[1024,256]{1,0:T(8,128)}, u32[]{:S(2)}) copy-start(f32[1024,256]{1,0:T(8,128)} %get-tuple-element.89.dx_ref) | copy-start | bytes 3145732
  28.6 4.5 %collective-permute-start.6 = (bf16[256,128]{1,0:T(8,128)(2,1)S(1)}, bf16[256,128]{1,0:T(8,128)(2,1)S(1)}, u32[]{:S(2)}, u32[]{:S(2)}) collective-permute-start(bf16[256,128]{1,0:T(8,128)(2,1)S(1)} %get-tuple-element.71), channel_id=1, source_target_pairs={{0,1},{1,2},{2,3},{3,0},{4,5},{5,6},{6,7},{7,4},{8,9},{9,10},{10,1... | collective-permute-start | bytes 196616 | tf_op jit(solution)/shard_map/ppermute | solution.py:347
  29.4 4.7 %collective-permute-start.7 = (bf16[256,128]{1,0:T(8,128)(2,1)S(1)}, bf16[256,128]{1,0:T(8,128)(2,1)S(1)}, u32[]{:S(2)}, u32[]{:S(2)}) collective-permute-start(bf16[256,128]{1,0:T(8,128)(2,1)S(1)} %get-tuple-element.72), channel_id=1, source_target_pairs={{0,2},{1,3},{2,0},{3,1},{4,6},{5,7},{6,4},{7,5},{8,10},{9,11},{10,... | collective-permute-start | bytes 196616 | tf_op jit(solution)/shard_map/ppermute | solution.py:347
  29.6 5.0 %collective-permute-start.8 = (bf16[256,128]{1,0:T(8,128)(2,1)S(1)}, bf16[256,128]{1,0:T(8,128)(2,1)S(1)}, u32[]{:S(2)}, u32[]{:S(2)}) collective-permute-start(bf16[256,128]{1,0:T(8,128)(2,1)S(1)} %get-tuple-element.73), channel_id=1, source_target_pairs={{0,3},{1,0},{2,1},{3,2},{4,7},{5,4},{6,5},{7,6},{8,11},{9,8},{10,9... | collective-permute-start | bytes 196616 | tf_op jit(solution)/shard_map/ppermute | solution.py:347
  31.9 1.0 %copy-start.4 = (bf16[1024,256]{1,0:T(8,128)(2,1)S(1)}, bf16[1024,256]{1,0:T(8,128)(2,1)}, u32[]{:S(2)}) copy-start(bf16[1024,256]{1,0:T(8,128)(2,1)} %get-tuple-element.76.tx_ref) | copy-start | bytes 1572868
  33.0 1.7 %copy-start.7 = (f32[128,256]{1,0:T(8,128)S(1)}, f32[128,256]{1,0:T(8,128)}, u32[]{:S(2)}) copy-start(f32[128,256]{1,0:T(8,128)} %get-tuple-element.85.dbt_ref) | copy-start | bytes 393220
  33.0 1.7 %copy-start.8 = (bf16[128,256]{1,0:T(8,128)(2,1)S(1)}, bf16[128,256]{1,0:T(8,128)(2,1)}, u32[]{:S(2)}) copy-start(bf16[128,256]{1,0:T(8,128)(2,1)} %get-tuple-element.83.bt_ref) | copy-start | bytes 196612
  33.0 1.7 %copy-start.9 = (bf16[128,256]{1,0:T(8,128)(2,1)S(1)}, bf16[128,256]{1,0:T(8,128)(2,1)}, u32[]{:S(2)}) copy-start(bf16[128,256]{1,0:T(8,128)(2,1)} %get-tuple-element.86.dct_ref) | copy-start | bytes 196612
  89.2 4.9 %collective-permute-start.10 = (bf16[512,896]{1,0:T(8,128)(2,1)S(1)}, bf16[512,896]{1,0:T(8,128)(2,1)S(1)}, u32[]{:S(2)}, u32[]{:S(2)}) collective-permute-start(bf16[512,896]{1,0:T(8,128)(2,1)S(1)} %bitcast.16), channel_id=1, source_target_pairs={{0,16},{16,0},{1,17},{17,1},{2,18},{18,2},{3,19},{19,3},{4,20},{20... | collective-permute-start | bytes 2752520 | tf_op jit(solution)/shard_map/ppermute | solution.py:410

commit v12 on v11

--- a/solution.py
+++ b/solution.py
@@ -202,7 +202,7 @@
         st = start[h : h + 1, :]
         skip = skip_ref[h]
         y_ref[lo:hi, :] = dot(x_h, weights) + SC * st * y_ref[lo:hi, :] + skip * x_f
-        dx_ref[lo:hi, :] = dot(dy_h, weights, NT) + skip * dy_f
+        dx_ref[lo:hi, :] = (dot(dy_h, weights, NT) + skip * dy_f).astype(BF)
         sdy_ref[lo:hi, :] = (st * dy_f).astype(BF)
         tx_ref[lo:hi, :] = (tail[h : h + 1, :] * x_f).astype(BF)
         x_pair = x_ref[:, (h // 2) * N : (h // 2 + 1) * N]
@@ -268,7 +268,7 @@
     entering = dot(carry, bt_ref[...])
     for h in range(H):
         lo, hi = h * HP, (h + 1) * HP
-        d_ref[lo:hi, :] = (dx_ref[lo:hi, :] + tail[h : h + 1, :] * entering[lo:hi, :]).astype(BF)
+        d_ref[lo:hi, :] = (dx_ref[lo:hi, :].astype(F32) + tail[h : h + 1, :] * entering[lo:hi, :]).astype(BF)
     d_ref[INNER + N :, :] = dct_ref[...]
     d_ref[INNER : INNER + N, :] = (dbt_ref[...] + dot(carry, tx_ref[...], TN)).astype(BF)
     d = d_ref[...]
@@ -297,7 +297,8 @@
     halves = [jnp.sum(outer[:, c].reshape(DEV // 2, 8, E).astype(F32), axis=0) for c in range(2)]
     chunk = jnp.concatenate([total[:, :E], side] + halves, axis=1)
     chunk_ref[...] = jnp.broadcast_to(chunk[None], chunk_ref.shape).astype(BF)
-    skip_ref[...] = total[6:7, E + 128 : E + 256]
+    skip_row = total[6:7, E + 128 : E + 256]
+    skip_ref[...] = skip_row[:, :H] + skip_row[:, 32 : 32 + H]
 
 
 def table_kernel(got_ref, table_ref):
@@ -365,7 +366,7 @@
     sums = sums[:1] + [hop(v, "z", k + 1) for k, v in enumerate(sums[1:])]
     keep, give, dx, tx, bt, dbt, dct, extra = call(
         local_kernel,
-        [((INNER // 2, D), BF), ((INNER // 2, D), BF), ((INNER, T), F32), ((INNER, T), BF), ((N, T), BF),
+        [((INNER // 2, D), BF), ((INNER // 2, D), BF), ((INNER, T), BF), ((INNER, T), BF), ((N, T), BF),
          ((N, T), F32), ((N, T), BF), ((1, T), F32)],
         BIG, 2_500_000_000, 6_000_000,
         in_specs=[VM] * 8 + [SM] * 2, out_specs=(VM,) * 8,
@@ -403,7 +404,7 @@
     )(z, *carries, outer, bt, cum, tx, dbt, dct, rows, w_up, hits, misc, dx, w_in)
     pay_got = lax.all_to_all(pay.reshape(DEV, 8, 3 * E), every, 0, 0, tiled=True)
     chunk, skip_sum = call(
-        sum_kernel, [((DEV // 2, 8, 7 * N), BF), ((1, 128), F32)], 12, 2_000_000, 3_000_000,
+        sum_kernel, [((DEV // 2, 8, 7 * N), BF), ((1, H), F32)], 12, 2_000_000, 3_000_000,
         in_specs=[VM], out_specs=(VM,) * 2,
     )(pay_got)
     whole = lax.all_to_all(chunk, ("x", "y", "z"), 0, 0, tiled=True).reshape(DEV * 4, 7 * N)
@@ -423,7 +424,7 @@
         compiler_params=pltpu.CompilerParams(vmem_limit_bytes=28 * MB),
         cost_estimate=pl.CostEstimate(flops=700_000_000, bytes_accessed=8_000_000, transcendentals=0),
     )(core, whole, other, w_up, w_in)
-    grad_skip = skip_sum[0, :H] + skip_sum[0, 32 : 32 + H]
+    grad_skip = skip_sum.reshape(H)
     return (grad_up, grad_in, grad_out, grad_skip, table)
 
 

time: 97.9 us -> 98.1 us (level)
  waiting for transfers between devices: 6.25 us -> 7.81 us
  local copies, waits for them, and re-layouts: 1.77 us -> 0.73 us
    unnamed x26, local copies, waits for them, and re-layouts: 1.77 us -> 0.73 us
  transfers between devices with their start and end apart: 11 -> 11, of which waited for: 4 -> 6; matrix products, arithmetic and copies ran while one was open for 1% -> 0% of each run, Pallas kernels for 9% -> 8%
where the time goes in v12:
time: 98.1 us; the launch traced here: 97.8 us
  blocking collectives  52.1 us (53%)
  Pallas kernels  18.2 us (19%)
  starting transfers between devices  18.2 us (19%)
  waiting for transfers between devices  7.81 us (8%)
    all_to_all x1, blocking collectives, local(): lax.all_to_all(pay.reshape(DEV, 8, 3 * E), every, 0, 0, tiled=True)  31.7 us
    all_to_all x1, blocking collectives, local(): lax.all_to_all(chunk, ('x', 'y', 'z'), 0, 0, tiled=True)  20.4 us
    ppermute x9, starting transfers between devices, hop(): return lax.ppermute(value, axis, [(i, (i + step) % 4) for i in range(4)])  13.7 us
    ppermute x9, waiting for transfers between devices, hop(): return lax.ppermute(value, axis, [(i, (i + step) % 4) for i in range(4)])  7.18 us
    pallas_call x1, Pallas kernels, local(): call(local_kernel, [((INNER // 2, D), BF), ((INNER // 2, D), BF), ((INNER...  5.75 us
    pallas_call x1, Pallas kernels, local(): call(project_kernel, [((T, D), BF), ((T, N), BF), ((INNER, T), BF), ((H,...  3.74 us
    pallas_call x1, Pallas kernels, local(): pl.pallas_call(last_kernel, grid=(2,), out_shape=tuple((jax.ShapeDtypeStr...  3.44 us
    ppermute x1, starting transfers between devices, local(): other = lax.ppermute(whole, 'core', [(0, 1), (1, 0)])  2.83 us
  transfers between devices with their start and end apart: 11, of which 6 were waited for; matrix products, arithmetic and copies ran while one was open for 0% of the time, Pallas kernels for 8%

profile of v12, /device:TPU:1, one launch (start us, length us, event | category | flops | bytes accessed | tf_op | source)
XLA Modules:
  0.0 97.8 jit_solution(10579241364342752461)
XLA Ops:
  0.6 3.7 %shard_map.128 = (bf16[256,512]{1,0:T(8,128)(2,1)}, bf16[256,128]{1,0:T(8,128)(2,1)}, bf16[1024,256]{1,0:T(8,128)(2,1)}, f32[16,256]{1,0:T(8,128)}, f32[256,16]{...) custom-call(s32[1]{0:T(128)} %bitcast.1.z_ref, ...), custom_call_target="tpu_custom_call" | custom-call | flops 750000000 | bytes 4500000 | tf_op jit(solution)/shard_map/pallas_call | solution.py:355
  4.4 2.5 %collective-permute-start = (bf16[272,128]{1,0:T(8,128)(2,1)}, bf16[272,128]{1,0:T(8,128)(2,1)S(1)}, u32[]{:S(2)}, u32[]{:S(2)}) collective-permute-start(bf16[272,128]{1,0:T(8,128)(2,1)} %get-tuple-element.51), channel_id=1, source_target_pairs={{0,1},{1,2},{2,3},{3,0},{4,5},{5,6},{6,7},{7,4},{8,9},{9,10},{10,1... | collective-permute-start | bytes 208904 | tf_op jit(solution)/shard_map/ppermute | solution.py:348
  6.9 3.3 %collective-permute-start.1 = (bf16[272,128]{1,0:T(8,128)(2,1)}, bf16[272,128]{1,0:T(8,128)(2,1)S(1)}, u32[]{:S(2)}, u32[]{:S(2)}) collective-permute-start(bf16[272,128]{1,0:T(8,128)(2,1)} %get-tuple-element.52), channel_id=1, source_target_pairs={{0,2},{1,3},{2,0},{3,1},{4,6},{5,7},{6,4},{7,5},{8,10},{9,11},{10,... | collective-permute-start | bytes 208904 | tf_op jit(solution)/shard_map/ppermute | solution.py:348
  10.2 0.7 collective-permute-start.2
  11.0 5.8 %shard_map.129 = (bf16[512,512]{1,0:T(8,128)(2,1)}, bf16[512,512]{1,0:T(8,128)(2,1)}, bf16[1024,256]{1,0:T(8,128)(2,1)}, bf16[1024,256]{1,0:T(8,128)(2,1)}, bf16...) custom-call(bf16[256,512]{1,0:T(8,128)(2,1)} %get-tuple-element.54.u_ref, ...), custom_call_target="tpu_custom_call" | custom-call | flops 2500000000 | bytes 6000000 | tf_op jit(solution)/shard_map/pallas_call | solution.py:367
  16.8 1.6 %collective-permute-start.9 = (bf16[512,512]{1,0:T(8,128)(2,1)}, bf16[512,512]{1,0:T(8,128)(2,1)S(1)}, u32[]{:S(2)}, u32[]{:S(2)}) collective-permute-start(bf16[512,512]{1,0:T(8,128)(2,1)} %get-tuple-element.75), channel_id=1, source_target_pairs={{0,16},{16,0},{1,17},{17,1},{2,18},{18,2},{3,19},{19,3},{4,20},{20... | collective-permute-start | bytes 1572872 | tf_op jit(solution)/shard_map/ppermute | solution.py:398
  18.5 2.8 %collective-permute-start.5 = (bf16[272,128]{1,0:T(8,128)(2,1)S(1)}, bf16[272,128]{1,0:T(8,128)(2,1)S(1)}, u32[]{:S(2)}, u32[]{:S(2)}) collective-permute-start(bf16[272,128]{1,0:T(8,128)(2,1)S(1)} %shard_map.130.ta_ref), channel_id=1, source_target_pairs={{0,12},{4,0},{8,4},{12,8},{1,13},{5,1},{9,5},{13,9},{2,14},{6,2},{... | collective-permute-start | bytes 208904 | tf_op jit(solution)/shard_map/ppermute | solution.py:348
  21.6 0.7 collective-permute-start.3
  22.3 0.7 copy-done.12
  23.0 0.6 shard_map.131
  23.7 2.3 %collective-permute-done.4.tc_ref = bf16[272,128]{1,0:T(8,128)(2,1)S(1)} collective-permute-done((bf16[272,128]{1,0:T(8,128)(2,1)S(1)}, bf16[272,128]{1,0:T(8,128)(2,1)S(1)}, u32[]{:S(2)}, u32[]{:S(2)}) %collective-permute-start.4) | collective-permute-done | bytes 69664 | tf_op jit(solution)/shard_map/ppermute | solution.py:348
  26.0 2.3 %collective-permute-done.3.tb_ref = bf16[272,128]{1,0:T(8,128)(2,1)S(1)} collective-permute-done((bf16[272,128]{1,0:T(8,128)(2,1)S(1)}, bf16[272,128]{1,0:T(8,128)(2,1)S(1)}, u32[]{:S(2)}, u32[]{:S(2)}) %collective-permute-start.3) | collective-permute-done | bytes 69664 | tf_op jit(solution)/shard_map/ppermute | solution.py:348
  28.5 0.8 collective-permute-start.6
  29.4 2.3 %collective-permute-start.8 = (bf16[256,128]{1,0:T(8,128)(2,1)S(1)}, bf16[256,128]{1,0:T(8,128)(2,1)S(1)}, u32[]{:S(2)}, u32[]{:S(2)}) collective-permute-start(bf16[256,128]{1,0:T(8,128)(2,1)S(1)} %get-tuple-element.73), channel_id=1, source_target_pairs={{0,3},{1,0},{2,1},{3,2},{4,7},{5,4},{6,5},{7,6},{8,11},{9,8},{10,9... | collective-permute-start | bytes 196616 | tf_op jit(solution)/shard_map/ppermute | solution.py:348
  31.9 0.9 collective-permute-done.6.c1_ref
  32.9 1.2 %collective-permute-done.7.c2_ref = bf16[256,128]{1,0:T(8,128)(2,1)S(1)} collective-permute-done((bf16[256,128]{1,0:T(8,128)(2,1)S(1)}, bf16[256,128]{1,0:T(8,128)(2,1)S(1)}, u32[]{:S(2)}, u32[]{:S(2)}) %collective-permute-start.7) | collective-permute-done | bytes 65568 | tf_op jit(solution)/shard_map/ppermute | solution.py:348
  34.5 2.1 %shard_map.134 = bf16[1024,768]{1,0:T(8,128)(2,1)S(1)} custom-call(s32[1]{0:T(128)} %bitcast.1.z_ref, bf16[256,128]{1,0:T(8,128)(2,1)S(1)} %get-tuple-element.78.c0_ref, bf16[256,128]{1,0:T(8,128)(2,1)S(1)} %collective-permute-done.6.c1_ref, bf16[256,128]{1,0:T(8,128)(2,1)S(1)} %collective-permute-done.7.c2_ref, ...), custom_call_target="tpu_custom_call" | custom-call | flops 1400000000 | bytes 6000000 | tf_op jit(solution)/shard_map/pallas_call | solution.py:400
  36.6 31.7 %all_to_all.10.got_ref = bf16[128,8,768]{2,1,0:T(8,128)(2,1)S(1)} all-to-all(bf16[128,8,768]{2,1,0:T(8,128)(2,1)S(1)} %bitcast.14), channel_id=1, replica_groups=mesh['x'=4,'core'=2,'y'=4,'z'=4] {'x','core','y','z'}, dimensions={0} | all-to-all | bytes 3145728 | tf_op jit(solution)/shard_map/all_to_all | solution.py:405
  68.3 0.7 shard_map.135
  69.0 20.4 %all_to_all.11 = bf16[64,8,896]{2,1,0:T(8,128)(2,1)S(1)} all-to-all(bf16[64,8,896]{2,1,0:T(8,128)(2,1)S(1)} %get-tuple-element.90), channel_id=1, replica_groups=mesh['x'=4,'core'=2,'y'=4,'z'=4] {'x','y','z'}, dimensions={0} | all-to-all | bytes 1835008 | tf_op jit(solution)/shard_map/all_to_all | solution.py:410
  89.5 2.8 %collective-permute-start.10 = (bf16[512,896]{1,0:T(8,128)(2,1)S(1)}, bf16[512,896]{1,0:T(8,128)(2,1)S(1)}, u32[]{:S(2)}, u32[]{:S(2)}) collective-permute-start(bf16[512,896]{1,0:T(8,128)(2,1)S(1)} %bitcast.15), channel_id=1, source_target_pairs={{0,16},{16,0},{1,17},{17,1},{2,18},{18,2},{3,19},{19,3},{4,20},{20... | collective-permute-start | bytes 2752520 | tf_op jit(solution)/shard_map/ppermute | solution.py:411
  92.3 1.5 %shard_map.137 = f32[512,256]{1,0:T(8,128)} custom-call(bf16[128,8,768]{2,1,0:T(8,128)(2,1)S(1)} %all_to_all.10.got_ref), custom_call_target="tpu_custom_call" | custom-call | flops 400000000 | bytes 2000000 | tf_op jit(solution)/shard_map/pallas_call | solution.py:412
  93.8 0.6 collective-permute-done.10.other_ref
  94.4 3.4 %shard_map.136 = (f32[256,512]{1,0:T(8,128)}, f32[512,1280]{1,0:T(8,128)}, f32[1024,512]{1,0:T(8,128)}) custom-call(s32[1]{0:T(128)} %bitcast.core_ref, bf16[512,896]{1,0:T(8,128)(2,1)S(1)} %bitcast.16, bf16[512,896]{1,0:T(8,128)(2,1)S(1)} %collective-permute-done.10.other_ref, bf16[256,512]{1,0:T(8,128)(2,1)S(1)} %copy-done.1, bf16[512,1280]{1,0:T(8,128)(2,1)S(1)} %copy-done), custom_call_target="tpu_custom_call" | custom-call | flops 700000000 | bytes 8000000 | tf_op jit(solution)/shard_map/pallas_call | solution.py:417
  (36 shorter events, 1.5 us)
Async XLA Ops:
  4.4 12.4 %collective-permute-start = (bf16[272,128]{1,0:T(8,128)(2,1)}, bf16[272,128]{1,0:T(8,128)(2,1)S(1)}, u32[]{:S(2)}, u32[]{:S(2)}) collective-permute-start(bf16[272,128]{1,0:T(8,128)(2,1)} %get-tuple-element.51), channel_id=1, source_target_pairs={{0,1},{1,2},{2,3},{3,0},{4,5},{5,6},{6,7},{7,4},{8,9},{9,10},{10,1... | collective-permute-start | bytes 208904 | tf_op jit(solution)/shard_map/ppermute | solution.py:348
  6.9 9.8 %collective-permute-start.1 = (bf16[272,128]{1,0:T(8,128)(2,1)}, bf16[272,128]{1,0:T(8,128)(2,1)S(1)}, u32[]{:S(2)}, u32[]{:S(2)}) collective-permute-start(bf16[272,128]{1,0:T(8,128)(2,1)} %get-tuple-element.52), channel_id=1, source_target_pairs={{0,2},{1,3},{2,0},{3,1},{4,6},{5,7},{6,4},{7,5},{8,10},{9,11},{10,... | collective-permute-start | bytes 208904 | tf_op jit(solution)/shard_map/ppermute | solution.py:348
  10.2 6.5 %collective-permute-start.2 = (bf16[272,128]{1,0:T(8,128)(2,1)}, bf16[272,128]{1,0:T(8,128)(2,1)S(1)}, u32[]{:S(2)}, u32[]{:S(2)}) collective-permute-start(bf16[272,128]{1,0:T(8,128)(2,1)} %get-tuple-element.53), channel_id=1, source_target_pairs={{0,3},{1,0},{2,1},{3,2},{4,7},{5,4},{6,5},{7,6},{8,11},{9,8},{10,9... | collective-permute-start | bytes 208904 | tf_op jit(solution)/shard_map/ppermute | solution.py:348
  11.0 7.4 %copy-start.6 = (bf16[272,128]{1,0:T(8,128)(2,1)S(1)}, bf16[272,128]{1,0:T(8,128)(2,1)}, u32[]{:S(2)}) copy-start(bf16[272,128]{1,0:T(8,128)(2,1)} %get-tuple-element.60.a_ref) | copy-start | bytes 208900
  11.0 11.3 %copy-start.11 = (s32[1,256]{1,0:T(1,128)S(1)}, s32[1,256]{1,0:T(1,128)}, u32[]{:S(2)}) copy-start(s32[1,256]{1,0:T(1,128)} %index_ref.1) | copy-start | bytes 3076
  16.7 15.0 %copy-start.3 = (bf16[512,512]{1,0:T(8,128)(2,1)S(1)}, bf16[512,512]{1,0:T(8,128)(2,1)}, u32[]{:S(2)}) copy-start(bf16[512,512]{1,0:T(8,128)(2,1)} %get-tuple-element.74.keep_ref) | copy-start | bytes 1572868
  16.7 15.0 %copy-start.4 = (bf16[1024,256]{1,0:T(8,128)(2,1)S(1)}, bf16[1024,256]{1,0:T(8,128)(2,1)}, u32[]{:S(2)}) copy-start(bf16[1024,256]{1,0:T(8,128)(2,1)} %get-tuple-element.76.tx_ref) | copy-start | bytes 1572868
  16.8 15.0 %collective-permute-start.9 = (bf16[512,512]{1,0:T(8,128)(2,1)}, bf16[512,512]{1,0:T(8,128)(2,1)S(1)}, u32[]{:S(2)}, u32[]{:S(2)}) collective-permute-start(bf16[512,512]{1,0:T(8,128)(2,1)} %get-tuple-element.75), channel_id=1, source_target_pairs={{0,16},{16,0},{1,17},{17,1},{2,18},{18,2},{3,19},{19,3},{4,20},{20... | collective-permute-start | bytes 1572872 | tf_op jit(solution)/shard_map/ppermute | solution.py:398
  18.5 5.2 %collective-permute-start.5 = (bf16[272,128]{1,0:T(8,128)(2,1)S(1)}, bf16[272,128]{1,0:T(8,128)(2,1)S(1)}, u32[]{:S(2)}, u32[]{:S(2)}) collective-permute-start(bf16[272,128]{1,0:T(8,128)(2,1)S(1)} %shard_map.130.ta_ref), channel_id=1, source_target_pairs={{0,12},{4,0},{8,4},{12,8},{1,13},{5,1},{9,5},{13,9},{2,14},{6,2},{... | collective-permute-start | bytes 208904 | tf_op jit(solution)/shard_map/ppermute | solution.py:348
  21.3 4.7 %collective-permute-start.4 = (bf16[272,128]{1,0:T(8,128)(2,1)S(1)}, bf16[272,128]{1,0:T(8,128)(2,1)S(1)}, u32[]{:S(2)}, u32[]{:S(2)}) collective-permute-start(bf16[272,128]{1,0:T(8,128)(2,1)S(1)} %shard_map.130.ta_ref), channel_id=1, source_target_pairs={{0,8},{4,12},{8,0},{12,4},{1,9},{5,13},{9,1},{13,5},{2,10},{6,14},... | collective-permute-start | bytes 208904 | tf_op jit(solution)/shard_map/ppermute | solution.py:348
  21.6 6.7 %collective-permute-start.3 = (bf16[272,128]{1,0:T(8,128)(2,1)S(1)}, bf16[272,128]{1,0:T(8,128)(2,1)S(1)}, u32[]{:S(2)}, u32[]{:S(2)}) collective-permute-start(bf16[272,128]{1,0:T(8,128)(2,1)S(1)} %shard_map.130.ta_ref), channel_id=1, source_target_pairs={{0,4},{4,8},{8,12},{12,0},{1,5},{5,9},{9,13},{13,1},{2,6},{6,10},{... | collective-permute-start | bytes 208904 | tf_op jit(solution)/shard_map/ppermute | solution.py:348
  22.3 0.7 copy-start.12
  23.0 11.5 %copy-start = (bf16[512,1280]{1,0:T(8,128)(2,1)S(1)}, bf16[512,1280]{1,0:T(8,128)(2,1)}, u32[]{:S(2)}) copy-start(bf16[512,1280]{1,0:T(8,128)(2,1)} %w_in_ref.5) | copy-start | bytes 3932164
  23.0 11.5 %copy-start.1 = (bf16[256,512]{1,0:T(8,128)(2,1)S(1)}, bf16[256,512]{1,0:T(8,128)(2,1)}, u32[]{:S(2)}) copy-start(bf16[256,512]{1,0:T(8,128)(2,1)} %w_up_ref.3) | copy-start | bytes 786436
  23.0 11.5 %copy-start.2 = (bf16[1024,256]{1,0:T(8,128)(2,1)S(1)}, bf16[1024,256]{1,0:T(8,128)(2,1)}, u32[]{:S(2)}) copy-start(bf16[1024,256]{1,0:T(8,128)(2,1)} %get-tuple-element.89.dx_ref) | copy-start | bytes 1572868
  23.0 11.5 %copy-start.5 = (bf16[1,256,256]{2,1,0:T(8,128)(2,1)S(1)}, bf16[1,256,256]{2,1,0:T(8,128)(2,1)}, u32[]{:S(2)}) copy-start(bf16[1,256,256]{2,1,0:T(8,128)(2,1)} %param.9) | copy-start | bytes 393220
  23.0 11.5 %copy-start.7 = (f32[128,256]{1,0:T(8,128)S(1)}, f32[128,256]{1,0:T(8,128)}, u32[]{:S(2)}) copy-start(f32[128,256]{1,0:T(8,128)} %get-tuple-element.85.dbt_ref) | copy-start | bytes 393220
  23.0 11.5 %copy-start.8 = (bf16[128,256]{1,0:T(8,128)(2,1)S(1)}, bf16[128,256]{1,0:T(8,128)(2,1)}, u32[]{:S(2)}) copy-start(bf16[128,256]{1,0:T(8,128)(2,1)} %get-tuple-element.83.bt_ref) | copy-start | bytes 196612
  23.0 11.5 %copy-start.9 = (bf16[128,256]{1,0:T(8,128)(2,1)S(1)}, bf16[128,256]{1,0:T(8,128)(2,1)}, u32[]{:S(2)}) copy-start(bf16[128,256]{1,0:T(8,128)(2,1)} %get-tuple-element.86.dct_ref) | copy-start | bytes 196612
  23.0 11.5 %copy-start.10 = (f32[16,256]{1,0:T(8,128)S(1)}, f32[16,256]{1,0:T(8,128)}, u32[]{:S(2)}) copy-start(f32[16,256]{1,0:T(8,128)} %get-tuple-element.57.cum_ref) | copy-start | bytes 49156
  28.5 4.4 %collective-permute-start.6 = (bf16[256,128]{1,0:T(8,128)(2,1)S(1)}, bf16[256,128]{1,0:T(8,128)(2,1)S(1)}, u32[]{:S(2)}, u32[]{:S(2)}) collective-permute-start(bf16[256,128]{1,0:T(8,128)(2,1)S(1)} %get-tuple-element.71), channel_id=1, source_target_pairs={{0,1},{1,2},{2,3},{3,0},{4,5},{5,6},{6,7},{7,4},{8,9},{9,10},{10,1... | collective-permute-start | bytes 196616 | tf_op jit(solution)/shard_map/ppermute | solution.py:348
  29.3 4.7 %collective-permute-start.7 = (bf16[256,128]{1,0:T(8,128)(2,1)S(1)}, bf16[256,128]{1,0:T(8,128)(2,1)S(1)}, u32[]{:S(2)}, u32[]{:S(2)}) collective-permute-start(bf16[256,128]{1,0:T(8,128)(2,1)S(1)} %get-tuple-element.72), channel_id=1, source_target_pairs={{0,2},{1,3},{2,0},{3,1},{4,6},{5,7},{6,4},{7,5},{8,10},{9,11},{10,... | collective-permute-start | bytes 196616 | tf_op jit(solution)/shard_map/ppermute | solution.py:348
  29.4 5.0 %collective-permute-start.8 = (bf16[256,128]{1,0:T(8,128)(2,1)S(1)}, bf16[256,128]{1,0:T(8,128)(2,1)S(1)}, u32[]{:S(2)}, u32[]{:S(2)}) collective-permute-start(bf16[256,128]{1,0:T(8,128)(2,1)S(1)} %get-tuple-element.73), channel_id=1, source_target_pairs={{0,3},{1,0},{2,1},{3,2},{4,7},{5,4},{6,5},{7,6},{8,11},{9,8},{10,9... | collective-permute-start | bytes 196616 | tf_op jit(solution)/shard_map/ppermute | solution.py:348
  89.5 4.9 %collective-permute-start.10 = (bf16[512,896]{1,0:T(8,128)(2,1)S(1)}, bf16[512,896]{1,0:T(8,128)(2,1)S(1)}, u32[]{:S(2)}, u32[]{:S(2)}) collective-permute-start(bf16[512,896]{1,0:T(8,128)(2,1)S(1)} %bitcast.15), channel_id=1, source_target_pairs={{0,16},{16,0},{1,17},{17,1},{2,18},{18,2},{3,19},{19,3},{4,20},{20... | collective-permute-start | bytes 2752520 | tf_op jit(solution)/shard_map/ppermute | solution.py:411

commit v13 on v11

--- a/solution.py
+++ b/solution.py
@@ -157,8 +157,8 @@
         ref[...] = ct_ref[(z + k) & 3]
 
 
-def local_kernel(u_ref, c_ref, w_in_ref, dy_ref, cum_ref, cumt_ref, h0_ref, dout_ref, skip_ref, core_ref,
-                 keep_ref, give_ref, dx_ref, tx_ref, bt_ref, dbt_ref, dct_ref, extra_ref, x_ref, y_ref, sdy_ref, h0t_ref, sum_ref):
+def local_kernel(u_ref, c_ref, w_in_ref, dy_ref, cum_ref, cumt_ref, h0_ref, skip_ref,
+                 yt_ref, dx_ref, tx_ref, bt_ref, dbt_ref, dct_ref, extra_ref, x_ref, y_ref, sdy_ref, h0t_ref, sum_ref):
     x_ref[...] = dot(u_ref[...], w_in_ref[:, : INNER + N]).astype(BF)
     proj_t = jnp.transpose(x_ref[...])
     bt = proj_t[INNER:, :]
@@ -202,7 +202,7 @@
         st = start[h : h + 1, :]
         skip = skip_ref[h]
         y_ref[lo:hi, :] = dot(x_h, weights) + SC * st * y_ref[lo:hi, :] + skip * x_f
-        dx_ref[lo:hi, :] = dot(dy_h, weights, NT) + skip * dy_f
+        dx_ref[lo:hi, :] = (dot(dy_h, weights, NT) + skip * dy_f).astype(BF)
         sdy_ref[lo:hi, :] = (st * dy_f).astype(BF)
         tx_ref[lo:hi, :] = (tail[h : h + 1, :] * x_f).astype(BF)
         x_pair = x_ref[:, (h // 2) * N : (h // 2 + 1) * N]
@@ -213,12 +213,7 @@
         a01 += m01 * q0[:, N:]
         a11 += m11 * q11
         skip_sums.append(jnp.sum(x_f * dy_f, keepdims=True))
-    core = core_ref[0]
-    half = INNER // 2
-    mine = pl.ds(pl.multiple_of(core * half, half), half)
-    other = pl.ds(pl.multiple_of((1 - core) * half, half), half)
-    give_ref[...] = dot(y_ref[other, :].astype(BF), dout_ref[...]).astype(BF)
-    keep_ref[...] = dot(y_ref[mine, :].astype(BF), dout_ref[...]).astype(BF)
+    yt_ref[...] = y_ref[...].astype(BF)
     sum_ref[:N, :N] = a00.astype(BF)
     sum_ref[:N, N:] = a01.astype(BF)
     sum_ref[N:, :N] = zero
@@ -233,6 +228,15 @@
         top = whole.astype(BF).astype(F32)
         extra = extra + jnp.where(lane == 128 + h, top, 0.0) + jnp.where(lane == 160 + h, whole - top, 0.0)
     extra_ref[...] = extra
+
+
+def out_kernel(core_ref, y_ref, dout_ref, keep_ref, give_ref):
+    core = core_ref[0]
+    half = INNER // 2
+    mine = pl.ds(pl.multiple_of(core * half, half), half)
+    other = pl.ds(pl.multiple_of((1 - core) * half, half), half)
+    give_ref[...] = dot(y_ref[other, :], dout_ref[...]).astype(BF)
+    keep_ref[...] = dot(y_ref[mine, :], dout_ref[...]).astype(BF)
 
 
 def slot_kernel(index_ref, extra_ref, misc_ref, hits_ref):
@@ -268,7 +272,7 @@
     entering = dot(carry, bt_ref[...])
     for h in range(H):
         lo, hi = h * HP, (h + 1) * HP
-        d_ref[lo:hi, :] = (dx_ref[lo:hi, :] + tail[h : h + 1, :] * entering[lo:hi, :]).astype(BF)
+        d_ref[lo:hi, :] = (dx_ref[lo:hi, :].astype(F32) + tail[h : h + 1, :] * entering[lo:hi, :]).astype(BF)
     d_ref[INNER + N :, :] = dct_ref[...]
     d_ref[INNER : INNER + N, :] = (dbt_ref[...] + dot(carry, tx_ref[...], TN)).astype(BF)
     d = d_ref[...]
@@ -363,29 +367,30 @@
         ],
     )(z, rows, d_out, decay[0], w_up, w_in, w_out)
     sums = sums[:1] + [hop(v, "z", k + 1) for k, v in enumerate(sums[1:])]
-    keep, give, dx, tx, bt, dbt, dct, extra = call(
+    yt, dx, tx, bt, dbt, dct, extra = call(
         local_kernel,
-        [((INNER // 2, D), BF), ((INNER // 2, D), BF), ((INNER, T), F32), ((INNER, T), BF), ((N, T), BF),
+        [((INNER, T), BF), ((INNER, T), BF), ((INNER, T), BF), ((N, T), BF),
          ((N, T), F32), ((N, T), BF), ((1, T), F32)],
         BIG, 2_500_000_000, 6_000_000,
-        in_specs=[VM] * 8 + [SM] * 2, out_specs=(VM,) * 8,
+        in_specs=[VM] * 7 + [SM], out_specs=(VM,) * 7,
         scratch_shapes=[
             pltpu.VMEM((T, INNER + N), BF),
             pltpu.VMEM((INNER, T), F32), pltpu.VMEM((INNER, T), BF),
             pltpu.VMEM((INNER, N), BF), pltpu.VMEM((T, T), BF),
         ],
-    )(u, c_nat, w_in, dy, cum, cumt, jnp.swapaxes(saved_state[0, 0], 1, 2).reshape(INNER, N), d_out, skip, core)
-    sums, give = lax.optimization_barrier((sums, give))
+    )(u, c_nat, w_in, dy, cum, cumt, jnp.swapaxes(saved_state[0, 0], 1, 2).reshape(INNER, N), skip)
+    sums, yt = lax.optimization_barrier((sums, yt))
     (total,) = call(
         inner_kernel, [((MR, N), BF)], 8, 2_000_000, 400_000,
         in_specs=[SM] + [VM] * 4, out_specs=(VM,), scratch_shapes=[pltpu.VMEM((4, MR, N), BF)],
     )(z, *sums)
+    total, yt = lax.optimization_barrier((total, yt))
     totals = [total] + [hop(total, "y", k) for k in range(1, 4)]
-    misc, hits = call(
-        slot_kernel, [((8 * DEV, E), BF), ((8 * DEV, T), BF)], 16, 300_000_000, 1_500_000,
-        in_specs=[VM] * 2, out_specs=(VM,) * 2,
-    )(event_index, extra)
-    totals, hits = lax.optimization_barrier((totals, hits))
+    keep, give = call(
+        out_kernel, [((INNER // 2, D), BF), ((INNER // 2, D), BF)], BIG, 270_000_000, 2_000_000,
+        in_specs=[SM] + [VM] * 2, out_specs=(VM,) * 2,
+    )(core, yt, d_out)
+    totals, give, extra = lax.optimization_barrier((totals, give, extra))
     carries = call(
         outer_kernel, [((GR, N), BF)] * 4, 8, 4_000_000, 800_000,
         in_specs=[SM] * 2 + [VM] * 8, out_specs=(VM,) * 4,
@@ -395,7 +400,11 @@
     outer, tx = call(
         pair_kernel, [((8 * DEV, E), BF), ((INNER, T), BF)], 8, 300_000, 3_000_000, in_specs=[VM] * 3, out_specs=(VM,) * 2
     )(keep, lax.ppermute(give, "core", [(0, 1), (1, 0)]), tx)
-    carries, outer = lax.optimization_barrier((carries, outer))
+    misc, hits = call(
+        slot_kernel, [((8 * DEV, E), BF), ((8 * DEV, T), BF)], 16, 300_000_000, 1_500_000,
+        in_specs=[VM] * 2, out_specs=(VM,) * 2,
+    )(event_index, extra)
+    carries, outer, hits = lax.optimization_barrier((carries, outer, hits))
     (pay,) = call(
         finish_kernel, [((8 * DEV, 3 * E), BF)], 36, 1_400_000_000, 6_000_000,
         in_specs=[SM] + [VM] * 16, out_specs=(VM,),

time: 97.9 us -> 97.7 us (level)
  Pallas kernels: 18 us -> 19.9 us
  local copies, waits for them, and re-layouts: 1.77 us -> 0.05 us
  waiting for transfers between devices: 6.25 us -> 4.6 us
  starting transfers between devices: 18.1 us -> 19.5 us
    pallas_call x1 -> x2, Pallas kernels: 5.92 us -> 7.8 us  [the longest x1 5.42 us: local(): call(local_kernel, [((INNER, T), BF), ((INNER, T), BF), ((INNER, T), BF),...]
    unnamed x26, local copies, waits for them, and re-layouts: 1.77 us -> 0.05 us
    ppermute x9, waiting for transfers between devices: 6.21 us -> 4.57 us  [hop(): return lax.ppermute(value, axis, [(i, (i + step) % 4) for i in range(4)])]
    ppermute x1, starting transfers between devices: 1.6 us -> 2.95 us  [local(): lax.ppermute(give, 'core', [(0, 1), (1, 0)])]
  transfers between devices with their start and end apart: 11 -> 11, of which waited for: 4 -> 5; matrix products, arithmetic and copies ran while one was open for 1% -> 1% of each run, Pallas kernels for 9% -> 10%
where the time goes in v13:
time: 97.7 us; the launch traced here: 97.5 us
  blocking collectives  52 us (53%)
  Pallas kernels  19.9 us (20%)
  starting transfers between devices  19.5 us (20%)
  waiting for transfers between devices  4.6 us (5%)
    all_to_all x1, blocking collectives, local(): lax.all_to_all(pay.reshape(DEV, 8, 3 * E), every, 0, 0, tiled=True)  31.6 us
    all_to_all x1, blocking collectives, local(): lax.all_to_all(chunk, ('x', 'y', 'z'), 0, 0, tiled=True)  20.4 us
    ppermute x9, starting transfers between devices, hop(): return lax.ppermute(value, axis, [(i, (i + step) % 4) for i in range(4)])  13.7 us
    pallas_call x1, Pallas kernels, local(): call(local_kernel, [((INNER, T), BF), ((INNER, T), BF), ((INNER, T), BF),...  5.42 us
    ppermute x9, waiting for transfers between devices, hop(): return lax.ppermute(value, axis, [(i, (i + step) % 4) for i in range(4)])  4.57 us
    pallas_call x1, Pallas kernels, local(): call(project_kernel, [((T, D), BF), ((T, N), BF), ((INNER, T), BF), ((H,...  3.74 us
    pallas_call x1, Pallas kernels, local(): pl.pallas_call(last_kernel, grid=(2,), out_shape=tuple((jax.ShapeDtypeStr...  3.44 us
    ppermute x1, starting transfers between devices, local(): lax.ppermute(give, 'core', [(0, 1), (1, 0)])  2.95 us
  transfers between devices with their start and end apart: 11, of which 5 were waited for; matrix products, arithmetic and copies ran while one was open for 1% of the time, Pallas kernels for 10%

profile of v13, /device:TPU:1, one launch (start us, length us, event | category | flops | bytes accessed | tf_op | source)
XLA Modules:
  0.0 97.5 jit_solution(8608754598992753397)
XLA Ops:
  0.6 3.7 %shard_map.128 = (bf16[256,512]{1,0:T(8,128)(2,1)}, bf16[256,128]{1,0:T(8,128)(2,1)}, bf16[1024,256]{1,0:T(8,128)(2,1)}, f32[16,256]{1,0:T(8,128)}, f32[256,16]{...) custom-call(s32[1]{0:T(128)} %bitcast.1.z_ref, ...), custom_call_target="tpu_custom_call" | custom-call | flops 750000000 | bytes 4500000 | tf_op jit(solution)/shard_map/pallas_call | solution.py:358
  4.4 2.5 %collective-permute-start = (bf16[272,128]{1,0:T(8,128)(2,1)}, bf16[272,128]{1,0:T(8,128)(2,1)S(1)}, u32[]{:S(2)}, u32[]{:S(2)}) collective-permute-start(bf16[272,128]{1,0:T(8,128)(2,1)} %get-tuple-element.56), channel_id=1, source_target_pairs={{0,1},{1,2},{2,3},{3,0},{4,5},{5,6},{6,7},{7,4},{8,9},{9,10},{10,1... | collective-permute-start | bytes 208904 | tf_op jit(solution)/shard_map/ppermute | solution.py:351
  6.9 3.3 %collective-permute-start.1 = (bf16[272,128]{1,0:T(8,128)(2,1)}, bf16[272,128]{1,0:T(8,128)(2,1)S(1)}, u32[]{:S(2)}, u32[]{:S(2)}) collective-permute-start(bf16[272,128]{1,0:T(8,128)(2,1)} %get-tuple-element.57), channel_id=1, source_target_pairs={{0,2},{1,3},{2,0},{3,1},{4,6},{5,7},{6,4},{7,5},{8,10},{9,11},{10,... | collective-permute-start | bytes 208904 | tf_op jit(solution)/shard_map/ppermute | solution.py:351
  10.2 0.7 collective-permute-start.2
  11.0 5.4 %shard_map.129 = (bf16[1024,256]{1,0:T(8,128)(2,1)}, bf16[1024,256]{1,0:T(8,128)(2,1)}, bf16[1024,256]{1,0:T(8,128)(2,1)}, bf16[128,256]{1,0:T(8,128)(2,1)}, f32...) custom-call(bf16[256,512]{1,0:T(8,128)(2,1)} %get-tuple-element.59.u_ref, ...), custom_call_target="tpu_custom_call" | custom-call | flops 2500000000 | bytes 6000000 | tf_op jit(solution)/shard_map/pallas_call | solution.py:370
  16.6 2.8 %collective-permute-start.5 = (bf16[272,128]{1,0:T(8,128)(2,1)S(1)}, bf16[272,128]{1,0:T(8,128)(2,1)S(1)}, u32[]{:S(2)}, u32[]{:S(2)}) collective-permute-start(bf16[272,128]{1,0:T(8,128)(2,1)S(1)} %shard_map.130.ta_ref), channel_id=1, source_target_pairs={{0,12},{4,0},{8,4},{12,8},{1,13},{5,1},{9,5},{13,9},{2,14},{6,2},{... | collective-permute-start | bytes 208904 | tf_op jit(solution)/shard_map/ppermute | solution.py:351
  19.7 0.7 collective-permute-start.3
  20.4 2.4 %shard_map.131 = (bf16[512,512]{1,0:T(8,128)(2,1)}, bf16[512,512]{1,0:T(8,128)(2,1)}) custom-call(s32[1]{0:T(128)} %bitcast.core_ref, bf16[1024,256]{1,0:T(8,128)(2,1)} %get-tuple-element.71.y_ref, bf16[256,512]{1,0:T(8,128)(2,1)} %bitcast.21), custom_call_target="tpu_custom_call" | custom-call | flops 270000000 | bytes 2000000 | tf_op jit(solution)/shard_map/pallas_call | solution.py:389
  22.8 1.3 %collective-permute-done.4.tc_ref = bf16[272,128]{1,0:T(8,128)(2,1)S(1)} collective-permute-done((bf16[272,128]{1,0:T(8,128)(2,1)S(1)}, bf16[272,128]{1,0:T(8,128)(2,1)S(1)}, u32[]{:S(2)}, u32[]{:S(2)}) %collective-permute-start.4) | collective-permute-done | bytes 69664 | tf_op jit(solution)/shard_map/ppermute | solution.py:351
  24.1 0.7 collective-permute-done.3.tb_ref
  24.8 2.9 %collective-permute-start.9 = (bf16[512,512]{1,0:T(8,128)(2,1)}, bf16[512,512]{1,0:T(8,128)(2,1)S(1)}, u32[]{:S(2)}, u32[]{:S(2)}) collective-permute-start(bf16[512,512]{1,0:T(8,128)(2,1)} %get-tuple-element.83), channel_id=1, source_target_pairs={{0,16},{16,0},{1,17},{17,1},{2,18},{18,2},{3,19},{19,3},{4,20},{20... | collective-permute-start | bytes 1572872 | tf_op jit(solution)/shard_map/ppermute | solution.py:402
  27.9 0.8 collective-permute-start.6
  29.1 2.1 %collective-permute-start.8 = (bf16[256,128]{1,0:T(8,128)(2,1)S(1)}, bf16[256,128]{1,0:T(8,128)(2,1)S(1)}, u32[]{:S(2)}, u32[]{:S(2)}) collective-permute-start(bf16[256,128]{1,0:T(8,128)(2,1)S(1)} %get-tuple-element.81), channel_id=1, source_target_pairs={{0,3},{1,0},{2,1},{3,2},{4,7},{5,4},{6,5},{7,6},{8,11},{9,8},{10,9... | collective-permute-start | bytes 196616 | tf_op jit(solution)/shard_map/ppermute | solution.py:351
  31.2 0.6 shard_map.134
  32.0 0.9 collective-permute-done.6.c1_ref
  32.9 0.5 collective-permute-done.7.c2_ref
  33.5 1.1 %collective-permute-done.8.c3_ref = bf16[256,128]{1,0:T(8,128)(2,1)S(1)} collective-permute-done((bf16[256,128]{1,0:T(8,128)(2,1)S(1)}, bf16[256,128]{1,0:T(8,128)(2,1)S(1)}, u32[]{:S(2)}, u32[]{:S(2)}) %collective-permute-start.8) | collective-permute-done | bytes 65568 | tf_op jit(solution)/shard_map/ppermute | solution.py:351
  34.7 2.1 %shard_map.135 = bf16[1024,768]{1,0:T(8,128)(2,1)S(1)} custom-call(s32[1]{0:T(128)} %bitcast.1.z_ref, bf16[256,128]{1,0:T(8,128)(2,1)S(1)} %get-tuple-element.88.c0_ref, bf16[256,128]{1,0:T(8,128)(2,1)S(1)} %collective-permute-done.6.c1_ref, bf16[256,128]{1,0:T(8,128)(2,1)S(1)} %collective-permute-done.7.c2_ref, ...), custom_call_target="tpu_custom_call" | custom-call | flops 1400000000 | bytes 6000000 | tf_op jit(solution)/shard_map/pallas_call | solution.py:408
  36.8 31.6 %all_to_all.10.got_ref = bf16[128,8,768]{2,1,0:T(8,128)(2,1)S(1)} all-to-all(bf16[128,8,768]{2,1,0:T(8,128)(2,1)S(1)} %bitcast.15), channel_id=1, replica_groups=mesh['x'=4,'core'=2,'y'=4,'z'=4] {'x','core','y','z'}, dimensions={0} | all-to-all | bytes 3145728 | tf_op jit(solution)/shard_map/all_to_all | solution.py:413
  68.7 20.4 %all_to_all.11 = bf16[64,8,896]{2,1,0:T(8,128)(2,1)S(1)} all-to-all(bf16[64,8,896]{2,1,0:T(8,128)(2,1)S(1)} %get-tuple-element.100), channel_id=1, replica_groups=mesh['x'=4,'core'=2,'y'=4,'z'=4] {'x','y','z'}, dimensions={0} | all-to-all | bytes 1835008 | tf_op jit(solution)/shard_map/all_to_all | solution.py:418
  89.1 2.8 %collective-permute-start.10 = (bf16[512,896]{1,0:T(8,128)(2,1)S(1)}, bf16[512,896]{1,0:T(8,128)(2,1)S(1)}, u32[]{:S(2)}, u32[]{:S(2)}) collective-permute-start(bf16[512,896]{1,0:T(8,128)(2,1)S(1)} %bitcast.16), channel_id=1, source_target_pairs={{0,16},{16,0},{1,17},{17,1},{2,18},{18,2},{3,19},{19,3},{4,20},{20... | collective-permute-start | bytes 2752520 | tf_op jit(solution)/shard_map/ppermute | solution.py:419
  91.9 1.5 %shard_map.138 = f32[512,256]{1,0:T(8,128)} custom-call(bf16[128,8,768]{2,1,0:T(8,128)(2,1)S(1)} %all_to_all.10.got_ref), custom_call_target="tpu_custom_call" | custom-call | flops 400000000 | bytes 2000000 | tf_op jit(solution)/shard_map/pallas_call | solution.py:420
  93.4 0.6 add_bitcast_fusion
  94.0 3.4 %shard_map.137 = (f32[256,512]{1,0:T(8,128)}, f32[512,1280]{1,0:T(8,128)}, f32[1024,512]{1,0:T(8,128)}) custom-call(s32[1]{0:T(128)} %bitcast.core_ref, bf16[512,896]{1,0:T(8,128)(2,1)S(1)} %bitcast.17, bf16[512,896]{1,0:T(8,128)(2,1)S(1)} %collective-permute-done.10.other_ref, bf16[256,512]{1,0:T(8,128)(2,1)S(1)} %copy-done.1, bf16[512,1280]{1,0:T(8,128)(2,1)S(1)} %copy-done), custom_call_target="tpu_custom_call" | custom-call | flops 700000000 | bytes 8000000 | tf_op jit(solution)/shard_map/pallas_call | solution.py:425
  (38 shorter events, 1.6 us)
Async XLA Ops:
  4.4 12.0 %collective-permute-start = (bf16[272,128]{1,0:T(8,128)(2,1)}, bf16[272,128]{1,0:T(8,128)(2,1)S(1)}, u32[]{:S(2)}, u32[]{:S(2)}) collective-permute-start(bf16[272,128]{1,0:T(8,128)(2,1)} %get-tuple-element.56), channel_id=1, source_target_pairs={{0,1},{1,2},{2,3},{3,0},{4,5},{5,6},{6,7},{7,4},{8,9},{9,10},{10,1... | collective-permute-start | bytes 208904 | tf_op jit(solution)/shard_map/ppermute | solution.py:351
  6.9 9.5 %collective-permute-start.1 = (bf16[272,128]{1,0:T(8,128)(2,1)}, bf16[272,128]{1,0:T(8,128)(2,1)S(1)}, u32[]{:S(2)}, u32[]{:S(2)}) collective-permute-start(bf16[272,128]{1,0:T(8,128)(2,1)} %get-tuple-element.57), channel_id=1, source_target_pairs={{0,2},{1,3},{2,0},{3,1},{4,6},{5,7},{6,4},{7,5},{8,10},{9,11},{10,... | collective-permute-start | bytes 208904 | tf_op jit(solution)/shard_map/ppermute | solution.py:351
  10.2 6.2 %collective-permute-start.2 = (bf16[272,128]{1,0:T(8,128)(2,1)}, bf16[272,128]{1,0:T(8,128)(2,1)S(1)}, u32[]{:S(2)}, u32[]{:S(2)}) collective-permute-start(bf16[272,128]{1,0:T(8,128)(2,1)} %get-tuple-element.58), channel_id=1, source_target_pairs={{0,3},{1,0},{2,1},{3,2},{4,7},{5,4},{6,5},{7,6},{8,11},{9,8},{10,9... | collective-permute-start | bytes 208904 | tf_op jit(solution)/shard_map/ppermute | solution.py:351
  11.0 5.5 %copy-start.6 = (bf16[272,128]{1,0:T(8,128)(2,1)S(1)}, bf16[272,128]{1,0:T(8,128)(2,1)}, u32[]{:S(2)}) copy-start(bf16[272,128]{1,0:T(8,128)(2,1)} %get-tuple-element.65.a_ref) | copy-start | bytes 208900
  16.4 14.8 %copy-start.11 = (s32[1,256]{1,0:T(1,128)S(1)}, s32[1,256]{1,0:T(1,128)}, u32[]{:S(2)}) copy-start(s32[1,256]{1,0:T(1,128)} %index_ref.1) | copy-start | bytes 3076
  16.4 14.8 %copy-start.12 = (f32[1,256]{1,0:T(1,128)S(1)}, f32[1,256]{1,0:T(1,128)}, u32[]{:S(2)}) copy-start(f32[1,256]{1,0:T(1,128)} %get-tuple-element.86.extra_ref) | copy-start | bytes 3076
  16.4 15.4 %copy-start.3 = (bf16[1024,256]{1,0:T(8,128)(2,1)S(1)}, bf16[1024,256]{1,0:T(8,128)(2,1)}, u32[]{:S(2)}) copy-start(bf16[1024,256]{1,0:T(8,128)(2,1)} %get-tuple-element.84.tx_ref) | copy-start | bytes 1572868
  16.6 6.2 %collective-permute-start.5 = (bf16[272,128]{1,0:T(8,128)(2,1)S(1)}, bf16[272,128]{1,0:T(8,128)(2,1)S(1)}, u32[]{:S(2)}, u32[]{:S(2)}) collective-permute-start(bf16[272,128]{1,0:T(8,128)(2,1)S(1)} %shard_map.130.ta_ref), channel_id=1, source_target_pairs={{0,12},{4,0},{8,4},{12,8},{1,13},{5,1},{9,5},{13,9},{2,14},{6,2},{... | collective-permute-start | bytes 208904 | tf_op jit(solution)/shard_map/ppermute | solution.py:351
  19.4 4.7 %collective-permute-start.4 = (bf16[272,128]{1,0:T(8,128)(2,1)S(1)}, bf16[272,128]{1,0:T(8,128)(2,1)S(1)}, u32[]{:S(2)}, u32[]{:S(2)}) collective-permute-start(bf16[272,128]{1,0:T(8,128)(2,1)S(1)} %shard_map.130.ta_ref), channel_id=1, source_target_pairs={{0,8},{4,12},{8,0},{12,4},{1,9},{5,13},{9,1},{13,5},{2,10},{6,14},... | collective-permute-start | bytes 208904 | tf_op jit(solution)/shard_map/ppermute | solution.py:351
  19.7 5.1 %collective-permute-start.3 = (bf16[272,128]{1,0:T(8,128)(2,1)S(1)}, bf16[272,128]{1,0:T(8,128)(2,1)S(1)}, u32[]{:S(2)}, u32[]{:S(2)}) collective-permute-start(bf16[272,128]{1,0:T(8,128)(2,1)S(1)} %shard_map.130.ta_ref), channel_id=1, source_target_pairs={{0,4},{4,8},{8,12},{12,0},{1,5},{5,9},{9,13},{13,1},{2,6},{6,10},{... | collective-permute-start | bytes 208904 | tf_op jit(solution)/shard_map/ppermute | solution.py:351
  22.8 9.1 %copy-start.4 = (bf16[512,512]{1,0:T(8,128)(2,1)S(1)}, bf16[512,512]{1,0:T(8,128)(2,1)}, u32[]{:S(2)}) copy-start(bf16[512,512]{1,0:T(8,128)(2,1)} %get-tuple-element.82.keep_ref) | copy-start | bytes 1572868
  24.8 7.1 %collective-permute-start.9 = (bf16[512,512]{1,0:T(8,128)(2,1)}, bf16[512,512]{1,0:T(8,128)(2,1)S(1)}, u32[]{:S(2)}, u32[]{:S(2)}) collective-permute-start(bf16[512,512]{1,0:T(8,128)(2,1)} %get-tuple-element.83), channel_id=1, source_target_pairs={{0,16},{16,0},{1,17},{17,1},{2,18},{18,2},{3,19},{19,3},{4,20},{20... | collective-permute-start | bytes 1572872 | tf_op jit(solution)/shard_map/ppermute | solution.py:402
  27.7 6.9 %copy-start = (bf16[512,1280]{1,0:T(8,128)(2,1)S(1)}, bf16[512,1280]{1,0:T(8,128)(2,1)}, u32[]{:S(2)}) copy-start(bf16[512,1280]{1,0:T(8,128)(2,1)} %w_in_ref.5) | copy-start | bytes 3932164
  27.7 6.9 %copy-start.1 = (bf16[256,512]{1,0:T(8,128)(2,1)S(1)}, bf16[256,512]{1,0:T(8,128)(2,1)}, u32[]{:S(2)}) copy-start(bf16[256,512]{1,0:T(8,128)(2,1)} %w_up_ref.3) | copy-start | bytes 786436
  27.7 6.9 %copy-start.2 = (bf16[1024,256]{1,0:T(8,128)(2,1)S(1)}, bf16[1024,256]{1,0:T(8,128)(2,1)}, u32[]{:S(2)}) copy-start(bf16[1024,256]{1,0:T(8,128)(2,1)} %get-tuple-element.99.dx_ref) | copy-start | bytes 1572868
  27.7 6.9 %copy-start.5 = (bf16[1,256,256]{2,1,0:T(8,128)(2,1)S(1)}, bf16[1,256,256]{2,1,0:T(8,128)(2,1)}, u32[]{:S(2)}) copy-start(bf16[1,256,256]{2,1,0:T(8,128)(2,1)} %param.9) | copy-start | bytes 393220
  27.7 6.9 %copy-start.7 = (f32[128,256]{1,0:T(8,128)S(1)}, f32[128,256]{1,0:T(8,128)}, u32[]{:S(2)}) copy-start(f32[128,256]{1,0:T(8,128)} %get-tuple-element.95.dbt_ref) | copy-start | bytes 393220
  27.7 6.9 %copy-start.8 = (bf16[128,256]{1,0:T(8,128)(2,1)S(1)}, bf16[128,256]{1,0:T(8,128)(2,1)}, u32[]{:S(2)}) copy-start(bf16[128,256]{1,0:T(8,128)(2,1)} %get-tuple-element.93.bt_ref) | copy-start | bytes 196612
  27.7 6.9 %copy-start.9 = (bf16[128,256]{1,0:T(8,128)(2,1)S(1)}, bf16[128,256]{1,0:T(8,128)(2,1)}, u32[]{:S(2)}) copy-start(bf16[128,256]{1,0:T(8,128)(2,1)} %get-tuple-element.96.dct_ref) | copy-start | bytes 196612
  27.8 6.9 %copy-start.10 = (f32[16,256]{1,0:T(8,128)S(1)}, f32[16,256]{1,0:T(8,128)}, u32[]{:S(2)}) copy-start(f32[16,256]{1,0:T(8,128)} %get-tuple-element.62.cum_ref) | copy-start | bytes 49156
  27.9 5.0 %collective-permute-start.6 = (bf16[256,128]{1,0:T(8,128)(2,1)S(1)}, bf16[256,128]{1,0:T(8,128)(2,1)S(1)}, u32[]{:S(2)}, u32[]{:S(2)}) collective-permute-start(bf16[256,128]{1,0:T(8,128)(2,1)S(1)} %get-tuple-element.79), channel_id=1, source_target_pairs={{0,1},{1,2},{2,3},{3,0},{4,5},{5,6},{6,7},{7,4},{8,9},{9,10},{10,1... | collective-permute-start | bytes 196616 | tf_op jit(solution)/shard_map/ppermute | solution.py:351
  28.7 4.7 %collective-permute-start.7 = (bf16[256,128]{1,0:T(8,128)(2,1)S(1)}, bf16[256,128]{1,0:T(8,128)(2,1)S(1)}, u32[]{:S(2)}, u32[]{:S(2)}) collective-permute-start(bf16[256,128]{1,0:T(8,128)(2,1)S(1)} %get-tuple-element.80), channel_id=1, source_target_pairs={{0,2},{1,3},{2,0},{3,1},{4,6},{5,7},{6,4},{7,5},{8,10},{9,11},{10,... | collective-permute-start | bytes 196616 | tf_op jit(solution)/shard_map/ppermute | solution.py:351
  29.1 5.4 %collective-permute-start.8 = (bf16[256,128]{1,0:T(8,128)(2,1)S(1)}, bf16[256,128]{1,0:T(8,128)(2,1)S(1)}, u32[]{:S(2)}, u32[]{:S(2)}) collective-permute-start(bf16[256,128]{1,0:T(8,128)(2,1)S(1)} %get-tuple-element.81), channel_id=1, source_target_pairs={{0,3},{1,0},{2,1},{3,2},{4,7},{5,4},{6,5},{7,6},{8,11},{9,8},{10,9... | collective-permute-start | bytes 196616 | tf_op jit(solution)/shard_map/ppermute | solution.py:351
  89.1 4.9 %collective-permute-start.10 = (bf16[512,896]{1,0:T(8,128)(2,1)S(1)}, bf16[512,896]{1,0:T(8,128)(2,1)S(1)}, u32[]{:S(2)}, u32[]{:S(2)}) collective-permute-start(bf16[512,896]{1,0:T(8,128)(2,1)S(1)} %bitcast.16), channel_id=1, source_target_pairs={{0,16},{16,0},{1,17},{17,1},{2,18},{18,2},{3,19},{19,3},{4,20},{20... | collective-permute-start | bytes 2752520 | tf_op jit(solution)/shard_map/ppermute | solution.py:419

commit v14 on v13

--- a/solution.py
+++ b/solution.py
@@ -390,12 +390,13 @@
         out_kernel, [((INNER // 2, D), BF), ((INNER // 2, D), BF)], BIG, 270_000_000, 2_000_000,
         in_specs=[SM] + [VM] * 2, out_specs=(VM,) * 2,
     )(core, yt, d_out)
-    totals, give, extra = lax.optimization_barrier((totals, give, extra))
+    totals, keep, extra = lax.optimization_barrier((totals, keep, extra))
     carries = call(
         outer_kernel, [((GR, N), BF)] * 4, 8, 4_000_000, 800_000,
         in_specs=[SM] * 2 + [VM] * 8, out_specs=(VM,) * 4,
         scratch_shapes=[pltpu.VMEM((4, MR, N), BF)] * 2 + [pltpu.VMEM((4, GR, N), BF)],
     )(y, z, *sums, *totals)
+    carries, give = lax.optimization_barrier((carries, give))
     carries = [carries[0]] + [hop(v, "z", k + 1) for k, v in enumerate(carries[1:])]
     outer, tx = call(
         pair_kernel, [((8 * DEV, E), BF), ((INNER, T), BF)], 8, 300_000, 3_000_000, in_specs=[VM] * 3, out_specs=(VM,) * 2

time: 97.7 us -> 97.7 us (level)
  no operation moved by 1% of the time
where the time goes in v14:
time: 97.7 us; the launch traced here: 97.5 us
  blocking collectives  52.1 us (53%)
  Pallas kernels  19.9 us (20%)
  starting transfers between devices  19.4 us (20%)
  waiting for transfers between devices  4.64 us (5%)
    all_to_all x1, blocking collectives, local(): lax.all_to_all(pay.reshape(DEV, 8, 3 * E), every, 0, 0, tiled=True)  31.6 us
    all_to_all x1, blocking collectives, local(): lax.all_to_all(chunk, ('x', 'y', 'z'), 0, 0, tiled=True)  20.4 us
    ppermute x9, starting transfers between devices, hop(): return lax.ppermute(value, axis, [(i, (i + step) % 4) for i in range(4)])  13.6 us
    pallas_call x1, Pallas kernels, local(): call(local_kernel, [((INNER, T), BF), ((INNER, T), BF), ((INNER, T), BF),...  5.42 us
    ppermute x9, waiting for transfers between devices, hop(): return lax.ppermute(value, axis, [(i, (i + step) % 4) for i in range(4)])  4.6 us
    pallas_call x1, Pallas kernels, local(): call(project_kernel, [((T, D), BF), ((T, N), BF), ((INNER, T), BF), ((H,...  3.74 us
    pallas_call x1, Pallas kernels, local(): pl.pallas_call(last_kernel, grid=(2,), out_shape=tuple((jax.ShapeDtypeStr...  3.44 us
    ppermute x1, starting transfers between devices, local(): lax.ppermute(give, 'core', [(0, 1), (1, 0)])  3.02 us
  transfers between devices with their start and end apart: 11, of which 5 were waited for; matrix products, arithmetic and copies ran while one was open for 1% of the time, Pallas kernels for 10%

profile of v14, /device:TPU:1, one launch (start us, length us, event | category | flops | bytes accessed | tf_op | source)
XLA Modules:
  0.0 97.5 jit_solution(17296411552863432276)
XLA Ops:
  0.6 3.7 %shard_map.128 = (bf16[256,512]{1,0:T(8,128)(2,1)}, bf16[256,128]{1,0:T(8,128)(2,1)}, bf16[1024,256]{1,0:T(8,128)(2,1)}, f32[16,256]{1,0:T(8,128)}, f32[256,16]{...) custom-call(s32[1]{0:T(128)} %bitcast.1.z_ref, ...), custom_call_target="tpu_custom_call" | custom-call | flops 750000000 | bytes 4500000 | tf_op jit(solution)/shard_map/pallas_call | solution.py:358
  4.4 2.5 %collective-permute-start = (bf16[272,128]{1,0:T(8,128)(2,1)}, bf16[272,128]{1,0:T(8,128)(2,1)S(1)}, u32[]{:S(2)}, u32[]{:S(2)}) collective-permute-start(bf16[272,128]{1,0:T(8,128)(2,1)} %get-tuple-element.61), channel_id=1, source_target_pairs={{0,1},{1,2},{2,3},{3,0},{4,5},{5,6},{6,7},{7,4},{8,9},{9,10},{10,1... | collective-permute-start | bytes 208904 | tf_op jit(solution)/shard_map/ppermute | solution.py:351
  6.9 3.3 %collective-permute-start.1 = (bf16[272,128]{1,0:T(8,128)(2,1)}, bf16[272,128]{1,0:T(8,128)(2,1)S(1)}, u32[]{:S(2)}, u32[]{:S(2)}) collective-permute-start(bf16[272,128]{1,0:T(8,128)(2,1)} %get-tuple-element.62), channel_id=1, source_target_pairs={{0,2},{1,3},{2,0},{3,1},{4,6},{5,7},{6,4},{7,5},{8,10},{9,11},{10,... | collective-permute-start | bytes 208904 | tf_op jit(solution)/shard_map/ppermute | solution.py:351
  10.2 0.7 collective-permute-start.2
  11.0 5.4 %shard_map.129 = (bf16[1024,256]{1,0:T(8,128)(2,1)}, bf16[1024,256]{1,0:T(8,128)(2,1)}, bf16[1024,256]{1,0:T(8,128)(2,1)}, bf16[128,256]{1,0:T(8,128)(2,1)}, f32...) custom-call(bf16[256,512]{1,0:T(8,128)(2,1)} %get-tuple-element.64.u_ref, ...), custom_call_target="tpu_custom_call" | custom-call | flops 2500000000 | bytes 6000000 | tf_op jit(solution)/shard_map/pallas_call | solution.py:370
  16.6 2.8 %collective-permute-start.5 = (bf16[272,128]{1,0:T(8,128)(2,1)S(1)}, bf16[272,128]{1,0:T(8,128)(2,1)S(1)}, u32[]{:S(2)}, u32[]{:S(2)}) collective-permute-start(bf16[272,128]{1,0:T(8,128)(2,1)S(1)} %shard_map.130.ta_ref), channel_id=1, source_target_pairs={{0,12},{4,0},{8,4},{12,8},{1,13},{5,1},{9,5},{13,9},{2,14},{6,2},{... | collective-permute-start | bytes 208904 | tf_op jit(solution)/shard_map/ppermute | solution.py:351
  19.7 0.7 collective-permute-start.3
  20.4 2.4 %shard_map.131 = (bf16[512,512]{1,0:T(8,128)(2,1)}, bf16[512,512]{1,0:T(8,128)(2,1)}) custom-call(s32[1]{0:T(128)} %bitcast.core_ref, bf16[1024,256]{1,0:T(8,128)(2,1)} %get-tuple-element.76.y_ref, bf16[256,512]{1,0:T(8,128)(2,1)} %bitcast.21), custom_call_target="tpu_custom_call" | custom-call | flops 270000000 | bytes 2000000 | tf_op jit(solution)/shard_map/pallas_call | solution.py:389
  22.8 1.3 %collective-permute-done.4.tc_ref = bf16[272,128]{1,0:T(8,128)(2,1)S(1)} collective-permute-done((bf16[272,128]{1,0:T(8,128)(2,1)S(1)}, bf16[272,128]{1,0:T(8,128)(2,1)S(1)}, u32[]{:S(2)}, u32[]{:S(2)}) %collective-permute-start.4) | collective-permute-done | bytes 69664 | tf_op jit(solution)/shard_map/ppermute | solution.py:351
  24.1 0.7 collective-permute-done.3.tb_ref
  25.0 3.0 %collective-permute-start.9 = (bf16[512,512]{1,0:T(8,128)(2,1)}, bf16[512,512]{1,0:T(8,128)(2,1)S(1)}, u32[]{:S(2)}, u32[]{:S(2)}) collective-permute-start(bf16[512,512]{1,0:T(8,128)(2,1)} %get-tuple-element.93), channel_id=1, source_target_pairs={{0,16},{16,0},{1,17},{17,1},{2,18},{18,2},{3,19},{19,3},{4,20},{20... | collective-permute-start | bytes 1572872 | tf_op jit(solution)/shard_map/ppermute | solution.py:403
  28.0 0.8 collective-permute-start.6
  29.2 2.0 %collective-permute-start.8 = (bf16[256,128]{1,0:T(8,128)(2,1)S(1)}, bf16[256,128]{1,0:T(8,128)(2,1)S(1)}, u32[]{:S(2)}, u32[]{:S(2)}) collective-permute-start(bf16[256,128]{1,0:T(8,128)(2,1)S(1)} %get-tuple-element.91), channel_id=1, source_target_pairs={{0,3},{1,0},{2,1},{3,2},{4,7},{5,4},{6,5},{7,6},{8,11},{9,8},{10,9... | collective-permute-start | bytes 196616 | tf_op jit(solution)/shard_map/ppermute | solution.py:351
  31.2 0.6 shard_map.134
  31.9 0.9 collective-permute-done.6.c1_ref
  32.9 0.6 collective-permute-done.7.c2_ref
  33.5 1.1 %collective-permute-done.8.c3_ref = bf16[256,128]{1,0:T(8,128)(2,1)S(1)} collective-permute-done((bf16[256,128]{1,0:T(8,128)(2,1)S(1)}, bf16[256,128]{1,0:T(8,128)(2,1)S(1)}, u32[]{:S(2)}, u32[]{:S(2)}) %collective-permute-start.8) | collective-permute-done | bytes 65568 | tf_op jit(solution)/shard_map/ppermute | solution.py:351
  34.6 2.1 %shard_map.135 = bf16[1024,768]{1,0:T(8,128)(2,1)S(1)} custom-call(s32[1]{0:T(128)} %bitcast.1.z_ref, bf16[256,128]{1,0:T(8,128)(2,1)S(1)} %get-tuple-element.98.c0_ref, bf16[256,128]{1,0:T(8,128)(2,1)S(1)} %collective-permute-done.6.c1_ref, bf16[256,128]{1,0:T(8,128)(2,1)S(1)} %collective-permute-done.7.c2_ref, ...), custom_call_target="tpu_custom_call" | custom-call | flops 1400000000 | bytes 6000000 | tf_op jit(solution)/shard_map/pallas_call | solution.py:409
  36.7 31.6 %all_to_all.10.got_ref = bf16[128,8,768]{2,1,0:T(8,128)(2,1)S(1)} all-to-all(bf16[128,8,768]{2,1,0:T(8,128)(2,1)S(1)} %bitcast.15), channel_id=1, replica_groups=mesh['x'=4,'core'=2,'y'=4,'z'=4] {'x','core','y','z'}, dimensions={0} | all-to-all | bytes 3145728 | tf_op jit(solution)/shard_map/all_to_all | solution.py:414
  68.7 20.4 %all_to_all.11 = bf16[64,8,896]{2,1,0:T(8,128)(2,1)S(1)} all-to-all(bf16[64,8,896]{2,1,0:T(8,128)(2,1)S(1)} %get-tuple-element.110), channel_id=1, replica_groups=mesh['x'=4,'core'=2,'y'=4,'z'=4] {'x','y','z'}, dimensions={0} | all-to-all | bytes 1835008 | tf_op jit(solution)/shard_map/all_to_all | solution.py:419
  89.1 2.8 %collective-permute-start.10 = (bf16[512,896]{1,0:T(8,128)(2,1)S(1)}, bf16[512,896]{1,0:T(8,128)(2,1)S(1)}, u32[]{:S(2)}, u32[]{:S(2)}) collective-permute-start(bf16[512,896]{1,0:T(8,128)(2,1)S(1)} %bitcast.16), channel_id=1, source_target_pairs={{0,16},{16,0},{1,17},{17,1},{2,18},{18,2},{3,19},{19,3},{4,20},{20... | collective-permute-start | bytes 2752520 | tf_op jit(solution)/shard_map/ppermute | solution.py:420
  92.0 1.5 %shard_map.138 = f32[512,256]{1,0:T(8,128)} custom-call(bf16[128,8,768]{2,1,0:T(8,128)(2,1)S(1)} %all_to_all.10.got_ref), custom_call_target="tpu_custom_call" | custom-call | flops 400000000 | bytes 2000000 | tf_op jit(solution)/shard_map/pallas_call | solution.py:421
  93.4 0.6 add_bitcast_fusion
  94.1 3.4 %shard_map.137 = (f32[256,512]{1,0:T(8,128)}, f32[512,1280]{1,0:T(8,128)}, f32[1024,512]{1,0:T(8,128)}) custom-call(s32[1]{0:T(128)} %bitcast.core_ref, bf16[512,896]{1,0:T(8,128)(2,1)S(1)} %bitcast.17, bf16[512,896]{1,0:T(8,128)(2,1)S(1)} %collective-permute-done.10.other_ref, bf16[256,512]{1,0:T(8,128)(2,1)S(1)} %copy-done.1, bf16[512,1280]{1,0:T(8,128)(2,1)S(1)} %copy-done), custom_call_target="tpu_custom_call" | custom-call | flops 700000000 | bytes 8000000 | tf_op jit(solution)/shard_map/pallas_call | solution.py:426
  (38 shorter events, 1.6 us)
Async XLA Ops:
  4.4 12.0 %collective-permute-start = (bf16[272,128]{1,0:T(8,128)(2,1)}, bf16[272,128]{1,0:T(8,128)(2,1)S(1)}, u32[]{:S(2)}, u32[]{:S(2)}) collective-permute-start(bf16[272,128]{1,0:T(8,128)(2,1)} %get-tuple-element.61), channel_id=1, source_target_pairs={{0,1},{1,2},{2,3},{3,0},{4,5},{5,6},{6,7},{7,4},{8,9},{9,10},{10,1... | collective-permute-start | bytes 208904 | tf_op jit(solution)/shard_map/ppermute | solution.py:351
  6.9 9.5 %collective-permute-start.1 = (bf16[272,128]{1,0:T(8,128)(2,1)}, bf16[272,128]{1,0:T(8,128)(2,1)S(1)}, u32[]{:S(2)}, u32[]{:S(2)}) collective-permute-start(bf16[272,128]{1,0:T(8,128)(2,1)} %get-tuple-element.62), channel_id=1, source_target_pairs={{0,2},{1,3},{2,0},{3,1},{4,6},{5,7},{6,4},{7,5},{8,10},{9,11},{10,... | collective-permute-start | bytes 208904 | tf_op jit(solution)/shard_map/ppermute | solution.py:351
  10.2 6.2 %collective-permute-start.2 = (bf16[272,128]{1,0:T(8,128)(2,1)}, bf16[272,128]{1,0:T(8,128)(2,1)S(1)}, u32[]{:S(2)}, u32[]{:S(2)}) collective-permute-start(bf16[272,128]{1,0:T(8,128)(2,1)} %get-tuple-element.63), channel_id=1, source_target_pairs={{0,3},{1,0},{2,1},{3,2},{4,7},{5,4},{6,5},{7,6},{8,11},{9,8},{10,9... | collective-permute-start | bytes 208904 | tf_op jit(solution)/shard_map/ppermute | solution.py:351
  11.0 5.5 %copy-start.6 = (bf16[272,128]{1,0:T(8,128)(2,1)S(1)}, bf16[272,128]{1,0:T(8,128)(2,1)}, u32[]{:S(2)}) copy-start(bf16[272,128]{1,0:T(8,128)(2,1)} %get-tuple-element.70.a_ref) | copy-start | bytes 208900
  16.4 14.8 %copy-start.11 = (s32[1,256]{1,0:T(1,128)S(1)}, s32[1,256]{1,0:T(1,128)}, u32[]{:S(2)}) copy-start(s32[1,256]{1,0:T(1,128)} %index_ref.1) | copy-start | bytes 3076
  16.4 14.8 %copy-start.12 = (f32[1,256]{1,0:T(1,128)S(1)}, f32[1,256]{1,0:T(1,128)}, u32[]{:S(2)}) copy-start(f32[1,256]{1,0:T(1,128)} %get-tuple-element.96.extra_ref) | copy-start | bytes 3076
  16.4 15.4 %copy-start.3 = (bf16[1024,256]{1,0:T(8,128)(2,1)S(1)}, bf16[1024,256]{1,0:T(8,128)(2,1)}, u32[]{:S(2)}) copy-start(bf16[1024,256]{1,0:T(8,128)(2,1)} %get-tuple-element.94.tx_ref) | copy-start | bytes 1572868
  16.6 6.2 %collective-permute-start.5 = (bf16[272,128]{1,0:T(8,128)(2,1)S(1)}, bf16[272,128]{1,0:T(8,128)(2,1)S(1)}, u32[]{:S(2)}, u32[]{:S(2)}) collective-permute-start(bf16[272,128]{1,0:T(8,128)(2,1)S(1)} %shard_map.130.ta_ref), channel_id=1, source_target_pairs={{0,12},{4,0},{8,4},{12,8},{1,13},{5,1},{9,5},{13,9},{2,14},{6,2},{... | collective-permute-start | bytes 208904 | tf_op jit(solution)/shard_map/ppermute | solution.py:351
  19.4 4.7 %collective-permute-start.4 = (bf16[272,128]{1,0:T(8,128)(2,1)S(1)}, bf16[272,128]{1,0:T(8,128)(2,1)S(1)}, u32[]{:S(2)}, u32[]{:S(2)}) collective-permute-start(bf16[272,128]{1,0:T(8,128)(2,1)S(1)} %shard_map.130.ta_ref), channel_id=1, source_target_pairs={{0,8},{4,12},{8,0},{12,4},{1,9},{5,13},{9,1},{13,5},{2,10},{6,14},... | collective-permute-start | bytes 208904 | tf_op jit(solution)/shard_map/ppermute | solution.py:351
  19.7 5.1 %collective-permute-start.3 = (bf16[272,128]{1,0:T(8,128)(2,1)S(1)}, bf16[272,128]{1,0:T(8,128)(2,1)S(1)}, u32[]{:S(2)}, u32[]{:S(2)}) collective-permute-start(bf16[272,128]{1,0:T(8,128)(2,1)S(1)} %shard_map.130.ta_ref), channel_id=1, source_target_pairs={{0,4},{4,8},{8,12},{12,0},{1,5},{5,9},{9,13},{13,1},{2,6},{6,10},{... | collective-permute-start | bytes 208904 | tf_op jit(solution)/shard_map/ppermute | solution.py:351
  22.8 9.0 %copy-start.4 = (bf16[512,512]{1,0:T(8,128)(2,1)S(1)}, bf16[512,512]{1,0:T(8,128)(2,1)}, u32[]{:S(2)}) copy-start(bf16[512,512]{1,0:T(8,128)(2,1)} %get-tuple-element.92.keep_ref) | copy-start | bytes 1572868
  24.8 9.8 %copy-start = (bf16[512,1280]{1,0:T(8,128)(2,1)S(1)}, bf16[512,1280]{1,0:T(8,128)(2,1)}, u32[]{:S(2)}) copy-start(bf16[512,1280]{1,0:T(8,128)(2,1)} %w_in_ref.5) | copy-start | bytes 3932164
  24.8 9.8 %copy-start.1 = (bf16[256,512]{1,0:T(8,128)(2,1)S(1)}, bf16[256,512]{1,0:T(8,128)(2,1)}, u32[]{:S(2)}) copy-start(bf16[256,512]{1,0:T(8,128)(2,1)} %w_up_ref.3) | copy-start | bytes 786436
  24.8 9.8 %copy-start.2 = (bf16[1024,256]{1,0:T(8,128)(2,1)S(1)}, bf16[1024,256]{1,0:T(8,128)(2,1)}, u32[]{:S(2)}) copy-start(bf16[1024,256]{1,0:T(8,128)(2,1)} %get-tuple-element.109.dx_ref) | copy-start | bytes 1572868
  24.8 9.8 %copy-start.5 = (bf16[1,256,256]{2,1,0:T(8,128)(2,1)S(1)}, bf16[1,256,256]{2,1,0:T(8,128)(2,1)}, u32[]{:S(2)}) copy-start(bf16[1,256,256]{2,1,0:T(8,128)(2,1)} %param.9) | copy-start | bytes 393220
  24.8 9.8 %copy-start.7 = (f32[128,256]{1,0:T(8,128)S(1)}, f32[128,256]{1,0:T(8,128)}, u32[]{:S(2)}) copy-start(f32[128,256]{1,0:T(8,128)} %get-tuple-element.105.dbt_ref) | copy-start | bytes 393220
  24.8 9.8 %copy-start.8 = (bf16[128,256]{1,0:T(8,128)(2,1)S(1)}, bf16[128,256]{1,0:T(8,128)(2,1)}, u32[]{:S(2)}) copy-start(bf16[128,256]{1,0:T(8,128)(2,1)} %get-tuple-element.103.bt_ref) | copy-start | bytes 196612
  24.8 9.8 %copy-start.9 = (bf16[128,256]{1,0:T(8,128)(2,1)S(1)}, bf16[128,256]{1,0:T(8,128)(2,1)}, u32[]{:S(2)}) copy-start(bf16[128,256]{1,0:T(8,128)(2,1)} %get-tuple-element.106.dct_ref) | copy-start | bytes 196612
  24.8 9.8 %copy-start.10 = (f32[16,256]{1,0:T(8,128)S(1)}, f32[16,256]{1,0:T(8,128)}, u32[]{:S(2)}) copy-start(f32[16,256]{1,0:T(8,128)} %get-tuple-element.67.cum_ref) | copy-start | bytes 49156
  25.0 6.8 %collective-permute-start.9 = (bf16[512,512]{1,0:T(8,128)(2,1)}, bf16[512,512]{1,0:T(8,128)(2,1)S(1)}, u32[]{:S(2)}, u32[]{:S(2)}) collective-permute-start(bf16[512,512]{1,0:T(8,128)(2,1)} %get-tuple-element.93), channel_id=1, source_target_pairs={{0,16},{16,0},{1,17},{17,1},{2,18},{18,2},{3,19},{19,3},{4,20},{20... | collective-permute-start | bytes 1572872 | tf_op jit(solution)/shard_map/ppermute | solution.py:403
  28.0 4.9 %collective-permute-start.6 = (bf16[256,128]{1,0:T(8,128)(2,1)S(1)}, bf16[256,128]{1,0:T(8,128)(2,1)S(1)}, u32[]{:S(2)}, u32[]{:S(2)}) collective-permute-start(bf16[256,128]{1,0:T(8,128)(2,1)S(1)} %get-tuple-element.89), channel_id=1, source_target_pairs={{0,1},{1,2},{2,3},{3,0},{4,5},{5,6},{6,7},{7,4},{8,9},{9,10},{10,1... | collective-permute-start | bytes 196616 | tf_op jit(solution)/shard_map/ppermute | solution.py:351
  28.8 4.7 %collective-permute-start.7 = (bf16[256,128]{1,0:T(8,128)(2,1)S(1)}, bf16[256,128]{1,0:T(8,128)(2,1)S(1)}, u32[]{:S(2)}, u32[]{:S(2)}) collective-permute-start(bf16[256,128]{1,0:T(8,128)(2,1)S(1)} %get-tuple-element.90), channel_id=1, source_target_pairs={{0,2},{1,3},{2,0},{3,1},{4,6},{5,7},{6,4},{7,5},{8,10},{9,11},{10,... | collective-permute-start | bytes 196616 | tf_op jit(solution)/shard_map/ppermute | solution.py:351
  29.2 5.4 %collective-permute-start.8 = (bf16[256,128]{1,0:T(8,128)(2,1)S(1)}, bf16[256,128]{1,0:T(8,128)(2,1)S(1)}, u32[]{:S(2)}, u32[]{:S(2)}) collective-permute-start(bf16[256,128]{1,0:T(8,128)(2,1)S(1)} %get-tuple-element.91), channel_id=1, source_target_pairs={{0,3},{1,0},{2,1},{3,2},{4,7},{5,4},{6,5},{7,6},{8,11},{9,8},{10,9... | collective-permute-start | bytes 196616 | tf_op jit(solution)/shard_map/ppermute | solution.py:351
  89.1 4.9 %collective-permute-start.10 = (bf16[512,896]{1,0:T(8,128)(2,1)S(1)}, bf16[512,896]{1,0:T(8,128)(2,1)S(1)}, u32[]{:S(2)}, u32[]{:S(2)}) collective-permute-start(bf16[512,896]{1,0:T(8,128)(2,1)S(1)} %bitcast.16), channel_id=1, source_target_pairs={{0,16},{16,0},{1,17},{17,1},{2,18},{18,2},{3,19},{19,3},{4,20},{20... | collective-permute-start | bytes 2752520 | tf_op jit(solution)/shard_map/ppermute | solution.py:420
